TPU v7x, 256 devices: a whole 4x4x8 slice. The times are simulated.
256 devices in a mesh: seed: 4 (over x), chan: 16 (over z, y_lo), fsdp: 4 (over y_hi, core).
Axes of the slice: x: 4, y: 4 (y_hi: 2, y_lo: 2; y = y_hi * 2 + y_lo), z: 8, core: 2. Of those that a mesh axis runs over, the one named last changes fastest.
Arguments:
- stream: bfloat16 [256, 144, 8192], P(('seed', 'fsdp'), None, 'chan'), parts along dimension 0, may hold values from -12.5 to 9.5
- mid: bfloat16 [256, 144, 2048], P(('seed', 'fsdp'), None, 'chan'), parts along dimension 0, may hold values from 0 to 2
- conv_weight: bfloat16 [8192, 8192], P(('seed', 'fsdp'), 'chan'), parts along dimension 0, may hold values from -0.125 to 0.125
- head_weight: bfloat16 [32768, 16384], P(('seed', 'chan'), 'fsdp'), parts along dimension 0, may hold values from -0.375 to 0.375
- labels: int32 [64], replicated, may hold values from 0 to 16383
- proj_act: bfloat16 [2048, 32], replicated, may hold values from -0.125 to 0.125
- proj_err: bfloat16 [8192, 64], P('chan'), may hold values from -6 to 6
Outputs:
- grad_proj: float32 [256, 2048], P(('seed', 'fsdp'), 'chan'), parts along dimension 0
There are 4 independent parts, one for each index of `seed`. A program takes and returns all parts, laid end to end along the dimension named above; an argument that names none is the same for every part. Nothing has to cross between parts.
All inputs are finite; a program needn't handle non-finite values.
Results may differ from a plain program's by a relative error of at most 0.01.
Values may be sent and summed in bfloat16 or wider, within the bound.
No kernel may reach another device: no remote copies, remote signals or barrier semaphores. Data moves between devices by JAX's collectives and lax.ppermute only.
A program may use at most 64 MiB of HBM per device.

v0:
```python
import jax
import jax.numpy as jnp
from jax import lax
from jax.sharding import PartitionSpec as P


def per_device(stream, mid, conv_weight, head_weight, labels, proj_act, proj_err):
    images = stream.shape[0]
    positions = stream.shape[1]
    width = stream.shape[2]
    rows = images * positions
    gathered = lax.all_gather(mid, "chan", axis=2, tiled=True)
    mid_rows = gathered.reshape(rows, gathered.shape[2])
    conv_out = jnp.dot(
        mid_rows,
        lax.all_gather(conv_weight, "fsdp", axis=0, tiled=True),
        preferred_element_type=jnp.float32,
    )
    acts_proj = jnp.dot(mid_rows, proj_act, preferred_element_type=jnp.float32)
    y_local = stream.astype(jnp.float32) + conv_out.reshape(images, positions, width)
    pooled = jnp.mean(jnp.maximum(y_local, 0.0), axis=1).astype(jnp.bfloat16)
    pooled_all = lax.all_gather(pooled, "fsdp", axis=0, tiled=True)
    partial_value = jnp.dot(pooled_all, head_weight, preferred_element_type=jnp.float32)
    block = head_weight.shape[1]
    block_start = lax.axis_index("fsdp") * block
    logits = lax.psum(partial_value, "chan")
    expo = jnp.exp(logits)
    total = lax.psum(jnp.sum(expo, axis=1), "fsdp")
    classes = block_start + jnp.arange(block, dtype=jnp.int32)
    onehot = (labels[:, None] == classes[None, :]).astype(jnp.float32)
    dlogits = (expo / total[:, None] - onehot).astype(jnp.bfloat16)
    dpooled = lax.psum_scatter(
        lax.dot_general(
            dlogits, head_weight, (((1,), (1,)), ((), ())), preferred_element_type=jnp.float32
        ),
        "fsdp",
        scatter_dimension=0,
        tiled=True,
    )
    error = jnp.where(y_local > 0.0, dpooled[:, None, :] / positions, 0.0).astype(jnp.bfloat16)
    err_part = jnp.dot(error.reshape(rows, width), proj_err, preferred_element_type=jnp.float32)
    acts_cube = acts_proj.reshape(images, positions, acts_proj.shape[1])
    err_full = lax.psum(err_part.astype(jnp.bfloat16), "chan").astype(jnp.float32)
    grads = jnp.einsum(
        "npa,npb->nab",
        acts_cube,
        err_full.reshape(images, positions, err_full.shape[1]),
        precision=lax.Precision.HIGHEST,
    )
    grads = grads.reshape(images, -1)
    share = grads.shape[1] // lax.axis_size("chan")
    return lax.dynamic_slice_in_dim(grads, lax.axis_index("chan") * share, share, 1)


def solution(mesh):
    in_specs = (
        P(("seed", "fsdp"), None, "chan"),
        P(("seed", "fsdp"), None, "chan"),
        P(("seed", "fsdp"), "chan"),
        P(("seed", "chan"), "fsdp"),
        P(),
        P(),
        P("chan", None),
    )
    out_specs = P(("seed", "fsdp"), "chan")
    return jax.shard_map(
        per_device, mesh=mesh, in_specs=in_specs, out_specs=out_specs, check_vma=False
    )
```

profile of v0, /device:TPU:2, one launch (start us, length us, event | category | flops | bytes accessed | tf_op | source)
XLA Modules:
  0.0 618.6 jit_solution(5644417789808126572)
XLA Ops:
  6.5 0.0 copy-start
  6.5 0.7 all-gather.5.cloned.1.call-update
  7.3 0.0 all-gather.3.cloned.1.call-start
  7.3 0.7 all-gather.3.cloned.1.call-update
  8.0 0.0 all-reduce.3.cloned.1.call-start
  8.1 33.3 %all-gather.5.cloned.1.call-done = bf16[2048,512]{1,0:T(8,128)(2,1)} async-done(((bf16[512,512]{1,0:T(8,128)(2,1)}), bf16[2048,512]{1,0:T(8,128)(2,1)}) %all-gather.5.cloned.1.call-update) | async-done | bytes 2097168 | tf_op jit(solution)/shard_map/all_gather | solution.py:16
  41.4 217.4 %all-gather.3.cloned.1.call-done = bf16[16,144,2048]{2,1,0:T(8,128)(2,1)} async-done(((bf16[16,144,128]{2,1,0:T(8,128)(2,1)}), bf16[16,144,2048]{2,1,0:T(8,128)(2,1)}) %all-gather.3.cloned.1.call-update) | async-done | bytes 9437200 | tf_op jit(solution)/shard_map/all_gather | solution.py:12
  258.7 11.5 %maximum_reduce_fusion = (f32[16,512]{1,0:T(8,128)S(1)}, f32[16,144,512]{2,1,0:T(8,128)}) fusion(bf16[16,144,512]{2,1,0:T(8,128)(2,1)} %param.7, bf16[16,144,2048]{2,1,0:T(8,128)(2,1)} %all-gather.3.cloned.1.call-done, bf16[2048,512]{1,0:T(8,128)(2,1)} %all-gather.5.cloned.1.call-done), kind=kOutput, calls=%fused_computation.1 | convolution fusion | flops 4836548608 | bytes 18644992 | tf_op jit(solution)/shard_map/dot_general | solution.py:14
  270.3 6.8 %all_gather.11 = bf16[64,512]{1,0:T(8,128)(2,1)S(1)} all-gather(bf16[16,512]{1,0:T(8,128)(2,1)S(1)} %multiply_convert_fusion), channel_id=1, replica_groups=mesh['seed'=4,'chan'=16,'fsdp'=4] {'fsdp'}, dimensions={0}, use_global_device_ids=true | all-gather | bytes 81920 | tf_op jit(solution)/shard_map/all_gather | solution.py:22
  277.0 1.8 fusion.8
  278.9 0.0 all-reduce.3.cloned.1.call-update
  278.9 0.0 reduce-scatter.2.cloned.1.call-start
  279.0 0.0 copy-start.2
  279.0 142.3 %all-reduce.3.cloned.1.call-done = f32[64,4096]{1,0:T(8,128)} async-done(((f32[64,4096]{1,0:T(8,128)}), f32[64,4096]{1,0:T(8,128)}) %all-reduce.3.cloned.1.call-update) | async-done | bytes 1048592 | tf_op jit(solution)/shard_map/psum | solution.py:26
  421.2 1.5 exponential_reduce_fusion
  422.7 7.2 %psum.22 = f32[64]{0:T(128)S(1)} all-reduce(f32[64]{0:T(128)S(1)} %exponential_reduce_fusion), channel_id=1, replica_groups=mesh['seed'=4,'chan'=16,'fsdp'=4] {'fsdp'}, use_global_device_ids=true, to_apply=%region_3.0 | all-reduce | flops 64 | bytes 512 | tf_op jit(solution)/shard_map/psum | solution.py:28
  429.9 4.6 fusion.2
  434.5 0.0 reduce-scatter.2.cloned.1.call-update
  434.5 0.0 all-reduce.5.cloned.1.call-start
  434.6 31.8 %reduce-scatter.2.cloned.1.call-done = f32[16,512]{1,0:T(8,128)} async-done(((f32[64,512]{1,0:T(8,128)}), f32[16,512]{1,0:T(8,128)}) %reduce-scatter.2.cloned.1.call-update) | async-done | bytes 32784 | tf_op jit(solution)/shard_map/reduce_scatter | solution.py:32
  466.4 0.8 broadcast_multiply_fusion
  467.2 0.0 copy-done.2
  467.2 3.2 select_convert_fusion
  470.4 0.8 convolution_convert_fusion
  471.2 0.9 reshape.25
  472.1 0.9 copy.8
  473.0 0.0 all-reduce.5.cloned.1.call-update
  473.1 6.9 %fusion.6 = f32[16,144,32]{1,2,0:T(8,128)S(1)} fusion(bf16[16,144,2048]{2,1,0:T(8,128)(2,1)} %all-gather.3.cloned.1.call-done, bf16[2048,32]{0,1:T(8,128)(2,1)S(1)} %copy-done), kind=kOutput, calls=%fused_computation.12 | convolution fusion | flops 301989888 | bytes 9863168 | tf_op jit(solution)/shard_map/dot_general | solution.py:19
  480.0 129.8 %all-reduce.5.cloned.1.call-done = bf16[16,144,64]{1,2,0:T(8,128)(2,1)} async-done(((bf16[16,144,64]{1,2,0:T(8,128)(2,1)}), bf16[16,144,64]{1,2,0:T(8,128)(2,1)}) %all-reduce.5.cloned.1.call-update) | async-done | bytes 294928 | tf_op jit(solution)/shard_map/psum | solution.py:43
  609.7 1.6 fusion.9
  611.3 0.1 reshape.26
  611.4 0.6 constant_dynamic-slice_fusion
  (10 shorter events, 0.0 us)
Async XLA Ops:
  6.5 466.5 %copy-start = (bf16[2048,32]{0,1:T(8,128)(2,1)S(1)}, bf16[2048,32]{0,1:T(8,128)(2,1)}, u32[]{:S(2)}) copy-start(bf16[2048,32]{0,1:T(8,128)(2,1)} %param.12) | copy-start | bytes 393220
  6.5 34.8 %all-gather.5.cloned.1.call-start = ((), (), s32[]{:S(2)}) async-start(), calls=%async_computation.2 | async-start | bytes 2621440 | tf_op jit(solution)/shard_map/all_gather | solution.py:16
  7.3 251.5 %all-gather.3.cloned.1.call-start = ((), (), s32[]{:S(2)}) async-start(), calls=%async_computation.1 | async-start | bytes 10027008 | tf_op jit(solution)/shard_map/all_gather | solution.py:12
  8.0 413.2 %all-reduce.3.cloned.1.call-start = ((), (), s32[]{:S(2)}) async-start(), calls=%async_computation.3 | async-start | bytes 2097152 | tf_op jit(solution)/shard_map/psum | solution.py:26
  258.7 18.3 %copy-start.1 = (bf16[512,4096]{1,0:T(8,128)(2,1)S(1)}, bf16[512,4096]{1,0:T(8,128)(2,1)}, u32[]{:S(2)}) copy-start(bf16[512,4096]{1,0:T(8,128)(2,1)} %param.10) | copy-start | bytes 12582916
  270.3 159.6 %copy-start.4 = (s32[64]{0:T(128)S(1)}, s32[64]{0:T(128)}, u32[]{:S(2)}) copy-start(s32[64]{0:T(128)} %param.11) | copy-start | bytes 772
  278.9 187.5 %reduce-scatter.2.cloned.1.call-start = ((), (), s32[]{:S(2)}) async-start(), calls=%async_computation.4 | async-start | bytes 163840 | tf_op jit(solution)/shard_map/reduce_scatter | solution.py:32
  279.0 188.2 %copy-start.2 = (bf16[16,144,512]{2,1,0:T(8,128)(2,1)S(1)}, bf16[16,144,512]{2,1,0:T(8,128)(2,1)}, u32[]{:S(2)}) copy-start(bf16[16,144,512]{2,1,0:T(8,128)(2,1)} %param.7) | copy-start | bytes 7077892
  434.5 175.2 %all-reduce.5.cloned.1.call-start = ((), (), s32[]{:S(2)}) async-start(), calls=%async_computation.5 | async-start | bytes 1048576 | tf_op jit(solution)/shard_map/psum | solution.py:43
  467.2 3.2 copy-start.3
Sparse Core Ops, SparseCore 0:
  9.2 32.1 all-gather.4
  43.1 215.6 all-gather.2
  279.0 142.1 all-reduce.2
  434.6 31.7 reduce-scatter.1
  473.2 136.5 all-reduce.4
where the time goes:
time: 619 us
  waiting for transfers between devices  556 us (90%)
  matrix products  27.2 us (4%)
  blocking collectives  13.9 us (2%)
  between operations  13.2 us (2%)
    all_gather x1, waiting for transfers between devices, per_device(): gathered = lax.all_gather(mid, 'chan', axis=2, tiled=True)  217 us
    psum x1, waiting for transfers between devices, per_device(): logits = lax.psum(partial_value, 'chan')  142 us
    psum x1, waiting for transfers between devices, per_device(): lax.psum(err_part.astype(jnp.bfloat16), 'chan').astype(jnp.float32)  130 us
    all_gather x1, waiting for transfers between devices, per_device(): lax.all_gather(conv_weight, 'fsdp', axis=0, tiled=True)  33.3 us
    reduce_scatter x1, waiting for transfers between devices, per_device(): lax.psum_scatter(lax.dot_general(dlogits, head_weight, (((1,), (1,)), (()...  31.8 us
  transfers between devices with their start and end apart: 5, of which 5 were waited for; matrix products, arithmetic and copies ran while one was open for 1% of the time, Pallas kernels for 0%

commit v1 on v0

v1 whole, which is shorter than its diff:
```python
import functools

import jax
import jax.numpy as jnp
from jax import lax
from jax.experimental import pallas as pl
from jax.experimental.pallas import tpu as pltpu
from jax.sharding import Mesh, PartitionSpec as P

CHAN = ("z", "ylo")
ROWS = ("yhi", "core", "ylo")
BF16_TOP = 3.3895313892515355e38
NT = (((1,), (1,)), ((), ()))
TN = (((0,), (0,)), ((), ()))


def conv_body(mid_ref, w_ref, stream_ref, pa_ref, pooled_ref, m_ref):
    z, two, imgs, pos, kz = mid_ref.shape
    x = jnp.concatenate(
        [mid_ref[a, b].reshape(imgs * pos, kz) for a in range(z) for b in range(two)], axis=1
    )
    acts = jnp.dot(x, pa_ref[...], preferred_element_type=jnp.float32)
    acts_hi = acts.astype(jnp.bfloat16)
    acts_lo = (acts - acts_hi.astype(jnp.float32)).astype(jnp.bfloat16)
    ka = acts.shape[1]
    acts_two = jnp.concatenate([acts_hi, acts_lo], axis=1)
    width = w_ref.shape[2]
    for h in range(two):
        y = jnp.dot(x, w_ref[h], preferred_element_type=jnp.float32)
        y = y.reshape(imgs, pos, width) + stream_ref[h].astype(jnp.float32)
        pooled_ref[0, h] = (jnp.sum(jnp.maximum(y, 0.0), axis=1) / pos).astype(jnp.bfloat16)
        mask = jnp.where(y > 0.0, 1.0, 0.0).astype(jnp.bfloat16)
        for i in range(imgs):
            both = lax.dot_general(
                acts_two[i * pos : (i + 1) * pos], mask[i], TN, preferred_element_type=jnp.float32
            )
            m_ref[i, :, h * width : (h + 1) * width] = both[:ka] + both[ka:]


def conv(mid_all, w_all, stream2, proj_act, step):
    z, two, half, pos, kz = mid_all.shape
    width = w_all.shape[2]
    depth, ka = proj_act.shape
    n = half // step
    return pl.pallas_call(
        conv_body,
        grid=(n,),
        in_specs=[
            pl.BlockSpec((z, two, step, pos, kz), lambda i: (0, 0, i, 0, 0)),
            pl.BlockSpec((two, depth, width), lambda i: (0, 0, 0), pipeline_mode=pl.Buffered(1)),
            pl.BlockSpec((two, step, pos, width), lambda i: (0, i, 0, 0)),
            pl.BlockSpec((depth, ka), lambda i: (0, 0)),
        ],
        out_specs=[
            pl.BlockSpec((1, two, step, width), lambda i: (i, 0, 0, 0)),
            pl.BlockSpec((step, ka, two * width), lambda i: (i, 0, 0)),
        ],
        out_shape=[
            jax.ShapeDtypeStruct((n, two, step, width), jnp.bfloat16),
            jax.ShapeDtypeStruct((half, ka, two * width), jnp.float32),
        ],
        compiler_params=pltpu.CompilerParams(vmem_limit_bytes=48 * 1024 * 1024),
        name="conv_pool_mask",
    )(mid_all, w_all, stream2, proj_act)


def logits_body(pooled_ref, head_ref, out_ref):
    out_ref[0] = jnp.dot(pooled_ref[...], head_ref[...], preferred_element_type=jnp.float32)


def logits_slices(pooled, head, n):
    rows, depth = pooled.shape
    share = head.shape[1] // n
    return pl.pallas_call(
        logits_body,
        grid=(n,),
        in_specs=[
            pl.BlockSpec((rows, depth), lambda i: (0, 0)),
            pl.BlockSpec((depth, share), lambda i: (0, i)),
        ],
        out_specs=pl.BlockSpec((1, rows, share), lambda i: (i, 0, 0)),
        out_shape=jax.ShapeDtypeStruct((n, rows, share), jnp.float32),
        name="logits_slices",
    )(pooled, head)


def back_body(expo_ref, head_ref, out_ref):
    depth = head_ref.shape[0]

    @pl.when(pl.program_id(0) == 0)
    def _():
        out_ref[...] = jnp.zeros_like(out_ref)

    e = expo_ref[0]
    out_ref[:, :depth] += lax.dot_general(e, head_ref[...], NT, preferred_element_type=jnp.float32)
    out_ref[:, depth:] += jnp.broadcast_to(
        jnp.sum(e.astype(jnp.float32), axis=1, keepdims=True), (out_ref.shape[0], 128)
    )


def back(expo, head):
    n, rows, share = expo.shape
    depth = head.shape[0]
    return pl.pallas_call(
        back_body,
        grid=(n,),
        in_specs=[
            pl.BlockSpec((1, rows, share), lambda i: (i, 0, 0)),
            pl.BlockSpec((depth, share), lambda i: (0, i)),
        ],
        out_specs=pl.BlockSpec((rows, depth + 128), lambda i: (0, 0)),
        out_shape=jax.ShapeDtypeStruct((rows, depth + 128), jnp.float32),
        name="back",
    )(expo, head)


def final_body(pos, m_ref, part_ref, hot_ref, pe_ref, out_ref):
    width = hot_ref.shape[3]
    imgs, ka, _ = m_ref.shape
    ke = pe_ref.shape[2]
    total = jnp.zeros((imgs, ka * ke // ka), jnp.float32)
    acc = jnp.zeros((imgs * ka, ke), jnp.float32)
    for h in range(2):
        part = sum(part_ref[a, h] for a in range(part_ref.shape[0]))
        hot = sum(hot_ref[a, h].astype(jnp.float32) for a in range(hot_ref.shape[0]))
        d = part[:, :width] / part[:, width : width + 1] - hot
        d = (d / pos).astype(jnp.bfloat16).astype(jnp.float32)
        v = (m_ref[:, :, h * width : (h + 1) * width] * d[:, None, :]).reshape(imgs * ka, width)
        v_hi = v.astype(jnp.bfloat16)
        v_lo = (v - v_hi.astype(jnp.float32)).astype(jnp.bfloat16)
        acc += jnp.dot(v_hi, pe_ref[h], preferred_element_type=jnp.float32)
        acc += jnp.dot(v_lo, pe_ref[h], preferred_element_type=jnp.float32)
    out_ref[...] = acc


def final(m, part, hot, pe, pos):
    imgs, ka, _ = m.shape
    ke = pe.shape[2]
    return pl.pallas_call(
        functools.partial(final_body, pos),
        out_shape=jax.ShapeDtypeStruct((imgs * ka, ke), jnp.float32),
        name="final",
    )(m, part, hot, pe)


def per_device(stream, mid, conv_weight, head_weight, labels, proj_act, proj_err):
    images, pos, width = stream.shape
    kz = mid.shape[2]
    half = images // 2
    parts = lax.axis_size("z") * 2
    fs = lax.axis_size("yhi") * lax.axis_size("core")
    block = head_weight.shape[1]
    me_y = lax.axis_index("ylo")
    f = lax.axis_index("yhi") * lax.axis_size("core") + lax.axis_index("core")

    mid2 = lax.all_to_all(mid.reshape(2, half, pos, kz), "ylo", 0, 0)
    mid_all = lax.all_gather(mid2, "z", axis=0)
    w_all = lax.all_gather(conv_weight, ("ylo", "yhi", "core"), axis=0)
    w_all = w_all.reshape(2, fs * conv_weight.shape[0], width)
    stream2 = lax.all_to_all(stream.reshape(2, half, pos, width), "ylo", 0, 0)
    pe = lax.all_gather(proj_err, "ylo", axis=0)

    classes = f * block + jnp.arange(block, dtype=jnp.int32)
    onehot = (labels[:, None] == classes[None, :]).astype(jnp.bfloat16)
    hot = lax.dot_general(onehot, head_weight, NT, preferred_element_type=jnp.float32)
    hot = hot.astype(jnp.bfloat16).reshape(fs, 2, half, width).reshape(2 * fs, half, width)
    hot = lax.all_to_all(hot, ROWS, 0, 0).reshape(fs, 2, half, width)

    pooled, m = conv(mid_all, w_all, stream2, proj_act, 4)
    pooled = pooled.transpose(0, 2, 1, 3).reshape(half, 2 * width)
    pooled_all = lax.all_gather(pooled, ROWS, axis=0, tiled=True)
    pooled_mine = lax.dynamic_slice_in_dim(pooled_all, me_y * width, width, 1)

    part = logits_slices(pooled_mine, head_weight, parts)
    part = lax.all_to_all(part, CHAN, 0, 0)
    expo = jnp.minimum(jnp.exp(jnp.sum(part, axis=0)), BF16_TOP).astype(jnp.bfloat16)
    expo = lax.all_gather(expo, CHAN, axis=0)

    part = back(expo, head_weight).reshape(2 * fs, half, width + 128)
    part = lax.all_to_all(part, ROWS, 0, 0).reshape(fs, 2, half, width + 128)

    grads = final(m, part, hot, pe, pos)
    grads = grads.reshape(half, parts, -1).transpose(1, 0, 2)
    grads = lax.all_to_all(grads, CHAN, 0, 0)
    grads = jnp.sum(grads.reshape(parts // 2, 2, half, -1), axis=0)
    return grads.reshape(images, -1)


def solution(mesh):
    fine = Mesh(mesh.devices.reshape(4, 8, 2, 2, 2), ("seed", "z", "ylo", "yhi", "core"))
    rows = ("seed", "yhi", "core")
    in_specs = (
        P(rows, None, CHAN),
        P(rows, None, CHAN),
        P(rows, CHAN),
        P(("seed", "z", "ylo"), ("yhi", "core")),
        P(),
        P(),
        P(CHAN, None),
    )
    return jax.shard_map(
        per_device, mesh=fine, in_specs=in_specs, out_specs=P(rows, CHAN), check_vma=False
    )
```

time: 619 us -> 302 us (0.49)
  waiting for transfers between devices: 556 us -> 134 us
  blocking collectives: 13.9 us -> 93.1 us
  Pallas kernels: 0 us -> 34.5 us
  matrix products: 27.2 us -> 4.21 us
  starting transfers between devices: 0.16 us -> 16.8 us
    psum x2 -> x0, waiting for transfers between devices: 272 us -> none  [the longest x1 142 us: per_device(): logits = lax.psum(partial_value, 'chan')]
    all_gather x2, waiting for transfers between devices: 251 us -> 69.2 us  [the longest x1 60 us: per_device(): mid_all = lax.all_gather(mid2, 'z', axis=0)]
    all_to_all x0 -> x4, waiting for transfers between devices: none -> 63.8 us  [the longest x1 40.2 us: per_device(): stream2 = lax.all_to_all(stream.reshape(2, half, pos, width), 'ylo', 0, 0)]
    all_gather x1 -> x3, blocking collectives: 6.75 us -> 65.1 us  [the longest x1 37.3 us: per_device(): expo = lax.all_gather(expo, CHAN, axis=0)]
    pallas_call x0 -> x4, Pallas kernels: none -> 34.5 us  [the longest x1 10.9 us: conv(): pl.pallas_call(conv_body, grid=(n,), in_specs=[pl.BlockSpec((z, two, step...]
    reduce_scatter x1 -> x0, waiting for transfers between devices: 31.8 us -> none  [per_device(): lax.psum_scatter(lax.dot_general(dlogits, head_weight, (((1,), (1,)), (()...]
    all_to_all x0 -> x2, blocking collectives: none -> 28.1 us  [the longest x1 14.8 us: per_device(): grads = lax.all_to_all(grads, CHAN, 0, 0)]
    dot_general x6 -> x1, matrix products: 27.2 us -> 4.21 us  [per_device(): lax.dot_general(onehot, head_weight, NT, preferred_element_type=jnp.float32)]
  transfers between devices with their start and end apart: 5 -> 6, of which waited for: 5 -> 4; matrix products, arithmetic and copies ran while one was open for 1% -> 2% of each run, Pallas kernels for 0% -> 3%
where the time goes in v1:
time: 302 us; the launch traced here: 301 us
  waiting for transfers between devices  134 us (44%)
  blocking collectives  93.1 us (31%)
  Pallas kernels  34.5 us (11%)
  starting transfers between devices  16.8 us (6%)
  between operations  13.5 us (4%)
  local copies, waits for them, and re-layouts  4.42 us (1%)
  matrix products  4.21 us (1%)
    all_gather x1, waiting for transfers between devices, per_device(): mid_all = lax.all_gather(mid2, 'z', axis=0)  60 us
    all_to_all x1, waiting for transfers between devices, per_device(): stream2 = lax.all_to_all(stream.reshape(2, half, pos, width), 'ylo', 0, 0)  40.2 us
    all_gather x1, blocking collectives, per_device(): expo = lax.all_gather(expo, CHAN, axis=0)  37.3 us
    all_to_all x1, waiting for transfers between devices, per_device(): part = lax.all_to_all(part, CHAN, 0, 0)  23.5 us
    all_gather x1, blocking collectives, per_device(): pooled_all = lax.all_gather(pooled, ROWS, axis=0, tiled=True)  21.4 us
    all_to_all x1, blocking collectives, per_device(): grads = lax.all_to_all(grads, CHAN, 0, 0)  14.8 us
    all_to_all x1, blocking collectives, per_device(): mid2 = lax.all_to_all(mid.reshape(2, half, pos, kz), 'ylo', 0, 0)  13.3 us
    pallas_call x1, Pallas kernels, conv(): pl.pallas_call(conv_body, grid=(n,), in_specs=[pl.BlockSpec((z, two, step...  10.9 us
  transfers between devices with their start and end apart: 6, of which 4 were waited for; matrix products, arithmetic and copies ran while one was open for 2% of the time, Pallas kernels for 3%

profile of v1, /device:TPU:2, one launch (start us, length us, event | category | flops | bytes accessed | tf_op | source)
XLA Modules:
  0.0 301.0 jit_solution(1162548155537047055)
XLA Ops:
  6.5 0.7 all-gather.9.cloned.1.call-update
  7.3 0.0 all-gather.7.cloned.1.call-start
  7.3 13.3 %all_to_all.30 = bf16[2,8,144,128]{3,2,1,0:T(8,128)(2,1)} all-to-all(bf16[2,8,144,128]{3,2,1,0:T(8,128)(2,1)} %bitcast.27), channel_id=1, replica_groups=mesh['seed'=4,'z'=8,'ylo'=2,'yhi'=2,'core'=2] {'ylo'}, dimensions={0} | all-to-all | bytes 1179648 | tf_op jit(solution)/shard_map/all_to_all | solution.py:156
  20.6 0.0 all-gather.7.cloned.1.call-update
  20.6 4.0 %all-to-all-start.1 = ((bf16[2,8,144,512]{3,2,1,0:T(8,128)(2,1)}), bf16[2,8,144,512]{3,2,1,0:T(8,128)(2,1)S(1)}, u32[]{:S(2)}, u32[]{:S(2)}) async-start(bf16[2,8,144,512]{3,2,1,0:T(8,128)(2,1)} %bitcast.22), calls=%async_computation.1 | async-start | bytes 4718592 | tf_op jit(solution)/shard_map/all_to_all | solution.py:160
  24.6 0.3 copy.19.pa_ref
  24.9 40.2 %all-to-all-done.1.stream_ref = bf16[2,8,144,512]{3,2,1,0:T(8,128)(2,1)S(1)} async-done(((bf16[2,8,144,512]{3,2,1,0:T(8,128)(2,1)}), bf16[2,8,144,512]{3,2,1,0:T(8,128)(2,1)S(1)}, u32[]{:S(2)}, u32[]{:S(2)}) %all-to-all-start.1) | async-done | bytes 2359328 | tf_op jit(solution)/shard_map/all_to_all | solution.py:160
  65.1 9.2 %all-gather.9.cloned.1.call-done = bf16[4096,512]{1,0:T(8,128)(2,1)} async-done(((bf16[512,512]{1,0:T(8,128)(2,1)}), bf16[4096,512]{1,0:T(8,128)(2,1)}) %all-gather.9.cloned.1.call-update) | async-done | bytes 4194320 | tf_op jit(solution)/shard_map/all_gather | solution.py:158
  74.3 60.0 %all-gather.7.cloned.1.call-done = bf16[16,8,144,128]{3,2,1,0:T(8,128)(2,1)} async-done(((bf16[2,8,144,128]{3,2,1,0:T(8,128)(2,1)}), bf16[16,8,144,128]{3,2,1,0:T(8,128)(2,1)}) %all-gather.7.cloned.1.call-update) | async-done | bytes 4718608 | tf_op jit(solution)/shard_map/all_gather | solution.py:157
  134.3 10.9 %conv_pool_mask.1 = (bf16[2,2,4,512]{3,2,1,0:T(4,128)(2,1)S(1)}, f32[8,32,1024]{2,1,0:T(8,128)S(1)}) custom-call(bf16[8,2,8,144,128]{4,3,2,1,0:T(8,128)(2,1)} %bitcast.20, bf16[2,2048,512]{2,1,0:T(8,128)(2,1)} %bitcast.21, bf16[2,8,144,512]{3,2,1,0:T(8,128)(2,1)S(1)} %all-to-all-done.1.stream_ref, bf16[2048,32]{1,0:T(8,128)(2,1)S(1)} %copy.19.pa_ref), custom_call_target="tpu_custom_call" | custom-call | tf_op jit(solution)/shard_map/conv_pool_mask/pallas_call | solution.py:45
  145.2 1.0 copy-done
  146.3 21.4 %all_gather.29 = bf16[64,1024]{1,0:T(8,128)(2,1)S(1)} all-gather(bf16[8,1024]{1,0:T(8,128)(2,1)S(1)} %bitcast.31), channel_id=1, replica_groups=mesh['seed'=4,'z'=8,'ylo'=2,'yhi'=2,'core'=2] {'yhi','core','ylo'}, dimensions={0}, use_global_device_ids=true | all-gather | bytes 147456 | tf_op jit(solution)/shard_map/all_gather | solution.py:171
  167.6 0.6 constant_dynamic-slice_fusion.pooled_ref
  168.3 10.6 %logits_slices.1 = f32[16,64,256]{2,1,0:T(8,128)} custom-call(bf16[64,512]{1,0:T(8,128)(2,1)} %constant_dynamic-slice_fusion.pooled_ref, bf16[512,4096]{1,0:T(8,128)(2,1)} %head_ref.3), custom_call_target="tpu_custom_call" | custom-call | tf_op jit(solution)/shard_map/logits_slices/pallas_call | solution.py:74
  178.9 5.4 %all-to-all-start.2 = ((f32[16,64,256]{2,1,0:T(8,128)}), f32[16,64,256]{2,1,0:T(8,128)S(1)}, u32[]{:S(2)}, u32[]{:S(2)}) async-start(f32[16,64,256]{2,1,0:T(8,128)} %logits_slices.1), calls=%async_computation.2 | async-start | bytes 2097152 | tf_op jit(solution)/shard_map/all_to_all | solution.py:175
  184.3 0.0 copy-done.5
  184.3 4.2 %fusion = bf16[8,8,512]{2,1,0:T(8,128)(2,1)} fusion(bf16[512,4096]{1,0:T(8,128)(2,1)} %head_ref.3, s32[4096]{0:T(1024)S(1)} %iota_add_fusion, s32[64]{0:T(128)S(1)} %copy-done.5), kind=kOutput, calls=%fused_computation.1 | convolution fusion | flops 268730368 | bytes 4276480 | tf_op jit(solution)/shard_map/dot_general | solution.py:165
  188.5 23.5 %all-to-all-done.2 = f32[16,64,256]{2,1,0:T(8,128)S(1)} async-done(((f32[16,64,256]{2,1,0:T(8,128)}), f32[16,64,256]{2,1,0:T(8,128)S(1)}, u32[]{:S(2)}, u32[]{:S(2)}) %all-to-all-start.2) | async-done | bytes 1048608 | tf_op jit(solution)/shard_map/all_to_all | solution.py:175
  212.1 3.7 %all-to-all-start.4 = ((bf16[8,8,512]{2,1,0:T(8,128)(2,1)}), bf16[8,8,512]{2,1,0:T(8,128)(2,1)S(1)}, u32[]{:S(2)}, u32[]{:S(2)}) async-start(bf16[8,8,512]{2,1,0:T(8,128)(2,1)} %fusion), calls=%async_computation.4 | async-start | bytes 131072 | tf_op jit(solution)/shard_map/all_to_all | solution.py:167
  215.7 0.1 reduce_sum.18
  215.8 37.3 %all-gather.2 = bf16[1024,256]{1,0:T(8,128)(2,1)} all-gather(bf16[64,256]{1,0:T(8,128)(2,1)S(1)} %minimum_convert_fusion), channel_id=4, replica_groups=mesh['seed'=4,'z'=8,'ylo'=2,'yhi'=2,'core'=2] {'z','ylo'}, dimensions={0}, use_global_device_ids=true | all-gather | bytes 557056 | tf_op jit(solution)/shard_map/all_gather | solution.py:177
  253.1 10.5 %back.1 = f32[64,640]{1,0:T(8,128)} custom-call(bf16[16,64,256]{2,1,0:T(8,128)(2,1)} %bitcast.23, bf16[512,4096]{1,0:T(8,128)(2,1)} %head_ref.3), custom_call_target="tpu_custom_call" | custom-call | tf_op jit(solution)/shard_map/back/pallas_call | solution.py:104
  263.6 0.0 all-to-all-done.4
  263.6 3.7 %all-to-all-start.3 = ((f32[8,8,640]{2,1,0:T(8,128)}), f32[8,8,640]{2,1,0:T(8,128)S(1)}, u32[]{:S(2)}, u32[]{:S(2)}) async-start(f32[8,8,640]{2,1,0:T(8,128)} %bitcast.25), calls=%async_computation.3 | async-start | bytes 327680 | tf_op jit(solution)/shard_map/all_to_all | solution.py:180
  267.3 6.4 %all-gather.3 = bf16[1024,64]{0,1:T(8,128)(2,1)S(1)} all-gather(bf16[512,64]{0,1:T(8,128)(2,1)S(1)} %copy-done.4), channel_id=5, replica_groups=mesh['seed'=4,'z'=8,'ylo'=2,'yhi'=2,'core'=2] {'ylo'}, dimensions={0}, use_global_device_ids=true | all-gather | bytes 196608 | tf_op jit(solution)/shard_map/all_gather | solution.py:161
  273.7 0.9 copy.21
  274.6 0.0 all-to-all-done.3
  274.6 0.7 copy-done.1
  275.2 2.5 final.1
  277.8 1.0 reshape.59
  278.8 14.8 %all_to_all.31 = f32[16,8,128]{2,1,0:T(8,128)S(1)} all-to-all(f32[16,8,128]{2,1,0:T(8,128)S(1)} %copy.22), channel_id=1, replica_groups=mesh['seed'=4,'z'=8,'ylo'=2,'yhi'=2,'core'=2] {'z','ylo'}, dimensions={0} | all-to-all | bytes 131072 | tf_op jit(solution)/shard_map/all_to_all | solution.py:184
  293.5 0.6 reduce_sum.19
  (15 shorter events, 0.1 us)
Async XLA Ops:
  6.5 18.1 %copy-start.3 = (bf16[2048,32]{0,1:T(8,128)(2,1)S(1)}, bf16[2048,32]{0,1:T(8,128)(2,1)}, u32[]{:S(2)}) copy-start(bf16[2048,32]{0,1:T(8,128)(2,1)} %param.12) | copy-start | bytes 393220
  6.5 67.8 %all-gather.9.cloned.1.call-start = ((), (), s32[]{:S(2)}) async-start(), calls=%async_computation.7 | async-start | bytes 4718592 | tf_op jit(solution)/shard_map/all_gather | solution.py:158
  7.3 127.1 %all-gather.7.cloned.1.call-start = ((), (), s32[]{:S(2)}) async-start(), calls=%async_computation.6 | async-start | bytes 5308416 | tf_op jit(solution)/shard_map/all_gather | solution.py:157
  20.6 44.5 %all-to-all-start.1 = ((bf16[2,8,144,512]{3,2,1,0:T(8,128)(2,1)}), bf16[2,8,144,512]{3,2,1,0:T(8,128)(2,1)S(1)}, u32[]{:S(2)}, u32[]{:S(2)}) async-start(bf16[2,8,144,512]{3,2,1,0:T(8,128)(2,1)} %bitcast.22), calls=%async_computation.1 | async-start | bytes 4718592 | tf_op jit(solution)/shard_map/all_to_all | solution.py:160
  145.2 1.0 copy-start
  146.2 38.1 %copy-start.5 = (s32[64]{0:T(128)S(1)}, s32[64]{0:T(128)}, u32[]{:S(2)}) copy-start(s32[64]{0:T(128)} %param.11) | copy-start | bytes 772
  178.9 33.2 %all-to-all-start.2 = ((f32[16,64,256]{2,1,0:T(8,128)}), f32[16,64,256]{2,1,0:T(8,128)S(1)}, u32[]{:S(2)}, u32[]{:S(2)}) async-start(f32[16,64,256]{2,1,0:T(8,128)} %logits_slices.1), calls=%async_computation.2 | async-start | bytes 2097152 | tf_op jit(solution)/shard_map/all_to_all | solution.py:175
  188.5 78.8 %copy-start.4 = (bf16[512,64]{0,1:T(8,128)(2,1)S(1)}, bf16[512,64]{0,1:T(8,128)(2,1)}, u32[]{:S(2)}) copy-start(bf16[512,64]{0,1:T(8,128)(2,1)} %param.13) | copy-start | bytes 196612
  212.1 51.5 %all-to-all-start.4 = ((bf16[8,8,512]{2,1,0:T(8,128)(2,1)}), bf16[8,8,512]{2,1,0:T(8,128)(2,1)S(1)}, u32[]{:S(2)}, u32[]{:S(2)}) async-start(bf16[8,8,512]{2,1,0:T(8,128)(2,1)} %fusion), calls=%async_computation.4 | async-start | bytes 131072 | tf_op jit(solution)/shard_map/all_to_all | solution.py:167
  263.6 11.0 %copy-start.2 = (bf16[8,8,512]{2,1,0:T(8,128)(2,1)}, bf16[8,8,512]{2,1,0:T(8,128)(2,1)S(1)}, u32[]{:S(2)}) copy-start(bf16[8,8,512]{2,1,0:T(8,128)(2,1)S(1)} %all-to-all-done.4) | copy-start | bytes 196612
  263.6 11.0 %all-to-all-start.3 = ((f32[8,8,640]{2,1,0:T(8,128)}), f32[8,8,640]{2,1,0:T(8,128)S(1)}, u32[]{:S(2)}, u32[]{:S(2)}) async-start(f32[8,8,640]{2,1,0:T(8,128)} %bitcast.25), calls=%async_computation.3 | async-start | bytes 327680 | tf_op jit(solution)/shard_map/all_to_all | solution.py:180
  274.6 0.7 copy-start.1
Sparse Core Ops, SparseCore 0:
  9.1 65.1 all-gather.8
  76.1 58.2 all-gather.6

commit v2 on v1

v2 whole, which is shorter than its diff:
```python
import functools

import jax
import jax.numpy as jnp
from jax import lax
from jax.experimental import pallas as pl
from jax.experimental.pallas import tpu as pltpu
from jax.sharding import Mesh, PartitionSpec as P

CHAN = ("z", "ylo")
ROWS = ("yhi", "core", "ylo")
BF16_TOP = 3.3895313892515355e38
NT = (((1,), (1,)), ((), ()))
TN = (((0,), (0,)), ((), ()))
VM = pl.BlockSpec(memory_space=pltpu.VMEM)
LIMIT = pltpu.CompilerParams(vmem_limit_bytes=48 * 1024 * 1024)


def ring(block, nz):
    right = [(i, (i + 1) % nz) for i in range(nz)]
    left = [(i, (i - 1) % nz) for i in range(nz)]
    got = [(0, 0, block)]
    r = l = block
    for k in range(1, nz // 2):
        r = lax.ppermute(r, "z", right)
        l = lax.ppermute(l, "z", left)
        got += [(k, 0, r), (nz - k, 0, l)]
    cut = block.shape[0] // 2
    got.append((nz // 2, 0, lax.ppermute(r[:cut], "z", right)))
    got.append((nz // 2, cut, lax.ppermute(l[cut:], "z", left)))
    return got


def conv_body(nz, plan, place_ref, *refs):
    count = len(plan)
    blocks = refs[:count]
    w_ref, own_ref, other_ref, pa_ref, pooled_ref, m_ref, x_ref, acts_ref = refs[count:]
    step = pl.program_id(0)
    imgs, pos, kz = blocks[0].shape
    ka = pa_ref.shape[1]

    @pl.when(step == 0)
    def _():
        me_z = place_ref[0]
        me_y = place_ref[1]
        for ref, (sub, shift, image) in zip(blocks, plan):
            which = me_y if sub == 0 else 1 - me_y
            source = lax.rem(me_z + (nz - shift), nz)
            lane = pl.multiple_of((source * 2 + which) * kz, kz)
            flat = ref[...].reshape(ref.shape[0] * pos, kz)
            x_ref[image * pos : image * pos + flat.shape[0], pl.ds(lane, kz)] = flat
        acts = jnp.dot(x_ref[...], pa_ref[...], preferred_element_type=jnp.float32)
        hi = acts.astype(jnp.bfloat16)
        acts_ref[:, :ka] = hi
        acts_ref[:, ka:] = (acts - hi.astype(jnp.float32)).astype(jnp.bfloat16)

    def finish(stream_ref):
        y = jnp.dot(x_ref[...], w_ref[0], preferred_element_type=jnp.float32)
        width = y.shape[1]
        y = y.reshape(imgs, pos, width) + stream_ref[...].astype(jnp.float32)
        pooled = (jnp.sum(jnp.maximum(y, 0.0), axis=1) / pos).astype(jnp.bfloat16)
        for f in range(pooled_ref.shape[0]):
            pooled_ref[f, 0] = pooled
        mask = jnp.where(y > 0.0, 1.0, 0.0).astype(jnp.bfloat16)
        for i in range(imgs):
            both = lax.dot_general(
                acts_ref[i * pos : (i + 1) * pos, :], mask[i], TN, preferred_element_type=jnp.float32
            )
            m_ref[i] = both[:ka] + both[ka:]

    @pl.when(step == 0)
    def _():
        finish(own_ref.at[0])

    @pl.when(step == 1)
    def _():
        finish(other_ref)


def conv(place, got, w_all, stream2, stream_other, proj_act, nz, fs):
    plan = tuple((sub, shift, image) for sub, shift, image, _ in got)
    blocks = [b for _, _, _, b in got]
    half, pos, kz = blocks[0].shape
    _, depth, width = w_all.shape
    ka = proj_act.shape[1]

    def column(i, place):
        return jnp.where(i == 0, place[1], 1 - place[1])

    def whole(shape):
        return pl.BlockSpec(shape, lambda i, p: (0,) * len(shape), pipeline_mode=pl.Buffered(1))

    grid = pltpu.PrefetchScalarGridSpec(
        num_scalar_prefetch=1,
        grid=(2,),
        in_specs=[whole(b.shape) for b in blocks]
        + [
            pl.BlockSpec((1, depth, width), lambda i, p: (column(i, p), 0, 0)),
            pl.BlockSpec((1, half, pos, width), lambda i, p: (p[1], 0, 0, 0), pipeline_mode=pl.Buffered(1)),
            whole(stream_other.shape),
            whole(proj_act.shape),
        ],
        out_specs=[
            pl.BlockSpec((fs, 1, half, width), lambda i, p: (0, column(i, p), 0, 0)),
            pl.BlockSpec((half, ka, width), lambda i, p: (0, 0, column(i, p))),
        ],
        scratch_shapes=[
            pltpu.VMEM((half * pos, depth), jnp.bfloat16),
            pltpu.VMEM((half * pos, 2 * ka), jnp.bfloat16),
        ],
    )
    return pl.pallas_call(
        functools.partial(conv_body, nz, plan),
        grid_spec=grid,
        out_shape=[
            jax.ShapeDtypeStruct((fs, 2, half, width), jnp.bfloat16),
            jax.ShapeDtypeStruct((half, ka, 2 * width), jnp.float32),
        ],
        compiler_params=LIMIT,
        name="conv_pool_mask",
    )(place, *blocks, w_all, stream2, stream_other, proj_act)


def logits_body(pooled_ref, head_ref, out_ref):
    share = out_ref.shape[2]
    for s in range(out_ref.shape[0]):
        out_ref[s] = jnp.dot(
            pooled_ref[...], head_ref[:, s * share : (s + 1) * share], preferred_element_type=jnp.float32
        )


def logits_slices(pooled, head, n):
    rows = pooled.shape[0]
    return pl.pallas_call(
        logits_body,
        in_specs=[VM, VM],
        out_specs=VM,
        out_shape=jax.ShapeDtypeStruct((n, rows, head.shape[1] // n), jnp.float32),
        compiler_params=LIMIT,
        name="logits_slices",
    )(pooled, head)


def back_body(expo_ref, head_ref, out_ref):
    depth = head_ref.shape[0]
    e = jnp.concatenate([expo_ref[s] for s in range(expo_ref.shape[0])], axis=1)
    out_ref[:, :depth] = lax.dot_general(e, head_ref[...], NT, preferred_element_type=jnp.float32)
    total = jnp.sum(e.astype(jnp.float32), axis=1, keepdims=True)
    out_ref[:, depth:] = jnp.broadcast_to(total, (out_ref.shape[0], 128))


def back(expo, head):
    rows = expo.shape[1]
    return pl.pallas_call(
        back_body,
        in_specs=[VM, VM],
        out_specs=VM,
        out_shape=jax.ShapeDtypeStruct((rows, head.shape[0] + 128), jnp.float32),
        compiler_params=LIMIT,
        name="back",
    )(expo, head)


def final_body(pos, m_ref, part_ref, hot_ref, pe_ref, out_ref):
    width = hot_ref.shape[3]
    imgs, ka, _ = m_ref.shape
    ke = pe_ref.shape[2]
    acc = jnp.zeros((imgs * ka, ke), jnp.float32)
    for h in range(2):
        part = sum(part_ref[a, h] for a in range(part_ref.shape[0]))
        hot = sum(hot_ref[a, h].astype(jnp.float32) for a in range(hot_ref.shape[0]))
        d = part[:, :width] / part[:, width : width + 1] - hot
        d = (d / pos).astype(jnp.bfloat16).astype(jnp.float32)
        v = (m_ref[:, :, h * width : (h + 1) * width] * d[:, None, :]).reshape(imgs * ka, width)
        v_hi = v.astype(jnp.bfloat16)
        v_lo = (v - v_hi.astype(jnp.float32)).astype(jnp.bfloat16)
        acc += jnp.dot(v_hi, pe_ref[h], preferred_element_type=jnp.float32)
        acc += jnp.dot(v_lo, pe_ref[h], preferred_element_type=jnp.float32)
    out_ref[...] = acc


def final(m, part, hot, pe, pos):
    imgs, ka, _ = m.shape
    return pl.pallas_call(
        functools.partial(final_body, pos),
        in_specs=[VM] * 4,
        out_specs=VM,
        out_shape=jax.ShapeDtypeStruct((imgs * ka, pe.shape[2]), jnp.float32),
        compiler_params=LIMIT,
        name="final",
    )(m, part, hot, pe)


def per_device(stream, mid, conv_weight, head_weight, labels, proj_act, proj_err):
    images, pos, width = stream.shape
    kz = mid.shape[2]
    half = images // 2
    nz = lax.axis_size("z")
    parts = nz * 2
    fs = lax.axis_size("yhi") * lax.axis_size("core")
    block = head_weight.shape[1]
    me_y = lax.axis_index("ylo")
    f = lax.axis_index("yhi") * lax.axis_size("core") + lax.axis_index("core")
    swap = [(0, 1), (1, 0)]

    mid = mid.reshape(2, half, pos, kz)
    stream = stream.reshape(2, half, pos, width)
    mine = lax.dynamic_index_in_dim(mid, me_y, 0, keepdims=False)
    theirs = lax.dynamic_index_in_dim(mid, 1 - me_y, 0, keepdims=False)
    swapped = lax.ppermute(theirs, "ylo", swap)
    w_all = lax.all_gather(conv_weight, ("ylo", "yhi", "core"), axis=0)
    w_all = w_all.reshape(2, fs * conv_weight.shape[0], width)
    got = [(0,) + g for g in ring(mine, nz)] + [(1,) + g for g in ring(swapped, nz)]
    stream_other = lax.ppermute(
        lax.dynamic_index_in_dim(stream, 1 - me_y, 0, keepdims=False), "ylo", swap
    )

    classes = f * block + jnp.arange(block, dtype=jnp.int32)
    onehot = (labels[:, None] == classes[None, :]).astype(jnp.bfloat16)
    hot = lax.dot_general(onehot, head_weight, NT, preferred_element_type=jnp.float32)
    hot = hot.astype(jnp.bfloat16).reshape(2 * fs, half, width)
    hot = lax.all_to_all(hot, ROWS, 0, 0).reshape(fs, 2, half, width)
    pe = lax.all_gather(proj_err, "ylo", axis=0)

    *blocks, w_all, stream_other, hot, pe = lax.optimization_barrier(
        [g[3] for g in got] + [w_all, stream_other, hot, pe]
    )
    got = [g[:3] + (b,) for g, b in zip(got, blocks)]
    place = jnp.stack([lax.axis_index("z"), me_y]).astype(jnp.int32)
    pooled, m = conv(place, got, w_all, stream, stream_other, proj_act, nz, fs)

    pooled = lax.all_to_all(pooled.reshape(2 * fs, half, width), ROWS, 0, 0)
    part = logits_slices(pooled.reshape(2 * fs * half, width), head_weight, parts)
    part = lax.all_to_all(part, CHAN, 0, 0)
    expo = jnp.minimum(jnp.exp(jnp.sum(part, axis=0)), BF16_TOP).astype(jnp.bfloat16)
    expo = lax.all_to_all(jnp.broadcast_to(expo, (parts,) + expo.shape), CHAN, 0, 0)

    part = back(expo, head_weight).reshape(2 * fs, half, width + 128)
    part = lax.all_to_all(part, ROWS, 0, 0).reshape(fs, 2, half, width + 128)

    grads = final(m, part, hot, pe, pos)
    grads = grads.reshape(half, parts, -1).transpose(1, 0, 2)
    grads = lax.all_to_all(grads, CHAN, 0, 0)
    grads = jnp.sum(grads.reshape(nz, 2, half, -1), axis=0)
    return grads.reshape(images, -1)


def solution(mesh):
    fine = Mesh(mesh.devices.reshape(4, 8, 2, 2, 2), ("seed", "z", "ylo", "yhi", "core"))
    rows = ("seed", "yhi", "core")
    in_specs = (
        P(rows, None, CHAN),
        P(rows, None, CHAN),
        P(rows, CHAN),
        P(("seed", "z", "ylo"), ("yhi", "core")),
        P(),
        P(),
        P(CHAN, None),
    )
    return jax.shard_map(
        per_device, mesh=fine, in_specs=in_specs, out_specs=P(rows, CHAN), check_vma=False
    )
```

time: 302 us -> 190 us (0.63)
  waiting for transfers between devices: 134 us -> 12.7 us
  starting transfers between devices: 16.8 us -> 38.9 us
  Pallas kernels: 34.5 us -> 16.1 us
  local copies, waits for them, and re-layouts: 4.42 us -> 12.6 us
    all_to_all x3 -> x0, waiting for transfers between devices: 63.8 us -> none  [the longest x1 40.2 us: per_device(): stream2 = lax.all_to_all(stream.reshape(2, half, pos, width), 'ylo', 0, 0)]
    all_to_all x1 -> x4, blocking collectives: 13.3 us -> 73.5 us  [the longest x1 33.8 us: per_device(): part = lax.all_to_all(part, CHAN, 0, 0)]
    all_gather x1 -> x0, waiting for transfers between devices: 60 us -> none  [per_device(): mid_all = lax.all_gather(mid2, 'z', axis=0)]
    all_gather x2 -> x0, blocking collectives: 58.7 us -> none  [the longest x1 37.3 us: per_device(): expo = lax.all_gather(expo, CHAN, axis=0)]
    ppermute x0 -> x18, starting transfers between devices: none -> 34.5 us  [the longest x6 20.9 us: ring(): l = lax.ppermute(l, 'z', left)]
    pallas_call x4, Pallas kernels: 34.5 us -> 16.1 us  [the longest x1 13.3 us: conv(): pl.pallas_call(functools.partial(conv_body, nz, plan), grid_spec=grid, ou...]
    all_to_all x3 -> x0, starting transfers between devices: 13.1 us -> none  [the longest x1 5.41 us: per_device(): part = lax.all_to_all(part, CHAN, 0, 0)]
    ppermute x0 -> x18, waiting for transfers between devices: none -> 11.9 us  [the longest x6 10.6 us: ring(): r = lax.ppermute(r, 'z', right)]
  transfers between devices with their start and end apart: 6 -> 20, of which waited for: 4 -> 5; matrix products, arithmetic and copies ran while one was open for 2% -> 6% of each run, Pallas kernels for 3% -> 0%
where the time goes in v2:
time: 190 us; the launch traced here: 189 us
  blocking collectives  90.6 us (48%)
  starting transfers between devices  38.9 us (20%)
  Pallas kernels  16.1 us (8%)
  between operations  13.6 us (7%)
  waiting for transfers between devices  12.7 us (7%)
  local copies, waits for them, and re-layouts  12.6 us (7%)
  matrix products  4.26 us (2%)
    all_to_all x1, blocking collectives, per_device(): part = lax.all_to_all(part, CHAN, 0, 0)  33.8 us
    ppermute x6, starting transfers between devices, ring(): l = lax.ppermute(l, 'z', left)  20.9 us
    all_to_all x1, blocking collectives, per_device(): lax.all_to_all(jnp.broadcast_to(expo, (parts,) + expo.shape), CHAN, 0, 0)  20.7 us
    pallas_call x1, Pallas kernels, conv(): pl.pallas_call(functools.partial(conv_body, nz, plan), grid_spec=grid, ou...  13.3 us
    all_to_all x1, blocking collectives, per_device(): grads = lax.all_to_all(grads, CHAN, 0, 0)  11.6 us
    ppermute x6, waiting for transfers between devices, ring(): r = lax.ppermute(r, 'z', right)  10.6 us
    all_to_all x1, blocking collectives, per_device(): pooled = lax.all_to_all(pooled.reshape(2 * fs, half, width), ROWS, 0, 0)  9.62 us
    all_to_all x1, blocking collectives, per_device(): part = lax.all_to_all(part, ROWS, 0, 0).reshape(fs, 2, half, width + 128)  9.38 us
  transfers between devices with their start and end apart: 20, of which 5 were waited for; matrix products, arithmetic and copies ran while one was open for 6% of the time, Pallas kernels for 0%

profile of v2, /device:TPU:2, one launch (start us, length us, event | category | flops | bytes accessed | tf_op | source)
XLA Modules:
  0.0 189.5 jit_solution(1211460971849147004)
XLA Ops:
  7.3 1.1 dynamic-slice_bitcast_fusion.1
  8.4 1.7 collective-permute-start.8
  10.0 1.9 %collective-permute-start = (bf16[8,144,128]{2,1,0:T(8,128)(2,1)S(1)}, bf16[8,144,128]{2,1,0:T(8,128)(2,1)S(1)}, u32[]{:S(2)}, u32[]{:S(2)}) collective-permute-start(bf16[8,144,128]{2,1,0:T(8,128)(2,1)S(1)} %get-tuple-element.29.refs_0_), channel_id=1, source_target_pairs={{0,8},{8,16},{16,24},{24,32},{32,40},{40,48},{48,56},{56,0},{1,9},... | collective-permute-start | bytes 884744 | tf_op jit(solution)/shard_map/ppermute | solution.py:25
  12.0 3.9 %collective-permute-start.1 = (bf16[8,144,128]{2,1,0:T(8,128)(2,1)S(1)}, bf16[8,144,128]{2,1,0:T(8,128)(2,1)S(1)}, u32[]{:S(2)}, u32[]{:S(2)}) collective-permute-start(bf16[8,144,128]{2,1,0:T(8,128)(2,1)S(1)} %get-tuple-element.29.refs_0_), channel_id=1, source_target_pairs={{0,56},{8,0},{16,8},{24,16},{32,24},{40,32},{48,40},{56,48},{1,57}... | collective-permute-start | bytes 884744 | tf_op jit(solution)/shard_map/ppermute | solution.py:26
  15.9 1.3 collective-permute-done.8.refs_9_
  17.2 1.9 %collective-permute-start.9 = (bf16[8,144,128]{2,1,0:T(8,128)(2,1)S(1)}, bf16[8,144,128]{2,1,0:T(8,128)(2,1)S(1)}, u32[]{:S(2)}, u32[]{:S(2)}) collective-permute-start(bf16[8,144,128]{2,1,0:T(8,128)(2,1)S(1)} %collective-permute-done.8.refs_9_), channel_id=1, source_target_pairs={{0,8},{8,16},{16,24},{24,32},{32,40},{40,48},{48,56},{56,0},{1,9},... | collective-permute-start | bytes 884744 | tf_op jit(solution)/shard_map/ppermute | solution.py:25
  19.1 3.9 %collective-permute-start.10 = (bf16[8,144,128]{2,1,0:T(8,128)(2,1)S(1)}, bf16[8,144,128]{2,1,0:T(8,128)(2,1)S(1)}, u32[]{:S(2)}, u32[]{:S(2)}) collective-permute-start(bf16[8,144,128]{2,1,0:T(8,128)(2,1)S(1)} %collective-permute-done.8.refs_9_), channel_id=1, source_target_pairs={{0,56},{8,0},{16,8},{24,16},{32,24},{40,32},{48,40},{56,48},{1,57}... | collective-permute-start | bytes 884744 | tf_op jit(solution)/shard_map/ppermute | solution.py:26
  23.1 2.4 %dynamic-slice_bitcast_fusion = bf16[8,144,512]{2,1,0:T(8,128)(2,1)} fusion(bf16[2,8,144,512]{3,2,1,0:T(8,128)(2,1)} %bitcast.29, s32[]{:T(128)S(6)} %select_n.10), kind=kLoop, calls=%fused_computation | loop fusion | bytes 2359300 | tf_op jit(solution)/shard_map/jit(dynamic_index_in_dim)/squeeze | solution.py:215
  25.5 1.6 collective-permute-start.17
  27.1 3.2 %collective-permute-start.3 = (bf16[8,144,128]{2,1,0:T(8,128)(2,1)S(1)}, bf16[8,144,128]{2,1,0:T(8,128)(2,1)}, u32[]{:S(2)}, u32[]{:S(2)}) collective-permute-start(bf16[8,144,128]{2,1,0:T(8,128)(2,1)S(1)} %collective-permute-done.1.refs_2_), channel_id=1, source_target_pairs={{0,56},{8,0},{16,8},{24,16},{32,24},{40,32},{48,40},{56,48},{1,57}... | collective-permute-start | bytes 884744 | tf_op jit(solution)/shard_map/ppermute | solution.py:26
  30.3 3.2 %collective-permute-start.12 = (bf16[8,144,128]{2,1,0:T(8,128)(2,1)S(1)}, bf16[8,144,128]{2,1,0:T(8,128)(2,1)}, u32[]{:S(2)}, u32[]{:S(2)}) collective-permute-start(bf16[8,144,128]{2,1,0:T(8,128)(2,1)S(1)} %collective-permute-done.10.refs_11_), channel_id=1, source_target_pairs={{0,56},{8,0},{16,8},{24,16},{32,24},{40,32},{48,40},{56,48},{1,57}... | collective-permute-start | bytes 884744 | tf_op jit(solution)/shard_map/ppermute | solution.py:26
  34.3 3.9 %collective-permute-done.2.refs_3_ = bf16[8,144,128]{2,1,0:T(8,128)(2,1)S(1)} collective-permute-done((bf16[8,144,128]{2,1,0:T(8,128)(2,1)S(1)}, bf16[8,144,128]{2,1,0:T(8,128)(2,1)S(1)}, u32[]{:S(2)}, u32[]{:S(2)}) %collective-permute-start.2) | collective-permute-done | bytes 294944 | tf_op jit(solution)/shard_map/ppermute | solution.py:25
  38.2 3.3 %collective-permute-start.5 = (bf16[8,144,128]{2,1,0:T(8,128)(2,1)}, bf16[8,144,128]{2,1,0:T(8,128)(2,1)S(1)}, u32[]{:S(2)}, u32[]{:S(2)}) collective-permute-start(bf16[8,144,128]{2,1,0:T(8,128)(2,1)} %collective-permute-done.3.refs_4_), channel_id=1, source_target_pairs={{0,56},{8,0},{16,8},{24,16},{32,24},{40,32},{48,40},{56,48},{1,57}... | collective-permute-start | bytes 884744 | tf_op jit(solution)/shard_map/ppermute | solution.py:26
  41.6 3.1 %collective-permute-done.11.refs_12_ = bf16[8,144,128]{2,1,0:T(8,128)(2,1)} collective-permute-done((bf16[8,144,128]{2,1,0:T(8,128)(2,1)S(1)}, bf16[8,144,128]{2,1,0:T(8,128)(2,1)}, u32[]{:S(2)}, u32[]{:S(2)}) %collective-permute-start.11) | collective-permute-done | bytes 294944 | tf_op jit(solution)/shard_map/ppermute | solution.py:25
  44.7 3.2 %collective-permute-start.14 = (bf16[8,144,128]{2,1,0:T(8,128)(2,1)}, bf16[8,144,128]{2,1,0:T(8,128)(2,1)S(1)}, u32[]{:S(2)}, u32[]{:S(2)}) collective-permute-start(bf16[8,144,128]{2,1,0:T(8,128)(2,1)} %collective-permute-done.12.refs_13_), channel_id=1, source_target_pairs={{0,56},{8,0},{16,8},{24,16},{32,24},{40,32},{48,40},{56,48},{1,57}... | collective-permute-start | bytes 884744 | tf_op jit(solution)/shard_map/ppermute | solution.py:26
  47.9 3.0 %collective-permute-done.4.refs_5_ = bf16[8,144,128]{2,1,0:T(8,128)(2,1)S(1)} collective-permute-done((bf16[8,144,128]{2,1,0:T(8,128)(2,1)S(1)}, bf16[8,144,128]{2,1,0:T(8,128)(2,1)S(1)}, u32[]{:S(2)}, u32[]{:S(2)}) %collective-permute-start.4) | collective-permute-done | bytes 294944 | tf_op jit(solution)/shard_map/ppermute | solution.py:25
  52.2 3.2 %collective-permute-start.7 = (bf16[4,144,128]{2,1,0:T(8,128)(2,1)}, bf16[4,144,128]{2,1,0:T(8,128)(2,1)}, u32[]{:S(2)}, u32[]{:S(2)}) collective-permute-start(bf16[4,144,128]{2,1,0:T(8,128)(2,1)} %slice.17), channel_id=1, source_target_pairs={{0,56},{8,0},{16,8},{24,16},{32,24},{40,32},{48,40},{56,48},{1,57}... | collective-permute-start | bytes 442376 | tf_op jit(solution)/shard_map/ppermute | solution.py:30
  57.4 3.2 %collective-permute-start.16 = (bf16[4,144,128]{2,1,0:T(8,128)(2,1)}, bf16[4,144,128]{2,1,0:T(8,128)(2,1)}, u32[]{:S(2)}, u32[]{:S(2)}) collective-permute-start(bf16[4,144,128]{2,1,0:T(8,128)(2,1)} %slice.19), channel_id=1, source_target_pairs={{0,56},{8,0},{16,8},{24,16},{32,24},{40,32},{48,40},{56,48},{1,57}... | collective-permute-start | bytes 442376 | tf_op jit(solution)/shard_map/ppermute | solution.py:30
  60.7 4.3 %fusion = bf16[8,8,512]{2,1,0:T(8,128)(2,1)} fusion(bf16[512,4096]{1,0:T(8,128)(2,1)} %head_ref.3, s32[4096]{0:T(1024)S(1)} %iota_add_fusion, s32[64]{0:T(128)S(1)} %copy-done.8), kind=kOutput, calls=%fused_computation.2 | convolution fusion | flops 268730368 | bytes 4276480 | tf_op jit(solution)/shard_map/dot_general | solution.py:220
  64.9 4.4 %all-to-all-start = ((bf16[8,8,512]{2,1,0:T(8,128)(2,1)}), bf16[8,8,512]{2,1,0:T(8,128)(2,1)S(1)}, u32[]{:S(2)}, u32[]{:S(2)}) async-start(bf16[8,8,512]{2,1,0:T(8,128)(2,1)} %fusion), calls=%async_computation | async-start | bytes 131072 | tf_op jit(solution)/shard_map/all_to_all | solution.py:222
  69.4 5.5 %all-gather.1 = bf16[1024,64]{0,1:T(8,128)(2,1)S(1)} all-gather(bf16[512,64]{0,1:T(8,128)(2,1)S(1)} %copy-done.7), channel_id=3, replica_groups=mesh['seed'=4,'z'=8,'ylo'=2,'yhi'=2,'core'=2] {'ylo'}, dimensions={0}, use_global_device_ids=true | all-gather | bytes 196608 | tf_op jit(solution)/shard_map/all_gather | solution.py:223
  75.1 1.2 copy.17.refs_21_
  76.4 1.0 copy-done.4
  77.4 1.0 copy-done.6
  78.3 13.3 %conv_pool_mask.1 = (bf16[4,2,8,512]{3,2,1,0:T(8,128)(2,1)S(1)}, f32[8,32,1024]{2,1,0:T(8,128)}) custom-call(s32[2]{0:T(128)S(1)} %pad_add_fusion.place_ref, bf16[8,144,128]{2,1,0:T(8,128)(2,1)S(1)} %get-tuple-element.29.refs_0_, bf16[8,144,128]{2,1,0:T(8,128)(2,1)S(1)} %collective-permute-done.refs_1_, ...), custom_call_target="tpu_custom_call" | custom-call | tf_op jit(solution)/shard_map/conv_pool_mask/pallas_call | solution.py:112
  91.7 9.6 %all_to_all.30 = bf16[8,8,512]{2,1,0:T(8,128)(2,1)S(1)} all-to-all(bf16[8,8,512]{2,1,0:T(8,128)(2,1)S(1)} %bitcast.28), channel_id=1, replica_groups=mesh['seed'=4,'z'=8,'ylo'=2,'yhi'=2,'core'=2] {'yhi','core','ylo'}, dimensions={0} | all-to-all | bytes 131072 | tf_op jit(solution)/shard_map/all_to_all | solution.py:232
  102.1 33.8 %all_to_all.31 = f32[16,64,256]{2,1,0:T(8,128)S(1)} all-to-all(f32[16,64,256]{2,1,0:T(8,128)S(1)} %logits_slices.1), channel_id=1, replica_groups=mesh['seed'=4,'z'=8,'ylo'=2,'yhi'=2,'core'=2] {'z','ylo'}, dimensions={0} | all-to-all | bytes 2097152 | tf_op jit(solution)/shard_map/all_to_all | solution.py:234
  136.0 20.7 %all_to_all.32.expo_ref = bf16[16,64,256]{2,1,0:T(8,128)(2,1)S(1)} all-to-all(bf16[16,64,256]{2,1,0:T(8,128)(2,1)S(1)} %broadcast_in_dim.2), channel_id=1, replica_groups=mesh['seed'=4,'z'=8,'ylo'=2,'yhi'=2,'core'=2] {'z','ylo'}, dimensions={0} | all-to-all | bytes 1048576 | tf_op jit(solution)/shard_map/all_to_all | solution.py:236
  156.8 2.2 %copy-done.1 = bf16[512,4096]{1,0:T(8,128)(2,1)S(1)} copy-done((bf16[512,4096]{1,0:T(8,128)(2,1)S(1)}, bf16[512,4096]{1,0:T(8,128)(2,1)}, u32[]{:S(2)}) %copy-start.1) | copy-done | bytes 4194328
  159.0 1.4 back.1
  160.3 9.4 %all_to_all.33 = f32[8,8,640]{2,1,0:T(8,128)S(1)} all-to-all(f32[8,8,640]{2,1,0:T(8,128)S(1)} %bitcast.24), channel_id=1, replica_groups=mesh['seed'=4,'z'=8,'ylo'=2,'yhi'=2,'core'=2] {'yhi','core','ylo'}, dimensions={0} | all-to-all | bytes 327680 | tf_op jit(solution)/shard_map/all_to_all | solution.py:239
  170.3 11.6 %all_to_all.34 = f32[16,8,128]{2,1,0:T(8,128)S(1)} all-to-all(f32[16,8,128]{2,1,0:T(8,128)S(1)} %copy.18), channel_id=1, replica_groups=mesh['seed'=4,'z'=8,'ylo'=2,'yhi'=2,'core'=2] {'z','ylo'}, dimensions={0} | all-to-all | bytes 131072 | tf_op jit(solution)/shard_map/all_to_all | solution.py:243
  (54 shorter events, 7.4 us)
Async XLA Ops:
  6.5 54.1 %copy-start.8 = (s32[64]{0:T(128)S(1)}, s32[64]{0:T(128)}, u32[]{:S(2)}) copy-start(s32[64]{0:T(128)} %param.11) | copy-start | bytes 772
  6.5 69.9 %all-gather.4.cloned.1.call-start = ((), (), s32[]{:S(2)}) async-start(), calls=%async_computation.6 | async-start | bytes 4718592 | tf_op jit(solution)/shard_map/all_gather | solution.py:211
  8.4 61.0 %copy-start.7 = (bf16[512,64]{0,1:T(8,128)(2,1)S(1)}, bf16[512,64]{0,1:T(8,128)(2,1)}, u32[]{:S(2)}) copy-start(bf16[512,64]{0,1:T(8,128)(2,1)} %param.13) | copy-start | bytes 196612
  8.4 8.8 %collective-permute-start.8 = (bf16[8,144,128]{2,1,0:T(8,128)(2,1)S(1)}, bf16[8,144,128]{2,1,0:T(8,128)(2,1)S(1)}, u32[]{:S(2)}, u32[]{:S(2)}) collective-permute-start(bf16[8,144,128]{2,1,0:T(8,128)(2,1)S(1)} %get-tuple-element.53), channel_id=1, source_target_pairs={{0,4},{4,0},{1,5},{5,1},{2,6},{6,2},{3,7},{7,3},{8,12},{12,8},{9,1... | collective-permute-start | bytes 884744 | tf_op jit(solution)/shard_map/ppermute | solution.py:210
  10.0 17.0 %collective-permute-start = (bf16[8,144,128]{2,1,0:T(8,128)(2,1)S(1)}, bf16[8,144,128]{2,1,0:T(8,128)(2,1)S(1)}, u32[]{:S(2)}, u32[]{:S(2)}) collective-permute-start(bf16[8,144,128]{2,1,0:T(8,128)(2,1)S(1)} %get-tuple-element.29.refs_0_), channel_id=1, source_target_pairs={{0,8},{8,16},{16,24},{24,32},{32,40},{40,48},{48,56},{56,0},{1,9},... | collective-permute-start | bytes 884744 | tf_op jit(solution)/shard_map/ppermute | solution.py:25
  12.0 15.1 %collective-permute-start.1 = (bf16[8,144,128]{2,1,0:T(8,128)(2,1)S(1)}, bf16[8,144,128]{2,1,0:T(8,128)(2,1)S(1)}, u32[]{:S(2)}, u32[]{:S(2)}) collective-permute-start(bf16[8,144,128]{2,1,0:T(8,128)(2,1)S(1)} %get-tuple-element.29.refs_0_), channel_id=1, source_target_pairs={{0,56},{8,0},{16,8},{24,16},{32,24},{40,32},{48,40},{56,48},{1,57}... | collective-permute-start | bytes 884744 | tf_op jit(solution)/shard_map/ppermute | solution.py:26
  17.2 13.1 %collective-permute-start.9 = (bf16[8,144,128]{2,1,0:T(8,128)(2,1)S(1)}, bf16[8,144,128]{2,1,0:T(8,128)(2,1)S(1)}, u32[]{:S(2)}, u32[]{:S(2)}) collective-permute-start(bf16[8,144,128]{2,1,0:T(8,128)(2,1)S(1)} %collective-permute-done.8.refs_9_), channel_id=1, source_target_pairs={{0,8},{8,16},{16,24},{24,32},{32,40},{40,48},{48,56},{56,0},{1,9},... | collective-permute-start | bytes 884744 | tf_op jit(solution)/shard_map/ppermute | solution.py:25
  19.1 11.2 %collective-permute-start.10 = (bf16[8,144,128]{2,1,0:T(8,128)(2,1)S(1)}, bf16[8,144,128]{2,1,0:T(8,128)(2,1)S(1)}, u32[]{:S(2)}, u32[]{:S(2)}) collective-permute-start(bf16[8,144,128]{2,1,0:T(8,128)(2,1)S(1)} %collective-permute-done.8.refs_9_), channel_id=1, source_target_pairs={{0,56},{8,0},{16,8},{24,16},{32,24},{40,32},{48,40},{56,48},{1,57}... | collective-permute-start | bytes 884744 | tf_op jit(solution)/shard_map/ppermute | solution.py:26
  25.5 50.9 %collective-permute-start.17 = (bf16[8,144,512]{2,1,0:T(8,128)(2,1)}, bf16[8,144,512]{2,1,0:T(8,128)(2,1)}, u32[]{:S(2)}, u32[]{:S(2)}) collective-permute-start(bf16[8,144,512]{2,1,0:T(8,128)(2,1)} %dynamic-slice_bitcast_fusion), channel_id=1, source_target_pairs={{0,4},{4,0},{1,5},{5,1},{2,6},{6,2},{3,7},{7,3},{8,12},{12,8},{9,1... | collective-permute-start | bytes 3538952 | tf_op jit(solution)/shard_map/ppermute | solution.py:214
  27.1 11.2 %collective-permute-start.2 = (bf16[8,144,128]{2,1,0:T(8,128)(2,1)S(1)}, bf16[8,144,128]{2,1,0:T(8,128)(2,1)S(1)}, u32[]{:S(2)}, u32[]{:S(2)}) collective-permute-start(bf16[8,144,128]{2,1,0:T(8,128)(2,1)S(1)} %collective-permute-done.refs_1_), channel_id=1, source_target_pairs={{0,8},{8,16},{16,24},{24,32},{32,40},{40,48},{48,56},{56,0},{1,9},... | collective-permute-start | bytes 884744 | tf_op jit(solution)/shard_map/ppermute | solution.py:25
  27.1 11.2 %collective-permute-start.3 = (bf16[8,144,128]{2,1,0:T(8,128)(2,1)S(1)}, bf16[8,144,128]{2,1,0:T(8,128)(2,1)}, u32[]{:S(2)}, u32[]{:S(2)}) collective-permute-start(bf16[8,144,128]{2,1,0:T(8,128)(2,1)S(1)} %collective-permute-done.1.refs_2_), channel_id=1, source_target_pairs={{0,56},{8,0},{16,8},{24,16},{32,24},{40,32},{48,40},{56,48},{1,57}... | collective-permute-start | bytes 884744 | tf_op jit(solution)/shard_map/ppermute | solution.py:26
  30.3 14.3 %collective-permute-start.11 = (bf16[8,144,128]{2,1,0:T(8,128)(2,1)S(1)}, bf16[8,144,128]{2,1,0:T(8,128)(2,1)}, u32[]{:S(2)}, u32[]{:S(2)}) collective-permute-start(bf16[8,144,128]{2,1,0:T(8,128)(2,1)S(1)} %collective-permute-done.9.refs_10_), channel_id=1, source_target_pairs={{0,8},{8,16},{16,24},{24,32},{32,40},{40,48},{48,56},{56,0},{1,9},... | collective-permute-start | bytes 884744 | tf_op jit(solution)/shard_map/ppermute | solution.py:25
  30.3 14.3 %collective-permute-start.12 = (bf16[8,144,128]{2,1,0:T(8,128)(2,1)S(1)}, bf16[8,144,128]{2,1,0:T(8,128)(2,1)}, u32[]{:S(2)}, u32[]{:S(2)}) collective-permute-start(bf16[8,144,128]{2,1,0:T(8,128)(2,1)S(1)} %collective-permute-done.10.refs_11_), channel_id=1, source_target_pairs={{0,56},{8,0},{16,8},{24,16},{32,24},{40,32},{48,40},{56,48},{1,57}... | collective-permute-start | bytes 884744 | tf_op jit(solution)/shard_map/ppermute | solution.py:26
  33.6 0.8 copy-start.3
  38.2 36.8 %copy-start.5 = (bf16[8,144,128]{2,1,0:T(8,128)(2,1)}, bf16[8,144,128]{2,1,0:T(8,128)(2,1)S(1)}, u32[]{:S(2)}) copy-start(bf16[8,144,128]{2,1,0:T(8,128)(2,1)S(1)} %collective-permute-done.2.refs_3_) | copy-start | bytes 884740
  38.2 12.6 %collective-permute-start.4 = (bf16[8,144,128]{2,1,0:T(8,128)(2,1)S(1)}, bf16[8,144,128]{2,1,0:T(8,128)(2,1)S(1)}, u32[]{:S(2)}, u32[]{:S(2)}) collective-permute-start(bf16[8,144,128]{2,1,0:T(8,128)(2,1)S(1)} %collective-permute-done.2.refs_3_), channel_id=1, source_target_pairs={{0,8},{8,16},{16,24},{24,32},{32,40},{40,48},{48,56},{56,0},{1,9},... | collective-permute-start | bytes 884744 | tf_op jit(solution)/shard_map/ppermute | solution.py:25
  38.2 13.3 %collective-permute-start.5 = (bf16[8,144,128]{2,1,0:T(8,128)(2,1)}, bf16[8,144,128]{2,1,0:T(8,128)(2,1)S(1)}, u32[]{:S(2)}, u32[]{:S(2)}) collective-permute-start(bf16[8,144,128]{2,1,0:T(8,128)(2,1)} %collective-permute-done.3.refs_4_), channel_id=1, source_target_pairs={{0,56},{8,0},{16,8},{24,16},{32,24},{40,32},{48,40},{56,48},{1,57}... | collective-permute-start | bytes 884744 | tf_op jit(solution)/shard_map/ppermute | solution.py:26
  44.7 11.5 %collective-permute-start.13 = (bf16[8,144,128]{2,1,0:T(8,128)(2,1)}, bf16[8,144,128]{2,1,0:T(8,128)(2,1)S(1)}, u32[]{:S(2)}, u32[]{:S(2)}) collective-permute-start(bf16[8,144,128]{2,1,0:T(8,128)(2,1)} %collective-permute-done.11.refs_12_), channel_id=1, source_target_pairs={{0,8},{8,16},{16,24},{24,32},{32,40},{40,48},{48,56},{56,0},{1,9},... | collective-permute-start | bytes 884744 | tf_op jit(solution)/shard_map/ppermute | solution.py:25
  44.7 12.1 %collective-permute-start.14 = (bf16[8,144,128]{2,1,0:T(8,128)(2,1)}, bf16[8,144,128]{2,1,0:T(8,128)(2,1)S(1)}, u32[]{:S(2)}, u32[]{:S(2)}) collective-permute-start(bf16[8,144,128]{2,1,0:T(8,128)(2,1)} %collective-permute-done.12.refs_13_), channel_id=1, source_target_pairs={{0,56},{8,0},{16,8},{24,16},{32,24},{40,32},{48,40},{56,48},{1,57}... | collective-permute-start | bytes 884744 | tf_op jit(solution)/shard_map/ppermute | solution.py:26
  51.5 24.8 %collective-permute-start.6 = (bf16[4,144,128]{2,1,0:T(8,128)(2,1)}, bf16[4,144,128]{2,1,0:T(8,128)(2,1)}, u32[]{:S(2)}, u32[]{:S(2)}) collective-permute-start(bf16[4,144,128]{2,1,0:T(8,128)(2,1)} %slice.16), channel_id=1, source_target_pairs={{0,8},{8,16},{16,24},{24,32},{32,40},{40,48},{48,56},{56,0},{1,9},... | collective-permute-start | bytes 442376 | tf_op jit(solution)/shard_map/ppermute | solution.py:29
  52.2 24.1 %collective-permute-start.7 = (bf16[4,144,128]{2,1,0:T(8,128)(2,1)}, bf16[4,144,128]{2,1,0:T(8,128)(2,1)}, u32[]{:S(2)}, u32[]{:S(2)}) collective-permute-start(bf16[4,144,128]{2,1,0:T(8,128)(2,1)} %slice.17), channel_id=1, source_target_pairs={{0,56},{8,0},{16,8},{24,16},{32,24},{40,32},{48,40},{56,48},{1,57}... | collective-permute-start | bytes 442376 | tf_op jit(solution)/shard_map/ppermute | solution.py:30
  56.8 19.6 %collective-permute-start.15 = (bf16[4,144,128]{2,1,0:T(8,128)(2,1)}, bf16[4,144,128]{2,1,0:T(8,128)(2,1)}, u32[]{:S(2)}, u32[]{:S(2)}) collective-permute-start(bf16[4,144,128]{2,1,0:T(8,128)(2,1)} %slice.18), channel_id=1, source_target_pairs={{0,8},{8,16},{16,24},{24,32},{32,40},{40,48},{48,56},{56,0},{1,9},... | collective-permute-start | bytes 442376 | tf_op jit(solution)/shard_map/ppermute | solution.py:29
  57.4 18.9 %collective-permute-start.16 = (bf16[4,144,128]{2,1,0:T(8,128)(2,1)}, bf16[4,144,128]{2,1,0:T(8,128)(2,1)}, u32[]{:S(2)}, u32[]{:S(2)}) collective-permute-start(bf16[4,144,128]{2,1,0:T(8,128)(2,1)} %slice.19), channel_id=1, source_target_pairs={{0,56},{8,0},{16,8},{24,16},{32,24},{40,32},{48,40},{56,48},{1,57}... | collective-permute-start | bytes 442376 | tf_op jit(solution)/shard_map/ppermute | solution.py:30
  64.9 11.4 %all-to-all-start = ((bf16[8,8,512]{2,1,0:T(8,128)(2,1)}), bf16[8,8,512]{2,1,0:T(8,128)(2,1)S(1)}, u32[]{:S(2)}, u32[]{:S(2)}) async-start(bf16[8,8,512]{2,1,0:T(8,128)(2,1)} %fusion), calls=%async_computation | async-start | bytes 131072 | tf_op jit(solution)/shard_map/all_to_all | solution.py:222
  76.4 1.0 copy-start.4
  77.4 1.0 copy-start.6
  78.3 22.9 %copy-start = (bf16[512,4096]{1,0:T(8,128)(2,1)S(1)}, bf16[512,4096]{1,0:T(8,128)(2,1)}, u32[]{:S(2)}) copy-start(bf16[512,4096]{1,0:T(8,128)(2,1)} %head_ref.3) | copy-start | bytes 12582916
  135.9 33.8 %copy-start.2 = (f32[8,32,1024]{2,1,0:T(8,128)S(1)}, f32[8,32,1024]{2,1,0:T(8,128)}, u32[]{:S(2)}) copy-start(f32[8,32,1024]{2,1,0:T(8,128)} %get-tuple-element.49.m_ref) | copy-start | bytes 3145732
  156.8 2.2 %copy-start.1 = (bf16[512,4096]{1,0:T(8,128)(2,1)S(1)}, bf16[512,4096]{1,0:T(8,128)(2,1)}, u32[]{:S(2)}) copy-start(bf16[512,4096]{1,0:T(8,128)(2,1)} %head_ref.3) | copy-start | bytes 12582916
Sparse Core Ops, SparseCore 0:
  9.1 63.9 all-gather.3

commit v3 on v2

v3 whole, which is shorter than its diff:
```python
import functools

import jax
import jax.numpy as jnp
from jax import lax
from jax.experimental import pallas as pl
from jax.experimental.pallas import tpu as pltpu
from jax.sharding import Mesh, PartitionSpec as P

CHAN = ("z", "ylo")
SPREAD = ("ylo", "z")
ROWS = ("yhi", "core", "ylo")
W_ORDER = ("yhi", "ylo", "core")
BF16_TOP = 3.3895313892515355e38
NT = (((1,), (1,)), ((), ()))
TN = (((0,), (0,)), ((), ()))
VM = pl.BlockSpec(memory_space=pltpu.VMEM)
HB = pl.BlockSpec(memory_space=pltpu.HBM)
LIMIT = pltpu.CompilerParams(vmem_limit_bytes=16 * 1024 * 1024)


def ring(block, nz, far):
    right = [(i, (i + 1) % nz) for i in range(nz)]
    left = [(i, (i - 1) % nz) for i in range(nz)]
    got = [(0, block)]
    r = l = block
    for k in range(1, nz // 2):
        r = lax.ppermute(r, "z", right)
        l = lax.ppermute(l, "z", left)
        got += [(k, r), (nz - k, l)]
    last = lax.ppermute(r, "z", right) if far == "right" else lax.ppermute(l, "z", left)
    return got + [(nz // 2, last)]


def conv_body(nz, plan, place_ref, *refs):
    count = len(plan)
    blocks = refs[:count]
    w_ref, own_ref, other_ref, pa_ref, hot_ref, pooled_ref, mask_ref, acts_ref = refs[count : count + 8]
    x_ref, wv_ref, sv_ref, mv_ref, x_sem, w_sem, s_sem, m_sem = refs[count + 8 :]
    imgs, pos, kz = blocks[0].shape
    cut = imgs // 2
    ka = pa_ref.shape[1]
    depth, width = wv_ref.shape[1:]
    rows_w = w_ref.shape[3]
    me_z = place_ref[0]
    me_y = place_ref[1]
    columns = (me_y, 1 - me_y)

    def copy_x(part):
        span = pl.ds(part * cut, cut)
        made = []
        for i, (ref, (sub, shift)) in enumerate(zip(blocks, plan)):
            source = lax.rem(me_z + (nz - shift), nz)
            lane = pl.multiple_of((source * 2 + columns[sub]) * kz, kz)
            made.append(
                pltpu.make_async_copy(ref.at[span], x_ref.at[span, :, pl.ds(lane, kz)], x_sem.at[part, i])
            )
        return made

    def copy_w(h):
        return [
            pltpu.make_async_copy(
                w_ref.at[hi, columns[h], core],
                wv_ref.at[h, pl.ds((hi * 2 + core) * rows_w, rows_w)],
                w_sem.at[h, hi * 2 + core],
            )
            for hi in range(2)
            for core in range(2)
        ]

    copies = [copy_w(0) + copy_x(0), copy_x(1), copy_w(1)]
    streams = [
        pltpu.make_async_copy(own_ref.at[me_y], sv_ref.at[0], s_sem.at[0]),
        pltpu.make_async_copy(other_ref, sv_ref.at[1], s_sem.at[1]),
    ]
    for c in copies[0] + [streams[0]] + copies[1] + copies[2] + [streams[1]]:
        c.start()
    pooled_ref[:, :, imgs:] = hot_ref[...]
    sends = []
    for h in range(2):
        for part in range(2):
            if h == 0:
                for c in copies[part]:
                    c.wait()
            elif part == 0:
                for c in copies[2]:
                    c.wait()
            x = x_ref[part * cut : (part + 1) * cut].reshape(cut * pos, depth)
            y = jnp.dot(x, wv_ref[h], preferred_element_type=jnp.float32)
            if h == 0:
                acts = jnp.dot(x, pa_ref[...], preferred_element_type=jnp.float32)
                hi = acts.astype(jnp.bfloat16)
                here = slice(part * cut * pos, (part + 1) * cut * pos)
                acts_ref[here, :ka] = hi
                acts_ref[here, ka:] = (acts - hi.astype(jnp.float32)).astype(jnp.bfloat16)
            if part == 0:
                streams[h].wait()
            y = y.reshape(cut, pos, width) + sv_ref[h, part * cut : (part + 1) * cut].astype(jnp.float32)
            pooled = (jnp.sum(jnp.maximum(y, 0.0), axis=1) / pos).astype(jnp.bfloat16)
            for f in range(pooled_ref.shape[0]):
                pooled_ref[f, columns[h], part * cut : (part + 1) * cut] = pooled
            mv_ref[h, part] = jnp.where(y > 0.0, 1.0, 0.0).astype(jnp.bfloat16)
            sends.append(
                pltpu.make_async_copy(
                    mv_ref.at[h, part], mask_ref.at[columns[h], pl.ds(part * cut, cut)], m_sem.at[h, part]
                )
            )
            sends[-1].start()
    for c in sends:
        c.wait()


def conv(place, got, w_all, stream2, stream_other, proj_act, hot, nz):
    plan = tuple((sub, shift) for sub, shift, _ in got)
    blocks = [b for _, _, b in got]
    half, pos, kz = blocks[0].shape
    fs, _, _, width = hot.shape
    depth, ka = proj_act.shape
    return pl.pallas_call(
        functools.partial(conv_body, nz, plan),
        in_specs=[pl.BlockSpec(memory_space=pltpu.SMEM)] + [HB] * (len(blocks) + 3) + [VM, VM],
        out_specs=[VM, HB, VM],
        out_shape=[
            jax.ShapeDtypeStruct((fs, 2, 2 * half, width), jnp.bfloat16),
            jax.ShapeDtypeStruct((2, half, pos, width), jnp.bfloat16),
            jax.ShapeDtypeStruct((half * pos, 2 * ka), jnp.bfloat16),
        ],
        scratch_shapes=[
            pltpu.VMEM((half, pos, depth), jnp.bfloat16),
            pltpu.VMEM((2, depth, width), jnp.bfloat16),
            pltpu.VMEM((2, half, pos, width), jnp.bfloat16),
            pltpu.VMEM((2, 2, half // 2, pos, width), jnp.bfloat16),
            pltpu.SemaphoreType.DMA((2, len(blocks))),
            pltpu.SemaphoreType.DMA((2, 4)),
            pltpu.SemaphoreType.DMA((2,)),
            pltpu.SemaphoreType.DMA((2, 2)),
        ],
        compiler_params=pltpu.CompilerParams(vmem_limit_bytes=32 * 1024 * 1024),
        name="conv_pool_mask",
    )(place, *[pltpu.with_memory_space_constraint(b, pltpu.HBM) for b in (*blocks, w_all, stream2, stream_other)], proj_act, hot)


def masked_body(acts_ref, mask_ref, m_ref):
    _, imgs, pos, _ = mask_ref.shape
    ka = m_ref.shape[1]
    for i in range(imgs):
        both = lax.dot_general(
            acts_ref[i * pos : (i + 1) * pos, :], mask_ref[0, i], TN, preferred_element_type=jnp.float32
        )
        m_ref[i] = both[:ka] + both[ka:]


def masked_sums(acts, mask):
    two, imgs, pos, width = mask.shape
    ka = acts.shape[1] // 2
    return pl.pallas_call(
        masked_body,
        grid=(two,),
        in_specs=[
            pl.BlockSpec(acts.shape, lambda h: (0, 0)),
            pl.BlockSpec((1, imgs, pos, width), lambda h: (h, 0, 0, 0)),
        ],
        out_specs=pl.BlockSpec((imgs, ka, width), lambda h: (0, 0, h)),
        out_shape=jax.ShapeDtypeStruct((imgs, ka, two * width), jnp.float32),
        compiler_params=LIMIT,
        name="masked_sums",
    )(acts, mask)


def logits_body(both_ref, head_ref, out_ref):
    share = out_ref.shape[2]
    some, rows, width = both_ref.shape
    pooled = both_ref[:, : rows // 2].astype(jnp.float32).reshape(some * rows // 2, width).astype(jnp.bfloat16)
    for s in range(out_ref.shape[0]):
        part = jnp.dot(pooled, head_ref[:, s * share : (s + 1) * share], preferred_element_type=jnp.float32)
        out_ref[s] = part.astype(jnp.bfloat16)


def logits_slices(both, head, n):
    some, rows, _ = both.shape
    return pl.pallas_call(
        logits_body,
        in_specs=[VM, VM],
        out_specs=VM,
        out_shape=jax.ShapeDtypeStruct((n, some * rows // 2, head.shape[1] // n), jnp.bfloat16),
        compiler_params=LIMIT,
        name="logits_slices",
    )(both, head)


def back_body(expo_ref, head_ref, out_ref, hv_ref, sem):
    depth, classes = head_ref.shape
    n, _, share = expo_ref.shape
    pieces = sem.shape[0]
    size = classes // pieces
    copies = [
        pltpu.make_async_copy(head_ref.at[:, pl.ds(p * size, size)], hv_ref.at[p], sem.at[p]) for p in range(pieces)
    ]
    for c in copies:
        c.start()
    e = jnp.concatenate([expo_ref[s] for s in range(n)], axis=1)
    total = jnp.sum(e.astype(jnp.float32), axis=1, keepdims=True)
    out_ref[:, depth:] = jnp.broadcast_to(total, (out_ref.shape[0], 128))
    acc = jnp.zeros((out_ref.shape[0], depth), jnp.float32)
    for p in range(pieces):
        copies[p].wait()
        acc += lax.dot_general(
            e[:, p * size : (p + 1) * size], hv_ref[p], NT, preferred_element_type=jnp.float32
        )
    out_ref[:, :depth] = acc


def back(expo, head):
    rows = expo.shape[1]
    depth, classes = head.shape
    pieces = 4
    return pl.pallas_call(
        back_body,
        in_specs=[VM, HB],
        out_specs=VM,
        out_shape=jax.ShapeDtypeStruct((rows, depth + 128), jnp.float32),
        scratch_shapes=[
            pltpu.VMEM((pieces, depth, classes // pieces), head.dtype),
            pltpu.SemaphoreType.DMA((pieces,)),
        ],
        compiler_params=LIMIT,
        name="back",
    )(expo, pltpu.with_memory_space_constraint(head, pltpu.HBM))


def final_body(pos, m_ref, part_ref, hot_ref, pe_ref, out_ref):
    width = hot_ref.shape[3]
    imgs, ka, _ = m_ref.shape
    ke = pe_ref.shape[2]
    acc = jnp.zeros((imgs * ka, ke), jnp.float32)
    for h in range(2):
        part = sum(part_ref[a, h] for a in range(part_ref.shape[0]))
        hot = sum(hot_ref[a, h, imgs:].astype(jnp.float32) for a in range(hot_ref.shape[0]))
        d = part[:, :width] / part[:, width : width + 1] - hot
        d = (d / pos).astype(jnp.bfloat16).astype(jnp.float32)
        v = (m_ref[:, :, h * width : (h + 1) * width] * d[:, None, :]).reshape(imgs * ka, width)
        v_hi = v.astype(jnp.bfloat16)
        v_lo = (v - v_hi.astype(jnp.float32)).astype(jnp.bfloat16)
        acc += jnp.dot(v_hi, pe_ref[h], preferred_element_type=jnp.float32)
        acc += jnp.dot(v_lo, pe_ref[h], preferred_element_type=jnp.float32)
    out_ref[...] = acc


def final(m, part, hot, pe, pos):
    imgs, ka, _ = m.shape
    return pl.pallas_call(
        functools.partial(final_body, pos),
        in_specs=[VM] * 4,
        out_specs=VM,
        out_shape=jax.ShapeDtypeStruct((imgs * ka, pe.shape[2]), jnp.float32),
        compiler_params=LIMIT,
        name="final",
    )(m, part, hot, pe)


def per_device(stream, mid, conv_weight, head_weight, labels, proj_act, proj_err):
    images, pos, width = stream.shape
    kz = mid.shape[2]
    half = images // 2
    nz = lax.axis_size("z")
    parts = nz * 2
    fs = lax.axis_size("yhi") * lax.axis_size("core")
    block = head_weight.shape[1]
    me_y = lax.axis_index("ylo")
    f = lax.axis_index("yhi") * lax.axis_size("core") + lax.axis_index("core")
    swap = [(0, 1), (1, 0)]

    mid = mid.reshape(2, half, pos, kz)
    stream = stream.reshape(2, half, pos, width)
    mine = lax.dynamic_index_in_dim(mid, me_y, 0, keepdims=False)
    theirs = lax.dynamic_index_in_dim(mid, 1 - me_y, 0, keepdims=False)
    swapped = lax.ppermute(theirs, "ylo", swap)
    w_all = lax.all_gather(conv_weight, W_ORDER, axis=0)
    w_all = w_all.reshape(2, 2, 2, *conv_weight.shape)
    got = [(0,) + g for g in ring(mine, nz, "right")] + [(1,) + g for g in ring(swapped, nz, "left")]
    stream_other = lax.ppermute(
        lax.dynamic_index_in_dim(stream, 1 - me_y, 0, keepdims=False), "ylo", swap
    )
    pe_other = lax.ppermute(proj_err, "ylo", swap)
    low = me_y == 0
    pe = jnp.stack([jnp.where(low, proj_err, pe_other), jnp.where(low, pe_other, proj_err)])

    classes = f * block + jnp.arange(block, dtype=jnp.int32)
    onehot = (labels[:, None] == classes[None, :]).astype(jnp.bfloat16)
    hot = lax.dot_general(onehot, head_weight, NT, preferred_element_type=jnp.float32)
    hot = hot.astype(jnp.bfloat16).reshape(fs, 2, half, width)

    *blocks, w_all, stream_other, pe, hot = lax.optimization_barrier(
        [g[2] for g in got] + [w_all, stream_other, pe, hot]
    )
    got = [g[:2] + (b,) for g, b in zip(got, blocks)]
    place = jnp.stack([lax.axis_index("z"), me_y]).astype(jnp.int32)
    both, mask, acts = conv(place, got, w_all, stream, stream_other, proj_act, hot, nz)

    both = lax.all_to_all(both.reshape(2 * fs, 2 * half, width), ROWS, 0, 0)
    part = lax.all_to_all(logits_slices(both, head_weight, parts), SPREAD, 0, 0)
    mask, both = lax.optimization_barrier((mask, both))
    m = masked_sums(acts, mask)
    part, m = lax.optimization_barrier((part, m))

    logits = jnp.sum(part.astype(jnp.float32), axis=0)
    expo = jnp.minimum(jnp.exp(logits), BF16_TOP).astype(jnp.bfloat16)
    expo = lax.all_to_all(jnp.broadcast_to(expo, (parts,) + expo.shape), SPREAD, 0, 0)

    part = back(expo, head_weight).reshape(2 * fs, half, width + 128)
    part = lax.all_to_all(part, ROWS, 0, 0).reshape(fs, 2, half, width + 128)

    grads = final(m, part, both.reshape(fs, 2, 2 * half, width), pe, pos)
    grads = grads.reshape(half, nz, 2, -1).transpose(2, 1, 0, 3).reshape(parts, half, -1)
    grads = lax.all_to_all(grads, SPREAD, 0, 0)
    grads = jnp.sum(grads.reshape(2, nz, half, -1), axis=1)
    return grads.reshape(images, -1)


def solution(mesh):
    fine = Mesh(mesh.devices.reshape(4, 8, 2, 2, 2), ("seed", "z", "ylo", "yhi", "core"))
    rows = ("seed", "yhi", "core")
    in_specs = (
        P(rows, None, CHAN),
        P(rows, None, CHAN),
        P(rows, CHAN),
        P(("seed", "z", "ylo"), ("yhi", "core")),
        P(),
        P(),
        P(CHAN, None),
    )
    return jax.shard_map(
        per_device, mesh=fine, in_specs=in_specs, out_specs=P(rows, CHAN), check_vma=False
    )
```

time: 190 us -> 213 us (1.12)
  waiting for transfers between devices: 12.7 us -> 84.6 us
  blocking collectives: 90.6 us -> 52.5 us
  starting transfers between devices: 38.9 us -> 30.1 us
  local copies, waits for them, and re-layouts: 12.6 us -> 6.43 us
  Pallas kernels: 16.1 us -> 19.5 us
    ppermute x4 -> x3, waiting for transfers between devices: 0.01 us -> 46.7 us  [the longest x1 43 us: per_device(): pe_other = lax.ppermute(proj_err, 'ylo', swap)]
    all_to_all x4 -> x3, blocking collectives: 75.7 us -> 42.5 us  [the longest x1 18.8 us: per_device(): lax.all_to_all(jnp.broadcast_to(expo, (parts,) + expo.shape), SPREAD, 0, 0)]
    all_to_all x1, waiting for transfers between devices: 0.01 us -> 13.9 us  [per_device(): part = lax.all_to_all(logits_slices(both, head_weight, parts), SPREAD, 0, 0)]
    ppermute x6, waiting for transfers between devices: 10.6 us -> 17.9 us  [ring(): r = lax.ppermute(r, 'z', right)]
    ppermute x6, starting transfers between devices: 20.9 us -> 14.8 us  [ring(): l = lax.ppermute(l, 'z', left)]
    all_gather x1 -> x0, blocking collectives: 5.52 us -> none  [per_device(): pe = lax.all_gather(proj_err, 'ylo', axis=0)]
    ppermute x1, waiting for transfers between devices: 1.31 us -> 5.36 us  [per_device(): swapped = lax.ppermute(theirs, 'ylo', swap)]
    ppermute x4 -> x3, starting transfers between devices: 6.47 us -> 3.76 us  [the longest x1 3.22 us: ring(): lax.ppermute(l, 'z', left)]
  transfers between devices with their start and end apart: 20 -> 19, of which waited for: 5 -> 8; matrix products, arithmetic and copies ran while one was open for 6% -> 3% of each run, Pallas kernels for 0% -> 0%
where the time goes in v3:
time: 213 us
  waiting for transfers between devices  84.6 us (40%)
  blocking collectives  52.5 us (25%)
  starting transfers between devices  30.1 us (14%)
  Pallas kernels  19.5 us (9%)
  between operations  13.7 us (6%)
  local copies, waits for them, and re-layouts  6.43 us (3%)
  matrix products  3.59 us (2%)
  other arithmetic  2.63 us (1%)
    ppermute x1, waiting for transfers between devices, per_device(): pe_other = lax.ppermute(proj_err, 'ylo', swap)  43 us
    all_to_all x1, blocking collectives, per_device(): lax.all_to_all(jnp.broadcast_to(expo, (parts,) + expo.shape), SPREAD, 0, 0)  18.8 us
    ppermute x6, waiting for transfers between devices, ring(): r = lax.ppermute(r, 'z', right)  17.9 us
    ppermute x6, starting transfers between devices, ring(): l = lax.ppermute(l, 'z', left)  14.8 us
    all_to_all x1, waiting for transfers between devices, per_device(): part = lax.all_to_all(logits_slices(both, head_weight, parts), SPREAD, 0, 0)  13.9 us
    pallas_call x1, Pallas kernels, conv(): pl.pallas_call(functools.partial(conv_body, nz, plan), in_specs=[pl.Block...  13.4 us
    all_to_all x1, blocking collectives, per_device(): grads = lax.all_to_all(grads, SPREAD, 0, 0)  12.8 us
    all_to_all x1, blocking collectives, per_device(): both = lax.all_to_all(both.reshape(2 * fs, 2 * half, width), ROWS, 0, 0)  10.9 us
  transfers between devices with their start and end apart: 19, of which 8 were waited for; matrix products, arithmetic and copies ran while one was open for 3% of the time, Pallas kernels for 0%

profile of v3, /device:TPU:2, one launch (start us, length us, event | category | flops | bytes accessed | tf_op | source)
XLA Modules:
  0.0 212.9 jit_solution(2283172676792814578)
XLA Ops:
  7.3 1.1 dynamic-slice_bitcast_fusion.1
  8.4 1.7 collective-permute-start.7
  10.0 1.9 collective-permute-start
  12.0 5.4 %collective-permute-done.7.refs_8_ = bf16[8,144,128]{2,1,0:T(8,128)(2,1)} collective-permute-done((bf16[8,144,128]{2,1,0:T(8,128)(2,1)S(1)}, bf16[8,144,128]{2,1,0:T(8,128)(2,1)}, u32[]{:S(2)}, u32[]{:S(2)}) %collective-permute-start.7) | collective-permute-done | bytes 294944 | tf_op jit(solution)/shard_map/ppermute | solution.py:277
  17.3 5.9 %collective-permute-start.9 = (bf16[8,144,128]{2,1,0:T(8,128)(2,1)}, bf16[8,144,128]{2,1,0:T(8,128)(2,1)}, u32[]{:S(2)}, u32[]{:S(2)}) collective-permute-start(bf16[8,144,128]{2,1,0:T(8,128)(2,1)} %collective-permute-done.7.refs_8_), channel_id=1, source_target_pairs={{0,56},{8,0},{16,8},{24,16},{32,24},{40,32},{48,40},{56,48},{1,57}... | collective-permute-start | bytes 884744 | tf_op jit(solution)/shard_map/ppermute | solution.py:29
  23.2 1.4 dynamic-slice_bitcast_fusion
  24.6 1.7 collective-permute-start.15
  26.9 0.9 collective-permute-start.1
  27.9 43.0 %collective-permute-done.16 = bf16[512,64]{1,0:T(8,128)(2,1)S(1)} collective-permute-done((bf16[512,64]{1,0:T(8,128)(2,1)S(1)}, bf16[512,64]{1,0:T(8,128)(2,1)S(1)}, u32[]{:S(2)}, u32[]{:S(2)}) %collective-permute-start.16) | collective-permute-done | bytes 65568 | tf_op jit(solution)/shard_map/ppermute | solution.py:284
  71.5 3.2 %collective-permute-start.11 = (bf16[8,144,128]{2,1,0:T(8,128)(2,1)}, bf16[8,144,128]{2,1,0:T(8,128)(2,1)}, u32[]{:S(2)}, u32[]{:S(2)}) collective-permute-start(bf16[8,144,128]{2,1,0:T(8,128)(2,1)} %collective-permute-done.9.refs_10_), channel_id=1, source_target_pairs={{0,56},{8,0},{16,8},{24,16},{32,24},{40,32},{48,40},{56,48},{1,57}... | collective-permute-start | bytes 884744 | tf_op jit(solution)/shard_map/ppermute | solution.py:29
  75.1 1.5 collective-permute-start.3
  76.6 5.8 %collective-permute-done.8.refs_9_ = bf16[8,144,128]{2,1,0:T(8,128)(2,1)} collective-permute-done((bf16[8,144,128]{2,1,0:T(8,128)(2,1)}, bf16[8,144,128]{2,1,0:T(8,128)(2,1)}, u32[]{:S(2)}, u32[]{:S(2)}) %collective-permute-start.8) | collective-permute-done | bytes 294944 | tf_op jit(solution)/shard_map/ppermute | solution.py:28
  82.3 6.3 %collective-permute-done.2.refs_3_ = bf16[8,144,128]{2,1,0:T(8,128)(2,1)} collective-permute-done((bf16[8,144,128]{2,1,0:T(8,128)(2,1)}, bf16[8,144,128]{2,1,0:T(8,128)(2,1)}, u32[]{:S(2)}, u32[]{:S(2)}) %collective-permute-start.2) | collective-permute-done | bytes 294944 | tf_op jit(solution)/shard_map/ppermute | solution.py:28
  88.6 3.2 %collective-permute-start.13 = (bf16[8,144,128]{2,1,0:T(8,128)(2,1)}, bf16[8,144,128]{2,1,0:T(8,128)(2,1)S(1)}, u32[]{:S(2)}, u32[]{:S(2)}) collective-permute-start(bf16[8,144,128]{2,1,0:T(8,128)(2,1)} %collective-permute-done.11.refs_12_), channel_id=1, source_target_pairs={{0,56},{8,0},{16,8},{24,16},{32,24},{40,32},{48,40},{56,48},{1,57}... | collective-permute-start | bytes 884744 | tf_op jit(solution)/shard_map/ppermute | solution.py:29
  91.9 3.6 %convolution_convert_fusion = bf16[64,512]{1,0:T(8,128)(2,1)S(1)} fusion(bf16[512,4096]{1,0:T(8,128)(2,1)} %head_ref.3, s32[4096]{0:T(1024)S(1)} %iota_add_fusion, s32[64]{0:T(128)S(1)} %copy-done.17), kind=kOutput, calls=%fused_computation.1 | convolution fusion | flops 268730368 | bytes 4276480 | tf_op jit(solution)/shard_map/dot_general | solution.py:290
  95.6 2.0 collective-permute-start.12
  97.6 3.6 %collective-permute-done.4.refs_5_ = bf16[8,144,128]{2,1,0:T(8,128)(2,1)S(1)} collective-permute-done((bf16[8,144,128]{2,1,0:T(8,128)(2,1)}, bf16[8,144,128]{2,1,0:T(8,128)(2,1)S(1)}, u32[]{:S(2)}, u32[]{:S(2)}) %collective-permute-start.4) | collective-permute-done | bytes 294944 | tf_op jit(solution)/shard_map/ppermute | solution.py:28
  101.2 3.2 %collective-permute-start.14 = (bf16[8,144,128]{2,1,0:T(8,128)(2,1)S(1)}, bf16[8,144,128]{2,1,0:T(8,128)(2,1)}, u32[]{:S(2)}, u32[]{:S(2)}) collective-permute-start(bf16[8,144,128]{2,1,0:T(8,128)(2,1)S(1)} %collective-permute-done.13.refs_14_), channel_id=1, source_target_pairs={{0,56},{8,0},{16,8},{24,16},{32,24},{40,32},{48,40},{56,48},{1,57}... | collective-permute-start | bytes 884744 | tf_op jit(solution)/shard_map/ppermute | solution.py:31
  105.2 2.3 %collective-permute-done.12.refs_13_ = bf16[8,144,128]{2,1,0:T(8,128)(2,1)S(1)} collective-permute-done((bf16[8,144,128]{2,1,0:T(8,128)(2,1)S(1)}, bf16[8,144,128]{2,1,0:T(8,128)(2,1)S(1)}, u32[]{:S(2)}, u32[]{:S(2)}) %collective-permute-start.12) | collective-permute-done | bytes 294944 | tf_op jit(solution)/shard_map/ppermute | solution.py:28
  107.5 3.7 %collective-permute-done.6.refs_7_ = bf16[8,144,128]{2,1,0:T(8,128)(2,1)S(1)} collective-permute-done((bf16[8,144,128]{2,1,0:T(8,128)(2,1)S(1)}, bf16[8,144,128]{2,1,0:T(8,128)(2,1)S(1)}, u32[]{:S(2)}, u32[]{:S(2)}) %collective-permute-start.6) | collective-permute-done | bytes 294944 | tf_op jit(solution)/shard_map/ppermute | solution.py:31
  111.9 1.1 copy-done.4
  113.0 13.4 %conv_pool_mask.1 = (bf16[4,2,16,512]{3,2,1,0:T(8,128)(2,1)S(1)}, bf16[2,8,144,512]{3,2,1,0:T(8,128)(2,1)S(1)}, bf16[1152,64]{1,0:T(8,128)(2,1)S(1)}) custom-call(s32[2]{0:T(128)S(1)} %pad_add_fusion.place_ref, bf16[8,144,128]{2,1,0:T(8,128)(2,1)} %copy-done.5, bf16[8,144,128]{2,1,0:T(8,128)(2,1)} %collective-permute-done.refs_1_, ...), custom_call_target="tpu_custom_call" | custom-call | tf_op jit(solution)/shard_map/conv_pool_mask/pallas_call | solution.py:119
  126.5 10.9 %all_to_all.25.both_ref = bf16[8,16,512]{2,1,0:T(8,128)(2,1)S(1)} all-to-all(bf16[8,16,512]{2,1,0:T(8,128)(2,1)S(1)} %bitcast.30), channel_id=1, replica_groups=mesh['seed'=4,'z'=8,'ylo'=2,'yhi'=2,'core'=2] {'yhi','core','ylo'}, dimensions={0} | all-to-all | bytes 262144 | tf_op jit(solution)/shard_map/all_to_all | solution.py:300
  137.4 1.6 logits_slices.1
  139.0 4.2 %all-to-all-start.1 = ((bf16[16,64,256]{2,1,0:T(8,128)(2,1)}), bf16[16,64,256]{2,1,0:T(8,128)(2,1)}, u32[]{:S(2)}, u32[]{:S(2)}) async-start(bf16[16,64,256]{2,1,0:T(8,128)(2,1)} %logits_slices.1), calls=%async_computation.1 | async-start | bytes 1048576 | tf_op jit(solution)/shard_map/all_to_all | solution.py:301
  143.3 1.0 copy-done.3
  145.0 13.9 %all-to-all-done.1 = bf16[16,64,256]{2,1,0:T(8,128)(2,1)} async-done(((bf16[16,64,256]{2,1,0:T(8,128)(2,1)}), bf16[16,64,256]{2,1,0:T(8,128)(2,1)}, u32[]{:S(2)}, u32[]{:S(2)}) %all-to-all-start.1) | async-done | bytes 524320 | tf_op jit(solution)/shard_map/all_to_all | solution.py:301
  158.9 1.1 convert_reduce_fusion
  160.1 18.8 %all_to_all.26.expo_ref = bf16[16,64,256]{2,1,0:T(8,128)(2,1)S(1)} all-to-all(bf16[16,64,256]{2,1,0:T(8,128)(2,1)S(1)} %broadcast_in_dim.2), channel_id=1, replica_groups=mesh['seed'=4,'z'=8,'ylo'=2,'yhi'=2,'core'=2] {'ylo','z'}, dimensions={0} | all-to-all | bytes 1048576 | tf_op jit(solution)/shard_map/all_to_all | solution.py:308
  178.9 3.1 %back.1 = f32[64,640]{1,0:T(8,128)S(1)} custom-call(bf16[16,64,256]{2,1,0:T(8,128)(2,1)S(1)} %all_to_all.26.expo_ref, bf16[512,4096]{1,0:T(8,128)(2,1)} %head_ref.3), custom_call_target="tpu_custom_call" | custom-call | tf_op jit(solution)/shard_map/back/pallas_call | solution.py:217
  182.1 10.0 %all_to_all.27 = f32[8,8,640]{2,1,0:T(8,128)S(1)} all-to-all(f32[8,8,640]{2,1,0:T(8,128)S(1)} %bitcast.27), channel_id=1, replica_groups=mesh['seed'=4,'z'=8,'ylo'=2,'yhi'=2,'core'=2] {'yhi','core','ylo'}, dimensions={0} | all-to-all | bytes 327680 | tf_op jit(solution)/shard_map/all_to_all | solution.py:311
  192.7 12.8 %all_to_all.28 = f32[16,8,128]{2,1,0:T(8,128)S(1)} all-to-all(f32[16,8,128]{2,1,0:T(8,128)S(1)} %bitcast.36), channel_id=1, replica_groups=mesh['seed'=4,'z'=8,'ylo'=2,'yhi'=2,'core'=2] {'ylo','z'}, dimensions={0} | all-to-all | bytes 131072 | tf_op jit(solution)/shard_map/all_to_all | solution.py:315
  (67 shorter events, 6.1 us)
Async XLA Ops:
  6.5 19.7 %copy-start.16 = (bf16[512,64]{0,1:T(8,128)(2,1)S(1)}, bf16[512,64]{0,1:T(8,128)(2,1)}, u32[]{:S(2)}) copy-start(bf16[512,64]{0,1:T(8,128)(2,1)} %param.13) | copy-start | bytes 196612
  6.5 68.2 %copy-start.13 = (bf16[2048,32]{0,1:T(8,128)(2,1)S(1)}, bf16[2048,32]{0,1:T(8,128)(2,1)}, u32[]{:S(2)}) copy-start(bf16[2048,32]{0,1:T(8,128)(2,1)} %param.12) | copy-start | bytes 393220
  6.5 105.4 %all-gather.3.cloned.1.call-start = ((), (), s32[]{:S(2)}) async-start(), calls=%async_computation.5 | async-start | bytes 4718592 | tf_op jit(solution)/shard_map/all_gather | solution.py:278
  7.3 84.6 %copy-start.17 = (s32[64]{0:T(128)S(1)}, s32[64]{0:T(128)}, u32[]{:S(2)}) copy-start(s32[64]{0:T(128)} %param.11) | copy-start | bytes 772
  8.4 87.1 %copy-start.5 = (bf16[8,144,128]{2,1,0:T(8,128)(2,1)}, bf16[8,144,128]{2,1,0:T(8,128)(2,1)S(1)}, u32[]{:S(2)}) copy-start(bf16[8,144,128]{2,1,0:T(8,128)(2,1)S(1)} %get-tuple-element.32.refs_0_) | copy-start | bytes 884740
  8.4 8.9 %collective-permute-start.7 = (bf16[8,144,128]{2,1,0:T(8,128)(2,1)S(1)}, bf16[8,144,128]{2,1,0:T(8,128)(2,1)}, u32[]{:S(2)}, u32[]{:S(2)}) collective-permute-start(bf16[8,144,128]{2,1,0:T(8,128)(2,1)S(1)} %get-tuple-element.59), channel_id=1, source_target_pairs={{0,4},{4,0},{1,5},{5,1},{2,6},{6,2},{3,7},{7,3},{8,12},{12,8},{9,1... | collective-permute-start | bytes 884744 | tf_op jit(solution)/shard_map/ppermute | solution.py:277
  10.0 60.8 %collective-permute-start = (bf16[8,144,128]{2,1,0:T(8,128)(2,1)S(1)}, bf16[8,144,128]{2,1,0:T(8,128)(2,1)}, u32[]{:S(2)}, u32[]{:S(2)}) collective-permute-start(bf16[8,144,128]{2,1,0:T(8,128)(2,1)S(1)} %get-tuple-element.32.refs_0_), channel_id=1, source_target_pairs={{0,8},{8,16},{16,24},{24,32},{32,40},{40,48},{48,56},{56,0},{1,9},... | collective-permute-start | bytes 884744 | tf_op jit(solution)/shard_map/ppermute | solution.py:28
  17.3 54.2 %collective-permute-start.9 = (bf16[8,144,128]{2,1,0:T(8,128)(2,1)}, bf16[8,144,128]{2,1,0:T(8,128)(2,1)}, u32[]{:S(2)}, u32[]{:S(2)}) collective-permute-start(bf16[8,144,128]{2,1,0:T(8,128)(2,1)} %collective-permute-done.7.refs_8_), channel_id=1, source_target_pairs={{0,56},{8,0},{16,8},{24,16},{32,24},{40,32},{48,40},{56,48},{1,57}... | collective-permute-start | bytes 884744 | tf_op jit(solution)/shard_map/ppermute | solution.py:29
  24.6 86.6 %collective-permute-start.15 = (bf16[8,144,512]{2,1,0:T(8,128)(2,1)S(1)}, bf16[8,144,512]{2,1,0:T(8,128)(2,1)S(1)}, u32[]{:S(2)}, u32[]{:S(2)}) collective-permute-start(bf16[8,144,512]{2,1,0:T(8,128)(2,1)S(1)} %dynamic-slice_bitcast_fusion), channel_id=1, source_target_pairs={{0,4},{4,0},{1,5},{5,1},{2,6},{6,2},{3,7},{7,3},{8,12},{12,8},{9,1... | collective-permute-start | bytes 3538952 | tf_op jit(solution)/shard_map/ppermute | solution.py:281
  26.4 44.4 %collective-permute-start.16 = (bf16[512,64]{1,0:T(8,128)(2,1)S(1)}, bf16[512,64]{1,0:T(8,128)(2,1)S(1)}, u32[]{:S(2)}, u32[]{:S(2)}) collective-permute-start(bf16[512,64]{1,0:T(8,128)(2,1)S(1)} %copy.13), channel_id=1, source_target_pairs={{0,4},{4,0},{1,5},{5,1},{2,6},{6,2},{3,7},{7,3},{8,12},{12,8},{9,1... | collective-permute-start | bytes 196616 | tf_op jit(solution)/shard_map/ppermute | solution.py:284
  26.9 48.2 %collective-permute-start.1 = (bf16[8,144,128]{2,1,0:T(8,128)(2,1)S(1)}, bf16[8,144,128]{2,1,0:T(8,128)(2,1)}, u32[]{:S(2)}, u32[]{:S(2)}) collective-permute-start(bf16[8,144,128]{2,1,0:T(8,128)(2,1)S(1)} %get-tuple-element.32.refs_0_), channel_id=1, source_target_pairs={{0,56},{8,0},{16,8},{24,16},{32,24},{40,32},{48,40},{56,48},{1,57}... | collective-permute-start | bytes 884744 | tf_op jit(solution)/shard_map/ppermute | solution.py:29
  70.8 11.5 %collective-permute-start.8 = (bf16[8,144,128]{2,1,0:T(8,128)(2,1)}, bf16[8,144,128]{2,1,0:T(8,128)(2,1)}, u32[]{:S(2)}, u32[]{:S(2)}) collective-permute-start(bf16[8,144,128]{2,1,0:T(8,128)(2,1)} %collective-permute-done.7.refs_8_), channel_id=1, source_target_pairs={{0,8},{8,16},{16,24},{24,32},{32,40},{40,48},{48,56},{56,0},{1,9},... | collective-permute-start | bytes 884744 | tf_op jit(solution)/shard_map/ppermute | solution.py:28
  71.5 17.1 %collective-permute-start.2 = (bf16[8,144,128]{2,1,0:T(8,128)(2,1)}, bf16[8,144,128]{2,1,0:T(8,128)(2,1)}, u32[]{:S(2)}, u32[]{:S(2)}) collective-permute-start(bf16[8,144,128]{2,1,0:T(8,128)(2,1)} %collective-permute-done.refs_1_), channel_id=1, source_target_pairs={{0,8},{8,16},{16,24},{24,32},{32,40},{40,48},{48,56},{56,0},{1,9},... | collective-permute-start | bytes 884744 | tf_op jit(solution)/shard_map/ppermute | solution.py:28
  71.5 17.1 %collective-permute-start.11 = (bf16[8,144,128]{2,1,0:T(8,128)(2,1)}, bf16[8,144,128]{2,1,0:T(8,128)(2,1)}, u32[]{:S(2)}, u32[]{:S(2)}) collective-permute-start(bf16[8,144,128]{2,1,0:T(8,128)(2,1)} %collective-permute-done.9.refs_10_), channel_id=1, source_target_pairs={{0,56},{8,0},{16,8},{24,16},{32,24},{40,32},{48,40},{56,48},{1,57}... | collective-permute-start | bytes 884744 | tf_op jit(solution)/shard_map/ppermute | solution.py:29
  75.0 29.4 %copy-start.15 = (bf16[512,64]{1,0:T(8,128)(2,1)S(1)}, bf16[512,64]{1,0:T(8,128)(2,1)}, u32[]{:S(2)}) copy-start(bf16[512,64]{1,0:T(8,128)(2,1)} %copy-done.14) | copy-start | bytes 196612
  75.1 20.4 %collective-permute-start.3 = (bf16[8,144,128]{2,1,0:T(8,128)(2,1)}, bf16[8,144,128]{2,1,0:T(8,128)(2,1)S(1)}, u32[]{:S(2)}, u32[]{:S(2)}) collective-permute-start(bf16[8,144,128]{2,1,0:T(8,128)(2,1)} %collective-permute-done.1.refs_2_), channel_id=1, source_target_pairs={{0,56},{8,0},{16,8},{24,16},{32,24},{40,32},{48,40},{56,48},{1,57}... | collective-permute-start | bytes 884744 | tf_op jit(solution)/shard_map/ppermute | solution.py:29
  82.3 13.3 %collective-permute-start.10 = (bf16[8,144,128]{2,1,0:T(8,128)(2,1)}, bf16[8,144,128]{2,1,0:T(8,128)(2,1)S(1)}, u32[]{:S(2)}, u32[]{:S(2)}) collective-permute-start(bf16[8,144,128]{2,1,0:T(8,128)(2,1)} %collective-permute-done.8.refs_9_), channel_id=1, source_target_pairs={{0,8},{8,16},{16,24},{24,32},{32,40},{40,48},{48,56},{56,0},{1,9},... | collective-permute-start | bytes 884744 | tf_op jit(solution)/shard_map/ppermute | solution.py:28
  88.6 12.5 %collective-permute-start.4 = (bf16[8,144,128]{2,1,0:T(8,128)(2,1)}, bf16[8,144,128]{2,1,0:T(8,128)(2,1)S(1)}, u32[]{:S(2)}, u32[]{:S(2)}) collective-permute-start(bf16[8,144,128]{2,1,0:T(8,128)(2,1)} %collective-permute-done.2.refs_3_), channel_id=1, source_target_pairs={{0,8},{8,16},{16,24},{24,32},{32,40},{40,48},{48,56},{56,0},{1,9},... | collective-permute-start | bytes 884744 | tf_op jit(solution)/shard_map/ppermute | solution.py:28
  88.6 12.5 %collective-permute-start.13 = (bf16[8,144,128]{2,1,0:T(8,128)(2,1)}, bf16[8,144,128]{2,1,0:T(8,128)(2,1)S(1)}, u32[]{:S(2)}, u32[]{:S(2)}) collective-permute-start(bf16[8,144,128]{2,1,0:T(8,128)(2,1)} %collective-permute-done.11.refs_12_), channel_id=1, source_target_pairs={{0,56},{8,0},{16,8},{24,16},{32,24},{40,32},{48,40},{56,48},{1,57}... | collective-permute-start | bytes 884744 | tf_op jit(solution)/shard_map/ppermute | solution.py:29
  95.5 15.7 %copy-start.6 = (bf16[8,144,128]{2,1,0:T(8,128)(2,1)}, bf16[8,144,128]{2,1,0:T(8,128)(2,1)S(1)}, u32[]{:S(2)}) copy-start(bf16[8,144,128]{2,1,0:T(8,128)(2,1)S(1)} %collective-permute-done.3.refs_4_) | copy-start | bytes 884740
  95.5 9.7 %collective-permute-start.5 = (bf16[8,144,128]{2,1,0:T(8,128)(2,1)S(1)}, bf16[8,144,128]{2,1,0:T(8,128)(2,1)S(1)}, u32[]{:S(2)}, u32[]{:S(2)}) collective-permute-start(bf16[8,144,128]{2,1,0:T(8,128)(2,1)S(1)} %collective-permute-done.3.refs_4_), channel_id=1, source_target_pairs={{0,56},{8,0},{16,8},{24,16},{32,24},{40,32},{48,40},{56,48},{1,57}... | collective-permute-start | bytes 884744 | tf_op jit(solution)/shard_map/ppermute | solution.py:29
  95.6 15.6 %copy-start.7 = (bf16[8,144,128]{2,1,0:T(8,128)(2,1)}, bf16[8,144,128]{2,1,0:T(8,128)(2,1)S(1)}, u32[]{:S(2)}) copy-start(bf16[8,144,128]{2,1,0:T(8,128)(2,1)S(1)} %collective-permute-done.10.refs_11_) | copy-start | bytes 884740
  95.6 11.9 %collective-permute-start.12 = (bf16[8,144,128]{2,1,0:T(8,128)(2,1)S(1)}, bf16[8,144,128]{2,1,0:T(8,128)(2,1)S(1)}, u32[]{:S(2)}, u32[]{:S(2)}) collective-permute-start(bf16[8,144,128]{2,1,0:T(8,128)(2,1)S(1)} %collective-permute-done.10.refs_11_), channel_id=1, source_target_pairs={{0,8},{8,16},{16,24},{24,32},{32,40},{40,48},{48,56},{56,0},{1,9},... | collective-permute-start | bytes 884744 | tf_op jit(solution)/shard_map/ppermute | solution.py:28
  101.2 10.1 %copy-start.8 = (bf16[8,144,128]{2,1,0:T(8,128)(2,1)}, bf16[8,144,128]{2,1,0:T(8,128)(2,1)S(1)}, u32[]{:S(2)}) copy-start(bf16[8,144,128]{2,1,0:T(8,128)(2,1)S(1)} %collective-permute-done.4.refs_5_) | copy-start | bytes 884740
  101.2 10.0 %collective-permute-start.6 = (bf16[8,144,128]{2,1,0:T(8,128)(2,1)S(1)}, bf16[8,144,128]{2,1,0:T(8,128)(2,1)S(1)}, u32[]{:S(2)}, u32[]{:S(2)}) collective-permute-start(bf16[8,144,128]{2,1,0:T(8,128)(2,1)S(1)} %collective-permute-done.4.refs_5_), channel_id=1, source_target_pairs={{0,8},{8,16},{16,24},{24,32},{32,40},{40,48},{48,56},{56,0},{1,9},... | collective-permute-start | bytes 884744 | tf_op jit(solution)/shard_map/ppermute | solution.py:31
  101.2 10.1 %copy-start.9 = (bf16[8,144,128]{2,1,0:T(8,128)(2,1)}, bf16[8,144,128]{2,1,0:T(8,128)(2,1)S(1)}, u32[]{:S(2)}) copy-start(bf16[8,144,128]{2,1,0:T(8,128)(2,1)S(1)} %collective-permute-done.13.refs_14_) | copy-start | bytes 884740
  101.2 10.8 %collective-permute-start.14 = (bf16[8,144,128]{2,1,0:T(8,128)(2,1)S(1)}, bf16[8,144,128]{2,1,0:T(8,128)(2,1)}, u32[]{:S(2)}, u32[]{:S(2)}) collective-permute-start(bf16[8,144,128]{2,1,0:T(8,128)(2,1)S(1)} %collective-permute-done.13.refs_14_), channel_id=1, source_target_pairs={{0,56},{8,0},{16,8},{24,16},{32,24},{40,32},{48,40},{56,48},{1,57}... | collective-permute-start | bytes 884744 | tf_op jit(solution)/shard_map/ppermute | solution.py:31
  105.2 6.0 %copy-start.10 = (bf16[8,144,128]{2,1,0:T(8,128)(2,1)}, bf16[8,144,128]{2,1,0:T(8,128)(2,1)S(1)}, u32[]{:S(2)}) copy-start(bf16[8,144,128]{2,1,0:T(8,128)(2,1)S(1)} %collective-permute-done.5.refs_6_) | copy-start | bytes 884740
  113.0 24.4 %copy-start = (bf16[512,4096]{1,0:T(8,128)(2,1)S(1)}, bf16[512,4096]{1,0:T(8,128)(2,1)}, u32[]{:S(2)}) copy-start(bf16[512,4096]{1,0:T(8,128)(2,1)} %head_ref.3) | copy-start | bytes 12582916
  126.4 12.6 %copy-start.2 = (bf16[1152,64]{1,0:T(8,128)(2,1)}, bf16[1152,64]{1,0:T(8,128)(2,1)S(1)}, u32[]{:S(2)}) copy-start(bf16[1152,64]{1,0:T(8,128)(2,1)S(1)} %get-tuple-element.52.acts_ref) | copy-start | bytes 442372
  139.0 19.9 %all-to-all-start.1 = ((bf16[16,64,256]{2,1,0:T(8,128)(2,1)}), bf16[16,64,256]{2,1,0:T(8,128)(2,1)}, u32[]{:S(2)}, u32[]{:S(2)}) async-start(bf16[16,64,256]{2,1,0:T(8,128)(2,1)} %logits_slices.1), calls=%async_computation.1 | async-start | bytes 1048576 | tf_op jit(solution)/shard_map/all_to_all | solution.py:301
  178.9 13.1 %copy-start.1 = (bf16[2,512,64]{2,1,0:T(8,128)(2,1)S(1)}, bf16[2,512,64]{2,1,0:T(8,128)(2,1)}, u32[]{:S(2)}) copy-start(bf16[2,512,64]{2,1,0:T(8,128)(2,1)} %pad_maximum_fusion.pe_ref) | copy-start | bytes 393220
  (5 other events, 7.2 us)
Sparse Core Ops, SparseCore 0:
  9.2 53.4 all-gather.2

commit v4 on v3

--- a/solution.py
+++ b/solution.py
@@ -19,17 +19,24 @@
 LIMIT = pltpu.CompilerParams(vmem_limit_bytes=16 * 1024 * 1024)
 
 
-def ring(block, nz, far):
+def rings(mine, swapped, nz):
     right = [(i, (i + 1) % nz) for i in range(nz)]
     left = [(i, (i - 1) % nz) for i in range(nz)]
-    got = [(0, block)]
-    r = l = block
+    got = [(0, 0, mine), (1, 0, swapped)]
+    r = [mine, swapped]
+    l = [mine, swapped]
     for k in range(1, nz // 2):
-        r = lax.ppermute(r, "z", right)
-        l = lax.ppermute(l, "z", left)
-        got += [(k, r), (nz - k, l)]
-    last = lax.ppermute(r, "z", right) if far == "right" else lax.ppermute(l, "z", left)
-    return got + [(nz // 2, last)]
+        for sub in range(2):
+            r[sub] = lax.ppermute(r[sub], "z", right)
+            l[sub] = lax.ppermute(l[sub], "z", left)
+            if k < nz // 2 - 1:
+                got += [(sub, k, r[sub]), (sub, nz - k, l[sub])]
+    ends = [*r, *l]
+    for sub in range(2):
+        got += [(sub, nz // 2 - 1, ends[sub]), (sub, nz // 2 + 1, ends[2 + sub])]
+    got.append((0, nz // 2, lax.ppermute(ends[0], "z", right)))
+    got.append((1, nz // 2, lax.ppermute(ends[3], "z", left)))
+    return got
 
 
 def conv_body(nz, plan, place_ref, *refs):
@@ -39,7 +46,7 @@
     x_ref, wv_ref, sv_ref, mv_ref, x_sem, w_sem, s_sem, m_sem = refs[count + 8 :]
     imgs, pos, kz = blocks[0].shape
     cut = imgs // 2
-    ka = pa_ref.shape[1]
+    ka = pa_ref.shape[0]
     depth, width = wv_ref.shape[1:]
     rows_w = w_ref.shape[3]
     me_z = place_ref[0]
@@ -71,7 +78,7 @@
     copies = [copy_w(0) + copy_x(0), copy_x(1), copy_w(1)]
     streams = [
         pltpu.make_async_copy(own_ref.at[me_y], sv_ref.at[0], s_sem.at[0]),
-        pltpu.make_async_copy(other_ref, sv_ref.at[1], s_sem.at[1]),
+        pltpu.make_async_copy(other_ref.at[pl.ds(0, imgs * pos)], sv_ref.at[1], s_sem.at[1]),
     ]
     for c in copies[0] + [streams[0]] + copies[1] + copies[2] + [streams[1]]:
         c.start()
@@ -88,14 +95,14 @@
             x = x_ref[part * cut : (part + 1) * cut].reshape(cut * pos, depth)
             y = jnp.dot(x, wv_ref[h], preferred_element_type=jnp.float32)
             if h == 0:
-                acts = jnp.dot(x, pa_ref[...], preferred_element_type=jnp.float32)
+                acts = lax.dot_general(x, pa_ref[...], NT, preferred_element_type=jnp.float32)
                 hi = acts.astype(jnp.bfloat16)
                 here = slice(part * cut * pos, (part + 1) * cut * pos)
                 acts_ref[here, :ka] = hi
                 acts_ref[here, ka:] = (acts - hi.astype(jnp.float32)).astype(jnp.bfloat16)
             if part == 0:
                 streams[h].wait()
-            y = y.reshape(cut, pos, width) + sv_ref[h, part * cut : (part + 1) * cut].astype(jnp.float32)
+            y = (y + sv_ref[h, part * cut * pos : (part + 1) * cut * pos].astype(jnp.float32)).reshape(cut, pos, width)
             pooled = (jnp.sum(jnp.maximum(y, 0.0), axis=1) / pos).astype(jnp.bfloat16)
             for f in range(pooled_ref.shape[0]):
                 pooled_ref[f, columns[h], part * cut : (part + 1) * cut] = pooled
@@ -115,7 +122,7 @@
     blocks = [b for _, _, b in got]
     half, pos, kz = blocks[0].shape
     fs, _, _, width = hot.shape
-    depth, ka = proj_act.shape
+    ka, depth = proj_act.shape
     return pl.pallas_call(
         functools.partial(conv_body, nz, plan),
         in_specs=[pl.BlockSpec(memory_space=pltpu.SMEM)] + [HB] * (len(blocks) + 3) + [VM, VM],
@@ -128,7 +135,7 @@
         scratch_shapes=[
             pltpu.VMEM((half, pos, depth), jnp.bfloat16),
             pltpu.VMEM((2, depth, width), jnp.bfloat16),
-            pltpu.VMEM((2, half, pos, width), jnp.bfloat16),
+            pltpu.VMEM((2, half * pos, width), jnp.bfloat16),
             pltpu.VMEM((2, 2, half // 2, pos, width), jnp.bfloat16),
             pltpu.SemaphoreType.DMA((2, len(blocks))),
             pltpu.SemaphoreType.DMA((2, 4)),
@@ -228,34 +235,35 @@
     )(expo, pltpu.with_memory_space_constraint(head, pltpu.HBM))
 
 
-def final_body(pos, m_ref, part_ref, hot_ref, pe_ref, out_ref):
+def final_body(pos, place_ref, m_ref, part_ref, hot_ref, own_ref, other_ref, out_ref):
     width = hot_ref.shape[3]
     imgs, ka, _ = m_ref.shape
-    ke = pe_ref.shape[2]
-    acc = jnp.zeros((imgs * ka, ke), jnp.float32)
-    for h in range(2):
+    acc = jnp.zeros(out_ref.shape, jnp.float32)
+    for k, pe_ref in enumerate((own_ref, other_ref)):
+        h = place_ref[1] if k == 0 else 1 - place_ref[1]
         part = sum(part_ref[a, h] for a in range(part_ref.shape[0]))
-        hot = sum(hot_ref[a, h, imgs:].astype(jnp.float32) for a in range(hot_ref.shape[0]))
+        hot = sum(hot_ref[a, h].astype(jnp.float32)[imgs:] for a in range(hot_ref.shape[0]))
         d = part[:, :width] / part[:, width : width + 1] - hot
         d = (d / pos).astype(jnp.bfloat16).astype(jnp.float32)
-        v = (m_ref[:, :, h * width : (h + 1) * width] * d[:, None, :]).reshape(imgs * ka, width)
+        lane = pl.multiple_of(h * width, width)
+        v = (m_ref[:, :, pl.ds(lane, width)] * d[:, None, :]).reshape(imgs * ka, width)
         v_hi = v.astype(jnp.bfloat16)
         v_lo = (v - v_hi.astype(jnp.float32)).astype(jnp.bfloat16)
-        acc += jnp.dot(v_hi, pe_ref[h], preferred_element_type=jnp.float32)
-        acc += jnp.dot(v_lo, pe_ref[h], preferred_element_type=jnp.float32)
+        acc += lax.dot_general(v_hi, pe_ref[...], NT, preferred_element_type=jnp.float32)
+        acc += lax.dot_general(v_lo, pe_ref[...], NT, preferred_element_type=jnp.float32)
     out_ref[...] = acc
 
 
-def final(m, part, hot, pe, pos):
+def final(place, m, part, hot, pe_own, pe_other, pos):
     imgs, ka, _ = m.shape
     return pl.pallas_call(
         functools.partial(final_body, pos),
-        in_specs=[VM] * 4,
+        in_specs=[pl.BlockSpec(memory_space=pltpu.SMEM)] + [VM] * 5,
         out_specs=VM,
-        out_shape=jax.ShapeDtypeStruct((imgs * ka, pe.shape[2]), jnp.float32),
+        out_shape=jax.ShapeDtypeStruct((imgs * ka, pe_own.shape[0]), jnp.float32),
         compiler_params=LIMIT,
         name="final",
-    )(m, part, hot, pe)
+    )(place, m, part, hot, pe_own, pe_other)
 
 
 def per_device(stream, mid, conv_weight, head_weight, labels, proj_act, proj_err):
@@ -275,33 +283,33 @@
     mine = lax.dynamic_index_in_dim(mid, me_y, 0, keepdims=False)
     theirs = lax.dynamic_index_in_dim(mid, 1 - me_y, 0, keepdims=False)
     swapped = lax.ppermute(theirs, "ylo", swap)
+    pe_own = proj_err.T
+    sent = lax.dynamic_index_in_dim(stream, 1 - me_y, 0, keepdims=False).reshape(half * pos, width)
+    stream_other = lax.ppermute(jnp.concatenate([sent, pe_own], axis=0), "ylo", swap)
     w_all = lax.all_gather(conv_weight, W_ORDER, axis=0)
-    w_all = w_all.reshape(2, 2, 2, *conv_weight.shape)
-    got = [(0,) + g for g in ring(mine, nz, "right")] + [(1,) + g for g in ring(swapped, nz, "left")]
-    stream_other = lax.ppermute(
-        lax.dynamic_index_in_dim(stream, 1 - me_y, 0, keepdims=False), "ylo", swap
-    )
-    pe_other = lax.ppermute(proj_err, "ylo", swap)
-    low = me_y == 0
-    pe = jnp.stack([jnp.where(low, proj_err, pe_other), jnp.where(low, pe_other, proj_err)])
+    got = rings(mine, swapped, nz)
 
     classes = f * block + jnp.arange(block, dtype=jnp.int32)
     onehot = (labels[:, None] == classes[None, :]).astype(jnp.bfloat16)
     hot = lax.dot_general(onehot, head_weight, NT, preferred_element_type=jnp.float32)
     hot = hot.astype(jnp.bfloat16).reshape(fs, 2, half, width)
 
-    *blocks, w_all, stream_other, pe, hot = lax.optimization_barrier(
-        [g[2] for g in got] + [w_all, stream_other, pe, hot]
+    *blocks, w_all, stream_other, hot = lax.optimization_barrier(
+        [g[2] for g in got] + [w_all, stream_other, hot]
     )
     got = [g[:2] + (b,) for g, b in zip(got, blocks)]
     place = jnp.stack([lax.axis_index("z"), me_y]).astype(jnp.int32)
-    both, mask, acts = conv(place, got, w_all, stream, stream_other, proj_act, hot, nz)
+    both, mask, acts = conv(
+        place, got, w_all.reshape(2, 2, 2, *conv_weight.shape),
+        stream.reshape(2, half * pos, width), stream_other, proj_act.T, hot, nz,
+    )
 
     both = lax.all_to_all(both.reshape(2 * fs, 2 * half, width), ROWS, 0, 0)
     part = lax.all_to_all(logits_slices(both, head_weight, parts), SPREAD, 0, 0)
     mask, both = lax.optimization_barrier((mask, both))
     m = masked_sums(acts, mask)
-    part, m = lax.optimization_barrier((part, m))
+    pe_other = stream_other[half * pos :]
+    part, m, pe_other = lax.optimization_barrier((part, m, pe_other))
 
     logits = jnp.sum(part.astype(jnp.float32), axis=0)
     expo = jnp.minimum(jnp.exp(logits), BF16_TOP).astype(jnp.bfloat16)
@@ -310,7 +318,7 @@
     part = back(expo, head_weight).reshape(2 * fs, half, width + 128)
     part = lax.all_to_all(part, ROWS, 0, 0).reshape(fs, 2, half, width + 128)
 
-    grads = final(m, part, both.reshape(fs, 2, 2 * half, width), pe, pos)
+    grads = final(place, m, part, both.reshape(fs, 2, 2 * half, width), pe_own, pe_other, pos)
     grads = grads.reshape(half, nz, 2, -1).transpose(2, 1, 0, 3).reshape(parts, half, -1)
     grads = lax.all_to_all(grads, SPREAD, 0, 0)
     grads = jnp.sum(grads.reshape(2, nz, half, -1), axis=1)

time: 213 us -> 168 us (0.79)
  waiting for transfers between devices: 84.6 us -> 33.5 us
  starting transfers between devices: 30.1 us -> 36.1 us
    ppermute x16 -> x15, waiting for transfers between devices: 64.6 us -> 16.8 us  [the longest x6 15.4 us: rings(): l[sub] = lax.ppermute(l[sub], 'z', left)]
    ppermute x16 -> x15, starting transfers between devices: 24.2 us -> 29.2 us  [the longest x6 21.6 us: rings(): l[sub] = lax.ppermute(l[sub], 'z', left)]
    all_to_all x1, waiting for transfers between devices: 13.9 us -> 11.6 us  [per_device(): part = lax.all_to_all(logits_slices(both, head_weight, parts), SPREAD, 0, 0)]
  transfers between devices with their start and end apart: 19 -> 18, of which waited for: 8 -> 9; matrix products, arithmetic and copies ran while one was open for 3% -> 5% of each run, Pallas kernels for 0% -> 0%
where the time goes in v4:
time: 168 us; the launch traced here: 167 us
  blocking collectives  51.8 us (31%)
  starting transfers between devices  36.1 us (21%)
  waiting for transfers between devices  33.5 us (20%)
  Pallas kernels  20 us (12%)
  between operations  13.7 us (8%)
  local copies, waits for them, and re-layouts  6.53 us (4%)
  matrix products  3.61 us (2%)
  other arithmetic  1.91 us (1%)
    ppermute x6, starting transfers between devices, rings(): l[sub] = lax.ppermute(l[sub], 'z', left)  21.6 us
    all_to_all x1, blocking collectives, per_device(): lax.all_to_all(jnp.broadcast_to(expo, (parts,) + expo.shape), SPREAD, 0, 0)  18.9 us
    ppermute x6, waiting for transfers between devices, rings(): l[sub] = lax.ppermute(l[sub], 'z', left)  15.4 us
    pallas_call x1, Pallas kernels, conv(): pl.pallas_call(functools.partial(conv_body, nz, plan), in_specs=[pl.Block...  13.5 us
    all_to_all x1, blocking collectives, per_device(): grads = lax.all_to_all(grads, SPREAD, 0, 0)  12.9 us
    all_to_all x1, waiting for transfers between devices, per_device(): part = lax.all_to_all(logits_slices(both, head_weight, parts), SPREAD, 0, 0)  11.6 us
    all_to_all x1, blocking collectives, per_device(): both = lax.all_to_all(both.reshape(2 * fs, 2 * half, width), ROWS, 0, 0)  10.4 us
    all_to_all x1, blocking collectives, per_device(): part = lax.all_to_all(part, ROWS, 0, 0).reshape(fs, 2, half, width + 128)  9.63 us
  transfers between devices with their start and end apart: 18, of which 9 were waited for; matrix products, arithmetic and copies ran while one was open for 5% of the time, Pallas kernels for 0%

profile of v4, /device:TPU:2, one launch (start us, length us, event | category | flops | bytes accessed | tf_op | source)
XLA Modules:
  0.0 167.2 jit_solution(10374281199433512422)
XLA Ops:
  7.3 1.1 dynamic-slice_bitcast_fusion
  8.4 1.7 collective-permute-start
  10.0 1.4 constant_dynamic-slice_fusion
  12.1 1.9 %collective-permute-start.1 = (bf16[8,144,128]{2,1,0:T(8,128)(2,1)S(1)}, bf16[8,144,128]{2,1,0:T(8,128)(2,1)S(1)}, u32[]{:S(2)}, u32[]{:S(2)}) collective-permute-start(bf16[8,144,128]{2,1,0:T(8,128)(2,1)S(1)} %get-tuple-element.32.refs_0_), channel_id=1, source_target_pairs={{0,8},{8,16},{16,24},{24,32},{32,40},{40,48},{48,56},{56,0},{1,9},... | collective-permute-start | bytes 884744 | tf_op jit(solution)/shard_map/ppermute | solution.py:30
  14.0 4.4 %collective-permute-done.refs_1_ = bf16[8,144,128]{2,1,0:T(8,128)(2,1)S(1)} collective-permute-done((bf16[8,144,128]{2,1,0:T(8,128)(2,1)S(1)}, bf16[8,144,128]{2,1,0:T(8,128)(2,1)S(1)}, u32[]{:S(2)}, u32[]{:S(2)}) %collective-permute-start) | collective-permute-done | bytes 294944 | tf_op jit(solution)/shard_map/ppermute | solution.py:285
  18.4 5.9 %collective-permute-start.4 = (bf16[8,144,128]{2,1,0:T(8,128)(2,1)S(1)}, bf16[8,144,128]{2,1,0:T(8,128)(2,1)S(1)}, u32[]{:S(2)}, u32[]{:S(2)}) collective-permute-start(bf16[8,144,128]{2,1,0:T(8,128)(2,1)S(1)} %collective-permute-done.refs_1_), channel_id=1, source_target_pairs={{0,56},{8,0},{16,8},{24,16},{32,24},{40,32},{48,40},{56,48},{1,57}... | collective-permute-start | bytes 884744 | tf_op jit(solution)/shard_map/ppermute | solution.py:31
  24.2 1.0 collective-permute-start.2
  25.2 1.0 collective-permute-start.3
  26.3 5.3 %collective-permute-done.4.refs_5_ = bf16[8,144,128]{2,1,0:T(8,128)(2,1)S(1)} collective-permute-done((bf16[8,144,128]{2,1,0:T(8,128)(2,1)S(1)}, bf16[8,144,128]{2,1,0:T(8,128)(2,1)S(1)}, u32[]{:S(2)}, u32[]{:S(2)}) %collective-permute-start.4) | collective-permute-done | bytes 294944 | tf_op jit(solution)/shard_map/ppermute | solution.py:31
  31.7 3.7 %collective-permute-start.8 = (bf16[8,144,128]{2,1,0:T(8,128)(2,1)S(1)}, bf16[8,144,128]{2,1,0:T(8,128)(2,1)S(1)}, u32[]{:S(2)}, u32[]{:S(2)}) collective-permute-start(bf16[8,144,128]{2,1,0:T(8,128)(2,1)S(1)} %collective-permute-done.4.refs_5_), channel_id=1, source_target_pairs={{0,56},{8,0},{16,8},{24,16},{32,24},{40,32},{48,40},{56,48},{1,57}... | collective-permute-start | bytes 884744 | tf_op jit(solution)/shard_map/ppermute | solution.py:31
  35.4 2.6 %collective-permute-done.2.refs_3_ = bf16[8,144,128]{2,1,0:T(8,128)(2,1)S(1)} collective-permute-done((bf16[8,144,128]{2,1,0:T(8,128)(2,1)S(1)}, bf16[8,144,128]{2,1,0:T(8,128)(2,1)S(1)}, u32[]{:S(2)}, u32[]{:S(2)}) %collective-permute-start.2) | collective-permute-done | bytes 294944 | tf_op jit(solution)/shard_map/ppermute | solution.py:31
  38.0 3.7 %collective-permute-start.6 = (bf16[8,144,128]{2,1,0:T(8,128)(2,1)S(1)}, bf16[8,144,128]{2,1,0:T(8,128)(2,1)S(1)}, u32[]{:S(2)}, u32[]{:S(2)}) collective-permute-start(bf16[8,144,128]{2,1,0:T(8,128)(2,1)S(1)} %collective-permute-done.2.refs_3_), channel_id=1, source_target_pairs={{0,56},{8,0},{16,8},{24,16},{32,24},{40,32},{48,40},{56,48},{1,57}... | collective-permute-start | bytes 884744 | tf_op jit(solution)/shard_map/ppermute | solution.py:31
  41.9 2.4 %collective-permute-done.8.refs_9_ = bf16[8,144,128]{2,1,0:T(8,128)(2,1)S(1)} collective-permute-done((bf16[8,144,128]{2,1,0:T(8,128)(2,1)S(1)}, bf16[8,144,128]{2,1,0:T(8,128)(2,1)S(1)}, u32[]{:S(2)}, u32[]{:S(2)}) %collective-permute-start.8) | collective-permute-done | bytes 294944 | tf_op jit(solution)/shard_map/ppermute | solution.py:31
  44.3 3.7 %collective-permute-start.12 = (bf16[8,144,128]{2,1,0:T(8,128)(2,1)S(1)}, bf16[8,144,128]{2,1,0:T(8,128)(2,1)}, u32[]{:S(2)}, u32[]{:S(2)}) collective-permute-start(bf16[8,144,128]{2,1,0:T(8,128)(2,1)S(1)} %collective-permute-done.8.refs_9_), channel_id=1, source_target_pairs={{0,56},{8,0},{16,8},{24,16},{32,24},{40,32},{48,40},{56,48},{1,57}... | collective-permute-start | bytes 884744 | tf_op jit(solution)/shard_map/ppermute | solution.py:31
  48.1 2.5 %collective-permute-done.6.refs_7_ = bf16[8,144,128]{2,1,0:T(8,128)(2,1)S(1)} collective-permute-done((bf16[8,144,128]{2,1,0:T(8,128)(2,1)S(1)}, bf16[8,144,128]{2,1,0:T(8,128)(2,1)S(1)}, u32[]{:S(2)}, u32[]{:S(2)}) %collective-permute-start.6) | collective-permute-done | bytes 294944 | tf_op jit(solution)/shard_map/ppermute | solution.py:31
  50.6 3.7 %collective-permute-start.10 = (bf16[8,144,128]{2,1,0:T(8,128)(2,1)S(1)}, bf16[8,144,128]{2,1,0:T(8,128)(2,1)S(1)}, u32[]{:S(2)}, u32[]{:S(2)}) collective-permute-start(bf16[8,144,128]{2,1,0:T(8,128)(2,1)S(1)} %collective-permute-done.6.refs_7_), channel_id=1, source_target_pairs={{0,56},{8,0},{16,8},{24,16},{32,24},{40,32},{48,40},{56,48},{1,57}... | collective-permute-start | bytes 884744 | tf_op jit(solution)/shard_map/ppermute | solution.py:31
  54.5 2.5 %collective-permute-done.12.refs_13_ = bf16[8,144,128]{2,1,0:T(8,128)(2,1)} collective-permute-done((bf16[8,144,128]{2,1,0:T(8,128)(2,1)S(1)}, bf16[8,144,128]{2,1,0:T(8,128)(2,1)}, u32[]{:S(2)}, u32[]{:S(2)}) %collective-permute-start.12) | collective-permute-done | bytes 294944 | tf_op jit(solution)/shard_map/ppermute | solution.py:31
  57.0 3.8 %collective-permute-start.14 = (bf16[8,144,128]{2,1,0:T(8,128)(2,1)}, bf16[8,144,128]{2,1,0:T(8,128)(2,1)}, u32[]{:S(2)}, u32[]{:S(2)}) collective-permute-start(bf16[8,144,128]{2,1,0:T(8,128)(2,1)} %collective-permute-done.12.refs_13_), channel_id=1, source_target_pairs={{0,56},{8,0},{16,8},{24,16},{32,24},{40,32},{48,40},{56,48},{1,57}... | collective-permute-start | bytes 884744 | tf_op jit(solution)/shard_map/ppermute | solution.py:38
  60.8 3.6 %convolution_convert_fusion = bf16[64,512]{1,0:T(8,128)(2,1)S(1)} fusion(bf16[512,4096]{1,0:T(8,128)(2,1)} %head_ref.3, s32[4096]{0:T(1024)S(1)} %iota_add_fusion, s32[64]{0:T(128)S(1)} %copy-done.21), kind=kOutput, calls=%fused_computation.1 | convolution fusion | flops 268730368 | bytes 4276480 | tf_op jit(solution)/shard_map/dot_general | solution.py:294
  64.4 1.1 collective-permute-done.13.refs_14_
  66.6 13.5 %conv_pool_mask.1 = (bf16[4,2,16,512]{3,2,1,0:T(8,128)(2,1)S(1)}, bf16[2,8,144,512]{3,2,1,0:T(8,128)(2,1)S(1)}, bf16[1152,64]{1,0:T(8,128)(2,1)S(1)}) custom-call(s32[2]{0:T(128)S(1)} %pad_add_fusion.place_ref, bf16[8,144,128]{2,1,0:T(8,128)(2,1)} %copy-done.7, bf16[8,144,128]{2,1,0:T(8,128)(2,1)} %copy-done.8, bf16[8,144,128]{2,1,0:T(8,128)(2,1)} %copy-done.9, ...), custom_call_target="tpu_custom_call" | custom-call | tf_op jit(solution)/shard_map/conv_pool_mask/pallas_call | solution.py:126
  80.8 10.4 %all_to_all.25.both_ref = bf16[8,16,512]{2,1,0:T(8,128)(2,1)S(1)} all-to-all(bf16[8,16,512]{2,1,0:T(8,128)(2,1)S(1)} %bitcast.32), channel_id=1, replica_groups=mesh['seed'=4,'z'=8,'ylo'=2,'yhi'=2,'core'=2] {'yhi','core','ylo'}, dimensions={0} | all-to-all | bytes 262144 | tf_op jit(solution)/shard_map/all_to_all | solution.py:307
  91.2 1.7 logits_slices.1
  92.8 5.2 %all-to-all-start.1 = ((bf16[16,64,256]{2,1,0:T(8,128)(2,1)}), bf16[16,64,256]{2,1,0:T(8,128)(2,1)}, u32[]{:S(2)}, u32[]{:S(2)}) async-start(bf16[16,64,256]{2,1,0:T(8,128)(2,1)} %logits_slices.1), calls=%async_computation.1 | async-start | bytes 1048576 | tf_op jit(solution)/shard_map/all_to_all | solution.py:308
  98.1 1.5 slice.3.other_ref
  101.3 11.6 %all-to-all-done.1 = bf16[16,64,256]{2,1,0:T(8,128)(2,1)} async-done(((bf16[16,64,256]{2,1,0:T(8,128)(2,1)}), bf16[16,64,256]{2,1,0:T(8,128)(2,1)}, u32[]{:S(2)}, u32[]{:S(2)}) %all-to-all-start.1) | async-done | bytes 524320 | tf_op jit(solution)/shard_map/all_to_all | solution.py:308
  112.9 1.1 convert_reduce_fusion
  114.1 18.9 %all_to_all.26.expo_ref = bf16[16,64,256]{2,1,0:T(8,128)(2,1)S(1)} all-to-all(bf16[16,64,256]{2,1,0:T(8,128)(2,1)S(1)} %broadcast_in_dim.2), channel_id=1, replica_groups=mesh['seed'=4,'z'=8,'ylo'=2,'yhi'=2,'core'=2] {'ylo','z'}, dimensions={0} | all-to-all | bytes 1048576 | tf_op jit(solution)/shard_map/all_to_all | solution.py:316
  133.0 3.1 %back.1 = f32[64,640]{1,0:T(8,128)S(1)} custom-call(bf16[16,64,256]{2,1,0:T(8,128)(2,1)S(1)} %all_to_all.26.expo_ref, bf16[512,4096]{1,0:T(8,128)(2,1)} %head_ref.3), custom_call_target="tpu_custom_call" | custom-call | tf_op jit(solution)/shard_map/back/pallas_call | solution.py:224
  136.1 9.6 %all_to_all.27 = f32[8,8,640]{2,1,0:T(8,128)S(1)} all-to-all(f32[8,8,640]{2,1,0:T(8,128)S(1)} %bitcast.26), channel_id=1, replica_groups=mesh['seed'=4,'z'=8,'ylo'=2,'yhi'=2,'core'=2] {'yhi','core','ylo'}, dimensions={0} | all-to-all | bytes 327680 | tf_op jit(solution)/shard_map/all_to_all | solution.py:319
  145.7 1.0 final.1
  146.9 12.9 %all_to_all.28 = f32[16,8,128]{2,1,0:T(8,128)S(1)} all-to-all(f32[16,8,128]{2,1,0:T(8,128)S(1)} %bitcast.39), channel_id=1, replica_groups=mesh['seed'=4,'z'=8,'ylo'=2,'yhi'=2,'core'=2] {'ylo','z'}, dimensions={0} | all-to-all | bytes 131072 | tf_op jit(solution)/shard_map/all_to_all | solution.py:323
  (71 shorter events, 6.0 us)
Async XLA Ops:
  6.5 60.0 %all-gather.3.cloned.1.call-start = ((), (), s32[]{:S(2)}) async-start(), calls=%async_computation.5 | async-start | bytes 4718592 | tf_op jit(solution)/shard_map/all_gather | solution.py:289
  8.4 15.9 %copy-start.7 = (bf16[8,144,128]{2,1,0:T(8,128)(2,1)}, bf16[8,144,128]{2,1,0:T(8,128)(2,1)S(1)}, u32[]{:S(2)}) copy-start(bf16[8,144,128]{2,1,0:T(8,128)(2,1)S(1)} %get-tuple-element.32.refs_0_) | copy-start | bytes 884740
  8.4 10.0 %collective-permute-start = (bf16[8,144,128]{2,1,0:T(8,128)(2,1)S(1)}, bf16[8,144,128]{2,1,0:T(8,128)(2,1)S(1)}, u32[]{:S(2)}, u32[]{:S(2)}) collective-permute-start(bf16[8,144,128]{2,1,0:T(8,128)(2,1)S(1)} %get-tuple-element.59), channel_id=1, source_target_pairs={{0,4},{4,0},{1,5},{5,1},{2,6},{6,2},{3,7},{7,3},{8,12},{12,8},{9,1... | collective-permute-start | bytes 884744 | tf_op jit(solution)/shard_map/ppermute | solution.py:285
  10.0 50.7 %copy-start.21 = (s32[64]{0:T(128)S(1)}, s32[64]{0:T(128)}, u32[]{:S(2)}) copy-start(s32[64]{0:T(128)} %param.11) | copy-start | bytes 772
  11.5 55.0 %copy-start.6 = (bf16[2048,32]{0,1:T(8,128)(2,1)S(1)}, bf16[2048,32]{0,1:T(8,128)(2,1)}, u32[]{:S(2)}) copy-start(bf16[2048,32]{0,1:T(8,128)(2,1)} %param.12) | copy-start | bytes 393220
  11.5 54.0 %collective-permute-start.15 = (bf16[1216,512]{1,0:T(8,128)(2,1)S(1)}, bf16[1216,512]{1,0:T(8,128)(2,1)}, u32[]{:S(2)}, u32[]{:S(2)}) collective-permute-start(bf16[1216,512]{1,0:T(8,128)(2,1)S(1)} %pad_maximum_fusion), channel_id=1, source_target_pairs={{0,4},{4,0},{1,5},{5,1},{2,6},{6,2},{3,7},{7,3},{8,12},{12,8},{9,1... | collective-permute-start | bytes 3735560 | tf_op jit(solution)/shard_map/ppermute | solution.py:288
  12.1 14.2 %collective-permute-start.1 = (bf16[8,144,128]{2,1,0:T(8,128)(2,1)S(1)}, bf16[8,144,128]{2,1,0:T(8,128)(2,1)S(1)}, u32[]{:S(2)}, u32[]{:S(2)}) collective-permute-start(bf16[8,144,128]{2,1,0:T(8,128)(2,1)S(1)} %get-tuple-element.32.refs_0_), channel_id=1, source_target_pairs={{0,8},{8,16},{16,24},{24,32},{32,40},{40,48},{48,56},{56,0},{1,9},... | collective-permute-start | bytes 884744 | tf_op jit(solution)/shard_map/ppermute | solution.py:30
  18.4 19.6 %copy-start.8 = (bf16[8,144,128]{2,1,0:T(8,128)(2,1)}, bf16[8,144,128]{2,1,0:T(8,128)(2,1)S(1)}, u32[]{:S(2)}) copy-start(bf16[8,144,128]{2,1,0:T(8,128)(2,1)S(1)} %collective-permute-done.refs_1_) | copy-start | bytes 884740
  18.4 13.3 %collective-permute-start.4 = (bf16[8,144,128]{2,1,0:T(8,128)(2,1)S(1)}, bf16[8,144,128]{2,1,0:T(8,128)(2,1)S(1)}, u32[]{:S(2)}, u32[]{:S(2)}) collective-permute-start(bf16[8,144,128]{2,1,0:T(8,128)(2,1)S(1)} %collective-permute-done.refs_1_), channel_id=1, source_target_pairs={{0,56},{8,0},{16,8},{24,16},{32,24},{40,32},{48,40},{56,48},{1,57}... | collective-permute-start | bytes 884744 | tf_op jit(solution)/shard_map/ppermute | solution.py:31
  24.2 13.8 %collective-permute-start.2 = (bf16[8,144,128]{2,1,0:T(8,128)(2,1)S(1)}, bf16[8,144,128]{2,1,0:T(8,128)(2,1)S(1)}, u32[]{:S(2)}, u32[]{:S(2)}) collective-permute-start(bf16[8,144,128]{2,1,0:T(8,128)(2,1)S(1)} %get-tuple-element.32.refs_0_), channel_id=1, source_target_pairs={{0,56},{8,0},{16,8},{24,16},{32,24},{40,32},{48,40},{56,48},{1,57}... | collective-permute-start | bytes 884744 | tf_op jit(solution)/shard_map/ppermute | solution.py:31
  25.2 16.5 %collective-permute-start.3 = (bf16[8,144,128]{2,1,0:T(8,128)(2,1)S(1)}, bf16[8,144,128]{2,1,0:T(8,128)(2,1)S(1)}, u32[]{:S(2)}, u32[]{:S(2)}) collective-permute-start(bf16[8,144,128]{2,1,0:T(8,128)(2,1)S(1)} %collective-permute-done.refs_1_), channel_id=1, source_target_pairs={{0,8},{8,16},{16,24},{24,32},{32,40},{40,48},{48,56},{56,0},{1,9},... | collective-permute-start | bytes 884744 | tf_op jit(solution)/shard_map/ppermute | solution.py:30
  26.2 15.5 %copy-start.9 = (bf16[8,144,128]{2,1,0:T(8,128)(2,1)}, bf16[8,144,128]{2,1,0:T(8,128)(2,1)S(1)}, u32[]{:S(2)}) copy-start(bf16[8,144,128]{2,1,0:T(8,128)(2,1)S(1)} %collective-permute-done.1.refs_2_) | copy-start | bytes 884740
  26.2 15.5 %collective-permute-start.5 = (bf16[8,144,128]{2,1,0:T(8,128)(2,1)S(1)}, bf16[8,144,128]{2,1,0:T(8,128)(2,1)S(1)}, u32[]{:S(2)}, u32[]{:S(2)}) collective-permute-start(bf16[8,144,128]{2,1,0:T(8,128)(2,1)S(1)} %collective-permute-done.1.refs_2_), channel_id=1, source_target_pairs={{0,8},{8,16},{16,24},{24,32},{32,40},{40,48},{48,56},{56,0},{1,9},... | collective-permute-start | bytes 884744 | tf_op jit(solution)/shard_map/ppermute | solution.py:30
  31.7 12.6 %collective-permute-start.8 = (bf16[8,144,128]{2,1,0:T(8,128)(2,1)S(1)}, bf16[8,144,128]{2,1,0:T(8,128)(2,1)S(1)}, u32[]{:S(2)}, u32[]{:S(2)}) collective-permute-start(bf16[8,144,128]{2,1,0:T(8,128)(2,1)S(1)} %collective-permute-done.4.refs_5_), channel_id=1, source_target_pairs={{0,56},{8,0},{16,8},{24,16},{32,24},{40,32},{48,40},{56,48},{1,57}... | collective-permute-start | bytes 884744 | tf_op jit(solution)/shard_map/ppermute | solution.py:31
  38.0 28.5 %copy-start.11 = (bf16[8,144,128]{2,1,0:T(8,128)(2,1)}, bf16[8,144,128]{2,1,0:T(8,128)(2,1)S(1)}, u32[]{:S(2)}) copy-start(bf16[8,144,128]{2,1,0:T(8,128)(2,1)S(1)} %collective-permute-done.2.refs_3_) | copy-start | bytes 884740
  38.0 12.6 %collective-permute-start.6 = (bf16[8,144,128]{2,1,0:T(8,128)(2,1)S(1)}, bf16[8,144,128]{2,1,0:T(8,128)(2,1)S(1)}, u32[]{:S(2)}, u32[]{:S(2)}) collective-permute-start(bf16[8,144,128]{2,1,0:T(8,128)(2,1)S(1)} %collective-permute-done.2.refs_3_), channel_id=1, source_target_pairs={{0,56},{8,0},{16,8},{24,16},{32,24},{40,32},{48,40},{56,48},{1,57}... | collective-permute-start | bytes 884744 | tf_op jit(solution)/shard_map/ppermute | solution.py:31
  41.7 24.8 %copy-start.12 = (bf16[8,144,128]{2,1,0:T(8,128)(2,1)}, bf16[8,144,128]{2,1,0:T(8,128)(2,1)S(1)}, u32[]{:S(2)}) copy-start(bf16[8,144,128]{2,1,0:T(8,128)(2,1)S(1)} %collective-permute-done.3.refs_4_) | copy-start | bytes 884740
  41.7 12.6 %collective-permute-start.7 = (bf16[8,144,128]{2,1,0:T(8,128)(2,1)S(1)}, bf16[8,144,128]{2,1,0:T(8,128)(2,1)S(1)}, u32[]{:S(2)}, u32[]{:S(2)}) collective-permute-start(bf16[8,144,128]{2,1,0:T(8,128)(2,1)S(1)} %collective-permute-done.3.refs_4_), channel_id=1, source_target_pairs={{0,8},{8,16},{16,24},{24,32},{32,40},{40,48},{48,56},{56,0},{1,9},... | collective-permute-start | bytes 884744 | tf_op jit(solution)/shard_map/ppermute | solution.py:30
  41.8 24.7 %copy-start.13 = (bf16[8,144,128]{2,1,0:T(8,128)(2,1)}, bf16[8,144,128]{2,1,0:T(8,128)(2,1)S(1)}, u32[]{:S(2)}) copy-start(bf16[8,144,128]{2,1,0:T(8,128)(2,1)S(1)} %collective-permute-done.5.refs_6_) | copy-start | bytes 884740
  41.8 12.5 %collective-permute-start.9 = (bf16[8,144,128]{2,1,0:T(8,128)(2,1)S(1)}, bf16[8,144,128]{2,1,0:T(8,128)(2,1)S(1)}, u32[]{:S(2)}, u32[]{:S(2)}) collective-permute-start(bf16[8,144,128]{2,1,0:T(8,128)(2,1)S(1)} %collective-permute-done.5.refs_6_), channel_id=1, source_target_pairs={{0,8},{8,16},{16,24},{24,32},{32,40},{40,48},{48,56},{56,0},{1,9},... | collective-permute-start | bytes 884744 | tf_op jit(solution)/shard_map/ppermute | solution.py:30
  44.3 22.2 %copy-start.14 = (bf16[8,144,128]{2,1,0:T(8,128)(2,1)}, bf16[8,144,128]{2,1,0:T(8,128)(2,1)S(1)}, u32[]{:S(2)}) copy-start(bf16[8,144,128]{2,1,0:T(8,128)(2,1)S(1)} %collective-permute-done.8.refs_9_) | copy-start | bytes 884740
  44.3 12.6 %collective-permute-start.12 = (bf16[8,144,128]{2,1,0:T(8,128)(2,1)S(1)}, bf16[8,144,128]{2,1,0:T(8,128)(2,1)}, u32[]{:S(2)}, u32[]{:S(2)}) collective-permute-start(bf16[8,144,128]{2,1,0:T(8,128)(2,1)S(1)} %collective-permute-done.8.refs_9_), channel_id=1, source_target_pairs={{0,56},{8,0},{16,8},{24,16},{32,24},{40,32},{48,40},{56,48},{1,57}... | collective-permute-start | bytes 884744 | tf_op jit(solution)/shard_map/ppermute | solution.py:31
  50.6 15.9 %copy-start.15 = (bf16[8,144,128]{2,1,0:T(8,128)(2,1)}, bf16[8,144,128]{2,1,0:T(8,128)(2,1)S(1)}, u32[]{:S(2)}) copy-start(bf16[8,144,128]{2,1,0:T(8,128)(2,1)S(1)} %collective-permute-done.6.refs_7_) | copy-start | bytes 884740
  50.6 13.7 %collective-permute-start.10 = (bf16[8,144,128]{2,1,0:T(8,128)(2,1)S(1)}, bf16[8,144,128]{2,1,0:T(8,128)(2,1)S(1)}, u32[]{:S(2)}, u32[]{:S(2)}) collective-permute-start(bf16[8,144,128]{2,1,0:T(8,128)(2,1)S(1)} %collective-permute-done.6.refs_7_), channel_id=1, source_target_pairs={{0,56},{8,0},{16,8},{24,16},{32,24},{40,32},{48,40},{56,48},{1,57}... | collective-permute-start | bytes 884744 | tf_op jit(solution)/shard_map/ppermute | solution.py:31
  54.3 12.2 %copy-start.16 = (bf16[8,144,128]{2,1,0:T(8,128)(2,1)}, bf16[8,144,128]{2,1,0:T(8,128)(2,1)S(1)}, u32[]{:S(2)}) copy-start(bf16[8,144,128]{2,1,0:T(8,128)(2,1)S(1)} %collective-permute-done.7.refs_8_) | copy-start | bytes 884740
  54.3 10.1 %collective-permute-start.11 = (bf16[8,144,128]{2,1,0:T(8,128)(2,1)S(1)}, bf16[8,144,128]{2,1,0:T(8,128)(2,1)S(1)}, u32[]{:S(2)}, u32[]{:S(2)}) collective-permute-start(bf16[8,144,128]{2,1,0:T(8,128)(2,1)S(1)} %collective-permute-done.7.refs_8_), channel_id=1, source_target_pairs={{0,8},{8,16},{16,24},{24,32},{32,40},{40,48},{48,56},{56,0},{1,9},... | collective-permute-start | bytes 884744 | tf_op jit(solution)/shard_map/ppermute | solution.py:30
  54.4 11.1 %collective-permute-start.13 = (bf16[8,144,128]{2,1,0:T(8,128)(2,1)S(1)}, bf16[8,144,128]{2,1,0:T(8,128)(2,1)S(1)}, u32[]{:S(2)}, u32[]{:S(2)}) collective-permute-start(bf16[8,144,128]{2,1,0:T(8,128)(2,1)S(1)} %collective-permute-done.9.refs_10_), channel_id=1, source_target_pairs={{0,8},{8,16},{16,24},{24,32},{32,40},{40,48},{48,56},{56,0},{1,9},... | collective-permute-start | bytes 884744 | tf_op jit(solution)/shard_map/ppermute | solution.py:37
  57.0 9.5 %collective-permute-start.14 = (bf16[8,144,128]{2,1,0:T(8,128)(2,1)}, bf16[8,144,128]{2,1,0:T(8,128)(2,1)}, u32[]{:S(2)}, u32[]{:S(2)}) collective-permute-start(bf16[8,144,128]{2,1,0:T(8,128)(2,1)} %collective-permute-done.12.refs_13_), channel_id=1, source_target_pairs={{0,56},{8,0},{16,8},{24,16},{32,24},{40,32},{48,40},{56,48},{1,57}... | collective-permute-start | bytes 884744 | tf_op jit(solution)/shard_map/ppermute | solution.py:38
  66.5 24.6 %copy-start = (bf16[512,4096]{1,0:T(8,128)(2,1)S(1)}, bf16[512,4096]{1,0:T(8,128)(2,1)}, u32[]{:S(2)}) copy-start(bf16[512,4096]{1,0:T(8,128)(2,1)} %head_ref.3) | copy-start | bytes 12582916
  92.8 20.1 %all-to-all-start.1 = ((bf16[16,64,256]{2,1,0:T(8,128)(2,1)}), bf16[16,64,256]{2,1,0:T(8,128)(2,1)}, u32[]{:S(2)}, u32[]{:S(2)}) async-start(bf16[16,64,256]{2,1,0:T(8,128)(2,1)} %logits_slices.1), calls=%async_computation.1 | async-start | bytes 1048576 | tf_op jit(solution)/shard_map/all_to_all | solution.py:308
  133.0 12.7 %copy-start.4 = (bf16[512,64]{0,1:T(8,128)(2,1)S(1)}, bf16[512,64]{0,1:T(8,128)(2,1)}, u32[]{:S(2)}) copy-start(bf16[512,64]{0,1:T(8,128)(2,1)} %param.13) | copy-start | bytes 196612
  133.0 12.7 %copy-start.5 = (bf16[64,512]{1,0:T(8,128)(2,1)S(1)}, bf16[64,512]{1,0:T(8,128)(2,1)}, u32[]{:S(2)}) copy-start(bf16[64,512]{1,0:T(8,128)(2,1)} %slice.3.other_ref) | copy-start | bytes 196612
  (8 other events, 31.8 us)
Sparse Core Ops, SparseCore 0:
  9.2 52.7 all-gather.2

commit v5 on v4

--- a/solution.py
+++ b/solution.py
@@ -10,7 +10,6 @@
 CHAN = ("z", "ylo")
 SPREAD = ("ylo", "z")
 ROWS = ("yhi", "core", "ylo")
-W_ORDER = ("yhi", "ylo", "core")
 BF16_TOP = 3.3895313892515355e38
 NT = (((1,), (1,)), ((), ()))
 TN = (((0,), (0,)), ((), ()))
@@ -19,38 +18,50 @@
 LIMIT = pltpu.CompilerParams(vmem_limit_bytes=16 * 1024 * 1024)
 
 
+def pass_weight(w):
+    swap = [(0, 1), (1, 0)]
+    across = [(i, 3 - i) for i in range(4)]
+    low = lax.ppermute(w, "ylo", swap)
+    high = lax.ppermute(w, ("ylo", "yhi"), across)
+    far = lax.ppermute(low, ("ylo", "yhi"), across)
+    return [b for v in (w, far, low, high) for b in (v, lax.ppermute(v, "core", swap))]
+
+
 def rings(mine, swapped, nz):
     right = [(i, (i + 1) % nz) for i in range(nz)]
     left = [(i, (i - 1) % nz) for i in range(nz)]
-    got = [(0, 0, mine), (1, 0, swapped)]
-    r = [mine, swapped]
-    l = [mine, swapped]
+    r = [lax.ppermute(mine, "z", right), None]
+    l = [lax.ppermute(mine, "z", left), None]
+    r[0], l[0], swapped = lax.optimization_barrier((r[0], l[0], swapped))
+    got = [(0, 0, mine), (1, 0, swapped), (0, 1, r[0]), (0, nz - 1, l[0])]
+    r[1] = l[1] = swapped
     for k in range(1, nz // 2):
         for sub in range(2):
-            r[sub] = lax.ppermute(r[sub], "z", right)
-            l[sub] = lax.ppermute(l[sub], "z", left)
-            if k < nz // 2 - 1:
-                got += [(sub, k, r[sub]), (sub, nz - k, l[sub])]
-    ends = [*r, *l]
-    for sub in range(2):
-        got += [(sub, nz // 2 - 1, ends[sub]), (sub, nz // 2 + 1, ends[2 + sub])]
-    got.append((0, nz // 2, lax.ppermute(ends[0], "z", right)))
-    got.append((1, nz // 2, lax.ppermute(ends[3], "z", left)))
+            step = k if sub else k + 1
+            if step < nz // 2:
+                r[sub] = lax.ppermute(r[sub], "z", right)
+                l[sub] = lax.ppermute(l[sub], "z", left)
+                got += [(sub, step, r[sub]), (sub, nz - step, l[sub])]
+    got.append((0, nz // 2, lax.ppermute(r[0], "z", right)))
+    got.append((1, nz // 2, lax.ppermute(l[1], "z", left)))
     return got
 
 
 def conv_body(nz, plan, place_ref, *refs):
     count = len(plan)
     blocks = refs[:count]
-    w_ref, own_ref, other_ref, pa_ref, hot_ref, pooled_ref, mask_ref, acts_ref = refs[count : count + 8]
-    x_ref, wv_ref, sv_ref, mv_ref, x_sem, w_sem, s_sem, m_sem = refs[count + 8 :]
+    w_refs = refs[count : count + 8]
+    own_ref, other_ref, pa_ref, hot_ref, pooled_ref, mask_ref, acts_ref = refs[count + 8 : count + 15]
+    x_ref, wv_ref, sv_ref, mv_ref, x_sem, w_sem, s_sem, m_sem = refs[count + 15 :]
     imgs, pos, kz = blocks[0].shape
     cut = imgs // 2
     ka = pa_ref.shape[0]
     depth, width = wv_ref.shape[1:]
-    rows_w = w_ref.shape[3]
+    rows_w = w_refs[0].shape[0]
     me_z = place_ref[0]
     me_y = place_ref[1]
+    me_hi = place_ref[2]
+    me_core = place_ref[3]
     columns = (me_y, 1 - me_y)
 
     def copy_x(part):
@@ -65,15 +76,13 @@
         return made
 
     def copy_w(h):
-        return [
-            pltpu.make_async_copy(
-                w_ref.at[hi, columns[h], core],
-                wv_ref.at[h, pl.ds((hi * 2 + core) * rows_w, rows_w)],
-                w_sem.at[h, hi * 2 + core],
-            )
-            for hi in range(2)
-            for core in range(2)
-        ]
+        made = []
+        for i in range(4):
+            hi = me_hi if i < 2 else 1 - me_hi
+            core = me_core if i % 2 == 0 else 1 - me_core
+            row = pl.multiple_of((hi * 2 + core) * rows_w, rows_w)
+            made.append(pltpu.make_async_copy(w_refs[4 * h + i], wv_ref.at[h, pl.ds(row, rows_w)], w_sem.at[h, i]))
+        return made
 
     copies = [copy_w(0) + copy_x(0), copy_x(1), copy_w(1)]
     streams = [
@@ -117,7 +126,7 @@
         c.wait()
 
 
-def conv(place, got, w_all, stream2, stream_other, proj_act, hot, nz):
+def conv(place, got, weights, stream2, stream_other, proj_act, hot, nz):
     plan = tuple((sub, shift) for sub, shift, _ in got)
     blocks = [b for _, _, b in got]
     half, pos, kz = blocks[0].shape
@@ -125,7 +134,7 @@
     ka, depth = proj_act.shape
     return pl.pallas_call(
         functools.partial(conv_body, nz, plan),
-        in_specs=[pl.BlockSpec(memory_space=pltpu.SMEM)] + [HB] * (len(blocks) + 3) + [VM, VM],
+        in_specs=[pl.BlockSpec(memory_space=pltpu.SMEM)] + [HB] * (len(blocks) + 10) + [VM, VM],
         out_specs=[VM, HB, VM],
         out_shape=[
             jax.ShapeDtypeStruct((fs, 2, 2 * half, width), jnp.bfloat16),
@@ -144,7 +153,7 @@
         ],
         compiler_params=pltpu.CompilerParams(vmem_limit_bytes=32 * 1024 * 1024),
         name="conv_pool_mask",
-    )(place, *[pltpu.with_memory_space_constraint(b, pltpu.HBM) for b in (*blocks, w_all, stream2, stream_other)], proj_act, hot)
+    )(place, *[pltpu.with_memory_space_constraint(b, pltpu.HBM) for b in (*blocks, *weights, stream2, stream_other)], proj_act, hot)
 
 
 def masked_body(acts_ref, mask_ref, m_ref):
@@ -286,7 +295,7 @@
     pe_own = proj_err.T
     sent = lax.dynamic_index_in_dim(stream, 1 - me_y, 0, keepdims=False).reshape(half * pos, width)
     stream_other = lax.ppermute(jnp.concatenate([sent, pe_own], axis=0), "ylo", swap)
-    w_all = lax.all_gather(conv_weight, W_ORDER, axis=0)
+    weights = pass_weight(conv_weight)
     got = rings(mine, swapped, nz)
 
     classes = f * block + jnp.arange(block, dtype=jnp.int32)
@@ -294,13 +303,11 @@
     hot = lax.dot_general(onehot, head_weight, NT, preferred_element_type=jnp.float32)
     hot = hot.astype(jnp.bfloat16).reshape(fs, 2, half, width)
 
-    *blocks, w_all, stream_other, hot = lax.optimization_barrier(
-        [g[2] for g in got] + [w_all, stream_other, hot]
-    )
+    blocks, weights, stream_other, hot = lax.optimization_barrier(([g[2] for g in got], weights, stream_other, hot))
     got = [g[:2] + (b,) for g, b in zip(got, blocks)]
-    place = jnp.stack([lax.axis_index("z"), me_y]).astype(jnp.int32)
+    place = jnp.stack([lax.axis_index(a) for a in ("z", "ylo", "yhi", "core")]).astype(jnp.int32)
     both, mask, acts = conv(
-        place, got, w_all.reshape(2, 2, 2, *conv_weight.shape),
+        place, got, weights,
         stream.reshape(2, half * pos, width), stream_other, proj_act.T, hot, nz,
     )
 

time: 168 us -> 166 us (0.988)
  between operations: 13.7 us -> 0.21 us
  waiting for transfers between devices: 33.5 us -> 42.6 us
  starting transfers between devices: 36.1 us -> 37.8 us
    ppermute x6 -> x5, waiting for transfers between devices: 0.02 us -> 13.3 us  [rings(): r[sub] = lax.ppermute(r[sub], 'z', right)]
    ppermute x2 -> x11, starting transfers between devices: 3.88 us -> 17 us  [the longest x1 5.86 us: rings(): l = [lax.ppermute(mine, 'z', left), None]]
    ppermute x6 -> x5, starting transfers between devices: 21.6 us -> 10.5 us  [rings(): l[sub] = lax.ppermute(l[sub], 'z', left)]
    ppermute x6 -> x5, waiting for transfers between devices: 15.4 us -> 11.4 us  [rings(): l[sub] = lax.ppermute(l[sub], 'z', left)]
    ppermute x2 -> x11, waiting for transfers between devices: 1.37 us -> 4.23 us  [the longest x1 3.41 us: rings(): r = [lax.ppermute(mine, 'z', right), None]]
    ppermute x1, waiting for transfers between devices: 4.37 us -> 2.01 us  [per_device(): swapped = lax.ppermute(theirs, 'ylo', swap)]
  transfers between devices with their start and end apart: 18 -> 24, of which waited for: 9 -> 12; matrix products, arithmetic and copies ran while one was open for 5% -> 4% of each run, Pallas kernels for 0% -> 0%
where the time goes in v5:
time: 166 us
  blocking collectives  52.6 us (32%)
  waiting for transfers between devices  42.6 us (26%)
  starting transfers between devices  37.8 us (23%)
  Pallas kernels  20 us (12%)
  local copies, waits for them, and re-layouts  7.01 us (4%)
  matrix products  3.58 us (2%)
  other arithmetic  1.91 us (1%)
    all_to_all x1, blocking collectives, per_device(): lax.all_to_all(jnp.broadcast_to(expo, (parts,) + expo.shape), SPREAD, 0, 0)  18.9 us
    pallas_call x1, Pallas kernels, conv(): pl.pallas_call(functools.partial(conv_body, nz, plan), in_specs=[pl.Block...  13.5 us
    ppermute x5, waiting for transfers between devices, rings(): r[sub] = lax.ppermute(r[sub], 'z', right)  13.3 us
    all_to_all x1, blocking collectives, per_device(): grads = lax.all_to_all(grads, SPREAD, 0, 0)  12.9 us
    all_to_all x1, waiting for transfers between devices, per_device(): part = lax.all_to_all(logits_slices(both, head_weight, parts), SPREAD, 0, 0)  11.6 us
    ppermute x5, waiting for transfers between devices, rings(): l[sub] = lax.ppermute(l[sub], 'z', left)  11.4 us
    all_to_all x1, blocking collectives, per_device(): both = lax.all_to_all(both.reshape(2 * fs, 2 * half, width), ROWS, 0, 0)  11.2 us
    ppermute x5, starting transfers between devices, rings(): l[sub] = lax.ppermute(l[sub], 'z', left)  10.5 us
  transfers between devices with their start and end apart: 24, of which 12 were waited for; matrix products, arithmetic and copies ran while one was open for 4% of the time, Pallas kernels for 0%

profile of v5, /device:TPU:2, one launch (start us, length us, event | category | flops | bytes accessed | tf_op | source)
XLA Modules:
  0.0 165.7 jit_solution(2735411536491670289)
XLA Ops:
  1.1 1.7 %collective-permute-start.2 = (bf16[8,144,128]{2,1,0:T(8,128)(2,1)S(1)}, bf16[8,144,128]{2,1,0:T(8,128)(2,1)S(1)}, u32[]{:S(2)}, u32[]{:S(2)}) collective-permute-start(bf16[8,144,128]{2,1,0:T(8,128)(2,1)S(1)} %get-tuple-element.79), channel_id=1, source_target_pairs={{0,4},{4,0},{1,5},{5,1},{2,6},{6,2},{3,7},{7,3},{8,12},{12,8},{9,1... | collective-permute-start | bytes 884744 | tf_op jit(solution)/shard_map/ppermute | solution.py:294
  3.3 5.9 %collective-permute-start.1 = (bf16[8,144,128]{2,1,0:T(8,128)(2,1)S(1)}, bf16[8,144,128]{2,1,0:T(8,128)(2,1)S(1)}, u32[]{:S(2)}, u32[]{:S(2)}) collective-permute-start(bf16[8,144,128]{2,1,0:T(8,128)(2,1)S(1)} %get-tuple-element.45.refs_0_), channel_id=1, source_target_pairs={{0,56},{8,0},{16,8},{24,16},{32,24},{40,32},{48,40},{56,48},{1,57}... | collective-permute-start | bytes 884744 | tf_op jit(solution)/shard_map/ppermute | solution.py:34
  9.1 2.0 %collective-permute-done.2.refs_1_ = bf16[8,144,128]{2,1,0:T(8,128)(2,1)S(1)} collective-permute-done((bf16[8,144,128]{2,1,0:T(8,128)(2,1)S(1)}, bf16[8,144,128]{2,1,0:T(8,128)(2,1)S(1)}, u32[]{:S(2)}, u32[]{:S(2)}) %collective-permute-start.2) | collective-permute-done | bytes 294944 | tf_op jit(solution)/shard_map/ppermute | solution.py:294
  11.1 3.0 %collective-permute-start.20 = (bf16[512,512]{1,0:T(8,128)(2,1)}, bf16[512,512]{1,0:T(8,128)(2,1)}, u32[]{:S(2)}, u32[]{:S(2)}) collective-permute-start(bf16[512,512]{1,0:T(8,128)(2,1)} %refs_16_), channel_id=1, source_target_pairs={{0,6},{2,4},{4,2},{6,0},{1,7},{3,5},{5,3},{7,1},{8,14},{10,12},{12... | collective-permute-start | bytes 1572872 | tf_op jit(solution)/shard_map/ppermute | solution.py:25
  14.1 1.4 constant_dynamic-slice_fusion
  16.1 3.4 %collective-permute-done.refs_2_ = bf16[8,144,128]{2,1,0:T(8,128)(2,1)S(1)} collective-permute-done((bf16[8,144,128]{2,1,0:T(8,128)(2,1)S(1)}, bf16[8,144,128]{2,1,0:T(8,128)(2,1)S(1)}, u32[]{:S(2)}, u32[]{:S(2)}) %collective-permute-start) | collective-permute-done | bytes 294944 | tf_op jit(solution)/shard_map/ppermute | solution.py:33
  19.5 2.0 %collective-permute-start.6 = (bf16[8,144,128]{2,1,0:T(8,128)(2,1)S(1)}, bf16[8,144,128]{2,1,0:T(8,128)(2,1)S(1)}, u32[]{:S(2)}, u32[]{:S(2)}) collective-permute-start(bf16[8,144,128]{2,1,0:T(8,128)(2,1)S(1)} %collective-permute-done.2.refs_1_), channel_id=1, source_target_pairs={{0,56},{8,0},{16,8},{24,16},{32,24},{40,32},{48,40},{56,48},{1,57}... | collective-permute-start | bytes 884744 | tf_op jit(solution)/shard_map/ppermute | solution.py:43
  21.5 1.6 collective-permute-start.3
  23.1 4.0 %collective-permute-start.4 = (bf16[8,144,128]{2,1,0:T(8,128)(2,1)S(1)}, bf16[8,144,128]{2,1,0:T(8,128)(2,1)S(1)}, u32[]{:S(2)}, u32[]{:S(2)}) collective-permute-start(bf16[8,144,128]{2,1,0:T(8,128)(2,1)S(1)} %collective-permute-done.1.refs_3_), channel_id=1, source_target_pairs={{0,56},{8,0},{16,8},{24,16},{32,24},{40,32},{48,40},{56,48},{1,57}... | collective-permute-start | bytes 884744 | tf_op jit(solution)/shard_map/ppermute | solution.py:43
  27.3 1.7 %collective-permute-start.22 = (bf16[1216,512]{1,0:T(8,128)(2,1)S(1)}, bf16[1216,512]{1,0:T(8,128)(2,1)S(1)}, u32[]{:S(2)}, u32[]{:S(2)}) collective-permute-start(bf16[1216,512]{1,0:T(8,128)(2,1)S(1)} %pad_maximum_fusion), channel_id=1, source_target_pairs={{0,4},{4,0},{1,5},{5,1},{2,6},{6,2},{3,7},{7,3},{8,12},{12,8},{9,1... | collective-permute-start | bytes 3735560 | tf_op jit(solution)/shard_map/ppermute | solution.py:297
  29.0 6.8 %collective-permute-done.3.refs_4_ = bf16[8,144,128]{2,1,0:T(8,128)(2,1)S(1)} collective-permute-done((bf16[8,144,128]{2,1,0:T(8,128)(2,1)S(1)}, bf16[8,144,128]{2,1,0:T(8,128)(2,1)S(1)}, u32[]{:S(2)}, u32[]{:S(2)}) %collective-permute-start.3) | collective-permute-done | bytes 294944 | tf_op jit(solution)/shard_map/ppermute | solution.py:42
  36.0 3.0 %collective-permute-start.8 = (bf16[8,144,128]{2,1,0:T(8,128)(2,1)S(1)}, bf16[8,144,128]{2,1,0:T(8,128)(2,1)S(1)}, u32[]{:S(2)}, u32[]{:S(2)}) collective-permute-start(bf16[8,144,128]{2,1,0:T(8,128)(2,1)S(1)} %collective-permute-done.4.refs_5_), channel_id=1, source_target_pairs={{0,56},{8,0},{16,8},{24,16},{32,24},{40,32},{48,40},{56,48},{1,57}... | collective-permute-start | bytes 884744 | tf_op jit(solution)/shard_map/ppermute | solution.py:43
  39.1 3.0 %collective-permute-start.17 = (bf16[512,512]{1,0:T(8,128)(2,1)S(1)}, bf16[512,512]{1,0:T(8,128)(2,1)}, u32[]{:S(2)}, u32[]{:S(2)}) collective-permute-start(bf16[512,512]{1,0:T(8,128)(2,1)S(1)} %collective-permute-done.16.refs_20_), channel_id=1, source_target_pairs={{0,6},{2,4},{4,2},{6,0},{1,7},{3,5},{5,3},{7,1},{8,14},{10,12},{12... | collective-permute-start | bytes 1572872 | tf_op jit(solution)/shard_map/ppermute | solution.py:26
  42.1 1.6 collective-permute-done.7.refs_8_
  44.0 1.9 %collective-permute-done.8.refs_9_ = bf16[8,144,128]{2,1,0:T(8,128)(2,1)S(1)} collective-permute-done((bf16[8,144,128]{2,1,0:T(8,128)(2,1)S(1)}, bf16[8,144,128]{2,1,0:T(8,128)(2,1)S(1)}, u32[]{:S(2)}, u32[]{:S(2)}) %collective-permute-start.8) | collective-permute-done | bytes 294944 | tf_op jit(solution)/shard_map/ppermute | solution.py:43
  46.0 3.4 %collective-permute-done.10.refs_11_ = bf16[8,144,128]{2,1,0:T(8,128)(2,1)} collective-permute-done((bf16[8,144,128]{2,1,0:T(8,128)(2,1)S(1)}, bf16[8,144,128]{2,1,0:T(8,128)(2,1)}, u32[]{:S(2)}, u32[]{:S(2)}) %collective-permute-start.10) | collective-permute-done | bytes 294944 | tf_op jit(solution)/shard_map/ppermute | solution.py:43
  49.3 2.4 %collective-permute-done.9.refs_10_ = bf16[8,144,128]{2,1,0:T(8,128)(2,1)} collective-permute-done((bf16[8,144,128]{2,1,0:T(8,128)(2,1)S(1)}, bf16[8,144,128]{2,1,0:T(8,128)(2,1)}, u32[]{:S(2)}, u32[]{:S(2)}) %collective-permute-start.9) | collective-permute-done | bytes 294944 | tf_op jit(solution)/shard_map/ppermute | solution.py:42
  51.7 1.3 collective-permute-start.12
  54.2 6.1 %collective-permute-done.12.refs_13_ = bf16[8,144,128]{2,1,0:T(8,128)(2,1)} collective-permute-done((bf16[8,144,128]{2,1,0:T(8,128)(2,1)}, bf16[8,144,128]{2,1,0:T(8,128)(2,1)}, u32[]{:S(2)}, u32[]{:S(2)}) %collective-permute-start.12) | collective-permute-done | bytes 294944 | tf_op jit(solution)/shard_map/ppermute | solution.py:43
  60.3 3.7 %collective-permute-start.14 = (bf16[8,144,128]{2,1,0:T(8,128)(2,1)}, bf16[8,144,128]{2,1,0:T(8,128)(2,1)S(1)}, u32[]{:S(2)}, u32[]{:S(2)}) collective-permute-start(bf16[8,144,128]{2,1,0:T(8,128)(2,1)} %collective-permute-done.12.refs_13_), channel_id=1, source_target_pairs={{0,56},{8,0},{16,8},{24,16},{32,24},{40,32},{48,40},{56,48},{1,57}... | collective-permute-start | bytes 884744 | tf_op jit(solution)/shard_map/ppermute | solution.py:46
  64.0 3.6 %convolution_convert_fusion = bf16[64,512]{1,0:T(8,128)(2,1)S(1)} fusion(bf16[512,4096]{1,0:T(8,128)(2,1)} %head_ref.3, s32[4096]{0:T(1024)S(1)} %iota_add_fusion, s32[64]{0:T(128)S(1)} %copy-done.24), kind=kOutput, calls=%fused_computation.1 | convolution fusion | flops 268730368 | bytes 4276480 | tf_op jit(solution)/shard_map/dot_general | solution.py:303
  67.6 2.6 %collective-permute-done.11.refs_12_ = bf16[8,144,128]{2,1,0:T(8,128)(2,1)S(1)} collective-permute-done((bf16[8,144,128]{2,1,0:T(8,128)(2,1)}, bf16[8,144,128]{2,1,0:T(8,128)(2,1)S(1)}, u32[]{:S(2)}, u32[]{:S(2)}) %collective-permute-start.11) | collective-permute-done | bytes 294944 | tf_op jit(solution)/shard_map/ppermute | solution.py:42
  71.5 13.5 %conv_pool_mask.1 = (bf16[4,2,16,512]{3,2,1,0:T(8,128)(2,1)S(1)}, bf16[2,8,144,512]{3,2,1,0:T(8,128)(2,1)S(1)}, bf16[1152,64]{1,0:T(8,128)(2,1)S(1)}) custom-call(s32[4]{0:T(128)S(1)} %pad_add_fusion.place_ref, bf16[8,144,128]{2,1,0:T(8,128)(2,1)} %copy-done.8, bf16[8,144,128]{2,1,0:T(8,128)(2,1)} %copy-done.12, bf16[8,144,128]{2,1,0:T(8,128)(2,1)} %copy-done.14, ...), custom_call_target="tpu_custom_call" | custom-call | tf_op jit(solution)/shard_map/conv_pool_mask/pallas_call | solution.py:135
  85.7 11.2 %all_to_all.25.both_ref = bf16[8,16,512]{2,1,0:T(8,128)(2,1)S(1)} all-to-all(bf16[8,16,512]{2,1,0:T(8,128)(2,1)S(1)} %bitcast.32), channel_id=1, replica_groups=mesh['seed'=4,'z'=8,'ylo'=2,'yhi'=2,'core'=2] {'yhi','core','ylo'}, dimensions={0} | all-to-all | bytes 262144 | tf_op jit(solution)/shard_map/all_to_all | solution.py:314
  97.0 1.6 logits_slices.1
  98.6 4.8 %all-to-all-start.1 = ((bf16[16,64,256]{2,1,0:T(8,128)(2,1)}), bf16[16,64,256]{2,1,0:T(8,128)(2,1)}, u32[]{:S(2)}, u32[]{:S(2)}) async-start(bf16[16,64,256]{2,1,0:T(8,128)(2,1)} %logits_slices.1), calls=%async_computation.1 | async-start | bytes 1048576 | tf_op jit(solution)/shard_map/all_to_all | solution.py:315
  103.4 1.5 slice.3.other_ref
  106.6 11.6 %all-to-all-done.1 = bf16[16,64,256]{2,1,0:T(8,128)(2,1)} async-done(((bf16[16,64,256]{2,1,0:T(8,128)(2,1)}), bf16[16,64,256]{2,1,0:T(8,128)(2,1)}, u32[]{:S(2)}, u32[]{:S(2)}) %all-to-all-start.1) | async-done | bytes 524320 | tf_op jit(solution)/shard_map/all_to_all | solution.py:315
  119.4 18.9 %all_to_all.26.expo_ref = bf16[16,64,256]{2,1,0:T(8,128)(2,1)S(1)} all-to-all(bf16[16,64,256]{2,1,0:T(8,128)(2,1)S(1)} %broadcast_in_dim.2), channel_id=1, replica_groups=mesh['seed'=4,'z'=8,'ylo'=2,'yhi'=2,'core'=2] {'ylo','z'}, dimensions={0} | all-to-all | bytes 1048576 | tf_op jit(solution)/shard_map/all_to_all | solution.py:323
  138.3 3.1 %back.1 = f32[64,640]{1,0:T(8,128)S(1)} custom-call(bf16[16,64,256]{2,1,0:T(8,128)(2,1)S(1)} %all_to_all.26.expo_ref, bf16[512,4096]{1,0:T(8,128)(2,1)} %head_ref.3), custom_call_target="tpu_custom_call" | custom-call | tf_op jit(solution)/shard_map/back/pallas_call | solution.py:233
  141.4 9.6 %all_to_all.27 = f32[8,8,640]{2,1,0:T(8,128)S(1)} all-to-all(f32[8,8,640]{2,1,0:T(8,128)S(1)} %bitcast.26), channel_id=1, replica_groups=mesh['seed'=4,'z'=8,'ylo'=2,'yhi'=2,'core'=2] {'yhi','core','ylo'}, dimensions={0} | all-to-all | bytes 327680 | tf_op jit(solution)/shard_map/all_to_all | solution.py:326
  152.2 12.9 %all_to_all.28 = f32[16,8,128]{2,1,0:T(8,128)S(1)} all-to-all(f32[16,8,128]{2,1,0:T(8,128)S(1)} %bitcast.38), channel_id=1, replica_groups=mesh['seed'=4,'z'=8,'ylo'=2,'yhi'=2,'core'=2] {'ylo','z'}, dimensions={0} | all-to-all | bytes 131072 | tf_op jit(solution)/shard_map/all_to_all | solution.py:330
  (88 shorter events, 10.9 us)
Async XLA Ops:
  0.0 27.2 %copy-start.3 = (bf16[512,64]{0,1:T(8,128)(2,1)S(1)}, bf16[512,64]{0,1:T(8,128)(2,1)}, u32[]{:S(2)}) copy-start(bf16[512,64]{0,1:T(8,128)(2,1)} %param.13) | copy-start | bytes 196612
  1.1 26.1 %copy-start.8 = (bf16[8,144,128]{2,1,0:T(8,128)(2,1)}, bf16[8,144,128]{2,1,0:T(8,128)(2,1)S(1)}, u32[]{:S(2)}) copy-start(bf16[8,144,128]{2,1,0:T(8,128)(2,1)S(1)} %get-tuple-element.45.refs_0_) | copy-start | bytes 884740
  1.1 10.0 %collective-permute-start.2 = (bf16[8,144,128]{2,1,0:T(8,128)(2,1)S(1)}, bf16[8,144,128]{2,1,0:T(8,128)(2,1)S(1)}, u32[]{:S(2)}, u32[]{:S(2)}) collective-permute-start(bf16[8,144,128]{2,1,0:T(8,128)(2,1)S(1)} %get-tuple-element.79), channel_id=1, source_target_pairs={{0,4},{4,0},{1,5},{5,1},{2,6},{6,2},{3,7},{7,3},{8,12},{12,8},{9,1... | collective-permute-start | bytes 884744 | tf_op jit(solution)/shard_map/ppermute | solution.py:294
  2.8 18.7 %collective-permute-start.16 = (bf16[512,512]{1,0:T(8,128)(2,1)}, bf16[512,512]{1,0:T(8,128)(2,1)S(1)}, u32[]{:S(2)}, u32[]{:S(2)}) collective-permute-start(bf16[512,512]{1,0:T(8,128)(2,1)} %refs_16_), channel_id=1, source_target_pairs={{0,4},{4,0},{1,5},{5,1},{2,6},{6,2},{3,7},{7,3},{8,12},{12,8},{9,1... | collective-permute-start | bytes 1572872 | tf_op jit(solution)/shard_map/ppermute | solution.py:24
  3.3 19.9 %collective-permute-start.15 = (bf16[512,512]{1,0:T(8,128)(2,1)}, bf16[512,512]{1,0:T(8,128)(2,1)S(1)}, u32[]{:S(2)}, u32[]{:S(2)}) collective-permute-start(bf16[512,512]{1,0:T(8,128)(2,1)} %refs_16_), channel_id=1, source_target_pairs={{0,1},{1,0},{2,3},{3,2},{4,5},{5,4},{6,7},{7,6},{8,9},{9,8},{10,11... | collective-permute-start | bytes 1572872 | tf_op jit(solution)/shard_map/ppermute | solution.py:27
  3.3 12.8 %collective-permute-start.1 = (bf16[8,144,128]{2,1,0:T(8,128)(2,1)S(1)}, bf16[8,144,128]{2,1,0:T(8,128)(2,1)S(1)}, u32[]{:S(2)}, u32[]{:S(2)}) collective-permute-start(bf16[8,144,128]{2,1,0:T(8,128)(2,1)S(1)} %get-tuple-element.45.refs_0_), channel_id=1, source_target_pairs={{0,56},{8,0},{16,8},{24,16},{32,24},{40,32},{48,40},{56,48},{1,57}... | collective-permute-start | bytes 884744 | tf_op jit(solution)/shard_map/ppermute | solution.py:34
  9.1 10.4 %collective-permute-start = (bf16[8,144,128]{2,1,0:T(8,128)(2,1)S(1)}, bf16[8,144,128]{2,1,0:T(8,128)(2,1)S(1)}, u32[]{:S(2)}, u32[]{:S(2)}) collective-permute-start(bf16[8,144,128]{2,1,0:T(8,128)(2,1)S(1)} %get-tuple-element.45.refs_0_), channel_id=1, source_target_pairs={{0,8},{8,16},{16,24},{24,32},{32,40},{40,48},{48,56},{56,0},{1,9},... | collective-permute-start | bytes 884744 | tf_op jit(solution)/shard_map/ppermute | solution.py:33
  11.1 16.2 %collective-permute-start.20 = (bf16[512,512]{1,0:T(8,128)(2,1)}, bf16[512,512]{1,0:T(8,128)(2,1)}, u32[]{:S(2)}, u32[]{:S(2)}) collective-permute-start(bf16[512,512]{1,0:T(8,128)(2,1)} %refs_16_), channel_id=1, source_target_pairs={{0,6},{2,4},{4,2},{6,0},{1,7},{3,5},{5,3},{7,1},{8,14},{10,12},{12... | collective-permute-start | bytes 1572872 | tf_op jit(solution)/shard_map/ppermute | solution.py:25
  14.1 49.8 %copy-start.24 = (s32[64]{0:T(128)S(1)}, s32[64]{0:T(128)}, u32[]{:S(2)}) copy-start(s32[64]{0:T(128)} %param.11) | copy-start | bytes 772
  16.1 28.0 %copy-start.13 = (bf16[8,144,128]{2,1,0:T(8,128)(2,1)}, bf16[8,144,128]{2,1,0:T(8,128)(2,1)S(1)}, u32[]{:S(2)}) copy-start(bf16[8,144,128]{2,1,0:T(8,128)(2,1)S(1)} %collective-permute-done.1.refs_3_) | copy-start | bytes 884740
  19.5 26.5 %copy-start.14 = (bf16[8,144,128]{2,1,0:T(8,128)(2,1)}, bf16[8,144,128]{2,1,0:T(8,128)(2,1)S(1)}, u32[]{:S(2)}) copy-start(bf16[8,144,128]{2,1,0:T(8,128)(2,1)S(1)} %collective-permute-done.refs_2_) | copy-start | bytes 884740
  19.5 19.5 %collective-permute-start.6 = (bf16[8,144,128]{2,1,0:T(8,128)(2,1)S(1)}, bf16[8,144,128]{2,1,0:T(8,128)(2,1)S(1)}, u32[]{:S(2)}, u32[]{:S(2)}) collective-permute-start(bf16[8,144,128]{2,1,0:T(8,128)(2,1)S(1)} %collective-permute-done.2.refs_1_), channel_id=1, source_target_pairs={{0,56},{8,0},{16,8},{24,16},{32,24},{40,32},{48,40},{56,48},{1,57}... | collective-permute-start | bytes 884744 | tf_op jit(solution)/shard_map/ppermute | solution.py:43
  21.5 17.6 %collective-permute-start.5 = (bf16[8,144,128]{2,1,0:T(8,128)(2,1)S(1)}, bf16[8,144,128]{2,1,0:T(8,128)(2,1)S(1)}, u32[]{:S(2)}, u32[]{:S(2)}) collective-permute-start(bf16[8,144,128]{2,1,0:T(8,128)(2,1)S(1)} %collective-permute-done.2.refs_1_), channel_id=1, source_target_pairs={{0,8},{8,16},{16,24},{24,32},{32,40},{40,48},{48,56},{56,0},{1,9},... | collective-permute-start | bytes 884744 | tf_op jit(solution)/shard_map/ppermute | solution.py:42
  21.5 46.0 %copy-start.9 = (bf16[512,512]{1,0:T(8,128)(2,1)}, bf16[512,512]{1,0:T(8,128)(2,1)S(1)}, u32[]{:S(2)}) copy-start(bf16[512,512]{1,0:T(8,128)(2,1)S(1)} %collective-permute-done.16.refs_20_) | copy-start | bytes 1572868
  21.5 14.2 %collective-permute-start.3 = (bf16[8,144,128]{2,1,0:T(8,128)(2,1)S(1)}, bf16[8,144,128]{2,1,0:T(8,128)(2,1)S(1)}, u32[]{:S(2)}, u32[]{:S(2)}) collective-permute-start(bf16[8,144,128]{2,1,0:T(8,128)(2,1)S(1)} %collective-permute-done.refs_2_), channel_id=1, source_target_pairs={{0,8},{8,16},{16,24},{24,32},{32,40},{40,48},{48,56},{56,0},{1,9},... | collective-permute-start | bytes 884744 | tf_op jit(solution)/shard_map/ppermute | solution.py:42
  23.1 12.8 %collective-permute-start.4 = (bf16[8,144,128]{2,1,0:T(8,128)(2,1)S(1)}, bf16[8,144,128]{2,1,0:T(8,128)(2,1)S(1)}, u32[]{:S(2)}, u32[]{:S(2)}) collective-permute-start(bf16[8,144,128]{2,1,0:T(8,128)(2,1)S(1)} %collective-permute-done.1.refs_3_), channel_id=1, source_target_pairs={{0,56},{8,0},{16,8},{24,16},{32,24},{40,32},{48,40},{56,48},{1,57}... | collective-permute-start | bytes 884744 | tf_op jit(solution)/shard_map/ppermute | solution.py:43
  27.3 44.3 %copy-start.6 = (bf16[2048,32]{0,1:T(8,128)(2,1)S(1)}, bf16[2048,32]{0,1:T(8,128)(2,1)}, u32[]{:S(2)}) copy-start(bf16[2048,32]{0,1:T(8,128)(2,1)} %param.12) | copy-start | bytes 393220
  27.3 42.8 %collective-permute-start.22 = (bf16[1216,512]{1,0:T(8,128)(2,1)S(1)}, bf16[1216,512]{1,0:T(8,128)(2,1)S(1)}, u32[]{:S(2)}, u32[]{:S(2)}) collective-permute-start(bf16[1216,512]{1,0:T(8,128)(2,1)S(1)} %pad_maximum_fusion), channel_id=1, source_target_pairs={{0,4},{4,0},{1,5},{5,1},{2,6},{6,2},{3,7},{7,3},{8,12},{12,8},{9,1... | collective-permute-start | bytes 3735560 | tf_op jit(solution)/shard_map/ppermute | solution.py:297
  35.7 7.9 %collective-permute-start.7 = (bf16[8,144,128]{2,1,0:T(8,128)(2,1)S(1)}, bf16[8,144,128]{2,1,0:T(8,128)(2,1)S(1)}, u32[]{:S(2)}, u32[]{:S(2)}) collective-permute-start(bf16[8,144,128]{2,1,0:T(8,128)(2,1)S(1)} %collective-permute-done.3.refs_4_), channel_id=1, source_target_pairs={{0,8},{8,16},{16,24},{24,32},{32,40},{40,48},{48,56},{56,0},{1,9},... | collective-permute-start | bytes 884744 | tf_op jit(solution)/shard_map/ppermute | solution.py:42
  36.0 10.0 %collective-permute-start.8 = (bf16[8,144,128]{2,1,0:T(8,128)(2,1)S(1)}, bf16[8,144,128]{2,1,0:T(8,128)(2,1)S(1)}, u32[]{:S(2)}, u32[]{:S(2)}) collective-permute-start(bf16[8,144,128]{2,1,0:T(8,128)(2,1)S(1)} %collective-permute-done.4.refs_5_), channel_id=1, source_target_pairs={{0,56},{8,0},{16,8},{24,16},{32,24},{40,32},{48,40},{56,48},{1,57}... | collective-permute-start | bytes 884744 | tf_op jit(solution)/shard_map/ppermute | solution.py:43
  39.0 10.3 %collective-permute-start.10 = (bf16[8,144,128]{2,1,0:T(8,128)(2,1)S(1)}, bf16[8,144,128]{2,1,0:T(8,128)(2,1)}, u32[]{:S(2)}, u32[]{:S(2)}) collective-permute-start(bf16[8,144,128]{2,1,0:T(8,128)(2,1)S(1)} %collective-permute-done.6.refs_7_), channel_id=1, source_target_pairs={{0,56},{8,0},{16,8},{24,16},{32,24},{40,32},{48,40},{56,48},{1,57}... | collective-permute-start | bytes 884744 | tf_op jit(solution)/shard_map/ppermute | solution.py:43
  39.1 13.9 %collective-permute-start.17 = (bf16[512,512]{1,0:T(8,128)(2,1)S(1)}, bf16[512,512]{1,0:T(8,128)(2,1)}, u32[]{:S(2)}, u32[]{:S(2)}) collective-permute-start(bf16[512,512]{1,0:T(8,128)(2,1)S(1)} %collective-permute-done.16.refs_20_), channel_id=1, source_target_pairs={{0,6},{2,4},{4,2},{6,0},{1,7},{3,5},{5,3},{7,1},{8,14},{10,12},{12... | collective-permute-start | bytes 1572872 | tf_op jit(solution)/shard_map/ppermute | solution.py:26
  43.7 27.6 %copy-start.19 = (bf16[8,144,128]{2,1,0:T(8,128)(2,1)}, bf16[8,144,128]{2,1,0:T(8,128)(2,1)S(1)}, u32[]{:S(2)}) copy-start(bf16[8,144,128]{2,1,0:T(8,128)(2,1)S(1)} %collective-permute-done.7.refs_8_) | copy-start | bytes 884740
  43.7 8.0 %collective-permute-start.9 = (bf16[8,144,128]{2,1,0:T(8,128)(2,1)S(1)}, bf16[8,144,128]{2,1,0:T(8,128)(2,1)}, u32[]{:S(2)}, u32[]{:S(2)}) collective-permute-start(bf16[8,144,128]{2,1,0:T(8,128)(2,1)S(1)} %collective-permute-done.5.refs_6_), channel_id=1, source_target_pairs={{0,8},{8,16},{16,24},{24,32},{32,40},{40,48},{48,56},{56,0},{1,9},... | collective-permute-start | bytes 884744 | tf_op jit(solution)/shard_map/ppermute | solution.py:42
  45.9 7.4 %collective-permute-start.19 = (bf16[512,512]{1,0:T(8,128)(2,1)S(1)}, bf16[512,512]{1,0:T(8,128)(2,1)}, u32[]{:S(2)}, u32[]{:S(2)}) collective-permute-start(bf16[512,512]{1,0:T(8,128)(2,1)S(1)} %collective-permute-done.16.refs_20_), channel_id=1, source_target_pairs={{0,1},{1,0},{2,3},{3,2},{4,5},{5,4},{6,7},{7,6},{8,9},{9,8},{10,11... | collective-permute-start | bytes 1572872 | tf_op jit(solution)/shard_map/ppermute | solution.py:27
  49.3 4.7 %collective-permute-start.21 = (bf16[512,512]{1,0:T(8,128)(2,1)}, bf16[512,512]{1,0:T(8,128)(2,1)}, u32[]{:S(2)}, u32[]{:S(2)}) collective-permute-start(bf16[512,512]{1,0:T(8,128)(2,1)} %collective-permute-done.20.refs_22_), channel_id=1, source_target_pairs={{0,1},{1,0},{2,3},{3,2},{4,5},{5,4},{6,7},{7,6},{8,9},{9,8},{10,11... | collective-permute-start | bytes 1572872 | tf_op jit(solution)/shard_map/ppermute | solution.py:27
  51.7 8.5 %collective-permute-start.12 = (bf16[8,144,128]{2,1,0:T(8,128)(2,1)}, bf16[8,144,128]{2,1,0:T(8,128)(2,1)}, u32[]{:S(2)}, u32[]{:S(2)}) collective-permute-start(bf16[8,144,128]{2,1,0:T(8,128)(2,1)} %collective-permute-done.10.refs_11_), channel_id=1, source_target_pairs={{0,56},{8,0},{16,8},{24,16},{32,24},{40,32},{48,40},{56,48},{1,57}... | collective-permute-start | bytes 884744 | tf_op jit(solution)/shard_map/ppermute | solution.py:43
  53.0 17.4 %collective-permute-start.18 = (bf16[512,512]{1,0:T(8,128)(2,1)}, bf16[512,512]{1,0:T(8,128)(2,1)S(1)}, u32[]{:S(2)}, u32[]{:S(2)}) collective-permute-start(bf16[512,512]{1,0:T(8,128)(2,1)} %collective-permute-done.17.refs_18_), channel_id=1, source_target_pairs={{0,1},{1,0},{2,3},{3,2},{4,5},{5,4},{6,7},{7,6},{8,9},{9,8},{10,11... | collective-permute-start | bytes 1572872 | tf_op jit(solution)/shard_map/ppermute | solution.py:27
  53.3 14.2 %collective-permute-start.13 = (bf16[8,144,128]{2,1,0:T(8,128)(2,1)S(1)}, bf16[8,144,128]{2,1,0:T(8,128)(2,1)S(1)}, u32[]{:S(2)}, u32[]{:S(2)}) collective-permute-start(bf16[8,144,128]{2,1,0:T(8,128)(2,1)S(1)} %collective-permute-done.7.refs_8_), channel_id=1, source_target_pairs={{0,8},{8,16},{16,24},{24,32},{32,40},{40,48},{48,56},{56,0},{1,9},... | collective-permute-start | bytes 884744 | tf_op jit(solution)/shard_map/ppermute | solution.py:45
  54.1 16.1 %collective-permute-start.11 = (bf16[8,144,128]{2,1,0:T(8,128)(2,1)}, bf16[8,144,128]{2,1,0:T(8,128)(2,1)S(1)}, u32[]{:S(2)}, u32[]{:S(2)}) collective-permute-start(bf16[8,144,128]{2,1,0:T(8,128)(2,1)} %collective-permute-done.9.refs_10_), channel_id=1, source_target_pairs={{0,8},{8,16},{16,24},{24,32},{32,40},{40,48},{48,56},{56,0},{1,9},... | collective-permute-start | bytes 884744 | tf_op jit(solution)/shard_map/ppermute | solution.py:42
  60.3 10.1 %collective-permute-start.14 = (bf16[8,144,128]{2,1,0:T(8,128)(2,1)}, bf16[8,144,128]{2,1,0:T(8,128)(2,1)S(1)}, u32[]{:S(2)}, u32[]{:S(2)}) collective-permute-start(bf16[8,144,128]{2,1,0:T(8,128)(2,1)} %collective-permute-done.12.refs_13_), channel_id=1, source_target_pairs={{0,56},{8,0},{16,8},{24,16},{32,24},{40,32},{48,40},{56,48},{1,57}... | collective-permute-start | bytes 884744 | tf_op jit(solution)/shard_map/ppermute | solution.py:46
  98.6 19.6 %all-to-all-start.1 = ((bf16[16,64,256]{2,1,0:T(8,128)(2,1)}), bf16[16,64,256]{2,1,0:T(8,128)(2,1)}, u32[]{:S(2)}, u32[]{:S(2)}) async-start(bf16[16,64,256]{2,1,0:T(8,128)(2,1)} %logits_slices.1), calls=%async_computation.1 | async-start | bytes 1048576 | tf_op jit(solution)/shard_map/all_to_all | solution.py:315
  (17 other events, 135.6 us)

commit v6 on v5

--- a/solution.py
+++ b/solution.py
@@ -18,46 +18,53 @@
 LIMIT = pltpu.CompilerParams(vmem_limit_bytes=16 * 1024 * 1024)
 
 
-def pass_weight(w):
+def rings(mine, swapped, nz, w, early):
+    right = [(i, (i + 1) % nz) for i in range(nz)]
+    left = [(i, (i - 1) % nz) for i in range(nz)]
+    r = lax.ppermute(mine, "z", right)
+    l = lax.ppermute(mine, "z", left)
+    r, l, swapped, w = lax.optimization_barrier((r, l, swapped, w))
     swap = [(0, 1), (1, 0)]
     across = [(i, 3 - i) for i in range(4)]
     low = lax.ppermute(w, "ylo", swap)
     high = lax.ppermute(w, ("ylo", "yhi"), across)
-    far = lax.ppermute(low, ("ylo", "yhi"), across)
-    return [b for v in (w, far, low, high) for b in (v, lax.ppermute(v, "core", swap))]
-
-
-def rings(mine, swapped, nz):
-    right = [(i, (i + 1) % nz) for i in range(nz)]
-    left = [(i, (i - 1) % nz) for i in range(nz)]
-    r = [lax.ppermute(mine, "z", right), None]
-    l = [lax.ppermute(mine, "z", left), None]
-    r[0], l[0], swapped = lax.optimization_barrier((r[0], l[0], swapped))
-    got = [(0, 0, mine), (1, 0, swapped), (0, 1, r[0]), (0, nz - 1, l[0])]
-    r[1] = l[1] = swapped
-    for k in range(1, nz // 2):
-        for sub in range(2):
-            step = k if sub else k + 1
-            if step < nz // 2:
-                r[sub] = lax.ppermute(r[sub], "z", right)
-                l[sub] = lax.ppermute(l[sub], "z", left)
-                got += [(sub, step, r[sub]), (sub, nz - step, l[sub])]
-    got.append((0, nz // 2, lax.ppermute(r[0], "z", right)))
-    got.append((1, nz // 2, lax.ppermute(l[1], "z", left)))
-    return got
-
-
-def conv_body(nz, plan, place_ref, *refs):
-    count = len(plan)
+    arrays = [mine, swapped, r, l]
+    plan = [(0, None, 0, 0), (1, None, 1, 0), (2, None, 0, 1), (3, None, 0, nz - 1)]
+    r = jnp.stack([r, swapped])
+    l = jnp.stack([l, swapped])
+    for k in range(2, nz // 2):
+        r = lax.ppermute(r, "z", right)
+        l = lax.ppermute(l, "z", left)
+        if k == 2:
+            far = lax.ppermute(lax.optimization_barrier((low, r, l))[0], ("ylo", "yhi"), across)
+        if k == nz // 2 - 1:
+            every = jnp.stack(lax.optimization_barrier((w, far, low, high, r, l, early))[:4])
+            weights = [every, lax.ppermute(every, "core", swap)]
+        for way, v in ((1, r), (-1, l)):
+            plan += [(len(arrays), 0, 0, way * k % nz), (len(arrays), 1, 1, way * (k - 1) % nz)]
+            arrays.append(v)
+    last = nz // 2
+    r = lax.ppermute(r, "z", right)
+    plan += [(len(arrays), 0, 0, last), (len(arrays), 1, 1, last - 1)]
+    arrays.append(r)
+    l = l[1]
+    for k in (last + 1, last):
+        l = lax.ppermute(l, "z", left)
+        plan.append((len(arrays), None, 1, k))
+        arrays.append(l)
+    return arrays, weights, tuple(plan)
+
+
+def conv_body(nz, count, plan, place_ref, *refs):
     blocks = refs[:count]
-    w_refs = refs[count : count + 8]
-    own_ref, other_ref, pa_ref, hot_ref, pooled_ref, mask_ref, acts_ref = refs[count + 8 : count + 15]
-    x_ref, wv_ref, sv_ref, mv_ref, x_sem, w_sem, s_sem, m_sem = refs[count + 15 :]
+    w_refs = refs[count : count + 2]
+    own_ref, first_ref, rest_ref, pa_ref, hot_ref, pooled_ref, mask_ref, acts_ref = refs[count + 2 : count + 10]
+    x_ref, wv_ref, sv_ref, mv_ref, x_sem, w_sem, s_sem, m_sem = refs[count + 10 :]
     imgs, pos, kz = blocks[0].shape
     cut = imgs // 2
     ka = pa_ref.shape[0]
     depth, width = wv_ref.shape[1:]
-    rows_w = w_refs[0].shape[0]
+    rows_w = w_refs[0].shape[1]
     me_z = place_ref[0]
     me_y = place_ref[1]
     me_hi = place_ref[2]
@@ -67,7 +74,8 @@
     def copy_x(part):
         span = pl.ds(part * cut, cut)
         made = []
-        for i, (ref, (sub, shift)) in enumerate(zip(blocks, plan)):
+        for i, (array, place, sub, shift) in enumerate(plan):
+            ref = blocks[array] if place is None else blocks[array].at[place]
             source = lax.rem(me_z + (nz - shift), nz)
             lane = pl.multiple_of((source * 2 + columns[sub]) * kz, kz)
             made.append(
@@ -77,19 +85,30 @@
 
     def copy_w(h):
         made = []
-        for i in range(4):
-            hi = me_hi if i < 2 else 1 - me_hi
-            core = me_core if i % 2 == 0 else 1 - me_core
-            row = pl.multiple_of((hi * 2 + core) * rows_w, rows_w)
-            made.append(pltpu.make_async_copy(w_refs[4 * h + i], wv_ref.at[h, pl.ds(row, rows_w)], w_sem.at[h, i]))
+        for i in range(2):
+            hi = me_hi if i == 0 else 1 - me_hi
+            for k in range(2):
+                core = me_core if k == 0 else 1 - me_core
+                row = pl.multiple_of((hi * 2 + core) * rows_w, rows_w)
+                made.append(
+                    pltpu.make_async_copy(
+                        w_refs[k].at[2 * h + i], wv_ref.at[h, pl.ds(row, rows_w)], w_sem.at[h, 2 * i + k]
+                    )
+                )
         return made
 
     copies = [copy_w(0) + copy_x(0), copy_x(1), copy_w(1)]
+    edge = first_ref.shape[0]
     streams = [
-        pltpu.make_async_copy(own_ref.at[me_y], sv_ref.at[0], s_sem.at[0]),
-        pltpu.make_async_copy(other_ref.at[pl.ds(0, imgs * pos)], sv_ref.at[1], s_sem.at[1]),
+        [pltpu.make_async_copy(own_ref.at[me_y], sv_ref.at[0], s_sem.at[0])],
+        [
+            pltpu.make_async_copy(first_ref, sv_ref.at[1, pl.ds(0, edge)], s_sem.at[1]),
+            pltpu.make_async_copy(
+                rest_ref.at[pl.ds(0, imgs * pos - edge)], sv_ref.at[1, pl.ds(edge, imgs * pos - edge)], s_sem.at[2]
+            ),
+        ],
     ]
-    for c in copies[0] + [streams[0]] + copies[1] + copies[2] + [streams[1]]:
+    for c in copies[0] + streams[0] + copies[1] + copies[2] + streams[1]:
         c.start()
     pooled_ref[:, :, imgs:] = hot_ref[...]
     sends = []
@@ -110,7 +129,8 @@
                 acts_ref[here, :ka] = hi
                 acts_ref[here, ka:] = (acts - hi.astype(jnp.float32)).astype(jnp.bfloat16)
             if part == 0:
-                streams[h].wait()
+                for c in streams[h]:
+                    c.wait()
             y = (y + sv_ref[h, part * cut * pos : (part + 1) * cut * pos].astype(jnp.float32)).reshape(cut, pos, width)
             pooled = (jnp.sum(jnp.maximum(y, 0.0), axis=1) / pos).astype(jnp.bfloat16)
             for f in range(pooled_ref.shape[0]):
@@ -126,15 +146,13 @@
         c.wait()
 
 
-def conv(place, got, weights, stream2, stream_other, proj_act, hot, nz):
-    plan = tuple((sub, shift) for sub, shift, _ in got)
-    blocks = [b for _, _, b in got]
+def conv(place, blocks, plan, weights, stream2, stream_first, stream_rest, proj_act, hot, nz):
     half, pos, kz = blocks[0].shape
     fs, _, _, width = hot.shape
     ka, depth = proj_act.shape
     return pl.pallas_call(
-        functools.partial(conv_body, nz, plan),
-        in_specs=[pl.BlockSpec(memory_space=pltpu.SMEM)] + [HB] * (len(blocks) + 10) + [VM, VM],
+        functools.partial(conv_body, nz, len(blocks), plan),
+        in_specs=[pl.BlockSpec(memory_space=pltpu.SMEM)] + [HB] * (len(blocks) + 5) + [VM, VM],
         out_specs=[VM, HB, VM],
         out_shape=[
             jax.ShapeDtypeStruct((fs, 2, 2 * half, width), jnp.bfloat16),
@@ -146,14 +164,14 @@
             pltpu.VMEM((2, depth, width), jnp.bfloat16),
             pltpu.VMEM((2, half * pos, width), jnp.bfloat16),
             pltpu.VMEM((2, 2, half // 2, pos, width), jnp.bfloat16),
-            pltpu.SemaphoreType.DMA((2, len(blocks))),
+            pltpu.SemaphoreType.DMA((2, len(plan))),
             pltpu.SemaphoreType.DMA((2, 4)),
-            pltpu.SemaphoreType.DMA((2,)),
+            pltpu.SemaphoreType.DMA((3,)),
             pltpu.SemaphoreType.DMA((2, 2)),
         ],
         compiler_params=pltpu.CompilerParams(vmem_limit_bytes=32 * 1024 * 1024),
         name="conv_pool_mask",
-    )(place, *[pltpu.with_memory_space_constraint(b, pltpu.HBM) for b in (*blocks, *weights, stream2, stream_other)], proj_act, hot)
+    )(place, *[pltpu.with_memory_space_constraint(b, pltpu.HBM) for b in (*blocks, *weights, stream2, stream_first, stream_rest)], proj_act, hot)
 
 
 def masked_body(acts_ref, mask_ref, m_ref):
@@ -294,28 +312,28 @@
     swapped = lax.ppermute(theirs, "ylo", swap)
     pe_own = proj_err.T
     sent = lax.dynamic_index_in_dim(stream, 1 - me_y, 0, keepdims=False).reshape(half * pos, width)
-    stream_other = lax.ppermute(jnp.concatenate([sent, pe_own], axis=0), "ylo", swap)
-    weights = pass_weight(conv_weight)
-    got = rings(mine, swapped, nz)
+    cut = (half * pos + pe_own.shape[0]) // 2
+    stream_first = lax.ppermute(sent[:cut], "ylo", swap)
+    stream_rest = lax.ppermute(jnp.concatenate([sent[cut:], pe_own], axis=0), "ylo", swap)
+    blocks, weights, plan = rings(mine, swapped, nz, conv_weight, stream_first)
 
     classes = f * block + jnp.arange(block, dtype=jnp.int32)
     onehot = (labels[:, None] == classes[None, :]).astype(jnp.bfloat16)
     hot = lax.dot_general(onehot, head_weight, NT, preferred_element_type=jnp.float32)
     hot = hot.astype(jnp.bfloat16).reshape(fs, 2, half, width)
 
-    blocks, weights, stream_other, hot = lax.optimization_barrier(([g[2] for g in got], weights, stream_other, hot))
-    got = [g[:2] + (b,) for g, b in zip(got, blocks)]
+    blocks, weights, stream_rest, hot = lax.optimization_barrier((blocks, weights, stream_rest, hot))
     place = jnp.stack([lax.axis_index(a) for a in ("z", "ylo", "yhi", "core")]).astype(jnp.int32)
     both, mask, acts = conv(
-        place, got, weights,
-        stream.reshape(2, half * pos, width), stream_other, proj_act.T, hot, nz,
+        place, blocks, plan, weights,
+        stream.reshape(2, half * pos, width), stream_first, stream_rest, proj_act.T, hot, nz,
     )
 
     both = lax.all_to_all(both.reshape(2 * fs, 2 * half, width), ROWS, 0, 0)
     part = lax.all_to_all(logits_slices(both, head_weight, parts), SPREAD, 0, 0)
     mask, both = lax.optimization_barrier((mask, both))
     m = masked_sums(acts, mask)
-    pe_other = stream_other[half * pos :]
+    pe_other = stream_rest[half * pos - cut :]
     part, m, pe_other = lax.optimization_barrier((part, m, pe_other))
 
     logits = jnp.sum(part.astype(jnp.float32), axis=0)

time: 166 us -> 172 us (1.036)
  waiting for transfers between devices: 42.6 us -> 60.2 us
  starting transfers between devices: 37.8 us -> 28.3 us
  blocking collectives: 52.6 us -> 50.7 us
    ppermute x22 -> x15, waiting for transfers between devices: 29 us -> 46.6 us  [the longest x4 16.3 us: rings(): l = lax.ppermute(l, 'z', left)]
    ppermute x22 -> x15, starting transfers between devices: 31.4 us -> 22.4 us  [the longest x4 8.71 us: rings(): l = lax.ppermute(l, 'z', left)]
  transfers between devices with their start and end apart: 24 -> 17, of which waited for: 12 -> 12; matrix products, arithmetic and copies ran while one was open for 4% -> 4% of each run, Pallas kernels for 0% -> 0%
where the time goes in v6:
time: 172 us
  waiting for transfers between devices  60.2 us (35%)
  blocking collectives  50.7 us (29%)
  starting transfers between devices  28.3 us (16%)
  Pallas kernels  20 us (12%)
  local copies, waits for them, and re-layouts  6.43 us (4%)
  matrix products  3.58 us (2%)
  other arithmetic  2.23 us (1%)
    all_to_all x1, blocking collectives, per_device(): lax.all_to_all(jnp.broadcast_to(expo, (parts,) + expo.shape), SPREAD, 0, 0)  18.5 us
    ppermute x4, waiting for transfers between devices, rings(): l = lax.ppermute(l, 'z', left)  16.3 us
    pallas_call x1, Pallas kernels, conv(): pl.pallas_call(functools.partial(conv_body, nz, len(blocks), plan), in_sp...  13.5 us
    all_to_all x1, blocking collectives, per_device(): grads = lax.all_to_all(grads, SPREAD, 0, 0)  12.9 us
    all_to_all x1, waiting for transfers between devices, per_device(): part = lax.all_to_all(logits_slices(both, head_weight, parts), SPREAD, 0, 0)  12.4 us
    all_to_all x1, blocking collectives, per_device(): both = lax.all_to_all(both.reshape(2 * fs, 2 * half, width), ROWS, 0, 0)  10.1 us
    all_to_all x1, blocking collectives, per_device(): part = lax.all_to_all(part, ROWS, 0, 0).reshape(fs, 2, half, width + 128)  9.23 us
    ppermute x4, starting transfers between devices, rings(): l = lax.ppermute(l, 'z', left)  8.71 us
  transfers between devices with their start and end apart: 17, of which 12 were waited for; matrix products, arithmetic and copies ran while one was open for 4% of the time, Pallas kernels for 0%

profile of v6, /device:TPU:2, one launch (start us, length us, event | category | flops | bytes accessed | tf_op | source)
XLA Modules:
  0.0 171.8 jit_solution(4592705125255259467)
XLA Ops:
  0.0 1.2 dynamic-slice_bitcast_fusion
  1.3 1.7 collective-permute-start.2
  2.9 5.9 %collective-permute-start.1 = (bf16[8,144,128]{2,1,0:T(8,128)(2,1)S(1)}, bf16[8,144,128]{2,1,0:T(8,128)(2,1)S(1)}, u32[]{:S(2)}, u32[]{:S(2)}) collective-permute-start(bf16[8,144,128]{2,1,0:T(8,128)(2,1)S(1)} %get-tuple-element.46.refs_0_), channel_id=1, source_target_pairs={{0,56},{8,0},{16,8},{24,16},{32,24},{40,32},{48,40},{56,48},{1,57}... | collective-permute-start | bytes 884744 | tf_op jit(solution)/shard_map/ppermute | solution.py:25
  8.8 1.3 collective-permute-done.2.refs_1_
  10.1 4.7 %collective-permute-done.1.refs_3_ = bf16[8,144,128]{2,1,0:T(8,128)(2,1)S(1)} collective-permute-done((bf16[8,144,128]{2,1,0:T(8,128)(2,1)S(1)}, bf16[8,144,128]{2,1,0:T(8,128)(2,1)S(1)}, u32[]{:S(2)}, u32[]{:S(2)}) %collective-permute-start.1) | collective-permute-done | bytes 294944 | tf_op jit(solution)/shard_map/ppermute | solution.py:25
  14.8 3.4 %collective-permute-done.refs_2_ = bf16[8,144,128]{2,1,0:T(8,128)(2,1)S(1)} collective-permute-done((bf16[8,144,128]{2,1,0:T(8,128)(2,1)S(1)}, bf16[8,144,128]{2,1,0:T(8,128)(2,1)S(1)}, u32[]{:S(2)}, u32[]{:S(2)}) %collective-permute-start) | collective-permute-done | bytes 294944 | tf_op jit(solution)/shard_map/ppermute | solution.py:24
  18.6 1.7 %collective-permute-start.3 = (bf16[2,8,144,128]{3,2,1,0:T(8,128)(2,1)S(1)}, bf16[2,8,144,128]{3,2,1,0:T(8,128)(2,1)S(1)}, u32[]{:S(2)}, u32[]{:S(2)}) collective-permute-start(bf16[2,8,144,128]{3,2,1,0:T(8,128)(2,1)S(1)} %get-tuple-element.72), channel_id=1, source_target_pairs={{0,8},{8,16},{16,24},{24,32},{32,40},{40,48},{48,56},{56,0},{1,9},... | collective-permute-start | bytes 1769480 | tf_op jit(solution)/shard_map/ppermute | solution.py:36
  21.0 1.7 collective-permute-start.13
  22.7 9.3 %collective-permute-done.4.refs_5_ = bf16[2,8,144,128]{3,2,1,0:T(8,128)(2,1)S(1)} collective-permute-done((bf16[2,8,144,128]{3,2,1,0:T(8,128)(2,1)S(1)}, bf16[2,8,144,128]{3,2,1,0:T(8,128)(2,1)S(1)}, u32[]{:S(2)}, u32[]{:S(2)}) %collective-permute-start.4) | collective-permute-done | bytes 589856 | tf_op jit(solution)/shard_map/ppermute | solution.py:37
  31.9 1.8 %collective-permute-start.6 = (bf16[2,8,144,128]{3,2,1,0:T(8,128)(2,1)S(1)}, bf16[2,8,144,128]{3,2,1,0:T(8,128)(2,1)S(1)}, u32[]{:S(2)}, u32[]{:S(2)}) collective-permute-start(bf16[2,8,144,128]{3,2,1,0:T(8,128)(2,1)S(1)} %collective-permute-done.4.refs_5_), channel_id=1, source_target_pairs={{0,56},{8,0},{16,8},{24,16},{32,24},{40,32},{48,40},{56,48},{1,57}... | collective-permute-start | bytes 1769480 | tf_op jit(solution)/shard_map/ppermute | solution.py:37
  34.0 2.2 %collective-permute-start.12 = (bf16[512,512]{1,0:T(8,128)(2,1)S(1)}, bf16[512,512]{1,0:T(8,128)(2,1)S(1)}, u32[]{:S(2)}, u32[]{:S(2)}) collective-permute-start(bf16[512,512]{1,0:T(8,128)(2,1)S(1)} %copy-done.18), channel_id=1, source_target_pairs={{0,6},{2,4},{4,2},{6,0},{1,7},{3,5},{5,3},{7,1},{8,14},{10,12},{12... | collective-permute-start | bytes 1572872 | tf_op jit(solution)/shard_map/ppermute | solution.py:30
  36.2 1.3 collective-permute-start.11
  37.4 7.9 %collective-permute-done.13.refs_14_ = bf16[608,512]{1,0:T(8,128)(2,1)S(1)} collective-permute-done((bf16[608,512]{1,0:T(8,128)(2,1)S(1)}, bf16[608,512]{1,0:T(8,128)(2,1)S(1)}, u32[]{:S(2)}, u32[]{:S(2)}) %collective-permute-start.13) | collective-permute-done | bytes 622624 | tf_op jit(solution)/shard_map/ppermute | solution.py:316
  45.3 4.7 %collective-permute-done.12 = bf16[512,512]{1,0:T(8,128)(2,1)S(1)} collective-permute-done((bf16[512,512]{1,0:T(8,128)(2,1)S(1)}, bf16[512,512]{1,0:T(8,128)(2,1)S(1)}, u32[]{:S(2)}, u32[]{:S(2)}) %collective-permute-start.12) | collective-permute-done | bytes 524320 | tf_op jit(solution)/shard_map/ppermute | solution.py:30
  50.0 7.5 %collective-permute-done.11 = bf16[512,512]{1,0:T(8,128)(2,1)S(1)} collective-permute-done((bf16[512,512]{1,0:T(8,128)(2,1)S(1)}, bf16[512,512]{1,0:T(8,128)(2,1)S(1)}, u32[]{:S(2)}, u32[]{:S(2)}) %collective-permute-start.11) | collective-permute-done | bytes 524320 | tf_op jit(solution)/shard_map/ppermute | solution.py:39
  59.3 2.9 %collective-permute-start.8 = (bf16[8,144,128]{2,1,0:T(8,128)(2,1)}, bf16[8,144,128]{2,1,0:T(8,128)(2,1)}, u32[]{:S(2)}, u32[]{:S(2)}) collective-permute-start(bf16[8,144,128]{2,1,0:T(8,128)(2,1)} %slice_bitcast_fusion), channel_id=1, source_target_pairs={{0,56},{8,0},{16,8},{24,16},{32,24},{40,32},{48,40},{56,48},{1,57}... | collective-permute-start | bytes 884744 | tf_op jit(solution)/shard_map/ppermute | solution.py:52
  62.5 6.4 %collective-permute-done.8.refs_9_ = bf16[8,144,128]{2,1,0:T(8,128)(2,1)} collective-permute-done((bf16[8,144,128]{2,1,0:T(8,128)(2,1)}, bf16[8,144,128]{2,1,0:T(8,128)(2,1)}, u32[]{:S(2)}, u32[]{:S(2)}) %collective-permute-start.8) | collective-permute-done | bytes 294944 | tf_op jit(solution)/shard_map/ppermute | solution.py:52
  68.9 3.7 %collective-permute-start.9 = (bf16[8,144,128]{2,1,0:T(8,128)(2,1)}, bf16[8,144,128]{2,1,0:T(8,128)(2,1)S(1)}, u32[]{:S(2)}, u32[]{:S(2)}) collective-permute-start(bf16[8,144,128]{2,1,0:T(8,128)(2,1)} %collective-permute-done.8.refs_9_), channel_id=1, source_target_pairs={{0,56},{8,0},{16,8},{24,16},{32,24},{40,32},{48,40},{56,48},{1,57}... | collective-permute-start | bytes 884744 | tf_op jit(solution)/shard_map/ppermute | solution.py:52
  72.6 3.6 %convolution_convert_fusion = bf16[64,512]{1,0:T(8,128)(2,1)S(1)} fusion(bf16[512,4096]{1,0:T(8,128)(2,1)} %head_ref.3, s32[4096]{0:T(1024)S(1)} %iota_add_fusion, s32[64]{0:T(128)S(1)} %copy-done.20), kind=kOutput, calls=%fused_computation.1 | convolution fusion | flops 268730368 | bytes 4276480 | tf_op jit(solution)/shard_map/dot_general | solution.py:322
  76.2 1.8 %collective-permute-done.15.refs_15_ = bf16[608,512]{1,0:T(8,128)(2,1)S(1)} collective-permute-done((bf16[608,512]{1,0:T(8,128)(2,1)S(1)}, bf16[608,512]{1,0:T(8,128)(2,1)S(1)}, u32[]{:S(2)}, u32[]{:S(2)}) %collective-permute-start.15) | collective-permute-done | bytes 622624 | tf_op jit(solution)/shard_map/ppermute | solution.py:317
  79.3 13.5 %conv_pool_mask.1 = (bf16[4,2,16,512]{3,2,1,0:T(8,128)(2,1)S(1)}, bf16[2,8,144,512]{3,2,1,0:T(8,128)(2,1)S(1)}, bf16[1152,64]{1,0:T(8,128)(2,1)S(1)}) custom-call(s32[4]{0:T(128)S(1)} %pad_add_fusion.place_ref, bf16[8,144,128]{2,1,0:T(8,128)(2,1)} %copy-done.10, bf16[8,144,128]{2,1,0:T(8,128)(2,1)} %copy-done.11, bf16[8,144,128]{2,1,0:T(8,128)(2,1)} %copy-done.13, ...), custom_call_target="tpu_custom_call" | custom-call | tf_op jit(solution)/shard_map/conv_pool_mask/pallas_call | solution.py:153
  93.4 10.1 %all_to_all.25.both_ref = bf16[8,16,512]{2,1,0:T(8,128)(2,1)S(1)} all-to-all(bf16[8,16,512]{2,1,0:T(8,128)(2,1)S(1)} %bitcast.41), channel_id=1, replica_groups=mesh['seed'=4,'z'=8,'ylo'=2,'yhi'=2,'core'=2] {'yhi','core','ylo'}, dimensions={0} | all-to-all | bytes 262144 | tf_op jit(solution)/shard_map/all_to_all | solution.py:332
  103.6 1.7 logits_slices.1
  105.2 4.3 %all-to-all-start.1 = ((bf16[16,64,256]{2,1,0:T(8,128)(2,1)}), bf16[16,64,256]{2,1,0:T(8,128)(2,1)}, u32[]{:S(2)}, u32[]{:S(2)}) async-start(bf16[16,64,256]{2,1,0:T(8,128)(2,1)} %logits_slices.1), calls=%async_computation.1 | async-start | bytes 1048576 | tf_op jit(solution)/shard_map/all_to_all | solution.py:333
  109.5 1.5 slice.15.other_ref
  112.7 12.4 %all-to-all-done.1 = bf16[16,64,256]{2,1,0:T(8,128)(2,1)} async-done(((bf16[16,64,256]{2,1,0:T(8,128)(2,1)}), bf16[16,64,256]{2,1,0:T(8,128)(2,1)}, u32[]{:S(2)}, u32[]{:S(2)}) %all-to-all-start.1) | async-done | bytes 524320 | tf_op jit(solution)/shard_map/all_to_all | solution.py:333
  125.1 1.1 convert_reduce_fusion
  126.3 18.5 %all_to_all.26.expo_ref = bf16[16,64,256]{2,1,0:T(8,128)(2,1)S(1)} all-to-all(bf16[16,64,256]{2,1,0:T(8,128)(2,1)S(1)} %broadcast_in_dim.2), channel_id=1, replica_groups=mesh['seed'=4,'z'=8,'ylo'=2,'yhi'=2,'core'=2] {'ylo','z'}, dimensions={0} | all-to-all | bytes 1048576 | tf_op jit(solution)/shard_map/all_to_all | solution.py:341
  144.8 3.1 %back.1 = f32[64,640]{1,0:T(8,128)S(1)} custom-call(bf16[16,64,256]{2,1,0:T(8,128)(2,1)S(1)} %all_to_all.26.expo_ref, bf16[512,4096]{1,0:T(8,128)(2,1)} %head_ref.3), custom_call_target="tpu_custom_call" | custom-call | tf_op jit(solution)/shard_map/back/pallas_call | solution.py:251
  147.9 9.2 %all_to_all.27 = f32[8,8,640]{2,1,0:T(8,128)S(1)} all-to-all(f32[8,8,640]{2,1,0:T(8,128)S(1)} %bitcast.35), channel_id=1, replica_groups=mesh['seed'=4,'z'=8,'ylo'=2,'yhi'=2,'core'=2] {'yhi','core','ylo'}, dimensions={0} | all-to-all | bytes 327680 | tf_op jit(solution)/shard_map/all_to_all | solution.py:344
  157.1 1.0 final.1
  158.3 12.9 %all_to_all.28 = f32[16,8,128]{2,1,0:T(8,128)S(1)} all-to-all(f32[16,8,128]{2,1,0:T(8,128)S(1)} %bitcast.55), channel_id=1, replica_groups=mesh['seed'=4,'z'=8,'ylo'=2,'yhi'=2,'core'=2] {'ylo','z'}, dimensions={0} | all-to-all | bytes 131072 | tf_op jit(solution)/shard_map/all_to_all | solution.py:348
  (71 shorter events, 7.8 us)
Async XLA Ops:
  0.0 20.4 %copy-start.18 = (bf16[512,512]{1,0:T(8,128)(2,1)S(1)}, bf16[512,512]{1,0:T(8,128)(2,1)}, u32[]{:S(2)}) copy-start(bf16[512,512]{1,0:T(8,128)(2,1)} %param.9) | copy-start | bytes 1572868
  0.0 20.8 %copy-start.8 = (bf16[16,144,512]{2,1,0:T(8,128)(2,1)S(1)}, bf16[16,144,512]{2,1,0:T(8,128)(2,1)}, u32[]{:S(2)}) copy-start(bf16[16,144,512]{2,1,0:T(8,128)(2,1)} %param.7) | copy-start | bytes 7077892
  1.2 7.5 %copy-start.10 = (bf16[8,144,128]{2,1,0:T(8,128)(2,1)}, bf16[8,144,128]{2,1,0:T(8,128)(2,1)S(1)}, u32[]{:S(2)}) copy-start(bf16[8,144,128]{2,1,0:T(8,128)(2,1)S(1)} %get-tuple-element.46.refs_0_) | copy-start | bytes 884740
  1.3 8.8 %collective-permute-start.2 = (bf16[8,144,128]{2,1,0:T(8,128)(2,1)S(1)}, bf16[8,144,128]{2,1,0:T(8,128)(2,1)S(1)}, u32[]{:S(2)}, u32[]{:S(2)}) collective-permute-start(bf16[8,144,128]{2,1,0:T(8,128)(2,1)S(1)} %get-tuple-element.69), channel_id=1, source_target_pairs={{0,4},{4,0},{1,5},{5,1},{2,6},{6,2},{3,7},{7,3},{8,12},{12,8},{9,1... | collective-permute-start | bytes 884744 | tf_op jit(solution)/shard_map/ppermute | solution.py:312
  2.9 11.8 %collective-permute-start.1 = (bf16[8,144,128]{2,1,0:T(8,128)(2,1)S(1)}, bf16[8,144,128]{2,1,0:T(8,128)(2,1)S(1)}, u32[]{:S(2)}, u32[]{:S(2)}) collective-permute-start(bf16[8,144,128]{2,1,0:T(8,128)(2,1)S(1)} %get-tuple-element.46.refs_0_), channel_id=1, source_target_pairs={{0,56},{8,0},{16,8},{24,16},{32,24},{40,32},{48,40},{56,48},{1,57}... | collective-permute-start | bytes 884744 | tf_op jit(solution)/shard_map/ppermute | solution.py:25
  8.8 9.4 %collective-permute-start = (bf16[8,144,128]{2,1,0:T(8,128)(2,1)S(1)}, bf16[8,144,128]{2,1,0:T(8,128)(2,1)S(1)}, u32[]{:S(2)}, u32[]{:S(2)}) collective-permute-start(bf16[8,144,128]{2,1,0:T(8,128)(2,1)S(1)} %get-tuple-element.46.refs_0_), channel_id=1, source_target_pairs={{0,8},{8,16},{16,24},{24,32},{32,40},{40,48},{48,56},{56,0},{1,9},... | collective-permute-start | bytes 884744 | tf_op jit(solution)/shard_map/ppermute | solution.py:24
  10.1 10.7 %copy-start.11 = (bf16[8,144,128]{2,1,0:T(8,128)(2,1)}, bf16[8,144,128]{2,1,0:T(8,128)(2,1)S(1)}, u32[]{:S(2)}) copy-start(bf16[8,144,128]{2,1,0:T(8,128)(2,1)S(1)} %collective-permute-done.2.refs_1_) | copy-start | bytes 884740
  14.8 6.1 %copy-start.12 = (bf16[8,144,128]{2,1,0:T(8,128)(2,1)}, bf16[8,144,128]{2,1,0:T(8,128)(2,1)S(1)}, u32[]{:S(2)}) copy-start(bf16[8,144,128]{2,1,0:T(8,128)(2,1)S(1)} %collective-permute-done.1.refs_3_) | copy-start | bytes 884740
  18.3 13.7 %collective-permute-start.4 = (bf16[2,8,144,128]{3,2,1,0:T(8,128)(2,1)S(1)}, bf16[2,8,144,128]{3,2,1,0:T(8,128)(2,1)S(1)}, u32[]{:S(2)}, u32[]{:S(2)}) collective-permute-start(bf16[2,8,144,128]{3,2,1,0:T(8,128)(2,1)S(1)} %get-tuple-element.71), channel_id=1, source_target_pairs={{0,56},{8,0},{16,8},{24,16},{32,24},{40,32},{48,40},{56,48},{1,57}... | collective-permute-start | bytes 1769480 | tf_op jit(solution)/shard_map/ppermute | solution.py:37
  18.6 15.1 %collective-permute-start.3 = (bf16[2,8,144,128]{3,2,1,0:T(8,128)(2,1)S(1)}, bf16[2,8,144,128]{3,2,1,0:T(8,128)(2,1)S(1)}, u32[]{:S(2)}, u32[]{:S(2)}) collective-permute-start(bf16[2,8,144,128]{3,2,1,0:T(8,128)(2,1)S(1)} %get-tuple-element.72), channel_id=1, source_target_pairs={{0,8},{8,16},{16,24},{24,32},{32,40},{40,48},{48,56},{56,0},{1,9},... | collective-permute-start | bytes 1769480 | tf_op jit(solution)/shard_map/ppermute | solution.py:36
  20.4 15.8 %collective-permute-start.10 = (bf16[512,512]{1,0:T(8,128)(2,1)S(1)}, bf16[512,512]{1,0:T(8,128)(2,1)S(1)}, u32[]{:S(2)}, u32[]{:S(2)}) collective-permute-start(bf16[512,512]{1,0:T(8,128)(2,1)S(1)} %copy-done.18), channel_id=1, source_target_pairs={{0,4},{4,0},{1,5},{5,1},{2,6},{6,2},{3,7},{7,3},{8,12},{12,8},{9,1... | collective-permute-start | bytes 1572872 | tf_op jit(solution)/shard_map/ppermute | solution.py:29
  21.0 24.3 %collective-permute-start.13 = (bf16[608,512]{1,0:T(8,128)(2,1)S(1)}, bf16[608,512]{1,0:T(8,128)(2,1)S(1)}, u32[]{:S(2)}, u32[]{:S(2)}) collective-permute-start(bf16[608,512]{1,0:T(8,128)(2,1)S(1)} %slice.17), channel_id=1, source_target_pairs={{0,4},{4,0},{1,5},{5,1},{2,6},{6,2},{3,7},{7,3},{8,12},{12,8},{9,1... | collective-permute-start | bytes 1867784 | tf_op jit(solution)/shard_map/ppermute | solution.py:316
  31.9 25.6 %copy-start.16 = (bf16[2,8,144,128]{3,2,1,0:T(8,128)(2,1)}, bf16[2,8,144,128]{3,2,1,0:T(8,128)(2,1)S(1)}, u32[]{:S(2)}) copy-start(bf16[2,8,144,128]{3,2,1,0:T(8,128)(2,1)S(1)} %collective-permute-done.4.refs_5_) | copy-start | bytes 1769476
  31.9 25.6 %collective-permute-start.6 = (bf16[2,8,144,128]{3,2,1,0:T(8,128)(2,1)S(1)}, bf16[2,8,144,128]{3,2,1,0:T(8,128)(2,1)S(1)}, u32[]{:S(2)}, u32[]{:S(2)}) collective-permute-start(bf16[2,8,144,128]{3,2,1,0:T(8,128)(2,1)S(1)} %collective-permute-done.4.refs_5_), channel_id=1, source_target_pairs={{0,56},{8,0},{16,8},{24,16},{32,24},{40,32},{48,40},{56,48},{1,57}... | collective-permute-start | bytes 1769480 | tf_op jit(solution)/shard_map/ppermute | solution.py:37
  33.7 23.8 %copy-start.17 = (bf16[2,8,144,128]{3,2,1,0:T(8,128)(2,1)}, bf16[2,8,144,128]{3,2,1,0:T(8,128)(2,1)S(1)}, u32[]{:S(2)}) copy-start(bf16[2,8,144,128]{3,2,1,0:T(8,128)(2,1)S(1)} %collective-permute-done.3.refs_4_) | copy-start | bytes 1769476
  33.7 23.8 %collective-permute-start.5 = (bf16[2,8,144,128]{3,2,1,0:T(8,128)(2,1)S(1)}, bf16[2,8,144,128]{3,2,1,0:T(8,128)(2,1)}, u32[]{:S(2)}, u32[]{:S(2)}) collective-permute-start(bf16[2,8,144,128]{3,2,1,0:T(8,128)(2,1)S(1)} %collective-permute-done.3.refs_4_), channel_id=1, source_target_pairs={{0,8},{8,16},{16,24},{24,32},{32,40},{40,48},{48,56},{56,0},{1,9},... | collective-permute-start | bytes 1769480 | tf_op jit(solution)/shard_map/ppermute | solution.py:36
  34.0 16.1 %collective-permute-start.12 = (bf16[512,512]{1,0:T(8,128)(2,1)S(1)}, bf16[512,512]{1,0:T(8,128)(2,1)S(1)}, u32[]{:S(2)}, u32[]{:S(2)}) collective-permute-start(bf16[512,512]{1,0:T(8,128)(2,1)S(1)} %copy-done.18), channel_id=1, source_target_pairs={{0,6},{2,4},{4,2},{6,0},{1,7},{3,5},{5,3},{7,1},{8,14},{10,12},{12... | collective-permute-start | bytes 1572872 | tf_op jit(solution)/shard_map/ppermute | solution.py:30
  36.2 21.4 %collective-permute-start.11 = (bf16[512,512]{1,0:T(8,128)(2,1)S(1)}, bf16[512,512]{1,0:T(8,128)(2,1)S(1)}, u32[]{:S(2)}, u32[]{:S(2)}) collective-permute-start(bf16[512,512]{1,0:T(8,128)(2,1)S(1)} %collective-permute-done.10), channel_id=1, source_target_pairs={{0,6},{2,4},{4,2},{6,0},{1,7},{3,5},{5,3},{7,1},{8,14},{10,12},{12... | collective-permute-start | bytes 1572872 | tf_op jit(solution)/shard_map/ppermute | solution.py:39
  45.3 12.2 %copy-start.15 = (bf16[608,512]{1,0:T(8,128)(2,1)}, bf16[608,512]{1,0:T(8,128)(2,1)S(1)}, u32[]{:S(2)}) copy-start(bf16[608,512]{1,0:T(8,128)(2,1)S(1)} %collective-permute-done.13.refs_14_) | copy-start | bytes 1867780
  57.6 4.6 %copy-start.3 = (bf16[512,64]{0,1:T(8,128)(2,1)S(1)}, bf16[512,64]{0,1:T(8,128)(2,1)}, u32[]{:S(2)}) copy-start(bf16[512,64]{0,1:T(8,128)(2,1)} %param.13) | copy-start | bytes 196612
  57.9 18.3 %copy-start.7 = (bf16[4,512,512]{2,1,0:T(8,128)(2,1)}, bf16[4,512,512]{2,1,0:T(8,128)(2,1)S(1)}, u32[]{:S(2)}) copy-start(bf16[4,512,512]{2,1,0:T(8,128)(2,1)S(1)} %pad_maximum_fusion.refs_11_) | copy-start | bytes 6291460
  57.9 14.7 %copy-start.20 = (s32[64]{0:T(128)S(1)}, s32[64]{0:T(128)}, u32[]{:S(2)}) copy-start(s32[64]{0:T(128)} %param.11) | copy-start | bytes 772
  57.9 21.0 %collective-permute-start.14 = (bf16[4,512,512]{2,1,0:T(8,128)(2,1)S(1)}, bf16[4,512,512]{2,1,0:T(8,128)(2,1)}, u32[]{:S(2)}, u32[]{:S(2)}) collective-permute-start(bf16[4,512,512]{2,1,0:T(8,128)(2,1)S(1)} %pad_maximum_fusion.refs_11_), channel_id=1, source_target_pairs={{0,1},{1,0},{2,3},{3,2},{4,5},{5,4},{6,7},{7,6},{8,9},{9,8},{10,11... | collective-permute-start | bytes 6291464 | tf_op jit(solution)/shard_map/ppermute | solution.py:42
  59.3 9.6 %collective-permute-start.8 = (bf16[8,144,128]{2,1,0:T(8,128)(2,1)}, bf16[8,144,128]{2,1,0:T(8,128)(2,1)}, u32[]{:S(2)}, u32[]{:S(2)}) collective-permute-start(bf16[8,144,128]{2,1,0:T(8,128)(2,1)} %slice_bitcast_fusion), channel_id=1, source_target_pairs={{0,56},{8,0},{16,8},{24,16},{32,24},{40,32},{48,40},{56,48},{1,57}... | collective-permute-start | bytes 884744 | tf_op jit(solution)/shard_map/ppermute | solution.py:52
  62.2 15.8 %collective-permute-start.15 = (bf16[608,512]{1,0:T(8,128)(2,1)S(1)}, bf16[608,512]{1,0:T(8,128)(2,1)S(1)}, u32[]{:S(2)}, u32[]{:S(2)}) collective-permute-start(bf16[608,512]{1,0:T(8,128)(2,1)S(1)} %pad_maximum_fusion.3), channel_id=1, source_target_pairs={{0,4},{4,0},{1,5},{5,1},{2,6},{6,2},{3,7},{7,3},{8,12},{12,8},{9,1... | collective-permute-start | bytes 1867784 | tf_op jit(solution)/shard_map/ppermute | solution.py:317
  62.3 16.6 %collective-permute-start.7 = (bf16[2,8,144,128]{3,2,1,0:T(8,128)(2,1)}, bf16[2,8,144,128]{3,2,1,0:T(8,128)(2,1)}, u32[]{:S(2)}, u32[]{:S(2)}) collective-permute-start(bf16[2,8,144,128]{3,2,1,0:T(8,128)(2,1)} %collective-permute-done.5.refs_6_), channel_id=1, source_target_pairs={{0,8},{8,16},{16,24},{24,32},{32,40},{40,48},{48,56},{56,0},{1,9},... | collective-permute-start | bytes 1769480 | tf_op jit(solution)/shard_map/ppermute | solution.py:47
  62.5 16.8 %copy-start.6 = (bf16[2048,32]{0,1:T(8,128)(2,1)S(1)}, bf16[2048,32]{0,1:T(8,128)(2,1)}, u32[]{:S(2)}) copy-start(bf16[2048,32]{0,1:T(8,128)(2,1)} %param.12) | copy-start | bytes 393220
  68.9 9.6 %collective-permute-start.9 = (bf16[8,144,128]{2,1,0:T(8,128)(2,1)}, bf16[8,144,128]{2,1,0:T(8,128)(2,1)S(1)}, u32[]{:S(2)}, u32[]{:S(2)}) collective-permute-start(bf16[8,144,128]{2,1,0:T(8,128)(2,1)} %collective-permute-done.8.refs_9_), channel_id=1, source_target_pairs={{0,56},{8,0},{16,8},{24,16},{32,24},{40,32},{48,40},{56,48},{1,57}... | collective-permute-start | bytes 884744 | tf_op jit(solution)/shard_map/ppermute | solution.py:52
  79.3 24.3 %copy-start = (bf16[512,4096]{1,0:T(8,128)(2,1)S(1)}, bf16[512,4096]{1,0:T(8,128)(2,1)}, u32[]{:S(2)}) copy-start(bf16[512,4096]{1,0:T(8,128)(2,1)} %head_ref.3) | copy-start | bytes 12582916
  105.2 19.8 %all-to-all-start.1 = ((bf16[16,64,256]{2,1,0:T(8,128)(2,1)}), bf16[16,64,256]{2,1,0:T(8,128)(2,1)}, u32[]{:S(2)}, u32[]{:S(2)}) async-start(bf16[16,64,256]{2,1,0:T(8,128)(2,1)} %logits_slices.1), calls=%async_computation.1 | async-start | bytes 1048576 | tf_op jit(solution)/shard_map/all_to_all | solution.py:333
  144.8 12.3 %copy-start.4 = (bf16[512,64]{0,1:T(8,128)(2,1)S(1)}, bf16[512,64]{0,1:T(8,128)(2,1)}, u32[]{:S(2)}) copy-start(bf16[512,64]{0,1:T(8,128)(2,1)} %param.13) | copy-start | bytes 196612
  144.8 12.3 %copy-start.5 = (bf16[64,512]{1,0:T(8,128)(2,1)S(1)}, bf16[64,512]{1,0:T(8,128)(2,1)}, u32[]{:S(2)}) copy-start(bf16[64,512]{1,0:T(8,128)(2,1)} %slice.15.other_ref) | copy-start | bytes 196612
  (6 other events, 6.8 us)

commit v7 on v6

--- a/solution.py
+++ b/solution.py
@@ -36,9 +36,11 @@
         r = lax.ppermute(r, "z", right)
         l = lax.ppermute(l, "z", left)
         if k == 2:
-            far = lax.ppermute(lax.optimization_barrier((low, r, l))[0], ("ylo", "yhi"), across)
-        if k == nz // 2 - 1:
-            every = jnp.stack(lax.optimization_barrier((w, far, low, high, r, l, early))[:4])
+            r, l, low, high = lax.optimization_barrier((r, l, low, high))
+            far = lax.ppermute(low, ("ylo", "yhi"), across)
+        elif k == nz // 2 - 1:
+            r, l, far, early = lax.optimization_barrier((r, l, far, early))
+            every = jnp.stack([w, far, low, high])
             weights = [every, lax.ppermute(every, "core", swap)]
         for way, v in ((1, r), (-1, l)):
             plan += [(len(arrays), 0, 0, way * k % nz), (len(arrays), 1, 1, way * (k - 1) % nz)]

time: 172 us -> 163 us (0.948)
  waiting for transfers between devices: 60.2 us -> 52.8 us
    ppermute x4, waiting for transfers between devices: 16.3 us -> 7.97 us  [rings(): l = lax.ppermute(l, 'z', left)]
    ppermute x1, waiting for transfers between devices: 0.01 us -> 4.21 us  [rings(): low = lax.ppermute(w, 'ylo', swap)]
    ppermute x1, waiting for transfers between devices: 4.7 us -> 8.37 us  [rings(): high = lax.ppermute(w, ('ylo', 'yhi'), across)]
    ppermute x1, waiting for transfers between devices: 7.5 us -> 3.91 us  [rings(): far = lax.ppermute(low, ('ylo', 'yhi'), across)]
    ppermute x4, starting transfers between devices: 8.71 us -> 6.14 us  [rings(): l = lax.ppermute(l, 'z', left)]
    ppermute x1, waiting for transfers between devices: 7.92 us -> 5.43 us  [per_device(): stream_first = lax.ppermute(sent[:cut], 'ylo', swap)]
where the time goes in v7:
time: 163 us; the launch traced here: 162 us
  waiting for transfers between devices  52.8 us (32%)
  blocking collectives  49.9 us (31%)
  starting transfers between devices  27 us (17%)
  Pallas kernels  20 us (12%)
  local copies, waits for them, and re-layouts  6.61 us (4%)
  matrix products  3.59 us (2%)
  other arithmetic  2.22 us (1%)
    all_to_all x1, blocking collectives, per_device(): lax.all_to_all(jnp.broadcast_to(expo, (parts,) + expo.shape), SPREAD, 0, 0)  18.9 us
    pallas_call x1, Pallas kernels, conv(): pl.pallas_call(functools.partial(conv_body, nz, len(blocks), plan), in_sp...  13.5 us
    all_to_all x1, blocking collectives, per_device(): grads = lax.all_to_all(grads, SPREAD, 0, 0)  12.9 us
    all_to_all x1, waiting for transfers between devices, per_device(): part = lax.all_to_all(logits_slices(both, head_weight, parts), SPREAD, 0, 0)  11.6 us
    all_to_all x1, blocking collectives, per_device(): part = lax.all_to_all(part, ROWS, 0, 0).reshape(fs, 2, half, width + 128)  9.63 us
    all_to_all x1, blocking collectives, per_device(): both = lax.all_to_all(both.reshape(2 * fs, 2 * half, width), ROWS, 0, 0)  8.52 us
    ppermute x1, waiting for transfers between devices, rings(): high = lax.ppermute(w, ('ylo', 'yhi'), across)  8.37 us
    ppermute x4, waiting for transfers between devices, rings(): l = lax.ppermute(l, 'z', left)  7.97 us
  transfers between devices with their start and end apart: 17, of which 12 were waited for; matrix products, arithmetic and copies ran while one was open for 4% of the time, Pallas kernels for 0%

profile of v7, /device:TPU:2, one launch (start us, length us, event | category | flops | bytes accessed | tf_op | source)
XLA Modules:
  0.0 162.3 jit_solution(13176049575394295800)
XLA Ops:
  0.0 1.2 dynamic-slice_bitcast_fusion
  1.3 1.7 %collective-permute-start.2 = (bf16[8,144,128]{2,1,0:T(8,128)(2,1)S(1)}, bf16[8,144,128]{2,1,0:T(8,128)(2,1)S(1)}, u32[]{:S(2)}, u32[]{:S(2)}) collective-permute-start(bf16[8,144,128]{2,1,0:T(8,128)(2,1)S(1)} %get-tuple-element.73), channel_id=1, source_target_pairs={{0,4},{4,0},{1,5},{5,1},{2,6},{6,2},{3,7},{7,3},{8,12},{12,8},{9,1... | collective-permute-start | bytes 884744 | tf_op jit(solution)/shard_map/ppermute | solution.py:314
  2.9 5.9 %collective-permute-start.1 = (bf16[8,144,128]{2,1,0:T(8,128)(2,1)S(1)}, bf16[8,144,128]{2,1,0:T(8,128)(2,1)S(1)}, u32[]{:S(2)}, u32[]{:S(2)}) collective-permute-start(bf16[8,144,128]{2,1,0:T(8,128)(2,1)S(1)} %get-tuple-element.50.refs_0_), channel_id=1, source_target_pairs={{0,56},{8,0},{16,8},{24,16},{32,24},{40,32},{48,40},{56,48},{1,57}... | collective-permute-start | bytes 884744 | tf_op jit(solution)/shard_map/ppermute | solution.py:25
  8.8 1.3 collective-permute-done.2.refs_1_
  10.1 4.7 %collective-permute-done.1.refs_3_ = bf16[8,144,128]{2,1,0:T(8,128)(2,1)S(1)} collective-permute-done((bf16[8,144,128]{2,1,0:T(8,128)(2,1)S(1)}, bf16[8,144,128]{2,1,0:T(8,128)(2,1)S(1)}, u32[]{:S(2)}, u32[]{:S(2)}) %collective-permute-start.1) | collective-permute-done | bytes 294944 | tf_op jit(solution)/shard_map/ppermute | solution.py:25
  14.8 3.4 %collective-permute-done.refs_2_ = bf16[8,144,128]{2,1,0:T(8,128)(2,1)S(1)} collective-permute-done((bf16[8,144,128]{2,1,0:T(8,128)(2,1)S(1)}, bf16[8,144,128]{2,1,0:T(8,128)(2,1)S(1)}, u32[]{:S(2)}, u32[]{:S(2)}) %collective-permute-start) | collective-permute-done | bytes 294944 | tf_op jit(solution)/shard_map/ppermute | solution.py:24
  18.6 1.7 %collective-permute-start.3 = (bf16[2,8,144,128]{3,2,1,0:T(8,128)(2,1)S(1)}, bf16[2,8,144,128]{3,2,1,0:T(8,128)(2,1)S(1)}, u32[]{:S(2)}, u32[]{:S(2)}) collective-permute-start(bf16[2,8,144,128]{3,2,1,0:T(8,128)(2,1)S(1)} %get-tuple-element.76), channel_id=1, source_target_pairs={{0,8},{8,16},{16,24},{24,32},{32,40},{40,48},{48,56},{56,0},{1,9},... | collective-permute-start | bytes 1769480 | tf_op jit(solution)/shard_map/ppermute | solution.py:36
  20.4 2.2 %collective-permute-start.6 = (bf16[512,512]{1,0:T(8,128)(2,1)S(1)}, bf16[512,512]{1,0:T(8,128)(2,1)S(1)}, u32[]{:S(2)}, u32[]{:S(2)}) collective-permute-start(bf16[512,512]{1,0:T(8,128)(2,1)S(1)} %copy-done.18), channel_id=1, source_target_pairs={{0,6},{2,4},{4,2},{6,0},{1,7},{3,5},{5,3},{7,1},{8,14},{10,12},{12... | collective-permute-start | bytes 1572872 | tf_op jit(solution)/shard_map/ppermute | solution.py:30
  23.4 1.4 collective-permute-start.10
  24.8 8.4 %collective-permute-done.6 = bf16[512,512]{1,0:T(8,128)(2,1)S(1)} collective-permute-done((bf16[512,512]{1,0:T(8,128)(2,1)S(1)}, bf16[512,512]{1,0:T(8,128)(2,1)S(1)}, u32[]{:S(2)}, u32[]{:S(2)}) %collective-permute-start.6) | collective-permute-done | bytes 524320 | tf_op jit(solution)/shard_map/ppermute | solution.py:30
  33.2 4.2 %collective-permute-done.5 = bf16[512,512]{1,0:T(8,128)(2,1)S(1)} collective-permute-done((bf16[512,512]{1,0:T(8,128)(2,1)S(1)}, bf16[512,512]{1,0:T(8,128)(2,1)S(1)}, u32[]{:S(2)}, u32[]{:S(2)}) %collective-permute-start.5) | collective-permute-done | bytes 524320 | tf_op jit(solution)/shard_map/ppermute | solution.py:29
  37.5 3.2 %collective-permute-start.8 = (bf16[2,8,144,128]{3,2,1,0:T(8,128)(2,1)S(1)}, bf16[2,8,144,128]{3,2,1,0:T(8,128)(2,1)S(1)}, u32[]{:S(2)}, u32[]{:S(2)}) collective-permute-start(bf16[2,8,144,128]{3,2,1,0:T(8,128)(2,1)S(1)} %collective-permute-done.4.refs_5_), channel_id=1, source_target_pairs={{0,56},{8,0},{16,8},{24,16},{32,24},{40,32},{48,40},{56,48},{1,57}... | collective-permute-start | bytes 1769480 | tf_op jit(solution)/shard_map/ppermute | solution.py:37
  40.8 1.1 collective-permute-start.9
  41.8 5.4 %collective-permute-done.10.refs_14_ = bf16[608,512]{1,0:T(8,128)(2,1)S(1)} collective-permute-done((bf16[608,512]{1,0:T(8,128)(2,1)S(1)}, bf16[608,512]{1,0:T(8,128)(2,1)S(1)}, u32[]{:S(2)}, u32[]{:S(2)}) %collective-permute-start.10) | collective-permute-done | bytes 622624 | tf_op jit(solution)/shard_map/ppermute | solution.py:318
  47.2 3.9 %collective-permute-done.9 = bf16[512,512]{1,0:T(8,128)(2,1)S(1)} collective-permute-done((bf16[512,512]{1,0:T(8,128)(2,1)S(1)}, bf16[512,512]{1,0:T(8,128)(2,1)S(1)}, u32[]{:S(2)}, u32[]{:S(2)}) %collective-permute-start.9) | collective-permute-done | bytes 524320 | tf_op jit(solution)/shard_map/ppermute | solution.py:40
  55.2 6.9 %collective-permute-done.12.refs_9_ = bf16[8,144,128]{2,1,0:T(8,128)(2,1)} collective-permute-done((bf16[8,144,128]{2,1,0:T(8,128)(2,1)}, bf16[8,144,128]{2,1,0:T(8,128)(2,1)}, u32[]{:S(2)}, u32[]{:S(2)}) %collective-permute-start.12) | collective-permute-done | bytes 294944 | tf_op jit(solution)/shard_map/ppermute | solution.py:54
  62.1 1.9 %collective-permute-start.13 = (bf16[8,144,128]{2,1,0:T(8,128)(2,1)}, bf16[8,144,128]{2,1,0:T(8,128)(2,1)S(1)}, u32[]{:S(2)}, u32[]{:S(2)}) collective-permute-start(bf16[8,144,128]{2,1,0:T(8,128)(2,1)} %collective-permute-done.12.refs_9_), channel_id=1, source_target_pairs={{0,56},{8,0},{16,8},{24,16},{32,24},{40,32},{48,40},{56,48},{1,57}... | collective-permute-start | bytes 884744 | tf_op jit(solution)/shard_map/ppermute | solution.py:54
  64.0 3.6 %convolution_convert_fusion = bf16[64,512]{1,0:T(8,128)(2,1)S(1)} fusion(bf16[512,4096]{1,0:T(8,128)(2,1)} %head_ref.3, s32[4096]{0:T(1024)S(1)} %iota_add_fusion, s32[64]{0:T(128)S(1)} %copy-done.20), kind=kOutput, calls=%fused_computation.1 | convolution fusion | flops 268730368 | bytes 4276480 | tf_op jit(solution)/shard_map/dot_general | solution.py:324
  67.6 1.8 %collective-permute-done.15.refs_15_ = bf16[608,512]{1,0:T(8,128)(2,1)S(1)} collective-permute-done((bf16[608,512]{1,0:T(8,128)(2,1)S(1)}, bf16[608,512]{1,0:T(8,128)(2,1)S(1)}, u32[]{:S(2)}, u32[]{:S(2)}) %collective-permute-start.15) | collective-permute-done | bytes 622624 | tf_op jit(solution)/shard_map/ppermute | solution.py:319
  69.4 1.1 collective-permute-done.13.refs_10_
  71.2 13.5 %conv_pool_mask.1 = (bf16[4,2,16,512]{3,2,1,0:T(8,128)(2,1)S(1)}, bf16[2,8,144,512]{3,2,1,0:T(8,128)(2,1)S(1)}, bf16[1152,64]{1,0:T(8,128)(2,1)S(1)}) custom-call(s32[4]{0:T(128)S(1)} %pad_add_fusion.place_ref, bf16[8,144,128]{2,1,0:T(8,128)(2,1)} %copy-done.10, bf16[8,144,128]{2,1,0:T(8,128)(2,1)} %copy-done.11, bf16[8,144,128]{2,1,0:T(8,128)(2,1)} %copy-done.13, ...), custom_call_target="tpu_custom_call" | custom-call | tf_op jit(solution)/shard_map/conv_pool_mask/pallas_call | solution.py:155
  85.4 8.5 %all_to_all.25.both_ref = bf16[8,16,512]{2,1,0:T(8,128)(2,1)S(1)} all-to-all(bf16[8,16,512]{2,1,0:T(8,128)(2,1)S(1)} %bitcast.41), channel_id=1, replica_groups=mesh['seed'=4,'z'=8,'ylo'=2,'yhi'=2,'core'=2] {'yhi','core','ylo'}, dimensions={0} | all-to-all | bytes 262144 | tf_op jit(solution)/shard_map/all_to_all | solution.py:334
  93.9 1.7 %logits_slices.1 = bf16[16,64,256]{2,1,0:T(8,128)(2,1)} custom-call(bf16[8,16,512]{2,1,0:T(8,128)(2,1)S(1)} %all_to_all.25.both_ref, bf16[512,4096]{1,0:T(8,128)(2,1)S(1)} %copy-done), custom_call_target="tpu_custom_call" | custom-call | tf_op jit(solution)/shard_map/logits_slices/pallas_call | solution.py:217
  95.5 4.5 %all-to-all-start.1 = ((bf16[16,64,256]{2,1,0:T(8,128)(2,1)}), bf16[16,64,256]{2,1,0:T(8,128)(2,1)}, u32[]{:S(2)}, u32[]{:S(2)}) async-start(bf16[16,64,256]{2,1,0:T(8,128)(2,1)} %logits_slices.1), calls=%async_computation.1 | async-start | bytes 1048576 | tf_op jit(solution)/shard_map/all_to_all | solution.py:335
  100.1 1.5 slice.15.other_ref
  103.3 11.6 %all-to-all-done.1 = bf16[16,64,256]{2,1,0:T(8,128)(2,1)} async-done(((bf16[16,64,256]{2,1,0:T(8,128)(2,1)}), bf16[16,64,256]{2,1,0:T(8,128)(2,1)}, u32[]{:S(2)}, u32[]{:S(2)}) %all-to-all-start.1) | async-done | bytes 524320 | tf_op jit(solution)/shard_map/all_to_all | solution.py:335
  114.9 1.1 convert_reduce_fusion
  116.1 18.9 %all_to_all.26.expo_ref = bf16[16,64,256]{2,1,0:T(8,128)(2,1)S(1)} all-to-all(bf16[16,64,256]{2,1,0:T(8,128)(2,1)S(1)} %broadcast_in_dim.2), channel_id=1, replica_groups=mesh['seed'=4,'z'=8,'ylo'=2,'yhi'=2,'core'=2] {'ylo','z'}, dimensions={0} | all-to-all | bytes 1048576 | tf_op jit(solution)/shard_map/all_to_all | solution.py:343
  135.0 3.1 %back.1 = f32[64,640]{1,0:T(8,128)S(1)} custom-call(bf16[16,64,256]{2,1,0:T(8,128)(2,1)S(1)} %all_to_all.26.expo_ref, bf16[512,4096]{1,0:T(8,128)(2,1)} %head_ref.3), custom_call_target="tpu_custom_call" | custom-call | tf_op jit(solution)/shard_map/back/pallas_call | solution.py:253
  138.1 9.6 %all_to_all.27 = f32[8,8,640]{2,1,0:T(8,128)S(1)} all-to-all(f32[8,8,640]{2,1,0:T(8,128)S(1)} %bitcast.35), channel_id=1, replica_groups=mesh['seed'=4,'z'=8,'ylo'=2,'yhi'=2,'core'=2] {'yhi','core','ylo'}, dimensions={0} | all-to-all | bytes 327680 | tf_op jit(solution)/shard_map/all_to_all | solution.py:346
  147.7 1.0 final.1
  148.9 12.9 %all_to_all.28 = f32[16,8,128]{2,1,0:T(8,128)S(1)} all-to-all(f32[16,8,128]{2,1,0:T(8,128)S(1)} %bitcast.55), channel_id=1, replica_groups=mesh['seed'=4,'z'=8,'ylo'=2,'yhi'=2,'core'=2] {'ylo','z'}, dimensions={0} | all-to-all | bytes 131072 | tf_op jit(solution)/shard_map/all_to_all | solution.py:350
  (71 shorter events, 9.4 us)
Async XLA Ops:
  0.0 20.4 %copy-start.18 = (bf16[512,512]{1,0:T(8,128)(2,1)S(1)}, bf16[512,512]{1,0:T(8,128)(2,1)}, u32[]{:S(2)}) copy-start(bf16[512,512]{1,0:T(8,128)(2,1)} %param.9) | copy-start | bytes 1572868
  0.0 23.2 %copy-start.8 = (bf16[16,144,512]{2,1,0:T(8,128)(2,1)S(1)}, bf16[16,144,512]{2,1,0:T(8,128)(2,1)}, u32[]{:S(2)}) copy-start(bf16[16,144,512]{2,1,0:T(8,128)(2,1)} %param.7) | copy-start | bytes 7077892
  1.2 7.5 %copy-start.10 = (bf16[8,144,128]{2,1,0:T(8,128)(2,1)}, bf16[8,144,128]{2,1,0:T(8,128)(2,1)S(1)}, u32[]{:S(2)}) copy-start(bf16[8,144,128]{2,1,0:T(8,128)(2,1)S(1)} %get-tuple-element.50.refs_0_) | copy-start | bytes 884740
  1.3 8.8 %collective-permute-start.2 = (bf16[8,144,128]{2,1,0:T(8,128)(2,1)S(1)}, bf16[8,144,128]{2,1,0:T(8,128)(2,1)S(1)}, u32[]{:S(2)}, u32[]{:S(2)}) collective-permute-start(bf16[8,144,128]{2,1,0:T(8,128)(2,1)S(1)} %get-tuple-element.73), channel_id=1, source_target_pairs={{0,4},{4,0},{1,5},{5,1},{2,6},{6,2},{3,7},{7,3},{8,12},{12,8},{9,1... | collective-permute-start | bytes 884744 | tf_op jit(solution)/shard_map/ppermute | solution.py:314
  2.9 11.8 %collective-permute-start.1 = (bf16[8,144,128]{2,1,0:T(8,128)(2,1)S(1)}, bf16[8,144,128]{2,1,0:T(8,128)(2,1)S(1)}, u32[]{:S(2)}, u32[]{:S(2)}) collective-permute-start(bf16[8,144,128]{2,1,0:T(8,128)(2,1)S(1)} %get-tuple-element.50.refs_0_), channel_id=1, source_target_pairs={{0,56},{8,0},{16,8},{24,16},{32,24},{40,32},{48,40},{56,48},{1,57}... | collective-permute-start | bytes 884744 | tf_op jit(solution)/shard_map/ppermute | solution.py:25
  8.8 9.4 %collective-permute-start = (bf16[8,144,128]{2,1,0:T(8,128)(2,1)S(1)}, bf16[8,144,128]{2,1,0:T(8,128)(2,1)S(1)}, u32[]{:S(2)}, u32[]{:S(2)}) collective-permute-start(bf16[8,144,128]{2,1,0:T(8,128)(2,1)S(1)} %get-tuple-element.50.refs_0_), channel_id=1, source_target_pairs={{0,8},{8,16},{16,24},{24,32},{32,40},{40,48},{48,56},{56,0},{1,9},... | collective-permute-start | bytes 884744 | tf_op jit(solution)/shard_map/ppermute | solution.py:24
  10.1 13.2 %copy-start.11 = (bf16[8,144,128]{2,1,0:T(8,128)(2,1)}, bf16[8,144,128]{2,1,0:T(8,128)(2,1)S(1)}, u32[]{:S(2)}) copy-start(bf16[8,144,128]{2,1,0:T(8,128)(2,1)S(1)} %collective-permute-done.2.refs_1_) | copy-start | bytes 884740
  14.8 8.5 %copy-start.12 = (bf16[8,144,128]{2,1,0:T(8,128)(2,1)}, bf16[8,144,128]{2,1,0:T(8,128)(2,1)S(1)}, u32[]{:S(2)}) copy-start(bf16[8,144,128]{2,1,0:T(8,128)(2,1)S(1)} %collective-permute-done.1.refs_3_) | copy-start | bytes 884740
  18.2 5.1 %copy-start.13 = (bf16[8,144,128]{2,1,0:T(8,128)(2,1)}, bf16[8,144,128]{2,1,0:T(8,128)(2,1)S(1)}, u32[]{:S(2)}) copy-start(bf16[8,144,128]{2,1,0:T(8,128)(2,1)S(1)} %collective-permute-done.refs_2_) | copy-start | bytes 884740
  18.3 19.2 %collective-permute-start.4 = (bf16[2,8,144,128]{3,2,1,0:T(8,128)(2,1)S(1)}, bf16[2,8,144,128]{3,2,1,0:T(8,128)(2,1)S(1)}, u32[]{:S(2)}, u32[]{:S(2)}) collective-permute-start(bf16[2,8,144,128]{3,2,1,0:T(8,128)(2,1)S(1)} %get-tuple-element.75), channel_id=1, source_target_pairs={{0,56},{8,0},{16,8},{24,16},{32,24},{40,32},{48,40},{56,48},{1,57}... | collective-permute-start | bytes 1769480 | tf_op jit(solution)/shard_map/ppermute | solution.py:37
  18.6 18.8 %collective-permute-start.3 = (bf16[2,8,144,128]{3,2,1,0:T(8,128)(2,1)S(1)}, bf16[2,8,144,128]{3,2,1,0:T(8,128)(2,1)S(1)}, u32[]{:S(2)}, u32[]{:S(2)}) collective-permute-start(bf16[2,8,144,128]{3,2,1,0:T(8,128)(2,1)S(1)} %get-tuple-element.76), channel_id=1, source_target_pairs={{0,8},{8,16},{16,24},{24,32},{32,40},{40,48},{48,56},{56,0},{1,9},... | collective-permute-start | bytes 1769480 | tf_op jit(solution)/shard_map/ppermute | solution.py:36
  20.4 12.8 %collective-permute-start.6 = (bf16[512,512]{1,0:T(8,128)(2,1)S(1)}, bf16[512,512]{1,0:T(8,128)(2,1)S(1)}, u32[]{:S(2)}, u32[]{:S(2)}) collective-permute-start(bf16[512,512]{1,0:T(8,128)(2,1)S(1)} %copy-done.18), channel_id=1, source_target_pairs={{0,6},{2,4},{4,2},{6,0},{1,7},{3,5},{5,3},{7,1},{8,14},{10,12},{12... | collective-permute-start | bytes 1572872 | tf_op jit(solution)/shard_map/ppermute | solution.py:30
  22.6 14.9 %collective-permute-start.5 = (bf16[512,512]{1,0:T(8,128)(2,1)S(1)}, bf16[512,512]{1,0:T(8,128)(2,1)S(1)}, u32[]{:S(2)}, u32[]{:S(2)}) collective-permute-start(bf16[512,512]{1,0:T(8,128)(2,1)S(1)} %copy-done.18), channel_id=1, source_target_pairs={{0,4},{4,0},{1,5},{5,1},{2,6},{6,2},{3,7},{7,3},{8,12},{12,8},{9,1... | collective-permute-start | bytes 1572872 | tf_op jit(solution)/shard_map/ppermute | solution.py:29
  23.4 23.8 %collective-permute-start.10 = (bf16[608,512]{1,0:T(8,128)(2,1)S(1)}, bf16[608,512]{1,0:T(8,128)(2,1)S(1)}, u32[]{:S(2)}, u32[]{:S(2)}) collective-permute-start(bf16[608,512]{1,0:T(8,128)(2,1)S(1)} %slice.16), channel_id=1, source_target_pairs={{0,4},{4,0},{1,5},{5,1},{2,6},{6,2},{3,7},{7,3},{8,12},{12,8},{9,1... | collective-permute-start | bytes 1867784 | tf_op jit(solution)/shard_map/ppermute | solution.py:318
  37.4 13.7 %copy-start.16 = (bf16[2,8,144,128]{3,2,1,0:T(8,128)(2,1)}, bf16[2,8,144,128]{3,2,1,0:T(8,128)(2,1)S(1)}, u32[]{:S(2)}) copy-start(bf16[2,8,144,128]{3,2,1,0:T(8,128)(2,1)S(1)} %collective-permute-done.4.refs_5_) | copy-start | bytes 1769476
  37.4 13.7 %copy-start.17 = (bf16[2,8,144,128]{3,2,1,0:T(8,128)(2,1)}, bf16[2,8,144,128]{3,2,1,0:T(8,128)(2,1)S(1)}, u32[]{:S(2)}) copy-start(bf16[2,8,144,128]{3,2,1,0:T(8,128)(2,1)S(1)} %collective-permute-done.3.refs_4_) | copy-start | bytes 1769476
  37.4 13.7 %collective-permute-start.7 = (bf16[2,8,144,128]{3,2,1,0:T(8,128)(2,1)S(1)}, bf16[2,8,144,128]{3,2,1,0:T(8,128)(2,1)}, u32[]{:S(2)}, u32[]{:S(2)}) collective-permute-start(bf16[2,8,144,128]{3,2,1,0:T(8,128)(2,1)S(1)} %collective-permute-done.3.refs_4_), channel_id=1, source_target_pairs={{0,8},{8,16},{16,24},{24,32},{32,40},{40,48},{48,56},{56,0},{1,9},... | collective-permute-start | bytes 1769480 | tf_op jit(solution)/shard_map/ppermute | solution.py:36
  37.5 13.6 %collective-permute-start.8 = (bf16[2,8,144,128]{3,2,1,0:T(8,128)(2,1)S(1)}, bf16[2,8,144,128]{3,2,1,0:T(8,128)(2,1)S(1)}, u32[]{:S(2)}, u32[]{:S(2)}) collective-permute-start(bf16[2,8,144,128]{3,2,1,0:T(8,128)(2,1)S(1)} %collective-permute-done.4.refs_5_), channel_id=1, source_target_pairs={{0,56},{8,0},{16,8},{24,16},{32,24},{40,32},{48,40},{56,48},{1,57}... | collective-permute-start | bytes 1769480 | tf_op jit(solution)/shard_map/ppermute | solution.py:37
  40.8 10.4 %collective-permute-start.9 = (bf16[512,512]{1,0:T(8,128)(2,1)S(1)}, bf16[512,512]{1,0:T(8,128)(2,1)S(1)}, u32[]{:S(2)}, u32[]{:S(2)}) collective-permute-start(bf16[512,512]{1,0:T(8,128)(2,1)S(1)} %collective-permute-done.5), channel_id=1, source_target_pairs={{0,6},{2,4},{4,2},{6,0},{1,7},{3,5},{5,3},{7,1},{8,14},{10,12},{12... | collective-permute-start | bytes 1572872 | tf_op jit(solution)/shard_map/ppermute | solution.py:40
  47.2 3.9 %copy-start.15 = (bf16[608,512]{1,0:T(8,128)(2,1)}, bf16[608,512]{1,0:T(8,128)(2,1)S(1)}, u32[]{:S(2)}) copy-start(bf16[608,512]{1,0:T(8,128)(2,1)S(1)} %collective-permute-done.10.refs_14_) | copy-start | bytes 1867780
  51.5 16.1 %copy-start.7 = (bf16[4,512,512]{2,1,0:T(8,128)(2,1)}, bf16[4,512,512]{2,1,0:T(8,128)(2,1)S(1)}, u32[]{:S(2)}) copy-start(bf16[4,512,512]{2,1,0:T(8,128)(2,1)S(1)} %pad_maximum_fusion.refs_11_) | copy-start | bytes 6291460
  51.5 12.5 %copy-start.20 = (s32[64]{0:T(128)S(1)}, s32[64]{0:T(128)}, u32[]{:S(2)}) copy-start(s32[64]{0:T(128)} %param.11) | copy-start | bytes 772
  51.5 19.1 %collective-permute-start.14 = (bf16[4,512,512]{2,1,0:T(8,128)(2,1)S(1)}, bf16[4,512,512]{2,1,0:T(8,128)(2,1)}, u32[]{:S(2)}, u32[]{:S(2)}) collective-permute-start(bf16[4,512,512]{2,1,0:T(8,128)(2,1)S(1)} %pad_maximum_fusion.refs_11_), channel_id=1, source_target_pairs={{0,1},{1,0},{2,3},{3,2},{4,5},{5,4},{6,7},{7,6},{8,9},{9,8},{10,11... | collective-permute-start | bytes 6291464 | tf_op jit(solution)/shard_map/ppermute | solution.py:44
  52.9 9.2 %collective-permute-start.12 = (bf16[8,144,128]{2,1,0:T(8,128)(2,1)}, bf16[8,144,128]{2,1,0:T(8,128)(2,1)}, u32[]{:S(2)}, u32[]{:S(2)}) collective-permute-start(bf16[8,144,128]{2,1,0:T(8,128)(2,1)} %slice_bitcast_fusion), channel_id=1, source_target_pairs={{0,56},{8,0},{16,8},{24,16},{32,24},{40,32},{48,40},{56,48},{1,57}... | collective-permute-start | bytes 884744 | tf_op jit(solution)/shard_map/ppermute | solution.py:54
  53.6 15.8 %collective-permute-start.15 = (bf16[608,512]{1,0:T(8,128)(2,1)S(1)}, bf16[608,512]{1,0:T(8,128)(2,1)S(1)}, u32[]{:S(2)}, u32[]{:S(2)}) collective-permute-start(bf16[608,512]{1,0:T(8,128)(2,1)S(1)} %pad_maximum_fusion.3), channel_id=1, source_target_pairs={{0,4},{4,0},{1,5},{5,1},{2,6},{6,2},{3,7},{7,3},{8,12},{12,8},{9,1... | collective-permute-start | bytes 1867784 | tf_op jit(solution)/shard_map/ppermute | solution.py:319
  54.4 16.2 %collective-permute-start.11 = (bf16[2,8,144,128]{3,2,1,0:T(8,128)(2,1)}, bf16[2,8,144,128]{3,2,1,0:T(8,128)(2,1)}, u32[]{:S(2)}, u32[]{:S(2)}) collective-permute-start(bf16[2,8,144,128]{3,2,1,0:T(8,128)(2,1)} %collective-permute-done.7.refs_6_), channel_id=1, source_target_pairs={{0,8},{8,16},{16,24},{24,32},{32,40},{40,48},{48,56},{56,0},{1,9},... | collective-permute-start | bytes 1769480 | tf_op jit(solution)/shard_map/ppermute | solution.py:49
  55.2 16.0 %copy-start.6 = (bf16[2048,32]{0,1:T(8,128)(2,1)S(1)}, bf16[2048,32]{0,1:T(8,128)(2,1)}, u32[]{:S(2)}) copy-start(bf16[2048,32]{0,1:T(8,128)(2,1)} %param.12) | copy-start | bytes 393220
  62.1 8.3 %collective-permute-start.13 = (bf16[8,144,128]{2,1,0:T(8,128)(2,1)}, bf16[8,144,128]{2,1,0:T(8,128)(2,1)S(1)}, u32[]{:S(2)}, u32[]{:S(2)}) collective-permute-start(bf16[8,144,128]{2,1,0:T(8,128)(2,1)} %collective-permute-done.12.refs_9_), channel_id=1, source_target_pairs={{0,56},{8,0},{16,8},{24,16},{32,24},{40,32},{48,40},{56,48},{1,57}... | collective-permute-start | bytes 884744 | tf_op jit(solution)/shard_map/ppermute | solution.py:54
  71.2 22.7 %copy-start = (bf16[512,4096]{1,0:T(8,128)(2,1)S(1)}, bf16[512,4096]{1,0:T(8,128)(2,1)}, u32[]{:S(2)}) copy-start(bf16[512,4096]{1,0:T(8,128)(2,1)} %head_ref.3) | copy-start | bytes 12582916
  95.5 19.4 %all-to-all-start.1 = ((bf16[16,64,256]{2,1,0:T(8,128)(2,1)}), bf16[16,64,256]{2,1,0:T(8,128)(2,1)}, u32[]{:S(2)}, u32[]{:S(2)}) async-start(bf16[16,64,256]{2,1,0:T(8,128)(2,1)} %logits_slices.1), calls=%async_computation.1 | async-start | bytes 1048576 | tf_op jit(solution)/shard_map/all_to_all | solution.py:335
  135.0 12.7 %copy-start.4 = (bf16[512,64]{0,1:T(8,128)(2,1)S(1)}, bf16[512,64]{0,1:T(8,128)(2,1)}, u32[]{:S(2)}) copy-start(bf16[512,64]{0,1:T(8,128)(2,1)} %param.13) | copy-start | bytes 196612
  135.0 12.7 %copy-start.5 = (bf16[64,512]{1,0:T(8,128)(2,1)S(1)}, bf16[64,512]{1,0:T(8,128)(2,1)}, u32[]{:S(2)}) copy-start(bf16[64,512]{1,0:T(8,128)(2,1)} %slice.15.other_ref) | copy-start | bytes 196612
  (6 other events, 6.9 us)

commit v8 on v7

--- a/solution.py
+++ b/solution.py
@@ -36,7 +36,8 @@
         r = lax.ppermute(r, "z", right)
         l = lax.ppermute(l, "z", left)
         if k == 2:
-            r, l, low, high = lax.optimization_barrier((r, l, low, high))
+            r, l = lax.optimization_barrier((r, l))
+            low, high, *_ = lax.optimization_barrier((low, high, r, l))
             far = lax.ppermute(low, ("ylo", "yhi"), across)
         elif k == nz // 2 - 1:
             r, l, far, early = lax.optimization_barrier((r, l, far, early))
@@ -57,33 +58,34 @@
     return arrays, weights, tuple(plan)
 
 
+def block_copies(nz, blocks, plan, place_ref, x_ref, sem, span):
+    kz = blocks[0].shape[2]
+    made = []
+    for i, (array, at, sub, shift) in enumerate(plan):
+        ref = blocks[array] if at is None else blocks[array].at[at]
+        source = lax.rem(place_ref[0] + (nz - shift), nz)
+        column = place_ref[1] if sub == 0 else 1 - place_ref[1]
+        lane = pl.multiple_of((source * 2 + column) * kz, kz)
+        made.append(pltpu.make_async_copy(ref.at[span], x_ref.at[span, :, pl.ds(lane, kz)], sem.at[i]))
+    return made
+
+
 def conv_body(nz, count, plan, place_ref, *refs):
     blocks = refs[:count]
     w_refs = refs[count : count + 2]
-    own_ref, first_ref, rest_ref, pa_ref, hot_ref, pooled_ref, mask_ref, acts_ref = refs[count + 2 : count + 10]
-    x_ref, wv_ref, sv_ref, mv_ref, x_sem, w_sem, s_sem, m_sem = refs[count + 10 :]
+    own_ref, first_ref, rest_ref, hot_ref, pooled_ref, mask_ref = refs[count + 2 : count + 8]
+    x_ref, wv_ref, sv_ref, mv_ref, x_sem, w_sem, s_sem, m_sem = refs[count + 8 :]
     imgs, pos, kz = blocks[0].shape
     cut = imgs // 2
-    ka = pa_ref.shape[0]
     depth, width = wv_ref.shape[1:]
     rows_w = w_refs[0].shape[1]
-    me_z = place_ref[0]
     me_y = place_ref[1]
     me_hi = place_ref[2]
     me_core = place_ref[3]
     columns = (me_y, 1 - me_y)
 
     def copy_x(part):
-        span = pl.ds(part * cut, cut)
-        made = []
-        for i, (array, place, sub, shift) in enumerate(plan):
-            ref = blocks[array] if place is None else blocks[array].at[place]
-            source = lax.rem(me_z + (nz - shift), nz)
-            lane = pl.multiple_of((source * 2 + columns[sub]) * kz, kz)
-            made.append(
-                pltpu.make_async_copy(ref.at[span], x_ref.at[span, :, pl.ds(lane, kz)], x_sem.at[part, i])
-            )
-        return made
+        return block_copies(nz, blocks, plan, place_ref, x_ref, x_sem.at[part], pl.ds(part * cut, cut))
 
     def copy_w(h):
         made = []
@@ -114,52 +116,51 @@
         c.start()
     pooled_ref[:, :, imgs:] = hot_ref[...]
     sends = []
-    for h in range(2):
-        for part in range(2):
-            if h == 0:
-                for c in copies[part]:
-                    c.wait()
-            elif part == 0:
-                for c in copies[2]:
-                    c.wait()
-            x = x_ref[part * cut : (part + 1) * cut].reshape(cut * pos, depth)
-            y = jnp.dot(x, wv_ref[h], preferred_element_type=jnp.float32)
-            if h == 0:
-                acts = lax.dot_general(x, pa_ref[...], NT, preferred_element_type=jnp.float32)
-                hi = acts.astype(jnp.bfloat16)
-                here = slice(part * cut * pos, (part + 1) * cut * pos)
-                acts_ref[here, :ka] = hi
-                acts_ref[here, ka:] = (acts - hi.astype(jnp.float32)).astype(jnp.bfloat16)
-            if part == 0:
-                for c in streams[h]:
-                    c.wait()
-            y = (y + sv_ref[h, part * cut * pos : (part + 1) * cut * pos].astype(jnp.float32)).reshape(cut, pos, width)
-            pooled = (jnp.sum(jnp.maximum(y, 0.0), axis=1) / pos).astype(jnp.bfloat16)
-            for f in range(pooled_ref.shape[0]):
-                pooled_ref[f, columns[h], part * cut : (part + 1) * cut] = pooled
-            mv_ref[h, part] = jnp.where(y > 0.0, 1.0, 0.0).astype(jnp.bfloat16)
-            sends.append(
-                pltpu.make_async_copy(
-                    mv_ref.at[h, part], mask_ref.at[columns[h], pl.ds(part * cut, cut)], m_sem.at[h, part]
-                )
+
+    def product(h, part):
+        for c in copies[part] if h == 0 else copies[2] if part == 0 else []:
+            c.wait()
+        x = x_ref[part * cut : (part + 1) * cut].reshape(cut * pos, depth)
+        if part == 0:
+            for c in streams[h]:
+                c.wait()
+        return jnp.dot(x, wv_ref[h], preferred_element_type=jnp.float32)
+
+    def finish(h, part, y):
+        y = (y + sv_ref[h, part * cut * pos : (part + 1) * cut * pos].astype(jnp.float32)).reshape(cut, pos, width)
+        pooled = (jnp.sum(jnp.maximum(y, 0.0), axis=1) / pos).astype(jnp.bfloat16)
+        for f in range(pooled_ref.shape[0]):
+            pooled_ref[f, columns[h], part * cut : (part + 1) * cut] = pooled
+        mv_ref[h, part] = jnp.where(y > 0.0, 1.0, 0.0).astype(jnp.bfloat16)
+        sends.append(
+            pltpu.make_async_copy(
+                mv_ref.at[h, part], mask_ref.at[columns[h], pl.ds(part * cut, cut)], m_sem.at[h, part]
             )
-            sends[-1].start()
+        )
+        sends[-1].start()
+
+    tiles = [(h, part) for h in range(2) for part in range(2)]
+    ahead = product(*tiles[0])
+    for i, tile in enumerate(tiles):
+        y = ahead
+        if i + 1 < len(tiles):
+            ahead = product(*tiles[i + 1])
+        finish(*tile, y)
     for c in sends:
         c.wait()
 
 
-def conv(place, blocks, plan, weights, stream2, stream_first, stream_rest, proj_act, hot, nz):
+def conv(place, blocks, plan, weights, stream2, stream_first, stream_rest, hot, nz):
     half, pos, kz = blocks[0].shape
     fs, _, _, width = hot.shape
-    ka, depth = proj_act.shape
+    depth = 2 * nz * kz
     return pl.pallas_call(
         functools.partial(conv_body, nz, len(blocks), plan),
-        in_specs=[pl.BlockSpec(memory_space=pltpu.SMEM)] + [HB] * (len(blocks) + 5) + [VM, VM],
-        out_specs=[VM, HB, VM],
+        in_specs=[pl.BlockSpec(memory_space=pltpu.SMEM)] + [HB] * (len(blocks) + 5) + [VM],
+        out_specs=[VM, HB],
         out_shape=[
             jax.ShapeDtypeStruct((fs, 2, 2 * half, width), jnp.bfloat16),
             jax.ShapeDtypeStruct((2, half, pos, width), jnp.bfloat16),
-            jax.ShapeDtypeStruct((half * pos, 2 * ka), jnp.bfloat16),
         ],
         scratch_shapes=[
             pltpu.VMEM((half, pos, depth), jnp.bfloat16),
@@ -173,34 +174,54 @@
         ],
         compiler_params=pltpu.CompilerParams(vmem_limit_bytes=32 * 1024 * 1024),
         name="conv_pool_mask",
-    )(place, *[pltpu.with_memory_space_constraint(b, pltpu.HBM) for b in (*blocks, *weights, stream2, stream_first, stream_rest)], proj_act, hot)
-
-
-def masked_body(acts_ref, mask_ref, m_ref):
-    _, imgs, pos, _ = mask_ref.shape
-    ka = m_ref.shape[1]
-    for i in range(imgs):
-        both = lax.dot_general(
-            acts_ref[i * pos : (i + 1) * pos, :], mask_ref[0, i], TN, preferred_element_type=jnp.float32
-        )
-        m_ref[i] = both[:ka] + both[ka:]
-
-
-def masked_sums(acts, mask):
+    )(place, *[pltpu.with_memory_space_constraint(b, pltpu.HBM) for b in (*blocks, *weights, stream2, stream_first, stream_rest)], hot)
+
+
+def masked_body(nz, count, plan, place_ref, *refs):
+    blocks = refs[:count]
+    mask_ref, pa_ref, m_ref, x_ref, mv_ref, x_sem, m_sem = refs[count:]
+    imgs, pos, depth = x_ref.shape
+    ka = pa_ref.shape[0]
+    width = mv_ref.shape[3]
+    copies = block_copies(nz, blocks, plan, place_ref, x_ref, x_sem, pl.ds(0, imgs))
+    masks = [pltpu.make_async_copy(mask_ref.at[h], mv_ref.at[h], m_sem.at[h]) for h in range(2)]
+    for c in copies + masks:
+        c.start()
+    for c in copies:
+        c.wait()
+    acts = lax.dot_general(
+        x_ref[...].reshape(imgs * pos, depth), pa_ref[...], NT, preferred_element_type=jnp.float32
+    )
+    hi = acts.astype(jnp.bfloat16)
+    lo = (acts - hi.astype(jnp.float32)).astype(jnp.bfloat16)
+    acts = jnp.concatenate([hi, lo], axis=1)
+    for c in masks:
+        c.wait()
+    for h in range(2):
+        for i in range(imgs):
+            both = lax.dot_general(
+                acts[i * pos : (i + 1) * pos, :], mv_ref[h, i], TN, preferred_element_type=jnp.float32
+            )
+            m_ref[i, :, h * width : (h + 1) * width] = both[:ka] + both[ka:]
+
+
+def masked_sums(place, blocks, plan, mask, proj_act, nz):
     two, imgs, pos, width = mask.shape
-    ka = acts.shape[1] // 2
-    return pl.pallas_call(
-        masked_body,
-        grid=(two,),
-        in_specs=[
-            pl.BlockSpec(acts.shape, lambda h: (0, 0)),
-            pl.BlockSpec((1, imgs, pos, width), lambda h: (h, 0, 0, 0)),
-        ],
-        out_specs=pl.BlockSpec((imgs, ka, width), lambda h: (0, 0, h)),
+    ka, depth = proj_act.shape
+    return pl.pallas_call(
+        functools.partial(masked_body, nz, len(blocks), plan),
+        in_specs=[pl.BlockSpec(memory_space=pltpu.SMEM)] + [HB] * (len(blocks) + 1) + [VM],
+        out_specs=VM,
         out_shape=jax.ShapeDtypeStruct((imgs, ka, two * width), jnp.float32),
-        compiler_params=LIMIT,
+        scratch_shapes=[
+            pltpu.VMEM((imgs, pos, depth), jnp.bfloat16),
+            pltpu.VMEM(mask.shape, jnp.bfloat16),
+            pltpu.SemaphoreType.DMA((len(plan),)),
+            pltpu.SemaphoreType.DMA((2,)),
+        ],
+        compiler_params=pltpu.CompilerParams(vmem_limit_bytes=32 * 1024 * 1024),
         name="masked_sums",
-    )(acts, mask)
+    )(place, *[pltpu.with_memory_space_constraint(b, pltpu.HBM) for b in blocks], mask, proj_act)
 
 
 def logits_body(both_ref, head_ref, out_ref):
@@ -326,15 +347,15 @@
 
     blocks, weights, stream_rest, hot = lax.optimization_barrier((blocks, weights, stream_rest, hot))
     place = jnp.stack([lax.axis_index(a) for a in ("z", "ylo", "yhi", "core")]).astype(jnp.int32)
-    both, mask, acts = conv(
+    both, mask = conv(
         place, blocks, plan, weights,
-        stream.reshape(2, half * pos, width), stream_first, stream_rest, proj_act.T, hot, nz,
+        stream.reshape(2, half * pos, width), stream_first, stream_rest, hot, nz,
     )
 
     both = lax.all_to_all(both.reshape(2 * fs, 2 * half, width), ROWS, 0, 0)
     part = lax.all_to_all(logits_slices(both, head_weight, parts), SPREAD, 0, 0)
     mask, both = lax.optimization_barrier((mask, both))
-    m = masked_sums(acts, mask)
+    m = masked_sums(place, blocks, plan, mask, proj_act.T, nz)
     pe_other = stream_rest[half * pos - cut :]
     part, m, pe_other = lax.optimization_barrier((part, m, pe_other))
 

time: 163 us -> 161 us (0.988)
  waiting for transfers between devices: 52.8 us -> 45.5 us
  Pallas kernels: 20 us -> 23.4 us
    ppermute x1, waiting for transfers between devices: 8.37 us -> 0.01 us  [rings(): high = lax.ppermute(w, ('ylo', 'yhi'), across)]
    ppermute x4, waiting for transfers between devices: 7.97 us -> 13.2 us  [rings(): l = lax.ppermute(l, 'z', left)]
    pallas_call x1, Pallas kernels: 0.76 us -> 5.55 us  [masked_sums(): pl.pallas_call(functools.partial(masked_body, nz, len(blocks), plan), in_...]
    all_to_all x1, waiting for transfers between devices: 11.6 us -> 7.73 us  [per_device(): part = lax.all_to_all(logits_slices(both, head_weight, parts), SPREAD, 0, 0)]
    ppermute x1, waiting for transfers between devices: 4.21 us -> 0.74 us  [rings(): low = lax.ppermute(w, 'ylo', swap)]
    ppermute x1, waiting for transfers between devices: 5.43 us -> 8.37 us  [per_device(): stream_first = lax.ppermute(sent[:cut], 'ylo', swap)]
    ppermute x1, waiting for transfers between devices: 3.91 us -> 1.37 us  [rings(): far = lax.ppermute(low, ('ylo', 'yhi'), across)]
    all_to_all x1, blocking collectives: 8.52 us -> 10.4 us  [per_device(): both = lax.all_to_all(both.reshape(2 * fs, 2 * half, width), ROWS, 0, 0)]
  transfers between devices with their start and end apart: 17 -> 17, of which waited for: 12 -> 12; matrix products, arithmetic and copies ran while one was open for 4% -> 4% of each run, Pallas kernels for 0% -> 3%
where the time goes in v8:
time: 161 us
  blocking collectives  50.9 us (32%)
  waiting for transfers between devices  45.5 us (28%)
  starting transfers between devices  27.9 us (17%)
  Pallas kernels  23.4 us (15%)
  local copies, waits for them, and re-layouts  6.15 us (4%)
  matrix products  3.59 us (2%)
  other arithmetic  3.06 us (2%)
    all_to_all x1, blocking collectives, per_device(): lax.all_to_all(jnp.broadcast_to(expo, (parts,) + expo.shape), SPREAD, 0, 0)  18.8 us
    ppermute x4, waiting for transfers between devices, rings(): l = lax.ppermute(l, 'z', left)  13.2 us
    all_to_all x1, blocking collectives, per_device(): grads = lax.all_to_all(grads, SPREAD, 0, 0)  12.8 us
    pallas_call x1, Pallas kernels, conv(): pl.pallas_call(functools.partial(conv_body, nz, len(blocks), plan), in_sp...  12.1 us
    all_to_all x1, blocking collectives, per_device(): both = lax.all_to_all(both.reshape(2 * fs, 2 * half, width), ROWS, 0, 0)  10.4 us
    all_to_all x1, blocking collectives, per_device(): part = lax.all_to_all(part, ROWS, 0, 0).reshape(fs, 2, half, width + 128)  8.88 us
    ppermute x1, waiting for transfers between devices, per_device(): stream_first = lax.ppermute(sent[:cut], 'ylo', swap)  8.37 us
    ppermute x4, starting transfers between devices, rings(): l = lax.ppermute(l, 'z', left)  7.83 us
  transfers between devices with their start and end apart: 17, of which 12 were waited for; matrix products, arithmetic and copies ran while one was open for 4% of the time, Pallas kernels for 3%

profile of v8, /device:TPU:2, one launch (start us, length us, event | category | flops | bytes accessed | tf_op | source)
XLA Modules:
  0.0 160.7 jit_solution(223925358002600493)
XLA Ops:
  0.0 1.2 dynamic-slice_bitcast_fusion
  1.3 1.7 %collective-permute-start.2 = (bf16[8,144,128]{2,1,0:T(8,128)(2,1)S(1)}, bf16[8,144,128]{2,1,0:T(8,128)(2,1)S(1)}, u32[]{:S(2)}, u32[]{:S(2)}) collective-permute-start(bf16[8,144,128]{2,1,0:T(8,128)(2,1)S(1)} %get-tuple-element.71), channel_id=1, source_target_pairs={{0,4},{4,0},{1,5},{5,1},{2,6},{6,2},{3,7},{7,3},{8,12},{12,8},{9,1... | collective-permute-start | bytes 884744 | tf_op jit(solution)/shard_map/ppermute | solution.py:335
  2.9 5.9 %collective-permute-start.1 = (bf16[8,144,128]{2,1,0:T(8,128)(2,1)S(1)}, bf16[8,144,128]{2,1,0:T(8,128)(2,1)S(1)}, u32[]{:S(2)}, u32[]{:S(2)}) collective-permute-start(bf16[8,144,128]{2,1,0:T(8,128)(2,1)S(1)} %get-tuple-element.49.refs_0_), channel_id=1, source_target_pairs={{0,56},{8,0},{16,8},{24,16},{32,24},{40,32},{48,40},{56,48},{1,57}... | collective-permute-start | bytes 884744 | tf_op jit(solution)/shard_map/ppermute | solution.py:25
  8.8 1.3 collective-permute-done.2.refs_1_
  10.1 4.7 %collective-permute-done.1.refs_3_ = bf16[8,144,128]{2,1,0:T(8,128)(2,1)S(1)} collective-permute-done((bf16[8,144,128]{2,1,0:T(8,128)(2,1)S(1)}, bf16[8,144,128]{2,1,0:T(8,128)(2,1)S(1)}, u32[]{:S(2)}, u32[]{:S(2)}) %collective-permute-start.1) | collective-permute-done | bytes 294944 | tf_op jit(solution)/shard_map/ppermute | solution.py:25
  14.8 3.4 %collective-permute-done.refs_2_ = bf16[8,144,128]{2,1,0:T(8,128)(2,1)S(1)} collective-permute-done((bf16[8,144,128]{2,1,0:T(8,128)(2,1)S(1)}, bf16[8,144,128]{2,1,0:T(8,128)(2,1)S(1)}, u32[]{:S(2)}, u32[]{:S(2)}) %collective-permute-start) | collective-permute-done | bytes 294944 | tf_op jit(solution)/shard_map/ppermute | solution.py:24
  18.6 1.7 %collective-permute-start.3 = (bf16[2,8,144,128]{3,2,1,0:T(8,128)(2,1)S(1)}, bf16[2,8,144,128]{3,2,1,0:T(8,128)(2,1)S(1)}, u32[]{:S(2)}, u32[]{:S(2)}) collective-permute-start(bf16[2,8,144,128]{3,2,1,0:T(8,128)(2,1)S(1)} %get-tuple-element.74), channel_id=1, source_target_pairs={{0,8},{8,16},{16,24},{24,32},{32,40},{40,48},{48,56},{56,0},{1,9},... | collective-permute-start | bytes 1769480 | tf_op jit(solution)/shard_map/ppermute | solution.py:36
  20.4 2.2 %collective-permute-start.8 = (bf16[512,512]{1,0:T(8,128)(2,1)S(1)}, bf16[512,512]{1,0:T(8,128)(2,1)S(1)}, u32[]{:S(2)}, u32[]{:S(2)}) collective-permute-start(bf16[512,512]{1,0:T(8,128)(2,1)S(1)} %copy-done.18), channel_id=1, source_target_pairs={{0,6},{2,4},{4,2},{6,0},{1,7},{3,5},{5,3},{7,1},{8,14},{10,12},{12... | collective-permute-start | bytes 1572872 | tf_op jit(solution)/shard_map/ppermute | solution.py:30
  23.4 1.4 collective-permute-start.10
  24.8 7.1 %collective-permute-done.4.refs_5_ = bf16[2,8,144,128]{3,2,1,0:T(8,128)(2,1)S(1)} collective-permute-done((bf16[2,8,144,128]{3,2,1,0:T(8,128)(2,1)S(1)}, bf16[2,8,144,128]{3,2,1,0:T(8,128)(2,1)S(1)}, u32[]{:S(2)}, u32[]{:S(2)}) %collective-permute-start.4) | collective-permute-done | bytes 589856 | tf_op jit(solution)/shard_map/ppermute | solution.py:37
  31.9 1.5 collective-permute-done.3.refs_4_
  33.7 3.0 %collective-permute-start.6 = (bf16[2,8,144,128]{3,2,1,0:T(8,128)(2,1)S(1)}, bf16[2,8,144,128]{3,2,1,0:T(8,128)(2,1)S(1)}, u32[]{:S(2)}, u32[]{:S(2)}) collective-permute-start(bf16[2,8,144,128]{3,2,1,0:T(8,128)(2,1)S(1)} %collective-permute-done.4.refs_5_), channel_id=1, source_target_pairs={{0,56},{8,0},{16,8},{24,16},{32,24},{40,32},{48,40},{56,48},{1,57}... | collective-permute-start | bytes 1769480 | tf_op jit(solution)/shard_map/ppermute | solution.py:37
  37.4 1.4 collective-permute-start.9
  38.9 8.4 %collective-permute-done.10.refs_14_ = bf16[608,512]{1,0:T(8,128)(2,1)S(1)} collective-permute-done((bf16[608,512]{1,0:T(8,128)(2,1)S(1)}, bf16[608,512]{1,0:T(8,128)(2,1)S(1)}, u32[]{:S(2)}, u32[]{:S(2)}) %collective-permute-start.10) | collective-permute-done | bytes 622624 | tf_op jit(solution)/shard_map/ppermute | solution.py:339
  47.2 1.4 collective-permute-done.9
  50.4 1.6 %collective-permute-start.12 = (bf16[8,144,128]{2,1,0:T(8,128)(2,1)}, bf16[8,144,128]{2,1,0:T(8,128)(2,1)}, u32[]{:S(2)}, u32[]{:S(2)}) collective-permute-start(bf16[8,144,128]{2,1,0:T(8,128)(2,1)} %slice_bitcast_fusion), channel_id=1, source_target_pairs={{0,56},{8,0},{16,8},{24,16},{32,24},{40,32},{48,40},{56,48},{1,57}... | collective-permute-start | bytes 884744 | tf_op jit(solution)/shard_map/ppermute | solution.py:55
  53.5 6.1 %collective-permute-done.12.refs_9_ = bf16[8,144,128]{2,1,0:T(8,128)(2,1)} collective-permute-done((bf16[8,144,128]{2,1,0:T(8,128)(2,1)}, bf16[8,144,128]{2,1,0:T(8,128)(2,1)}, u32[]{:S(2)}, u32[]{:S(2)}) %collective-permute-start.12) | collective-permute-done | bytes 294944 | tf_op jit(solution)/shard_map/ppermute | solution.py:55
  59.6 2.8 %collective-permute-start.13 = (bf16[8,144,128]{2,1,0:T(8,128)(2,1)}, bf16[8,144,128]{2,1,0:T(8,128)(2,1)S(1)}, u32[]{:S(2)}, u32[]{:S(2)}) collective-permute-start(bf16[8,144,128]{2,1,0:T(8,128)(2,1)} %collective-permute-done.12.refs_9_), channel_id=1, source_target_pairs={{0,56},{8,0},{16,8},{24,16},{32,24},{40,32},{48,40},{56,48},{1,57}... | collective-permute-start | bytes 884744 | tf_op jit(solution)/shard_map/ppermute | solution.py:55
  62.5 3.6 %convolution_convert_fusion = bf16[64,512]{1,0:T(8,128)(2,1)S(1)} fusion(bf16[512,4096]{1,0:T(8,128)(2,1)} %head_ref.3, s32[4096]{0:T(1024)S(1)} %iota_add_fusion, s32[64]{0:T(128)S(1)} %copy-done.19), kind=kOutput, calls=%fused_computation.1 | convolution fusion | flops 268730368 | bytes 4276480 | tf_op jit(solution)/shard_map/dot_general | solution.py:345
  66.1 2.8 %collective-permute-done.15.refs_15_ = bf16[608,512]{1,0:T(8,128)(2,1)} collective-permute-done((bf16[608,512]{1,0:T(8,128)(2,1)}, bf16[608,512]{1,0:T(8,128)(2,1)}, u32[]{:S(2)}, u32[]{:S(2)}) %collective-permute-start.15) | collective-permute-done | bytes 622624 | tf_op jit(solution)/shard_map/ppermute | solution.py:340
  70.1 12.1 %conv_pool_mask.1 = (bf16[4,2,16,512]{3,2,1,0:T(8,128)(2,1)S(1)}, bf16[2,8,144,512]{3,2,1,0:T(8,128)(2,1)S(1)}) custom-call(s32[4]{0:T(128)S(1)} %pad_add_fusion.place_ref, bf16[8,144,128]{2,1,0:T(8,128)(2,1)} %copy-done.8, bf16[8,144,128]{2,1,0:T(8,128)(2,1)} %copy-done.9, bf16[8,144,128]{2,1,0:T(8,128)(2,1)} %copy-done.11, ...), custom_call_target="tpu_custom_call" | custom-call | tf_op jit(solution)/shard_map/conv_pool_mask/pallas_call | solution.py:157
  82.2 10.4 %all_to_all.25.both_ref = bf16[8,16,512]{2,1,0:T(8,128)(2,1)S(1)} all-to-all(bf16[8,16,512]{2,1,0:T(8,128)(2,1)S(1)} %bitcast.41), channel_id=1, replica_groups=mesh['seed'=4,'z'=8,'ylo'=2,'yhi'=2,'core'=2] {'yhi','core','ylo'}, dimensions={0} | all-to-all | bytes 262144 | tf_op jit(solution)/shard_map/all_to_all | solution.py:355
  92.6 1.7 %logits_slices.1 = bf16[16,64,256]{2,1,0:T(8,128)(2,1)} custom-call(bf16[8,16,512]{2,1,0:T(8,128)(2,1)S(1)} %all_to_all.25.both_ref, bf16[512,4096]{1,0:T(8,128)(2,1)S(1)} %copy-done), custom_call_target="tpu_custom_call" | custom-call | tf_op jit(solution)/shard_map/logits_slices/pallas_call | solution.py:238
  94.2 4.2 %all-to-all-start.1 = ((bf16[16,64,256]{2,1,0:T(8,128)(2,1)}), bf16[16,64,256]{2,1,0:T(8,128)(2,1)}, u32[]{:S(2)}, u32[]{:S(2)}) async-start(bf16[16,64,256]{2,1,0:T(8,128)(2,1)} %logits_slices.1), calls=%async_computation.1 | async-start | bytes 1048576 | tf_op jit(solution)/shard_map/all_to_all | solution.py:356
  98.5 1.5 slice.15.other_ref
  100.9 5.5 %masked_sums.1.m_ref = f32[8,32,1024]{2,1,0:T(8,128)S(1)} custom-call(s32[4]{0:T(128)S(1)} %pad_add_fusion.place_ref, bf16[8,144,128]{2,1,0:T(8,128)(2,1)} %copy-done.8, bf16[8,144,128]{2,1,0:T(8,128)(2,1)} %copy-done.9, bf16[8,144,128]{2,1,0:T(8,128)(2,1)} %copy-done.11, bf16[8,144,128]{2,1,0:T(8,128)(2,1)} %copy-done.10, ...), custom_call_target="tpu_custom_call" | custom-call | tf_op jit(solution)/shard_map/masked_sums/pallas_call | solution.py:211
  106.4 7.7 %all-to-all-done.1 = bf16[16,64,256]{2,1,0:T(8,128)(2,1)} async-done(((bf16[16,64,256]{2,1,0:T(8,128)(2,1)}), bf16[16,64,256]{2,1,0:T(8,128)(2,1)}, u32[]{:S(2)}, u32[]{:S(2)}) %all-to-all-start.1) | async-done | bytes 524320 | tf_op jit(solution)/shard_map/all_to_all | solution.py:356
  114.1 1.1 convert_reduce_fusion
  115.3 18.8 %all_to_all.26.expo_ref = bf16[16,64,256]{2,1,0:T(8,128)(2,1)S(1)} all-to-all(bf16[16,64,256]{2,1,0:T(8,128)(2,1)S(1)} %broadcast_in_dim.2), channel_id=1, replica_groups=mesh['seed'=4,'z'=8,'ylo'=2,'yhi'=2,'core'=2] {'ylo','z'}, dimensions={0} | all-to-all | bytes 1048576 | tf_op jit(solution)/shard_map/all_to_all | solution.py:364
  134.2 3.1 %back.1 = f32[64,640]{1,0:T(8,128)S(1)} custom-call(bf16[16,64,256]{2,1,0:T(8,128)(2,1)S(1)} %all_to_all.26.expo_ref, bf16[512,4096]{1,0:T(8,128)(2,1)} %head_ref.3), custom_call_target="tpu_custom_call" | custom-call | tf_op jit(solution)/shard_map/back/pallas_call | solution.py:274
  137.3 8.9 %all_to_all.27 = f32[8,8,640]{2,1,0:T(8,128)S(1)} all-to-all(f32[8,8,640]{2,1,0:T(8,128)S(1)} %bitcast.35), channel_id=1, replica_groups=mesh['seed'=4,'z'=8,'ylo'=2,'yhi'=2,'core'=2] {'yhi','core','ylo'}, dimensions={0} | all-to-all | bytes 327680 | tf_op jit(solution)/shard_map/all_to_all | solution.py:367
  147.3 12.8 %all_to_all.28 = f32[16,8,128]{2,1,0:T(8,128)S(1)} all-to-all(f32[16,8,128]{2,1,0:T(8,128)S(1)} %bitcast.55), channel_id=1, replica_groups=mesh['seed'=4,'z'=8,'ylo'=2,'yhi'=2,'core'=2] {'ylo','z'}, dimensions={0} | all-to-all | bytes 131072 | tf_op jit(solution)/shard_map/all_to_all | solution.py:371
  (69 shorter events, 9.4 us)
Async XLA Ops:
  0.0 20.4 %copy-start.18 = (bf16[512,512]{1,0:T(8,128)(2,1)S(1)}, bf16[512,512]{1,0:T(8,128)(2,1)}, u32[]{:S(2)}) copy-start(bf16[512,512]{1,0:T(8,128)(2,1)} %param.9) | copy-start | bytes 1572868
  0.0 23.2 %copy-start.6 = (bf16[16,144,512]{2,1,0:T(8,128)(2,1)S(1)}, bf16[16,144,512]{2,1,0:T(8,128)(2,1)}, u32[]{:S(2)}) copy-start(bf16[16,144,512]{2,1,0:T(8,128)(2,1)} %param.7) | copy-start | bytes 7077892
  1.2 7.5 %copy-start.8 = (bf16[8,144,128]{2,1,0:T(8,128)(2,1)}, bf16[8,144,128]{2,1,0:T(8,128)(2,1)S(1)}, u32[]{:S(2)}) copy-start(bf16[8,144,128]{2,1,0:T(8,128)(2,1)S(1)} %get-tuple-element.49.refs_0_) | copy-start | bytes 884740
  1.3 8.8 %collective-permute-start.2 = (bf16[8,144,128]{2,1,0:T(8,128)(2,1)S(1)}, bf16[8,144,128]{2,1,0:T(8,128)(2,1)S(1)}, u32[]{:S(2)}, u32[]{:S(2)}) collective-permute-start(bf16[8,144,128]{2,1,0:T(8,128)(2,1)S(1)} %get-tuple-element.71), channel_id=1, source_target_pairs={{0,4},{4,0},{1,5},{5,1},{2,6},{6,2},{3,7},{7,3},{8,12},{12,8},{9,1... | collective-permute-start | bytes 884744 | tf_op jit(solution)/shard_map/ppermute | solution.py:335
  2.9 11.8 %collective-permute-start.1 = (bf16[8,144,128]{2,1,0:T(8,128)(2,1)S(1)}, bf16[8,144,128]{2,1,0:T(8,128)(2,1)S(1)}, u32[]{:S(2)}, u32[]{:S(2)}) collective-permute-start(bf16[8,144,128]{2,1,0:T(8,128)(2,1)S(1)} %get-tuple-element.49.refs_0_), channel_id=1, source_target_pairs={{0,56},{8,0},{16,8},{24,16},{32,24},{40,32},{48,40},{56,48},{1,57}... | collective-permute-start | bytes 884744 | tf_op jit(solution)/shard_map/ppermute | solution.py:25
  8.8 9.4 %collective-permute-start = (bf16[8,144,128]{2,1,0:T(8,128)(2,1)S(1)}, bf16[8,144,128]{2,1,0:T(8,128)(2,1)S(1)}, u32[]{:S(2)}, u32[]{:S(2)}) collective-permute-start(bf16[8,144,128]{2,1,0:T(8,128)(2,1)S(1)} %get-tuple-element.49.refs_0_), channel_id=1, source_target_pairs={{0,8},{8,16},{16,24},{24,32},{32,40},{40,48},{48,56},{56,0},{1,9},... | collective-permute-start | bytes 884744 | tf_op jit(solution)/shard_map/ppermute | solution.py:24
  10.1 13.2 %copy-start.9 = (bf16[8,144,128]{2,1,0:T(8,128)(2,1)}, bf16[8,144,128]{2,1,0:T(8,128)(2,1)S(1)}, u32[]{:S(2)}) copy-start(bf16[8,144,128]{2,1,0:T(8,128)(2,1)S(1)} %collective-permute-done.2.refs_1_) | copy-start | bytes 884740
  14.8 8.5 %copy-start.10 = (bf16[8,144,128]{2,1,0:T(8,128)(2,1)}, bf16[8,144,128]{2,1,0:T(8,128)(2,1)S(1)}, u32[]{:S(2)}) copy-start(bf16[8,144,128]{2,1,0:T(8,128)(2,1)S(1)} %collective-permute-done.1.refs_3_) | copy-start | bytes 884740
  18.2 5.1 %copy-start.11 = (bf16[8,144,128]{2,1,0:T(8,128)(2,1)}, bf16[8,144,128]{2,1,0:T(8,128)(2,1)S(1)}, u32[]{:S(2)}) copy-start(bf16[8,144,128]{2,1,0:T(8,128)(2,1)S(1)} %collective-permute-done.refs_2_) | copy-start | bytes 884740
  18.3 13.7 %collective-permute-start.4 = (bf16[2,8,144,128]{3,2,1,0:T(8,128)(2,1)S(1)}, bf16[2,8,144,128]{3,2,1,0:T(8,128)(2,1)S(1)}, u32[]{:S(2)}, u32[]{:S(2)}) collective-permute-start(bf16[2,8,144,128]{3,2,1,0:T(8,128)(2,1)S(1)} %get-tuple-element.73), channel_id=1, source_target_pairs={{0,56},{8,0},{16,8},{24,16},{32,24},{40,32},{48,40},{56,48},{1,57}... | collective-permute-start | bytes 1769480 | tf_op jit(solution)/shard_map/ppermute | solution.py:37
  18.6 14.8 %collective-permute-start.3 = (bf16[2,8,144,128]{3,2,1,0:T(8,128)(2,1)S(1)}, bf16[2,8,144,128]{3,2,1,0:T(8,128)(2,1)S(1)}, u32[]{:S(2)}, u32[]{:S(2)}) collective-permute-start(bf16[2,8,144,128]{3,2,1,0:T(8,128)(2,1)S(1)} %get-tuple-element.74), channel_id=1, source_target_pairs={{0,8},{8,16},{16,24},{24,32},{32,40},{40,48},{48,56},{56,0},{1,9},... | collective-permute-start | bytes 1769480 | tf_op jit(solution)/shard_map/ppermute | solution.py:36
  20.4 16.3 %collective-permute-start.8 = (bf16[512,512]{1,0:T(8,128)(2,1)S(1)}, bf16[512,512]{1,0:T(8,128)(2,1)S(1)}, u32[]{:S(2)}, u32[]{:S(2)}) collective-permute-start(bf16[512,512]{1,0:T(8,128)(2,1)S(1)} %copy-done.18), channel_id=1, source_target_pairs={{0,6},{2,4},{4,2},{6,0},{1,7},{3,5},{5,3},{7,1},{8,14},{10,12},{12... | collective-permute-start | bytes 1572872 | tf_op jit(solution)/shard_map/ppermute | solution.py:30
  22.6 14.9 %collective-permute-start.7 = (bf16[512,512]{1,0:T(8,128)(2,1)S(1)}, bf16[512,512]{1,0:T(8,128)(2,1)S(1)}, u32[]{:S(2)}, u32[]{:S(2)}) collective-permute-start(bf16[512,512]{1,0:T(8,128)(2,1)S(1)} %copy-done.18), channel_id=1, source_target_pairs={{0,4},{4,0},{1,5},{5,1},{2,6},{6,2},{3,7},{7,3},{8,12},{12,8},{9,1... | collective-permute-start | bytes 1572872 | tf_op jit(solution)/shard_map/ppermute | solution.py:29
  23.4 23.8 %collective-permute-start.10 = (bf16[608,512]{1,0:T(8,128)(2,1)S(1)}, bf16[608,512]{1,0:T(8,128)(2,1)S(1)}, u32[]{:S(2)}, u32[]{:S(2)}) collective-permute-start(bf16[608,512]{1,0:T(8,128)(2,1)S(1)} %slice.16), channel_id=1, source_target_pairs={{0,4},{4,0},{1,5},{5,1},{2,6},{6,2},{3,7},{7,3},{8,12},{12,8},{9,1... | collective-permute-start | bytes 1867784 | tf_op jit(solution)/shard_map/ppermute | solution.py:339
  31.9 16.7 %copy-start.12 = (bf16[2,8,144,128]{3,2,1,0:T(8,128)(2,1)}, bf16[2,8,144,128]{3,2,1,0:T(8,128)(2,1)S(1)}, u32[]{:S(2)}) copy-start(bf16[2,8,144,128]{3,2,1,0:T(8,128)(2,1)S(1)} %collective-permute-done.4.refs_5_) | copy-start | bytes 1769476
  33.4 15.2 %copy-start.13 = (bf16[2,8,144,128]{3,2,1,0:T(8,128)(2,1)}, bf16[2,8,144,128]{3,2,1,0:T(8,128)(2,1)S(1)}, u32[]{:S(2)}) copy-start(bf16[2,8,144,128]{3,2,1,0:T(8,128)(2,1)S(1)} %collective-permute-done.3.refs_4_) | copy-start | bytes 1769476
  33.4 15.2 %collective-permute-start.5 = (bf16[2,8,144,128]{3,2,1,0:T(8,128)(2,1)S(1)}, bf16[2,8,144,128]{3,2,1,0:T(8,128)(2,1)S(1)}, u32[]{:S(2)}, u32[]{:S(2)}) collective-permute-start(bf16[2,8,144,128]{3,2,1,0:T(8,128)(2,1)S(1)} %collective-permute-done.3.refs_4_), channel_id=1, source_target_pairs={{0,8},{8,16},{16,24},{24,32},{32,40},{40,48},{48,56},{56,0},{1,9},... | collective-permute-start | bytes 1769480 | tf_op jit(solution)/shard_map/ppermute | solution.py:36
  33.7 14.9 %collective-permute-start.6 = (bf16[2,8,144,128]{3,2,1,0:T(8,128)(2,1)S(1)}, bf16[2,8,144,128]{3,2,1,0:T(8,128)(2,1)S(1)}, u32[]{:S(2)}, u32[]{:S(2)}) collective-permute-start(bf16[2,8,144,128]{3,2,1,0:T(8,128)(2,1)S(1)} %collective-permute-done.4.refs_5_), channel_id=1, source_target_pairs={{0,56},{8,0},{16,8},{24,16},{32,24},{40,32},{48,40},{56,48},{1,57}... | collective-permute-start | bytes 1769480 | tf_op jit(solution)/shard_map/ppermute | solution.py:37
  37.4 11.2 %collective-permute-start.9 = (bf16[512,512]{1,0:T(8,128)(2,1)S(1)}, bf16[512,512]{1,0:T(8,128)(2,1)S(1)}, u32[]{:S(2)}, u32[]{:S(2)}) collective-permute-start(bf16[512,512]{1,0:T(8,128)(2,1)S(1)} %collective-permute-done.7), channel_id=1, source_target_pairs={{0,6},{2,4},{4,2},{6,0},{1,7},{3,5},{5,3},{7,1},{8,14},{10,12},{12... | collective-permute-start | bytes 1572872 | tf_op jit(solution)/shard_map/ppermute | solution.py:41
  48.6 4.8 %copy-start.14 = (bf16[2,8,144,128]{3,2,1,0:T(8,128)(2,1)}, bf16[2,8,144,128]{3,2,1,0:T(8,128)(2,1)S(1)}, u32[]{:S(2)}) copy-start(bf16[2,8,144,128]{3,2,1,0:T(8,128)(2,1)S(1)} %collective-permute-done.5.refs_6_) | copy-start | bytes 1769476
  48.7 3.4 %copy-start.1 = (bf16[512,64]{0,1:T(8,128)(2,1)S(1)}, bf16[512,64]{0,1:T(8,128)(2,1)}, u32[]{:S(2)}) copy-start(bf16[512,64]{0,1:T(8,128)(2,1)} %param.13) | copy-start | bytes 196612
  49.0 17.1 %copy-start.5 = (bf16[4,512,512]{2,1,0:T(8,128)(2,1)}, bf16[4,512,512]{2,1,0:T(8,128)(2,1)S(1)}, u32[]{:S(2)}) copy-start(bf16[4,512,512]{2,1,0:T(8,128)(2,1)S(1)} %pad_maximum_fusion.refs_11_) | copy-start | bytes 6291460
  49.0 13.5 %copy-start.19 = (s32[64]{0:T(128)S(1)}, s32[64]{0:T(128)}, u32[]{:S(2)}) copy-start(s32[64]{0:T(128)} %param.11) | copy-start | bytes 772
  49.0 20.3 %collective-permute-start.14 = (bf16[4,512,512]{2,1,0:T(8,128)(2,1)S(1)}, bf16[4,512,512]{2,1,0:T(8,128)(2,1)}, u32[]{:S(2)}, u32[]{:S(2)}) collective-permute-start(bf16[4,512,512]{2,1,0:T(8,128)(2,1)S(1)} %pad_maximum_fusion.refs_11_), channel_id=1, source_target_pairs={{0,1},{1,0},{2,3},{3,2},{4,5},{5,4},{6,7},{7,6},{8,9},{9,8},{10,11... | collective-permute-start | bytes 6291464 | tf_op jit(solution)/shard_map/ppermute | solution.py:45
  50.4 9.2 %collective-permute-start.12 = (bf16[8,144,128]{2,1,0:T(8,128)(2,1)}, bf16[8,144,128]{2,1,0:T(8,128)(2,1)}, u32[]{:S(2)}, u32[]{:S(2)}) collective-permute-start(bf16[8,144,128]{2,1,0:T(8,128)(2,1)} %slice_bitcast_fusion), channel_id=1, source_target_pairs={{0,56},{8,0},{16,8},{24,16},{32,24},{40,32},{48,40},{56,48},{1,57}... | collective-permute-start | bytes 884744 | tf_op jit(solution)/shard_map/ppermute | solution.py:55
  52.9 15.9 %collective-permute-start.15 = (bf16[608,512]{1,0:T(8,128)(2,1)}, bf16[608,512]{1,0:T(8,128)(2,1)}, u32[]{:S(2)}, u32[]{:S(2)}) collective-permute-start(bf16[608,512]{1,0:T(8,128)(2,1)} %pad_maximum_fusion.3), channel_id=1, source_target_pairs={{0,4},{4,0},{1,5},{5,1},{2,6},{6,2},{3,7},{7,3},{8,12},{12,8},{9,1... | collective-permute-start | bytes 1867784 | tf_op jit(solution)/shard_map/ppermute | solution.py:340
  53.4 15.9 %collective-permute-start.11 = (bf16[2,8,144,128]{3,2,1,0:T(8,128)(2,1)S(1)}, bf16[2,8,144,128]{3,2,1,0:T(8,128)(2,1)S(1)}, u32[]{:S(2)}, u32[]{:S(2)}) collective-permute-start(bf16[2,8,144,128]{3,2,1,0:T(8,128)(2,1)S(1)} %collective-permute-done.5.refs_6_), channel_id=1, source_target_pairs={{0,8},{8,16},{16,24},{24,32},{32,40},{40,48},{48,56},{56,0},{1,9},... | collective-permute-start | bytes 1769480 | tf_op jit(solution)/shard_map/ppermute | solution.py:50
  59.6 9.3 %collective-permute-start.13 = (bf16[8,144,128]{2,1,0:T(8,128)(2,1)}, bf16[8,144,128]{2,1,0:T(8,128)(2,1)S(1)}, u32[]{:S(2)}, u32[]{:S(2)}) collective-permute-start(bf16[8,144,128]{2,1,0:T(8,128)(2,1)} %collective-permute-done.12.refs_9_), channel_id=1, source_target_pairs={{0,56},{8,0},{16,8},{24,16},{32,24},{40,32},{48,40},{56,48},{1,57}... | collective-permute-start | bytes 884744 | tf_op jit(solution)/shard_map/ppermute | solution.py:55
  70.1 22.5 %copy-start = (bf16[512,4096]{1,0:T(8,128)(2,1)S(1)}, bf16[512,4096]{1,0:T(8,128)(2,1)}, u32[]{:S(2)}) copy-start(bf16[512,4096]{1,0:T(8,128)(2,1)} %head_ref.3) | copy-start | bytes 12582916
  94.2 19.9 %all-to-all-start.1 = ((bf16[16,64,256]{2,1,0:T(8,128)(2,1)}), bf16[16,64,256]{2,1,0:T(8,128)(2,1)}, u32[]{:S(2)}, u32[]{:S(2)}) async-start(bf16[16,64,256]{2,1,0:T(8,128)(2,1)} %logits_slices.1), calls=%async_computation.1 | async-start | bytes 1048576 | tf_op jit(solution)/shard_map/all_to_all | solution.py:356
  134.2 12.0 %copy-start.2 = (bf16[512,64]{0,1:T(8,128)(2,1)S(1)}, bf16[512,64]{0,1:T(8,128)(2,1)}, u32[]{:S(2)}) copy-start(bf16[512,64]{0,1:T(8,128)(2,1)} %param.13) | copy-start | bytes 196612
  134.2 12.0 %copy-start.3 = (bf16[64,512]{1,0:T(8,128)(2,1)S(1)}, bf16[64,512]{1,0:T(8,128)(2,1)}, u32[]{:S(2)}) copy-start(bf16[64,512]{1,0:T(8,128)(2,1)} %slice.15.other_ref) | copy-start | bytes 196612
  (5 other events, 5.2 us)

commit v9 on v8

--- a/solution.py
+++ b/solution.py
@@ -18,7 +18,7 @@
 LIMIT = pltpu.CompilerParams(vmem_limit_bytes=16 * 1024 * 1024)
 
 
-def rings(mine, swapped, nz, w, early):
+def rings(mine, swapped, nz, w, early, hot):
     right = [(i, (i + 1) % nz) for i in range(nz)]
     left = [(i, (i - 1) % nz) for i in range(nz)]
     r = lax.ppermute(mine, "z", right)
@@ -40,7 +40,7 @@
             low, high, *_ = lax.optimization_barrier((low, high, r, l))
             far = lax.ppermute(low, ("ylo", "yhi"), across)
         elif k == nz // 2 - 1:
-            r, l, far, early = lax.optimization_barrier((r, l, far, early))
+            r, l, far, early, hot = lax.optimization_barrier((r, l, far, early, hot))
             every = jnp.stack([w, far, low, high])
             weights = [every, lax.ppermute(every, "core", swap)]
         for way, v in ((1, r), (-1, l)):
@@ -55,16 +55,24 @@
         l = lax.ppermute(l, "z", left)
         plan.append((len(arrays), None, 1, k))
         arrays.append(l)
-    return arrays, weights, tuple(plan)
-
-
-def block_copies(nz, blocks, plan, place_ref, x_ref, sem, span):
+    return arrays, weights, hot, tuple(plan)
+
+
+def in_hbm(arrays):
+    return [pltpu.with_memory_space_constraint(a, pltpu.HBM) for a in arrays]
+
+
+def block_copies(nz, blocks, plan, place_ref, x_ref, sem, span, relative):
     kz = blocks[0].shape[2]
     made = []
     for i, (array, at, sub, shift) in enumerate(plan):
         ref = blocks[array] if at is None else blocks[array].at[at]
         source = lax.rem(place_ref[0] + (nz - shift), nz)
         column = place_ref[1] if sub == 0 else 1 - place_ref[1]
+        if relative:
+            hi = source // 4
+            core = lax.rem(source // 2, 2)
+            source = 4 * jnp.abs(hi - place_ref[2]) + 2 * jnp.abs(core - place_ref[3]) + lax.rem(source, 2)
         lane = pl.multiple_of((source * 2 + column) * kz, kz)
         made.append(pltpu.make_async_copy(ref.at[span], x_ref.at[span, :, pl.ds(lane, kz)], sem.at[i]))
     return made
@@ -74,34 +82,18 @@
     blocks = refs[:count]
     w_refs = refs[count : count + 2]
     own_ref, first_ref, rest_ref, hot_ref, pooled_ref, mask_ref = refs[count + 2 : count + 8]
-    x_ref, wv_ref, sv_ref, mv_ref, x_sem, w_sem, s_sem, m_sem = refs[count + 8 :]
+    x_ref, sv_ref, mv_ref, x_sem, s_sem, m_sem = refs[count + 8 :]
     imgs, pos, kz = blocks[0].shape
     cut = imgs // 2
-    depth, width = wv_ref.shape[1:]
-    rows_w = w_refs[0].shape[1]
+    depth = x_ref.shape[2]
+    width = sv_ref.shape[2]
     me_y = place_ref[1]
-    me_hi = place_ref[2]
-    me_core = place_ref[3]
     columns = (me_y, 1 - me_y)
 
     def copy_x(part):
-        return block_copies(nz, blocks, plan, place_ref, x_ref, x_sem.at[part], pl.ds(part * cut, cut))
-
-    def copy_w(h):
-        made = []
-        for i in range(2):
-            hi = me_hi if i == 0 else 1 - me_hi
-            for k in range(2):
-                core = me_core if k == 0 else 1 - me_core
-                row = pl.multiple_of((hi * 2 + core) * rows_w, rows_w)
-                made.append(
-                    pltpu.make_async_copy(
-                        w_refs[k].at[2 * h + i], wv_ref.at[h, pl.ds(row, rows_w)], w_sem.at[h, 2 * i + k]
-                    )
-                )
-        return made
-
-    copies = [copy_w(0) + copy_x(0), copy_x(1), copy_w(1)]
+        return block_copies(nz, blocks, plan, place_ref, x_ref, x_sem.at[part], pl.ds(part * cut, cut), True)
+
+    copies = [copy_x(0), copy_x(1)]
     edge = first_ref.shape[0]
     streams = [
         [pltpu.make_async_copy(own_ref.at[me_y], sv_ref.at[0], s_sem.at[0])],
@@ -112,19 +104,20 @@
             ),
         ],
     ]
-    for c in copies[0] + streams[0] + copies[1] + copies[2] + streams[1]:
+    for c in copies[0] + streams[0] + copies[1] + streams[1]:
         c.start()
     pooled_ref[:, :, imgs:] = hot_ref[...]
     sends = []
 
     def product(h, part):
-        for c in copies[part] if h == 0 else copies[2] if part == 0 else []:
+        for c in copies[part] if h == 0 else []:
             c.wait()
         x = x_ref[part * cut : (part + 1) * cut].reshape(cut * pos, depth)
         if part == 0:
             for c in streams[h]:
                 c.wait()
-        return jnp.dot(x, wv_ref[h], preferred_element_type=jnp.float32)
+        w = jnp.concatenate([w_refs[k][2 * h + i] for i in range(2) for k in range(2)], axis=0)
+        return jnp.dot(x, w, preferred_element_type=jnp.float32)
 
     def finish(h, part, y):
         y = (y + sv_ref[h, part * cut * pos : (part + 1) * cut * pos].astype(jnp.float32)).reshape(cut, pos, width)
@@ -156,7 +149,7 @@
     depth = 2 * nz * kz
     return pl.pallas_call(
         functools.partial(conv_body, nz, len(blocks), plan),
-        in_specs=[pl.BlockSpec(memory_space=pltpu.SMEM)] + [HB] * (len(blocks) + 5) + [VM],
+        in_specs=[pl.BlockSpec(memory_space=pltpu.SMEM)] + [HB] * len(blocks) + [VM, VM] + [HB] * 3 + [VM],
         out_specs=[VM, HB],
         out_shape=[
             jax.ShapeDtypeStruct((fs, 2, 2 * half, width), jnp.bfloat16),
@@ -164,17 +157,15 @@
         ],
         scratch_shapes=[
             pltpu.VMEM((half, pos, depth), jnp.bfloat16),
-            pltpu.VMEM((2, depth, width), jnp.bfloat16),
             pltpu.VMEM((2, half * pos, width), jnp.bfloat16),
             pltpu.VMEM((2, 2, half // 2, pos, width), jnp.bfloat16),
             pltpu.SemaphoreType.DMA((2, len(plan))),
-            pltpu.SemaphoreType.DMA((2, 4)),
             pltpu.SemaphoreType.DMA((3,)),
             pltpu.SemaphoreType.DMA((2, 2)),
         ],
-        compiler_params=pltpu.CompilerParams(vmem_limit_bytes=32 * 1024 * 1024),
+        compiler_params=pltpu.CompilerParams(vmem_limit_bytes=50 * 1024 * 1024),
         name="conv_pool_mask",
-    )(place, *[pltpu.with_memory_space_constraint(b, pltpu.HBM) for b in (*blocks, *weights, stream2, stream_first, stream_rest)], hot)
+    )(place, *in_hbm(blocks), *weights, *in_hbm((stream2, stream_first, stream_rest)), hot)
 
 
 def masked_body(nz, count, plan, place_ref, *refs):
@@ -183,7 +174,7 @@
     imgs, pos, depth = x_ref.shape
     ka = pa_ref.shape[0]
     width = mv_ref.shape[3]
-    copies = block_copies(nz, blocks, plan, place_ref, x_ref, x_sem, pl.ds(0, imgs))
+    copies = block_copies(nz, blocks, plan, place_ref, x_ref, x_sem, pl.ds(0, imgs), False)
     masks = [pltpu.make_async_copy(mask_ref.at[h], mv_ref.at[h], m_sem.at[h]) for h in range(2)]
     for c in copies + masks:
         c.start()
@@ -221,7 +212,7 @@
         ],
         compiler_params=pltpu.CompilerParams(vmem_limit_bytes=32 * 1024 * 1024),
         name="masked_sums",
-    )(place, *[pltpu.with_memory_space_constraint(b, pltpu.HBM) for b in blocks], mask, proj_act)
+    )(place, *in_hbm(blocks), mask, proj_act)
 
 
 def logits_body(both_ref, head_ref, out_ref):
@@ -338,12 +329,12 @@
     cut = (half * pos + pe_own.shape[0]) // 2
     stream_first = lax.ppermute(sent[:cut], "ylo", swap)
     stream_rest = lax.ppermute(jnp.concatenate([sent[cut:], pe_own], axis=0), "ylo", swap)
-    blocks, weights, plan = rings(mine, swapped, nz, conv_weight, stream_first)
-
     classes = f * block + jnp.arange(block, dtype=jnp.int32)
     onehot = (labels[:, None] == classes[None, :]).astype(jnp.bfloat16)
     hot = lax.dot_general(onehot, head_weight, NT, preferred_element_type=jnp.float32)
     hot = hot.astype(jnp.bfloat16).reshape(fs, 2, half, width)
+    blocks, weights, hot, plan = rings(mine, swapped, nz, conv_weight, stream_first, hot)
+
 
     blocks, weights, stream_rest, hot = lax.optimization_barrier((blocks, weights, stream_rest, hot))
     place = jnp.stack([lax.axis_index(a) for a in ("z", "ylo", "yhi", "core")]).astype(jnp.int32)

time: 161 us -> 164 us (1.019)
    ppermute x1, waiting for transfers between devices: 8.37 us -> 4.88 us  [per_device(): stream_first = lax.ppermute(sent[:cut], 'ylo', swap)]
    ppermute x4, waiting for transfers between devices: 13.2 us -> 16.1 us  [rings(): l = lax.ppermute(l, 'z', left)]
  transfers between devices with their start and end apart: 17 -> 17, of which waited for: 12 -> 13; matrix products, arithmetic and copies ran while one was open for 4% -> 4% of each run, Pallas kernels for 3% -> 3%
where the time goes in v9:
time: 164 us
  blocking collectives  51.8 us (32%)
  waiting for transfers between devices  45.9 us (28%)
  starting transfers between devices  28.3 us (17%)
  Pallas kernels  23.4 us (14%)
  local copies, waits for them, and re-layouts  5.76 us (4%)
  other arithmetic  4.59 us (3%)
  matrix products  3.59 us (2%)
    all_to_all x1, blocking collectives, per_device(): lax.all_to_all(jnp.broadcast_to(expo, (parts,) + expo.shape), SPREAD, 0, 0)  18.9 us
    ppermute x4, waiting for transfers between devices, rings(): l = lax.ppermute(l, 'z', left)  16.1 us
    all_to_all x1, blocking collectives, per_device(): grads = lax.all_to_all(grads, SPREAD, 0, 0)  12.9 us
    pallas_call x1, Pallas kernels, conv(): pl.pallas_call(functools.partial(conv_body, nz, len(blocks), plan), in_sp...  12.1 us
    all_to_all x1, blocking collectives, per_device(): both = lax.all_to_all(both.reshape(2 * fs, 2 * half, width), ROWS, 0, 0)  10.4 us
    all_to_all x1, blocking collectives, per_device(): part = lax.all_to_all(part, ROWS, 0, 0).reshape(fs, 2, half, width + 128)  9.63 us
    ppermute x4, starting transfers between devices, rings(): l = lax.ppermute(l, 'z', left)  8.35 us
    all_to_all x1, waiting for transfers between devices, per_device(): part = lax.all_to_all(logits_slices(both, head_weight, parts), SPREAD, 0, 0)  6.87 us
  transfers between devices with their start and end apart: 17, of which 13 were waited for; matrix products, arithmetic and copies ran while one was open for 4% of the time, Pallas kernels for 3%

profile of v9, /device:TPU:2, one launch (start us, length us, event | category | flops | bytes accessed | tf_op | source)
XLA Modules:
  0.0 163.5 jit_solution(8872862219830448036)
XLA Ops:
  1.3 1.7 %collective-permute-start.2 = (bf16[8,144,128]{2,1,0:T(8,128)(2,1)S(1)}, bf16[8,144,128]{2,1,0:T(8,128)(2,1)S(1)}, u32[]{:S(2)}, u32[]{:S(2)}) collective-permute-start(bf16[8,144,128]{2,1,0:T(8,128)(2,1)S(1)} %get-tuple-element.73), channel_id=1, source_target_pairs={{0,4},{4,0},{1,5},{5,1},{2,6},{6,2},{3,7},{7,3},{8,12},{12,8},{9,1... | collective-permute-start | bytes 884744 | tf_op jit(solution)/shard_map/ppermute | solution.py:326
  2.9 5.9 %collective-permute-start.1 = (bf16[8,144,128]{2,1,0:T(8,128)(2,1)S(1)}, bf16[8,144,128]{2,1,0:T(8,128)(2,1)S(1)}, u32[]{:S(2)}, u32[]{:S(2)}) collective-permute-start(bf16[8,144,128]{2,1,0:T(8,128)(2,1)S(1)} %get-tuple-element.51.refs_0_), channel_id=1, source_target_pairs={{0,56},{8,0},{16,8},{24,16},{32,24},{40,32},{48,40},{56,48},{1,57}... | collective-permute-start | bytes 884744 | tf_op jit(solution)/shard_map/ppermute | solution.py:25
  8.8 1.3 collective-permute-done.2.refs_1_
  10.1 4.7 %collective-permute-done.1.refs_3_ = bf16[8,144,128]{2,1,0:T(8,128)(2,1)S(1)} collective-permute-done((bf16[8,144,128]{2,1,0:T(8,128)(2,1)S(1)}, bf16[8,144,128]{2,1,0:T(8,128)(2,1)S(1)}, u32[]{:S(2)}, u32[]{:S(2)}) %collective-permute-start.1) | collective-permute-done | bytes 294944 | tf_op jit(solution)/shard_map/ppermute | solution.py:25
  14.8 3.4 %collective-permute-done.refs_2_ = bf16[8,144,128]{2,1,0:T(8,128)(2,1)S(1)} collective-permute-done((bf16[8,144,128]{2,1,0:T(8,128)(2,1)S(1)}, bf16[8,144,128]{2,1,0:T(8,128)(2,1)S(1)}, u32[]{:S(2)}, u32[]{:S(2)}) %collective-permute-start) | collective-permute-done | bytes 294944 | tf_op jit(solution)/shard_map/ppermute | solution.py:24
  18.6 1.7 %collective-permute-start.3 = (bf16[2,8,144,128]{3,2,1,0:T(8,128)(2,1)S(1)}, bf16[2,8,144,128]{3,2,1,0:T(8,128)(2,1)}, u32[]{:S(2)}, u32[]{:S(2)}) collective-permute-start(bf16[2,8,144,128]{3,2,1,0:T(8,128)(2,1)S(1)} %get-tuple-element.76), channel_id=1, source_target_pairs={{0,8},{8,16},{16,24},{24,32},{32,40},{40,48},{48,56},{56,0},{1,9},... | collective-permute-start | bytes 1769480 | tf_op jit(solution)/shard_map/ppermute | solution.py:36
  20.4 2.2 %collective-permute-start.8 = (bf16[512,512]{1,0:T(8,128)(2,1)}, bf16[512,512]{1,0:T(8,128)(2,1)}, u32[]{:S(2)}, u32[]{:S(2)}) collective-permute-start(bf16[512,512]{1,0:T(8,128)(2,1)} %param.9), channel_id=1, source_target_pairs={{0,6},{2,4},{4,2},{6,0},{1,7},{3,5},{5,3},{7,1},{8,14},{10,12},{12... | collective-permute-start | bytes 1572872 | tf_op jit(solution)/shard_map/ppermute | solution.py:30
  23.4 1.4 collective-permute-start.10
  24.8 7.2 %collective-permute-done.4.refs_5_ = bf16[2,8,144,128]{3,2,1,0:T(8,128)(2,1)} collective-permute-done((bf16[2,8,144,128]{3,2,1,0:T(8,128)(2,1)S(1)}, bf16[2,8,144,128]{3,2,1,0:T(8,128)(2,1)}, u32[]{:S(2)}, u32[]{:S(2)}) %collective-permute-start.4) | collective-permute-done | bytes 589856 | tf_op jit(solution)/shard_map/ppermute | solution.py:37
  32.1 1.5 collective-permute-done.3.refs_4_
  33.8 3.0 %collective-permute-start.6 = (bf16[2,8,144,128]{3,2,1,0:T(8,128)(2,1)}, bf16[2,8,144,128]{3,2,1,0:T(8,128)(2,1)S(1)}, u32[]{:S(2)}, u32[]{:S(2)}) collective-permute-start(bf16[2,8,144,128]{3,2,1,0:T(8,128)(2,1)} %collective-permute-done.4.refs_5_), channel_id=1, source_target_pairs={{0,56},{8,0},{16,8},{24,16},{32,24},{40,32},{48,40},{56,48},{1,57}... | collective-permute-start | bytes 1769480 | tf_op jit(solution)/shard_map/ppermute | solution.py:37
  37.7 1.2 collective-permute-start.9
  39.0 3.6 %convolution_convert_fusion = bf16[64,512]{1,0:T(8,128)(2,1)S(1)} fusion(bf16[512,4096]{1,0:T(8,128)(2,1)} %head_ref.3, s32[4096]{0:T(1024)S(1)} %iota_add_fusion, s32[64]{0:T(128)S(1)} %copy-done.17), kind=kOutput, calls=%fused_computation.1 | convolution fusion | flops 268730368 | bytes 4276480 | tf_op jit(solution)/shard_map/dot_general | solution.py:334
  42.6 4.9 %collective-permute-done.10.refs_14_ = bf16[608,512]{1,0:T(8,128)(2,1)S(1)} collective-permute-done((bf16[608,512]{1,0:T(8,128)(2,1)S(1)}, bf16[608,512]{1,0:T(8,128)(2,1)S(1)}, u32[]{:S(2)}, u32[]{:S(2)}) %collective-permute-start.10) | collective-permute-done | bytes 622624 | tf_op jit(solution)/shard_map/ppermute | solution.py:330
  47.5 1.6 collective-permute-done.9
  49.9 1.8 %pad_maximum_fusion.refs_11_ = bf16[4,512,512]{2,1,0:T(8,128)(2,1)S(1)} fusion(bf16[1,512,512]{2,1,0:T(8,128)(2,1)} %bitcast.17, bf16[1,512,512]{2,1,0:T(8,128)(2,1)} %bitcast.16, bf16[1,512,512]{2,1,0:T(8,128)(2,1)} %bitcast.15, bf16[1,512,512]{2,1,0:T(8,128)(2,1)} %bitcast.14), kind=kLoop, calls=%fused_computation | loop fusion | flops 3145728 | bytes 4194304 | tf_op jit(solution)/shard_map/stack | solution.py:44
  52.8 2.1 %collective-permute-start.12 = (bf16[8,144,128]{2,1,0:T(8,128)(2,1)S(1)}, bf16[8,144,128]{2,1,0:T(8,128)(2,1)S(1)}, u32[]{:S(2)}, u32[]{:S(2)}) collective-permute-start(bf16[8,144,128]{2,1,0:T(8,128)(2,1)S(1)} %slice_bitcast_fusion), channel_id=1, source_target_pairs={{0,56},{8,0},{16,8},{24,16},{32,24},{40,32},{48,40},{56,48},{1,57}... | collective-permute-start | bytes 884744 | tf_op jit(solution)/shard_map/ppermute | solution.py:55
  54.9 7.3 %collective-permute-done.12.refs_9_ = bf16[8,144,128]{2,1,0:T(8,128)(2,1)S(1)} collective-permute-done((bf16[8,144,128]{2,1,0:T(8,128)(2,1)S(1)}, bf16[8,144,128]{2,1,0:T(8,128)(2,1)S(1)}, u32[]{:S(2)}, u32[]{:S(2)}) %collective-permute-start.12) | collective-permute-done | bytes 294944 | tf_op jit(solution)/shard_map/ppermute | solution.py:55
  62.3 2.9 %collective-permute-start.13 = (bf16[8,144,128]{2,1,0:T(8,128)(2,1)S(1)}, bf16[8,144,128]{2,1,0:T(8,128)(2,1)S(1)}, u32[]{:S(2)}, u32[]{:S(2)}) collective-permute-start(bf16[8,144,128]{2,1,0:T(8,128)(2,1)S(1)} %collective-permute-done.12.refs_9_), channel_id=1, source_target_pairs={{0,56},{8,0},{16,8},{24,16},{32,24},{40,32},{48,40},{56,48},{1,57}... | collective-permute-start | bytes 884744 | tf_op jit(solution)/shard_map/ppermute | solution.py:55
  65.3 4.2 %collective-permute-done.15.refs_15_ = bf16[608,512]{1,0:T(8,128)(2,1)} collective-permute-done((bf16[608,512]{1,0:T(8,128)(2,1)}, bf16[608,512]{1,0:T(8,128)(2,1)}, u32[]{:S(2)}, u32[]{:S(2)}) %collective-permute-start.15) | collective-permute-done | bytes 622624 | tf_op jit(solution)/shard_map/ppermute | solution.py:331
  69.5 1.5 collective-permute-done.13.refs_10_
  72.3 12.1 %conv_pool_mask.1 = (bf16[4,2,16,512]{3,2,1,0:T(8,128)(2,1)S(1)}, bf16[2,8,144,512]{3,2,1,0:T(8,128)(2,1)}) custom-call(s32[4]{0:T(128)S(1)} %pad_add_fusion.place_ref, bf16[8,144,128]{2,1,0:T(8,128)(2,1)} %copy-done.9, bf16[8,144,128]{2,1,0:T(8,128)(2,1)} %copy-done.10, bf16[8,144,128]{2,1,0:T(8,128)(2,1)} %copy-done.12, bf16[8,144,128]{2,1,0:T(8,128)(2,1)} %copy-done.11, ...), custom_call_target="tpu_custom_call" | custom-call | tf_op jit(solution)/shard_map/conv_pool_mask/pallas_call | solution.py:150
  84.4 10.4 %all_to_all.25.both_ref = bf16[8,16,512]{2,1,0:T(8,128)(2,1)S(1)} all-to-all(bf16[8,16,512]{2,1,0:T(8,128)(2,1)S(1)} %bitcast.41), channel_id=1, replica_groups=mesh['seed'=4,'z'=8,'ylo'=2,'yhi'=2,'core'=2] {'yhi','core','ylo'}, dimensions={0} | all-to-all | bytes 262144 | tf_op jit(solution)/shard_map/all_to_all | solution.py:346
  94.8 1.6 %logits_slices.1 = bf16[16,64,256]{2,1,0:T(8,128)(2,1)} custom-call(bf16[8,16,512]{2,1,0:T(8,128)(2,1)S(1)} %all_to_all.25.both_ref, bf16[512,4096]{1,0:T(8,128)(2,1)S(1)} %copy-done), custom_call_target="tpu_custom_call" | custom-call | tf_op jit(solution)/shard_map/logits_slices/pallas_call | solution.py:229
  96.4 4.8 %all-to-all-start.1 = ((bf16[16,64,256]{2,1,0:T(8,128)(2,1)}), bf16[16,64,256]{2,1,0:T(8,128)(2,1)}, u32[]{:S(2)}, u32[]{:S(2)}) async-start(bf16[16,64,256]{2,1,0:T(8,128)(2,1)} %logits_slices.1), calls=%async_computation.1 | async-start | bytes 1048576 | tf_op jit(solution)/shard_map/all_to_all | solution.py:347
  101.2 1.5 slice.15.other_ref
  103.6 5.6 %masked_sums.1.m_ref = f32[8,32,1024]{2,1,0:T(8,128)S(1)} custom-call(s32[4]{0:T(128)S(1)} %pad_add_fusion.place_ref, bf16[8,144,128]{2,1,0:T(8,128)(2,1)} %copy-done.9, bf16[8,144,128]{2,1,0:T(8,128)(2,1)} %copy-done.10, bf16[8,144,128]{2,1,0:T(8,128)(2,1)} %copy-done.12, bf16[8,144,128]{2,1,0:T(8,128)(2,1)} %copy-done.11, ...), custom_call_target="tpu_custom_call" | custom-call | tf_op jit(solution)/shard_map/masked_sums/pallas_call | solution.py:202
  109.2 6.9 %all-to-all-done.1 = bf16[16,64,256]{2,1,0:T(8,128)(2,1)} async-done(((bf16[16,64,256]{2,1,0:T(8,128)(2,1)}), bf16[16,64,256]{2,1,0:T(8,128)(2,1)}, u32[]{:S(2)}, u32[]{:S(2)}) %all-to-all-start.1) | async-done | bytes 524320 | tf_op jit(solution)/shard_map/all_to_all | solution.py:347
  117.3 18.9 %all_to_all.26.expo_ref = bf16[16,64,256]{2,1,0:T(8,128)(2,1)S(1)} all-to-all(bf16[16,64,256]{2,1,0:T(8,128)(2,1)S(1)} %broadcast_in_dim.2), channel_id=1, replica_groups=mesh['seed'=4,'z'=8,'ylo'=2,'yhi'=2,'core'=2] {'ylo','z'}, dimensions={0} | all-to-all | bytes 1048576 | tf_op jit(solution)/shard_map/all_to_all | solution.py:355
  136.1 3.1 %back.1 = f32[64,640]{1,0:T(8,128)S(1)} custom-call(bf16[16,64,256]{2,1,0:T(8,128)(2,1)S(1)} %all_to_all.26.expo_ref, bf16[512,4096]{1,0:T(8,128)(2,1)} %head_ref.3), custom_call_target="tpu_custom_call" | custom-call | tf_op jit(solution)/shard_map/back/pallas_call | solution.py:265
  139.2 9.6 %all_to_all.27 = f32[8,8,640]{2,1,0:T(8,128)S(1)} all-to-all(f32[8,8,640]{2,1,0:T(8,128)S(1)} %bitcast.35), channel_id=1, replica_groups=mesh['seed'=4,'z'=8,'ylo'=2,'yhi'=2,'core'=2] {'yhi','core','ylo'}, dimensions={0} | all-to-all | bytes 327680 | tf_op jit(solution)/shard_map/all_to_all | solution.py:358
  150.1 12.9 %all_to_all.28 = f32[16,8,128]{2,1,0:T(8,128)S(1)} all-to-all(f32[16,8,128]{2,1,0:T(8,128)S(1)} %bitcast.51), channel_id=1, replica_groups=mesh['seed'=4,'z'=8,'ylo'=2,'yhi'=2,'core'=2] {'ylo','z'}, dimensions={0} | all-to-all | bytes 131072 | tf_op jit(solution)/shard_map/all_to_all | solution.py:362
  (65 shorter events, 10.9 us)
Async XLA Ops:
  0.0 23.3 %copy-start.6 = (bf16[16,144,512]{2,1,0:T(8,128)(2,1)S(1)}, bf16[16,144,512]{2,1,0:T(8,128)(2,1)}, u32[]{:S(2)}) copy-start(bf16[16,144,512]{2,1,0:T(8,128)(2,1)} %param.7) | copy-start | bytes 7077892
  1.2 7.5 %copy-start.9 = (bf16[8,144,128]{2,1,0:T(8,128)(2,1)}, bf16[8,144,128]{2,1,0:T(8,128)(2,1)S(1)}, u32[]{:S(2)}) copy-start(bf16[8,144,128]{2,1,0:T(8,128)(2,1)S(1)} %get-tuple-element.51.refs_0_) | copy-start | bytes 884740
  1.3 8.8 %collective-permute-start.2 = (bf16[8,144,128]{2,1,0:T(8,128)(2,1)S(1)}, bf16[8,144,128]{2,1,0:T(8,128)(2,1)S(1)}, u32[]{:S(2)}, u32[]{:S(2)}) collective-permute-start(bf16[8,144,128]{2,1,0:T(8,128)(2,1)S(1)} %get-tuple-element.73), channel_id=1, source_target_pairs={{0,4},{4,0},{1,5},{5,1},{2,6},{6,2},{3,7},{7,3},{8,12},{12,8},{9,1... | collective-permute-start | bytes 884744 | tf_op jit(solution)/shard_map/ppermute | solution.py:326
  2.9 11.8 %collective-permute-start.1 = (bf16[8,144,128]{2,1,0:T(8,128)(2,1)S(1)}, bf16[8,144,128]{2,1,0:T(8,128)(2,1)S(1)}, u32[]{:S(2)}, u32[]{:S(2)}) collective-permute-start(bf16[8,144,128]{2,1,0:T(8,128)(2,1)S(1)} %get-tuple-element.51.refs_0_), channel_id=1, source_target_pairs={{0,56},{8,0},{16,8},{24,16},{32,24},{40,32},{48,40},{56,48},{1,57}... | collective-permute-start | bytes 884744 | tf_op jit(solution)/shard_map/ppermute | solution.py:25
  8.8 9.4 %collective-permute-start = (bf16[8,144,128]{2,1,0:T(8,128)(2,1)S(1)}, bf16[8,144,128]{2,1,0:T(8,128)(2,1)S(1)}, u32[]{:S(2)}, u32[]{:S(2)}) collective-permute-start(bf16[8,144,128]{2,1,0:T(8,128)(2,1)S(1)} %get-tuple-element.51.refs_0_), channel_id=1, source_target_pairs={{0,8},{8,16},{16,24},{24,32},{32,40},{40,48},{48,56},{56,0},{1,9},... | collective-permute-start | bytes 884744 | tf_op jit(solution)/shard_map/ppermute | solution.py:24
  10.1 13.2 %copy-start.10 = (bf16[8,144,128]{2,1,0:T(8,128)(2,1)}, bf16[8,144,128]{2,1,0:T(8,128)(2,1)S(1)}, u32[]{:S(2)}) copy-start(bf16[8,144,128]{2,1,0:T(8,128)(2,1)S(1)} %collective-permute-done.2.refs_1_) | copy-start | bytes 884740
  14.8 8.5 %copy-start.11 = (bf16[8,144,128]{2,1,0:T(8,128)(2,1)}, bf16[8,144,128]{2,1,0:T(8,128)(2,1)S(1)}, u32[]{:S(2)}) copy-start(bf16[8,144,128]{2,1,0:T(8,128)(2,1)S(1)} %collective-permute-done.1.refs_3_) | copy-start | bytes 884740
  18.2 5.1 %copy-start.12 = (bf16[8,144,128]{2,1,0:T(8,128)(2,1)}, bf16[8,144,128]{2,1,0:T(8,128)(2,1)S(1)}, u32[]{:S(2)}) copy-start(bf16[8,144,128]{2,1,0:T(8,128)(2,1)S(1)} %collective-permute-done.refs_2_) | copy-start | bytes 884740
  18.3 20.7 %copy-start.17 = (s32[64]{0:T(128)S(1)}, s32[64]{0:T(128)}, u32[]{:S(2)}) copy-start(s32[64]{0:T(128)} %param.11) | copy-start | bytes 772
  18.3 13.8 %collective-permute-start.4 = (bf16[2,8,144,128]{3,2,1,0:T(8,128)(2,1)S(1)}, bf16[2,8,144,128]{3,2,1,0:T(8,128)(2,1)}, u32[]{:S(2)}, u32[]{:S(2)}) collective-permute-start(bf16[2,8,144,128]{3,2,1,0:T(8,128)(2,1)S(1)} %get-tuple-element.75), channel_id=1, source_target_pairs={{0,56},{8,0},{16,8},{24,16},{32,24},{40,32},{48,40},{56,48},{1,57}... | collective-permute-start | bytes 1769480 | tf_op jit(solution)/shard_map/ppermute | solution.py:37
  18.6 14.9 %collective-permute-start.3 = (bf16[2,8,144,128]{3,2,1,0:T(8,128)(2,1)S(1)}, bf16[2,8,144,128]{3,2,1,0:T(8,128)(2,1)}, u32[]{:S(2)}, u32[]{:S(2)}) collective-permute-start(bf16[2,8,144,128]{3,2,1,0:T(8,128)(2,1)S(1)} %get-tuple-element.76), channel_id=1, source_target_pairs={{0,8},{8,16},{16,24},{24,32},{32,40},{40,48},{48,56},{56,0},{1,9},... | collective-permute-start | bytes 1769480 | tf_op jit(solution)/shard_map/ppermute | solution.py:36
  20.4 16.4 %collective-permute-start.8 = (bf16[512,512]{1,0:T(8,128)(2,1)}, bf16[512,512]{1,0:T(8,128)(2,1)}, u32[]{:S(2)}, u32[]{:S(2)}) collective-permute-start(bf16[512,512]{1,0:T(8,128)(2,1)} %param.9), channel_id=1, source_target_pairs={{0,6},{2,4},{4,2},{6,0},{1,7},{3,5},{5,3},{7,1},{8,14},{10,12},{12... | collective-permute-start | bytes 1572872 | tf_op jit(solution)/shard_map/ppermute | solution.py:30
  22.6 15.2 %collective-permute-start.7 = (bf16[512,512]{1,0:T(8,128)(2,1)}, bf16[512,512]{1,0:T(8,128)(2,1)}, u32[]{:S(2)}, u32[]{:S(2)}) collective-permute-start(bf16[512,512]{1,0:T(8,128)(2,1)} %param.9), channel_id=1, source_target_pairs={{0,4},{4,0},{1,5},{5,1},{2,6},{6,2},{3,7},{7,3},{8,12},{12,8},{9,1... | collective-permute-start | bytes 1572872 | tf_op jit(solution)/shard_map/ppermute | solution.py:29
  23.4 24.1 %collective-permute-start.10 = (bf16[608,512]{1,0:T(8,128)(2,1)S(1)}, bf16[608,512]{1,0:T(8,128)(2,1)S(1)}, u32[]{:S(2)}, u32[]{:S(2)}) collective-permute-start(bf16[608,512]{1,0:T(8,128)(2,1)S(1)} %slice.16), channel_id=1, source_target_pairs={{0,4},{4,0},{1,5},{5,1},{2,6},{6,2},{3,7},{7,3},{8,12},{12,8},{9,1... | collective-permute-start | bytes 1867784 | tf_op jit(solution)/shard_map/ppermute | solution.py:330
  33.6 15.5 %collective-permute-start.5 = (bf16[2,8,144,128]{3,2,1,0:T(8,128)(2,1)}, bf16[2,8,144,128]{3,2,1,0:T(8,128)(2,1)}, u32[]{:S(2)}, u32[]{:S(2)}) collective-permute-start(bf16[2,8,144,128]{3,2,1,0:T(8,128)(2,1)} %collective-permute-done.3.refs_4_), channel_id=1, source_target_pairs={{0,8},{8,16},{16,24},{24,32},{32,40},{40,48},{48,56},{56,0},{1,9},... | collective-permute-start | bytes 1769480 | tf_op jit(solution)/shard_map/ppermute | solution.py:36
  33.8 15.3 %collective-permute-start.6 = (bf16[2,8,144,128]{3,2,1,0:T(8,128)(2,1)}, bf16[2,8,144,128]{3,2,1,0:T(8,128)(2,1)S(1)}, u32[]{:S(2)}, u32[]{:S(2)}) collective-permute-start(bf16[2,8,144,128]{3,2,1,0:T(8,128)(2,1)} %collective-permute-done.4.refs_5_), channel_id=1, source_target_pairs={{0,56},{8,0},{16,8},{24,16},{32,24},{40,32},{48,40},{56,48},{1,57}... | collective-permute-start | bytes 1769480 | tf_op jit(solution)/shard_map/ppermute | solution.py:37
  37.7 11.3 %collective-permute-start.9 = (bf16[512,512]{1,0:T(8,128)(2,1)}, bf16[512,512]{1,0:T(8,128)(2,1)}, u32[]{:S(2)}, u32[]{:S(2)}) collective-permute-start(bf16[512,512]{1,0:T(8,128)(2,1)} %collective-permute-done.7), channel_id=1, source_target_pairs={{0,6},{2,4},{4,2},{6,0},{1,7},{3,5},{5,3},{7,1},{8,14},{10,12},{12... | collective-permute-start | bytes 1572872 | tf_op jit(solution)/shard_map/ppermute | solution.py:41
  47.5 1.6 copy-start.16
  49.9 2.0 %copy-start.2 = (bf16[512,64]{0,1:T(8,128)(2,1)S(1)}, bf16[512,64]{0,1:T(8,128)(2,1)}, u32[]{:S(2)}) copy-start(bf16[512,64]{0,1:T(8,128)(2,1)} %param.13) | copy-start | bytes 196612
  51.7 1.1 copy-start.8
  51.7 19.7 %collective-permute-start.14 = (bf16[4,512,512]{2,1,0:T(8,128)(2,1)S(1)}, bf16[4,512,512]{2,1,0:T(8,128)(2,1)}, u32[]{:S(2)}, u32[]{:S(2)}) collective-permute-start(bf16[4,512,512]{2,1,0:T(8,128)(2,1)S(1)} %pad_maximum_fusion.refs_11_), channel_id=1, source_target_pairs={{0,1},{1,0},{2,3},{3,2},{4,5},{5,4},{6,7},{7,6},{8,9},{9,8},{10,11... | collective-permute-start | bytes 6291464 | tf_op jit(solution)/shard_map/ppermute | solution.py:45
  52.8 16.7 %collective-permute-start.15 = (bf16[608,512]{1,0:T(8,128)(2,1)}, bf16[608,512]{1,0:T(8,128)(2,1)}, u32[]{:S(2)}, u32[]{:S(2)}) collective-permute-start(bf16[608,512]{1,0:T(8,128)(2,1)} %pad_maximum_fusion.3), channel_id=1, source_target_pairs={{0,4},{4,0},{1,5},{5,1},{2,6},{6,2},{3,7},{7,3},{8,12},{12,8},{9,1... | collective-permute-start | bytes 1867784 | tf_op jit(solution)/shard_map/ppermute | solution.py:331
  52.8 9.5 %collective-permute-start.12 = (bf16[8,144,128]{2,1,0:T(8,128)(2,1)S(1)}, bf16[8,144,128]{2,1,0:T(8,128)(2,1)S(1)}, u32[]{:S(2)}, u32[]{:S(2)}) collective-permute-start(bf16[8,144,128]{2,1,0:T(8,128)(2,1)S(1)} %slice_bitcast_fusion), channel_id=1, source_target_pairs={{0,56},{8,0},{16,8},{24,16},{32,24},{40,32},{48,40},{56,48},{1,57}... | collective-permute-start | bytes 884744 | tf_op jit(solution)/shard_map/ppermute | solution.py:55
  54.9 16.6 %collective-permute-start.11 = (bf16[2,8,144,128]{3,2,1,0:T(8,128)(2,1)}, bf16[2,8,144,128]{3,2,1,0:T(8,128)(2,1)S(1)}, u32[]{:S(2)}, u32[]{:S(2)}) collective-permute-start(bf16[2,8,144,128]{3,2,1,0:T(8,128)(2,1)} %collective-permute-done.5.refs_6_), channel_id=1, source_target_pairs={{0,8},{8,16},{16,24},{24,32},{32,40},{40,48},{48,56},{56,0},{1,9},... | collective-permute-start | bytes 1769480 | tf_op jit(solution)/shard_map/ppermute | solution.py:50
  62.3 9.2 %copy-start.14 = (bf16[8,144,128]{2,1,0:T(8,128)(2,1)}, bf16[8,144,128]{2,1,0:T(8,128)(2,1)S(1)}, u32[]{:S(2)}) copy-start(bf16[8,144,128]{2,1,0:T(8,128)(2,1)S(1)} %collective-permute-done.12.refs_9_) | copy-start | bytes 884740
  62.3 8.8 %collective-permute-start.13 = (bf16[8,144,128]{2,1,0:T(8,128)(2,1)S(1)}, bf16[8,144,128]{2,1,0:T(8,128)(2,1)S(1)}, u32[]{:S(2)}, u32[]{:S(2)}) collective-permute-start(bf16[8,144,128]{2,1,0:T(8,128)(2,1)S(1)} %collective-permute-done.12.refs_9_), channel_id=1, source_target_pairs={{0,56},{8,0},{16,8},{24,16},{32,24},{40,32},{48,40},{56,48},{1,57}... | collective-permute-start | bytes 884744 | tf_op jit(solution)/shard_map/ppermute | solution.py:55
  72.3 22.5 %copy-start = (bf16[512,4096]{1,0:T(8,128)(2,1)S(1)}, bf16[512,4096]{1,0:T(8,128)(2,1)}, u32[]{:S(2)}) copy-start(bf16[512,4096]{1,0:T(8,128)(2,1)} %head_ref.3) | copy-start | bytes 12582916
  94.8 7.9 %copy-start.1 = (bf16[2,8,144,512]{3,2,1,0:T(8,128)(2,1)S(1)}, bf16[2,8,144,512]{3,2,1,0:T(8,128)(2,1)}, u32[]{:S(2)}) copy-start(bf16[2,8,144,512]{3,2,1,0:T(8,128)(2,1)} %get-tuple-element.68.refs_11_) | copy-start | bytes 7077892
  96.4 19.6 %all-to-all-start.1 = ((bf16[16,64,256]{2,1,0:T(8,128)(2,1)}), bf16[16,64,256]{2,1,0:T(8,128)(2,1)}, u32[]{:S(2)}, u32[]{:S(2)}) async-start(bf16[16,64,256]{2,1,0:T(8,128)(2,1)} %logits_slices.1), calls=%async_computation.1 | async-start | bytes 1048576 | tf_op jit(solution)/shard_map/all_to_all | solution.py:347
  102.7 0.9 copy-start.5
  136.1 12.7 %copy-start.3 = (bf16[512,64]{0,1:T(8,128)(2,1)S(1)}, bf16[512,64]{0,1:T(8,128)(2,1)}, u32[]{:S(2)}) copy-start(bf16[512,64]{0,1:T(8,128)(2,1)} %param.13) | copy-start | bytes 196612
  136.1 12.7 %copy-start.4 = (bf16[64,512]{1,0:T(8,128)(2,1)S(1)}, bf16[64,512]{1,0:T(8,128)(2,1)}, u32[]{:S(2)}) copy-start(bf16[64,512]{1,0:T(8,128)(2,1)} %slice.15.other_ref) | copy-start | bytes 196612
  (3 other events, 2.5 us)

commit v10 on v8

--- a/solution.py
+++ b/solution.py
@@ -33,24 +33,34 @@
     r = jnp.stack([r, swapped])
     l = jnp.stack([l, swapped])
     for k in range(2, nz // 2):
+        end = k == nz // 2 - 1
         r = lax.ppermute(r, "z", right)
-        l = lax.ppermute(l, "z", left)
+        if end:
+            follow = lax.ppermute(l[1], "z", left)
+            l = lax.ppermute(l[0], "z", left)
+        else:
+            l = lax.ppermute(l, "z", left)
         if k == 2:
             r, l = lax.optimization_barrier((r, l))
             low, high, *_ = lax.optimization_barrier((low, high, r, l))
             far = lax.ppermute(low, ("ylo", "yhi"), across)
-        elif k == nz // 2 - 1:
-            r, l, far, early = lax.optimization_barrier((r, l, far, early))
+        if end:
+            r, l, follow, far, early = lax.optimization_barrier((r, l, follow, far, early))
             every = jnp.stack([w, far, low, high])
             weights = [every, lax.ppermute(every, "core", swap)]
-        for way, v in ((1, r), (-1, l)):
-            plan += [(len(arrays), 0, 0, way * k % nz), (len(arrays), 1, 1, way * (k - 1) % nz)]
-            arrays.append(v)
+        plan += [(len(arrays), 0, 0, k), (len(arrays), 1, 1, k - 1)]
+        arrays.append(r)
+        if end:
+            plan += [(len(arrays), None, 0, nz - k), (len(arrays) + 1, None, 1, nz - k + 1)]
+            arrays += [l, follow]
+        else:
+            plan += [(len(arrays), 0, 0, nz - k), (len(arrays), 1, 1, nz - k + 1)]
+            arrays.append(l)
     last = nz // 2
     r = lax.ppermute(r, "z", right)
     plan += [(len(arrays), 0, 0, last), (len(arrays), 1, 1, last - 1)]
     arrays.append(r)
-    l = l[1]
+    l = follow
     for k in (last + 1, last):
         l = lax.ppermute(l, "z", left)
         plan.append((len(arrays), None, 1, k))

time: 161 us -> 162 us (level)
    ppermute x1, waiting for transfers between devices: 0.74 us -> 3.74 us  [rings(): low = lax.ppermute(w, 'ylo', swap)]
    ppermute x0 -> x2, starting transfers between devices: none -> 1.66 us  [the longest x1 1.57 us: rings(): follow = lax.ppermute(l[1], 'z', left)]
    ppermute x4 -> x3, waiting for transfers between devices: 13.2 us -> 12.7 us  [rings(): l = lax.ppermute(l, 'z', left)]
    ppermute x4 -> x3, starting transfers between devices: 7.83 us -> 7.82 us  [rings(): l = lax.ppermute(l, 'z', left)]
  transfers between devices with their start and end apart: 17 -> 18, of which waited for: 12 -> 12; matrix products, arithmetic and copies ran while one was open for 4% -> 4% of each run, Pallas kernels for 3% -> 3%
where the time goes in v10:
time: 162 us
  blocking collectives  49.5 us (31%)
  waiting for transfers between devices  46.9 us (29%)
  starting transfers between devices  29.3 us (18%)
  Pallas kernels  23.6 us (15%)
  local copies, waits for them, and re-layouts  5.57 us (3%)
  matrix products  3.59 us (2%)
  other arithmetic  3.07 us (2%)
    all_to_all x1, blocking collectives, per_device(): lax.all_to_all(jnp.broadcast_to(expo, (parts,) + expo.shape), SPREAD, 0, 0)  18.8 us
    all_to_all x1, blocking collectives, per_device(): grads = lax.all_to_all(grads, SPREAD, 0, 0)  12.8 us
    ppermute x3, waiting for transfers between devices, rings(): l = lax.ppermute(l, 'z', left)  12.7 us
    pallas_call x1, Pallas kernels, conv(): pl.pallas_call(functools.partial(conv_body, nz, len(blocks), plan), in_sp...  12.3 us
    all_to_all x1, blocking collectives, per_device(): both = lax.all_to_all(both.reshape(2 * fs, 2 * half, width), ROWS, 0, 0)  9.05 us
    all_to_all x1, blocking collectives, per_device(): part = lax.all_to_all(part, ROWS, 0, 0).reshape(fs, 2, half, width + 128)  8.88 us
    ppermute x3, starting transfers between devices, rings(): l = lax.ppermute(l, 'z', left)  7.82 us
    all_to_all x1, waiting for transfers between devices, per_device(): part = lax.all_to_all(logits_slices(both, head_weight, parts), SPREAD, 0, 0)  7.73 us
  transfers between devices with their start and end apart: 18, of which 12 were waited for; matrix products, arithmetic and copies ran while one was open for 4% of the time, Pallas kernels for 3%

profile of v10, /device:TPU:2, one launch (start us, length us, event | category | flops | bytes accessed | tf_op | source)
XLA Modules:
  0.0 161.8 jit_solution(4155111987928702016)
XLA Ops:
  0.0 1.2 dynamic-slice_bitcast_fusion
  1.3 1.7 %collective-permute-start.2 = (bf16[8,144,128]{2,1,0:T(8,128)(2,1)S(1)}, bf16[8,144,128]{2,1,0:T(8,128)(2,1)S(1)}, u32[]{:S(2)}, u32[]{:S(2)}) collective-permute-start(bf16[8,144,128]{2,1,0:T(8,128)(2,1)S(1)} %get-tuple-element.77), channel_id=1, source_target_pairs={{0,4},{4,0},{1,5},{5,1},{2,6},{6,2},{3,7},{7,3},{8,12},{12,8},{9,1... | collective-permute-start | bytes 884744 | tf_op jit(solution)/shard_map/ppermute | solution.py:345
  2.9 5.9 %collective-permute-start.1 = (bf16[8,144,128]{2,1,0:T(8,128)(2,1)S(1)}, bf16[8,144,128]{2,1,0:T(8,128)(2,1)S(1)}, u32[]{:S(2)}, u32[]{:S(2)}) collective-permute-start(bf16[8,144,128]{2,1,0:T(8,128)(2,1)S(1)} %get-tuple-element.52.refs_0_), channel_id=1, source_target_pairs={{0,56},{8,0},{16,8},{24,16},{32,24},{40,32},{48,40},{56,48},{1,57}... | collective-permute-start | bytes 884744 | tf_op jit(solution)/shard_map/ppermute | solution.py:25
  8.8 1.3 collective-permute-done.2.refs_1_
  10.1 4.7 %collective-permute-done.1.refs_3_ = bf16[8,144,128]{2,1,0:T(8,128)(2,1)S(1)} collective-permute-done((bf16[8,144,128]{2,1,0:T(8,128)(2,1)S(1)}, bf16[8,144,128]{2,1,0:T(8,128)(2,1)S(1)}, u32[]{:S(2)}, u32[]{:S(2)}) %collective-permute-start.1) | collective-permute-done | bytes 294944 | tf_op jit(solution)/shard_map/ppermute | solution.py:25
  14.8 3.4 %collective-permute-done.refs_2_ = bf16[8,144,128]{2,1,0:T(8,128)(2,1)S(1)} collective-permute-done((bf16[8,144,128]{2,1,0:T(8,128)(2,1)S(1)}, bf16[8,144,128]{2,1,0:T(8,128)(2,1)S(1)}, u32[]{:S(2)}, u32[]{:S(2)}) %collective-permute-start) | collective-permute-done | bytes 294944 | tf_op jit(solution)/shard_map/ppermute | solution.py:24
  18.6 1.7 %collective-permute-start.3 = (bf16[2,8,144,128]{3,2,1,0:T(8,128)(2,1)S(1)}, bf16[2,8,144,128]{3,2,1,0:T(8,128)(2,1)S(1)}, u32[]{:S(2)}, u32[]{:S(2)}) collective-permute-start(bf16[2,8,144,128]{3,2,1,0:T(8,128)(2,1)S(1)} %get-tuple-element.80), channel_id=1, source_target_pairs={{0,8},{8,16},{16,24},{24,32},{32,40},{40,48},{48,56},{56,0},{1,9},... | collective-permute-start | bytes 1769480 | tf_op jit(solution)/shard_map/ppermute | solution.py:37
  20.4 2.2 %collective-permute-start.9 = (bf16[512,512]{1,0:T(8,128)(2,1)S(1)}, bf16[512,512]{1,0:T(8,128)(2,1)S(1)}, u32[]{:S(2)}, u32[]{:S(2)}) collective-permute-start(bf16[512,512]{1,0:T(8,128)(2,1)S(1)} %copy-done.18), channel_id=1, source_target_pairs={{0,6},{2,4},{4,2},{6,0},{1,7},{3,5},{5,3},{7,1},{8,14},{10,12},{12... | collective-permute-start | bytes 1572872 | tf_op jit(solution)/shard_map/ppermute | solution.py:30
  23.4 1.4 collective-permute-start.11
  24.8 7.1 %collective-permute-done.4.refs_5_ = bf16[2,8,144,128]{3,2,1,0:T(8,128)(2,1)S(1)} collective-permute-done((bf16[2,8,144,128]{3,2,1,0:T(8,128)(2,1)S(1)}, bf16[2,8,144,128]{3,2,1,0:T(8,128)(2,1)S(1)}, u32[]{:S(2)}, u32[]{:S(2)}) %collective-permute-start.4) | collective-permute-done | bytes 589856 | tf_op jit(solution)/shard_map/ppermute | solution.py:42
  31.9 1.5 collective-permute-done.3.refs_4_
  33.7 3.7 %collective-permute-done.8 = bf16[512,512]{1,0:T(8,128)(2,1)S(1)} collective-permute-done((bf16[512,512]{1,0:T(8,128)(2,1)S(1)}, bf16[512,512]{1,0:T(8,128)(2,1)S(1)}, u32[]{:S(2)}, u32[]{:S(2)}) %collective-permute-start.8) | collective-permute-done | bytes 524320 | tf_op jit(solution)/shard_map/ppermute | solution.py:29
  38.5 1.6 collective-permute-start.7
  40.2 7.1 %collective-permute-done.11.refs_15_ = bf16[608,512]{1,0:T(8,128)(2,1)S(1)} collective-permute-done((bf16[608,512]{1,0:T(8,128)(2,1)S(1)}, bf16[608,512]{1,0:T(8,128)(2,1)S(1)}, u32[]{:S(2)}, u32[]{:S(2)}) %collective-permute-start.11) | collective-permute-done | bytes 622624 | tf_op jit(solution)/shard_map/ppermute | solution.py:349
  47.2 1.4 collective-permute-done.6.refs_7_
  49.8 3.8 %collective-permute-start.13 = (bf16[8,144,128]{2,1,0:T(8,128)(2,1)}, bf16[8,144,128]{2,1,0:T(8,128)(2,1)}, u32[]{:S(2)}, u32[]{:S(2)}) collective-permute-start(bf16[8,144,128]{2,1,0:T(8,128)(2,1)} %collective-permute-done.7.refs_8_), channel_id=1, source_target_pairs={{0,56},{8,0},{16,8},{24,16},{32,24},{40,32},{48,40},{56,48},{1,57}... | collective-permute-start | bytes 884744 | tf_op jit(solution)/shard_map/ppermute | solution.py:65
  55.2 5.6 %collective-permute-done.13.refs_10_ = bf16[8,144,128]{2,1,0:T(8,128)(2,1)} collective-permute-done((bf16[8,144,128]{2,1,0:T(8,128)(2,1)}, bf16[8,144,128]{2,1,0:T(8,128)(2,1)}, u32[]{:S(2)}, u32[]{:S(2)}) %collective-permute-start.13) | collective-permute-done | bytes 294944 | tf_op jit(solution)/shard_map/ppermute | solution.py:65
  60.8 3.7 %collective-permute-start.14 = (bf16[8,144,128]{2,1,0:T(8,128)(2,1)}, bf16[8,144,128]{2,1,0:T(8,128)(2,1)S(1)}, u32[]{:S(2)}, u32[]{:S(2)}) collective-permute-start(bf16[8,144,128]{2,1,0:T(8,128)(2,1)} %collective-permute-done.13.refs_10_), channel_id=1, source_target_pairs={{0,56},{8,0},{16,8},{24,16},{32,24},{40,32},{48,40},{56,48},{1,57}... | collective-permute-start | bytes 884744 | tf_op jit(solution)/shard_map/ppermute | solution.py:65
  64.5 3.6 %convolution_convert_fusion = bf16[64,512]{1,0:T(8,128)(2,1)S(1)} fusion(bf16[512,4096]{1,0:T(8,128)(2,1)} %head_ref.3, s32[4096]{0:T(1024)S(1)} %iota_add_fusion, s32[64]{0:T(128)S(1)} %copy-done.19), kind=kOutput, calls=%fused_computation.1 | convolution fusion | flops 268730368 | bytes 4276480 | tf_op jit(solution)/shard_map/dot_general | solution.py:355
  68.1 2.8 %collective-permute-done.16.refs_16_ = bf16[608,512]{1,0:T(8,128)(2,1)} collective-permute-done((bf16[608,512]{1,0:T(8,128)(2,1)}, bf16[608,512]{1,0:T(8,128)(2,1)}, u32[]{:S(2)}, u32[]{:S(2)}) %collective-permute-start.16) | collective-permute-done | bytes 622624 | tf_op jit(solution)/shard_map/ppermute | solution.py:350
  72.3 12.3 %conv_pool_mask.1 = (bf16[4,2,16,512]{3,2,1,0:T(8,128)(2,1)S(1)}, bf16[2,8,144,512]{3,2,1,0:T(8,128)(2,1)S(1)}) custom-call(s32[4]{0:T(128)S(1)} %pad_add_fusion.place_ref, bf16[8,144,128]{2,1,0:T(8,128)(2,1)} %copy-done.8, bf16[8,144,128]{2,1,0:T(8,128)(2,1)} %copy-done.9, bf16[8,144,128]{2,1,0:T(8,128)(2,1)} %copy-done.11, ...), custom_call_target="tpu_custom_call" | custom-call | tf_op jit(solution)/shard_map/conv_pool_mask/pallas_call | solution.py:167
  84.6 9.0 %all_to_all.25.both_ref = bf16[8,16,512]{2,1,0:T(8,128)(2,1)S(1)} all-to-all(bf16[8,16,512]{2,1,0:T(8,128)(2,1)S(1)} %bitcast.43), channel_id=1, replica_groups=mesh['seed'=4,'z'=8,'ylo'=2,'yhi'=2,'core'=2] {'yhi','core','ylo'}, dimensions={0} | all-to-all | bytes 262144 | tf_op jit(solution)/shard_map/all_to_all | solution.py:365
  93.7 1.6 %logits_slices.1 = bf16[16,64,256]{2,1,0:T(8,128)(2,1)} custom-call(bf16[8,16,512]{2,1,0:T(8,128)(2,1)S(1)} %all_to_all.25.both_ref, bf16[512,4096]{1,0:T(8,128)(2,1)S(1)} %copy-done), custom_call_target="tpu_custom_call" | custom-call | tf_op jit(solution)/shard_map/logits_slices/pallas_call | solution.py:248
  95.3 4.2 %all-to-all-start.1 = ((bf16[16,64,256]{2,1,0:T(8,128)(2,1)}), bf16[16,64,256]{2,1,0:T(8,128)(2,1)}, u32[]{:S(2)}, u32[]{:S(2)}) async-start(bf16[16,64,256]{2,1,0:T(8,128)(2,1)} %logits_slices.1), calls=%async_computation.1 | async-start | bytes 1048576 | tf_op jit(solution)/shard_map/all_to_all | solution.py:366
  99.6 1.5 slice.19.other_ref
  102.0 5.5 %masked_sums.1.m_ref = f32[8,32,1024]{2,1,0:T(8,128)S(1)} custom-call(s32[4]{0:T(128)S(1)} %pad_add_fusion.place_ref, bf16[8,144,128]{2,1,0:T(8,128)(2,1)} %copy-done.8, bf16[8,144,128]{2,1,0:T(8,128)(2,1)} %copy-done.9, bf16[8,144,128]{2,1,0:T(8,128)(2,1)} %copy-done.11, bf16[8,144,128]{2,1,0:T(8,128)(2,1)} %copy-done.10, ...), custom_call_target="tpu_custom_call" | custom-call | tf_op jit(solution)/shard_map/masked_sums/pallas_call | solution.py:221
  107.5 7.7 %all-to-all-done.1 = bf16[16,64,256]{2,1,0:T(8,128)(2,1)} async-done(((bf16[16,64,256]{2,1,0:T(8,128)(2,1)}), bf16[16,64,256]{2,1,0:T(8,128)(2,1)}, u32[]{:S(2)}, u32[]{:S(2)}) %all-to-all-start.1) | async-done | bytes 524320 | tf_op jit(solution)/shard_map/all_to_all | solution.py:366
  115.2 1.1 convert_reduce_fusion
  116.4 18.8 %all_to_all.26.expo_ref = bf16[16,64,256]{2,1,0:T(8,128)(2,1)S(1)} all-to-all(bf16[16,64,256]{2,1,0:T(8,128)(2,1)S(1)} %broadcast_in_dim.2), channel_id=1, replica_groups=mesh['seed'=4,'z'=8,'ylo'=2,'yhi'=2,'core'=2] {'ylo','z'}, dimensions={0} | all-to-all | bytes 1048576 | tf_op jit(solution)/shard_map/all_to_all | solution.py:374
  135.3 3.1 %back.1 = f32[64,640]{1,0:T(8,128)S(1)} custom-call(bf16[16,64,256]{2,1,0:T(8,128)(2,1)S(1)} %all_to_all.26.expo_ref, bf16[512,4096]{1,0:T(8,128)(2,1)} %head_ref.3), custom_call_target="tpu_custom_call" | custom-call | tf_op jit(solution)/shard_map/back/pallas_call | solution.py:284
  138.4 8.9 %all_to_all.27 = f32[8,8,640]{2,1,0:T(8,128)S(1)} all-to-all(f32[8,8,640]{2,1,0:T(8,128)S(1)} %bitcast.37), channel_id=1, replica_groups=mesh['seed'=4,'z'=8,'ylo'=2,'yhi'=2,'core'=2] {'yhi','core','ylo'}, dimensions={0} | all-to-all | bytes 327680 | tf_op jit(solution)/shard_map/all_to_all | solution.py:377
  148.4 12.8 %all_to_all.28 = f32[16,8,128]{2,1,0:T(8,128)S(1)} all-to-all(f32[16,8,128]{2,1,0:T(8,128)S(1)} %bitcast.57), channel_id=1, replica_groups=mesh['seed'=4,'z'=8,'ylo'=2,'yhi'=2,'core'=2] {'ylo','z'}, dimensions={0} | all-to-all | bytes 131072 | tf_op jit(solution)/shard_map/all_to_all | solution.py:381
  (71 shorter events, 9.7 us)
Async XLA Ops:
  0.0 20.4 %copy-start.18 = (bf16[512,512]{1,0:T(8,128)(2,1)S(1)}, bf16[512,512]{1,0:T(8,128)(2,1)}, u32[]{:S(2)}) copy-start(bf16[512,512]{1,0:T(8,128)(2,1)} %param.9) | copy-start | bytes 1572868
  0.0 23.2 %copy-start.7 = (bf16[16,144,512]{2,1,0:T(8,128)(2,1)S(1)}, bf16[16,144,512]{2,1,0:T(8,128)(2,1)}, u32[]{:S(2)}) copy-start(bf16[16,144,512]{2,1,0:T(8,128)(2,1)} %param.7) | copy-start | bytes 7077892
  1.2 7.5 %copy-start.8 = (bf16[8,144,128]{2,1,0:T(8,128)(2,1)}, bf16[8,144,128]{2,1,0:T(8,128)(2,1)S(1)}, u32[]{:S(2)}) copy-start(bf16[8,144,128]{2,1,0:T(8,128)(2,1)S(1)} %get-tuple-element.52.refs_0_) | copy-start | bytes 884740
  1.3 8.8 %collective-permute-start.2 = (bf16[8,144,128]{2,1,0:T(8,128)(2,1)S(1)}, bf16[8,144,128]{2,1,0:T(8,128)(2,1)S(1)}, u32[]{:S(2)}, u32[]{:S(2)}) collective-permute-start(bf16[8,144,128]{2,1,0:T(8,128)(2,1)S(1)} %get-tuple-element.77), channel_id=1, source_target_pairs={{0,4},{4,0},{1,5},{5,1},{2,6},{6,2},{3,7},{7,3},{8,12},{12,8},{9,1... | collective-permute-start | bytes 884744 | tf_op jit(solution)/shard_map/ppermute | solution.py:345
  2.9 11.8 %collective-permute-start.1 = (bf16[8,144,128]{2,1,0:T(8,128)(2,1)S(1)}, bf16[8,144,128]{2,1,0:T(8,128)(2,1)S(1)}, u32[]{:S(2)}, u32[]{:S(2)}) collective-permute-start(bf16[8,144,128]{2,1,0:T(8,128)(2,1)S(1)} %get-tuple-element.52.refs_0_), channel_id=1, source_target_pairs={{0,56},{8,0},{16,8},{24,16},{32,24},{40,32},{48,40},{56,48},{1,57}... | collective-permute-start | bytes 884744 | tf_op jit(solution)/shard_map/ppermute | solution.py:25
  8.8 9.4 %collective-permute-start = (bf16[8,144,128]{2,1,0:T(8,128)(2,1)S(1)}, bf16[8,144,128]{2,1,0:T(8,128)(2,1)S(1)}, u32[]{:S(2)}, u32[]{:S(2)}) collective-permute-start(bf16[8,144,128]{2,1,0:T(8,128)(2,1)S(1)} %get-tuple-element.52.refs_0_), channel_id=1, source_target_pairs={{0,8},{8,16},{16,24},{24,32},{32,40},{40,48},{48,56},{56,0},{1,9},... | collective-permute-start | bytes 884744 | tf_op jit(solution)/shard_map/ppermute | solution.py:24
  10.1 13.2 %copy-start.9 = (bf16[8,144,128]{2,1,0:T(8,128)(2,1)}, bf16[8,144,128]{2,1,0:T(8,128)(2,1)S(1)}, u32[]{:S(2)}) copy-start(bf16[8,144,128]{2,1,0:T(8,128)(2,1)S(1)} %collective-permute-done.2.refs_1_) | copy-start | bytes 884740
  14.8 8.5 %copy-start.10 = (bf16[8,144,128]{2,1,0:T(8,128)(2,1)}, bf16[8,144,128]{2,1,0:T(8,128)(2,1)S(1)}, u32[]{:S(2)}) copy-start(bf16[8,144,128]{2,1,0:T(8,128)(2,1)S(1)} %collective-permute-done.1.refs_3_) | copy-start | bytes 884740
  18.2 5.1 %copy-start.11 = (bf16[8,144,128]{2,1,0:T(8,128)(2,1)}, bf16[8,144,128]{2,1,0:T(8,128)(2,1)S(1)}, u32[]{:S(2)}) copy-start(bf16[8,144,128]{2,1,0:T(8,128)(2,1)S(1)} %collective-permute-done.refs_2_) | copy-start | bytes 884740
  18.3 13.7 %collective-permute-start.4 = (bf16[2,8,144,128]{3,2,1,0:T(8,128)(2,1)S(1)}, bf16[2,8,144,128]{3,2,1,0:T(8,128)(2,1)S(1)}, u32[]{:S(2)}, u32[]{:S(2)}) collective-permute-start(bf16[2,8,144,128]{3,2,1,0:T(8,128)(2,1)S(1)} %get-tuple-element.79), channel_id=1, source_target_pairs={{0,56},{8,0},{16,8},{24,16},{32,24},{40,32},{48,40},{56,48},{1,57}... | collective-permute-start | bytes 1769480 | tf_op jit(solution)/shard_map/ppermute | solution.py:42
  18.6 14.8 %collective-permute-start.3 = (bf16[2,8,144,128]{3,2,1,0:T(8,128)(2,1)S(1)}, bf16[2,8,144,128]{3,2,1,0:T(8,128)(2,1)S(1)}, u32[]{:S(2)}, u32[]{:S(2)}) collective-permute-start(bf16[2,8,144,128]{3,2,1,0:T(8,128)(2,1)S(1)} %get-tuple-element.80), channel_id=1, source_target_pairs={{0,8},{8,16},{16,24},{24,32},{32,40},{40,48},{48,56},{56,0},{1,9},... | collective-permute-start | bytes 1769480 | tf_op jit(solution)/shard_map/ppermute | solution.py:37
  20.4 13.3 %collective-permute-start.9 = (bf16[512,512]{1,0:T(8,128)(2,1)S(1)}, bf16[512,512]{1,0:T(8,128)(2,1)S(1)}, u32[]{:S(2)}, u32[]{:S(2)}) collective-permute-start(bf16[512,512]{1,0:T(8,128)(2,1)S(1)} %copy-done.18), channel_id=1, source_target_pairs={{0,6},{2,4},{4,2},{6,0},{1,7},{3,5},{5,3},{7,1},{8,14},{10,12},{12... | collective-permute-start | bytes 1572872 | tf_op jit(solution)/shard_map/ppermute | solution.py:30
  22.6 14.9 %collective-permute-start.8 = (bf16[512,512]{1,0:T(8,128)(2,1)S(1)}, bf16[512,512]{1,0:T(8,128)(2,1)S(1)}, u32[]{:S(2)}, u32[]{:S(2)}) collective-permute-start(bf16[512,512]{1,0:T(8,128)(2,1)S(1)} %copy-done.18), channel_id=1, source_target_pairs={{0,4},{4,0},{1,5},{5,1},{2,6},{6,2},{3,7},{7,3},{8,12},{12,8},{9,1... | collective-permute-start | bytes 1572872 | tf_op jit(solution)/shard_map/ppermute | solution.py:29
  23.4 23.8 %collective-permute-start.11 = (bf16[608,512]{1,0:T(8,128)(2,1)S(1)}, bf16[608,512]{1,0:T(8,128)(2,1)S(1)}, u32[]{:S(2)}, u32[]{:S(2)}) collective-permute-start(bf16[608,512]{1,0:T(8,128)(2,1)S(1)} %slice.20), channel_id=1, source_target_pairs={{0,4},{4,0},{1,5},{5,1},{2,6},{6,2},{3,7},{7,3},{8,12},{12,8},{9,1... | collective-permute-start | bytes 1867784 | tf_op jit(solution)/shard_map/ppermute | solution.py:349
  31.9 16.7 %copy-start.6 = (bf16[2,8,144,128]{3,2,1,0:T(8,128)(2,1)}, bf16[2,8,144,128]{3,2,1,0:T(8,128)(2,1)S(1)}, u32[]{:S(2)}) copy-start(bf16[2,8,144,128]{3,2,1,0:T(8,128)(2,1)S(1)} %collective-permute-done.4.refs_5_) | copy-start | bytes 1769476
  33.4 15.2 %copy-start.12 = (bf16[2,8,144,128]{3,2,1,0:T(8,128)(2,1)}, bf16[2,8,144,128]{3,2,1,0:T(8,128)(2,1)S(1)}, u32[]{:S(2)}) copy-start(bf16[2,8,144,128]{3,2,1,0:T(8,128)(2,1)S(1)} %collective-permute-done.3.refs_4_) | copy-start | bytes 1769476
  33.4 15.2 %collective-permute-start.5 = (bf16[2,8,144,128]{3,2,1,0:T(8,128)(2,1)S(1)}, bf16[2,8,144,128]{3,2,1,0:T(8,128)(2,1)S(1)}, u32[]{:S(2)}, u32[]{:S(2)}) collective-permute-start(bf16[2,8,144,128]{3,2,1,0:T(8,128)(2,1)S(1)} %collective-permute-done.3.refs_4_), channel_id=1, source_target_pairs={{0,8},{8,16},{16,24},{24,32},{32,40},{40,48},{48,56},{56,0},{1,9},... | collective-permute-start | bytes 1769480 | tf_op jit(solution)/shard_map/ppermute | solution.py:37
  37.4 11.2 %collective-permute-start.10 = (bf16[512,512]{1,0:T(8,128)(2,1)S(1)}, bf16[512,512]{1,0:T(8,128)(2,1)S(1)}, u32[]{:S(2)}, u32[]{:S(2)}) collective-permute-start(bf16[512,512]{1,0:T(8,128)(2,1)S(1)} %collective-permute-done.8), channel_id=1, source_target_pairs={{0,6},{2,4},{4,2},{6,0},{1,7},{3,5},{5,3},{7,1},{8,14},{10,12},{12... | collective-permute-start | bytes 1572872 | tf_op jit(solution)/shard_map/ppermute | solution.py:46
  38.5 8.7 %collective-permute-start.7 = (bf16[8,144,128]{2,1,0:T(8,128)(2,1)S(1)}, bf16[8,144,128]{2,1,0:T(8,128)(2,1)}, u32[]{:S(2)}, u32[]{:S(2)}) collective-permute-start(bf16[8,144,128]{2,1,0:T(8,128)(2,1)S(1)} %get-tuple-element.75), channel_id=1, source_target_pairs={{0,56},{8,0},{16,8},{24,16},{32,24},{40,32},{48,40},{56,48},{1,57}... | collective-permute-start | bytes 884744 | tf_op jit(solution)/shard_map/ppermute | solution.py:39
  40.1 8.5 %collective-permute-start.6 = (bf16[8,144,128]{2,1,0:T(8,128)(2,1)S(1)}, bf16[8,144,128]{2,1,0:T(8,128)(2,1)S(1)}, u32[]{:S(2)}, u32[]{:S(2)}) collective-permute-start(bf16[8,144,128]{2,1,0:T(8,128)(2,1)S(1)} %get-tuple-element.76), channel_id=1, source_target_pairs={{0,56},{8,0},{16,8},{24,16},{32,24},{40,32},{48,40},{56,48},{1,57}... | collective-permute-start | bytes 884744 | tf_op jit(solution)/shard_map/ppermute | solution.py:40
  48.6 6.5 %copy-start.13 = (bf16[2,8,144,128]{3,2,1,0:T(8,128)(2,1)}, bf16[2,8,144,128]{3,2,1,0:T(8,128)(2,1)S(1)}, u32[]{:S(2)}) copy-start(bf16[2,8,144,128]{3,2,1,0:T(8,128)(2,1)S(1)} %collective-permute-done.5.refs_6_) | copy-start | bytes 1769476
  49.6 18.5 %copy-start.5 = (bf16[4,512,512]{2,1,0:T(8,128)(2,1)}, bf16[4,512,512]{2,1,0:T(8,128)(2,1)S(1)}, u32[]{:S(2)}) copy-start(bf16[4,512,512]{2,1,0:T(8,128)(2,1)S(1)} %pad_maximum_fusion.refs_12_) | copy-start | bytes 6291460
  49.6 14.9 %copy-start.19 = (s32[64]{0:T(128)S(1)}, s32[64]{0:T(128)}, u32[]{:S(2)}) copy-start(s32[64]{0:T(128)} %param.11) | copy-start | bytes 772
  49.6 21.9 %collective-permute-start.15 = (bf16[4,512,512]{2,1,0:T(8,128)(2,1)S(1)}, bf16[4,512,512]{2,1,0:T(8,128)(2,1)}, u32[]{:S(2)}, u32[]{:S(2)}) collective-permute-start(bf16[4,512,512]{2,1,0:T(8,128)(2,1)S(1)} %pad_maximum_fusion.refs_12_), channel_id=1, source_target_pairs={{0,1},{1,0},{2,3},{3,2},{4,5},{5,4},{6,7},{7,6},{8,9},{9,8},{10,11... | collective-permute-start | bytes 6291464 | tf_op jit(solution)/shard_map/ppermute | solution.py:50
  49.8 11.0 %collective-permute-start.13 = (bf16[8,144,128]{2,1,0:T(8,128)(2,1)}, bf16[8,144,128]{2,1,0:T(8,128)(2,1)}, u32[]{:S(2)}, u32[]{:S(2)}) collective-permute-start(bf16[8,144,128]{2,1,0:T(8,128)(2,1)} %collective-permute-done.7.refs_8_), channel_id=1, source_target_pairs={{0,56},{8,0},{16,8},{24,16},{32,24},{40,32},{48,40},{56,48},{1,57}... | collective-permute-start | bytes 884744 | tf_op jit(solution)/shard_map/ppermute | solution.py:65
  54.5 16.5 %collective-permute-start.16 = (bf16[608,512]{1,0:T(8,128)(2,1)}, bf16[608,512]{1,0:T(8,128)(2,1)}, u32[]{:S(2)}, u32[]{:S(2)}) collective-permute-start(bf16[608,512]{1,0:T(8,128)(2,1)} %pad_maximum_fusion.3), channel_id=1, source_target_pairs={{0,4},{4,0},{1,5},{5,1},{2,6},{6,2},{3,7},{7,3},{8,12},{12,8},{9,1... | collective-permute-start | bytes 1867784 | tf_op jit(solution)/shard_map/ppermute | solution.py:350
  55.1 16.4 %collective-permute-start.12 = (bf16[2,8,144,128]{3,2,1,0:T(8,128)(2,1)S(1)}, bf16[2,8,144,128]{3,2,1,0:T(8,128)(2,1)S(1)}, u32[]{:S(2)}, u32[]{:S(2)}) collective-permute-start(bf16[2,8,144,128]{3,2,1,0:T(8,128)(2,1)S(1)} %collective-permute-done.5.refs_6_), channel_id=1, source_target_pairs={{0,8},{8,16},{16,24},{24,32},{32,40},{40,48},{48,56},{56,0},{1,9},... | collective-permute-start | bytes 1769480 | tf_op jit(solution)/shard_map/ppermute | solution.py:60
  60.8 10.1 %collective-permute-start.14 = (bf16[8,144,128]{2,1,0:T(8,128)(2,1)}, bf16[8,144,128]{2,1,0:T(8,128)(2,1)S(1)}, u32[]{:S(2)}, u32[]{:S(2)}) collective-permute-start(bf16[8,144,128]{2,1,0:T(8,128)(2,1)} %collective-permute-done.13.refs_10_), channel_id=1, source_target_pairs={{0,56},{8,0},{16,8},{24,16},{32,24},{40,32},{48,40},{56,48},{1,57}... | collective-permute-start | bytes 884744 | tf_op jit(solution)/shard_map/ppermute | solution.py:65
  72.3 21.4 %copy-start = (bf16[512,4096]{1,0:T(8,128)(2,1)S(1)}, bf16[512,4096]{1,0:T(8,128)(2,1)}, u32[]{:S(2)}) copy-start(bf16[512,4096]{1,0:T(8,128)(2,1)} %head_ref.3) | copy-start | bytes 12582916
  95.3 19.9 %all-to-all-start.1 = ((bf16[16,64,256]{2,1,0:T(8,128)(2,1)}), bf16[16,64,256]{2,1,0:T(8,128)(2,1)}, u32[]{:S(2)}, u32[]{:S(2)}) async-start(bf16[16,64,256]{2,1,0:T(8,128)(2,1)} %logits_slices.1), calls=%async_computation.1 | async-start | bytes 1048576 | tf_op jit(solution)/shard_map/all_to_all | solution.py:366
  135.3 12.0 %copy-start.2 = (bf16[512,64]{0,1:T(8,128)(2,1)S(1)}, bf16[512,64]{0,1:T(8,128)(2,1)}, u32[]{:S(2)}) copy-start(bf16[512,64]{0,1:T(8,128)(2,1)} %param.13) | copy-start | bytes 196612
  135.3 12.0 %copy-start.3 = (bf16[64,512]{1,0:T(8,128)(2,1)S(1)}, bf16[64,512]{1,0:T(8,128)(2,1)}, u32[]{:S(2)}) copy-start(bf16[64,512]{1,0:T(8,128)(2,1)} %slice.19.other_ref) | copy-start | bytes 196612
  (6 other events, 9.5 us)
